TPU v7x, 512 devices: a whole 4x8x8 slice. The times are simulated.
512 devices in a mesh: vel: 8 (over x, z_hi), sx: 8 (over y), sy: 8 (over z_lo, core).
Axes of the slice: x: 4, y: 8, z: 8 (z_hi: 2, z_lo: 4; z = z_hi * 4 + z_lo), core: 2. Of those that a mesh axis runs over, the one named last changes fastest.
Arguments:
- distribution: bfloat16 [24, 256, 32768], P('sx', 'sy', 'vel'), may hold values from 0.05 to 5, as said below
- plane_weights: bfloat16 [1024, 1024], P(('sx', 'sy')), may hold values from -0.1875 to 0.1875
- depth_weights: bfloat16 [32, 32], replicated, may hold values from -1 to 1
Outputs:
- advanced: bfloat16 [24, 256, 32768], P('sx', 'sy', 'vel')
Inputs may be any that keep to these rules, and one draw needn't show every extreme that they name: `distribution`: every entry is positive.
All inputs are finite; a program needn't handle non-finite values.
Results may differ from a plain program's by a relative error of at most 0.0028.
Values may be sent and summed in bfloat16 or wider, within the bound.
No kernel may reach another device: no remote copies, remote signals or barrier semaphores. Data moves between devices by JAX's collectives and lax.ppermute only.
A program may use at most 64 MiB of HBM per device.

v0:
```python
import jax
import jax.numpy as jnp
from jax import lax
from jax.sharding import PartitionSpec as P

NVZ = 32
NVX = 32
NVY = 32


COURANT = 0.45
RELAX_RATE = 0.3


def extended(block, sides, width):
    for axis, dim in sides:
        count = lax.axis_size(axis)
        forward = [(i, i + 1) for i in range(count - 1)]
        forward.append((count - 1, 0))
        backward = [(target, source) for source, target in forward]
        low = lax.ppermute(
            lax.slice_in_dim(block, block.shape[dim] - width, None, axis=dim), axis, forward
        )
        high = lax.ppermute(lax.slice_in_dim(block, 0, width, axis=dim), axis, backward)
        block = jnp.concatenate([low, block, high], axis=dim)
    return block


def plane_speeds():
    lane_ids = jnp.arange(NVX * NVY, dtype=jnp.int32)
    speed_across = ((lane_ids // NVY).astype(jnp.float32) - (NVX - 1) / 2.0) * (8.0 / NVX)
    speed_along = ((lane_ids % NVY).astype(jnp.float32) - (NVY - 1) / 2.0) * (8.0 / NVY)
    return (speed_across, speed_along)


def maxwellian(
    particle_concentration,
    momentum_across,
    momentum_along,
    momentum_depth,
    motion_work_content,
    speed_across,
    speed_along,
    speed_depth,
):
    mean_flow_transverse = momentum_across / particle_concentration
    mean_flow_streamwise = momentum_along / particle_concentration
    mean_flow_vertical = momentum_depth / particle_concentration
    cell_heat_level = (
        motion_work_content / particle_concentration
        - (mean_flow_transverse**2 + mean_flow_streamwise**2 + mean_flow_vertical**2)
    ) / 3.0
    speed_grid_cell_measure = 8.0 / NVX * (8.0 / NVY) * (8.0 / NVZ)
    scaling_divisor = (
        particle_concentration * speed_grid_cell_measure / (2.0 * jnp.pi * cell_heat_level) ** 1.5
    )
    maxwellian_width = (speed_across - mean_flow_transverse[:, None, None]) ** 2
    maxwellian_width = maxwellian_width + (speed_along - mean_flow_streamwise[:, None, None]) ** 2
    maxwellian_width = (
        maxwellian_width + (speed_depth[:, None] - mean_flow_vertical[:, None, None]) ** 2
    )
    return scaling_divisor[:, None, None] * jnp.exp(
        -maxwellian_width / (2.0 * cell_heat_level[:, None, None])
    )


def local(distribution, plane_weights, depth_weights):
    tile_rows, tile_cols, local_width = distribution.shape
    lanes_total = NVX * NVY
    depth_local = local_width // lanes_total
    cell_count = tile_rows * tile_cols
    plane_offset = lax.axis_index("vel") * depth_local
    speed_across, speed_along = plane_speeds()
    depth_ids = (plane_offset + jnp.arange(depth_local, dtype=jnp.int32)).astype(jnp.float32)
    speed_depth = (depth_ids - (NVZ - 1) / 2.0) * (8.0 / NVZ)
    lattice = distribution.reshape(tile_rows, tile_cols, depth_local, lanes_total)
    current = lattice.astype(jnp.float32)
    values = current.reshape(cell_count, depth_local, lanes_total)
    squared = speed_across**2 + speed_along**2 + speed_depth[:, None] ** 2
    particle_concentration = jnp.sum(values, axis=(1, 2))
    momentum_across = jnp.sum(values * speed_across, axis=(1, 2))
    momentum_along = jnp.sum(values * speed_along, axis=(1, 2))
    momentum_depth = jnp.sum(values * speed_depth[:, None], axis=(1, 2))
    motion_work_content = jnp.sum(values * squared, axis=(1, 2))
    particle_concentration, momentum_across, momentum_along, momentum_depth, motion_work_content = (
        lax.psum(
            (
                particle_concentration,
                momentum_across,
                momentum_along,
                momentum_depth,
                motion_work_content,
            ),
            "vel",
        )
    )
    equilibrium = maxwellian(
        particle_concentration,
        momentum_across,
        momentum_along,
        momentum_depth,
        motion_work_content,
        speed_across,
        speed_along,
        speed_depth,
    )
    deviation = (equilibrium - values).astype(jnp.bfloat16)
    mixed_plane = jnp.einsum(
        "czb,ab->cza",
        deviation,
        lax.all_gather(plane_weights, ("sx", "sy"), axis=0, tiled=True),
        preferred_element_type=jnp.float32,
    ).astype(jnp.bfloat16)
    own_rows = lax.dynamic_slice_in_dim(depth_weights, plane_offset, depth_local, 0)
    collision = jnp.einsum(
        "zw,cwk->czk",
        own_rows,
        lax.all_gather(mixed_plane, "vel", axis=1, tiled=True),
        preferred_element_type=jnp.float32,
    ).astype(jnp.bfloat16)
    collision = lax.optimization_barrier(collision).astype(jnp.float32)
    collision = collision.reshape(tile_rows, tile_cols, depth_local, lanes_total)
    positive_across = jnp.maximum(speed_across, 0.0)
    negative_across = jnp.minimum(speed_across, 0.0)
    padded = extended(lattice, (("sx", 0), ("sy", 1)), 1)
    lower_row = padded[:-2, 1:-1].astype(jnp.float32)
    upper_row = padded[2:, 1:-1].astype(jnp.float32)
    left_column = padded[1:-1, :-2].astype(jnp.float32)
    right_column = padded[1:-1, 2:].astype(jnp.float32)
    across = positive_across * (current - lower_row) + negative_across * (upper_row - current)
    along = jnp.maximum(speed_along, 0.0) * (current - left_column) + jnp.minimum(
        speed_along, 0.0
    ) * (right_column - current)
    courant_across = COURANT / (4.0 - 4.0 / NVX)
    courant_along = COURANT / (4.0 - 4.0 / NVY)
    advanced = current - (courant_across * across + courant_along * along) + RELAX_RATE * collision
    return advanced.reshape(tile_rows, tile_cols, local_width).astype(jnp.bfloat16)


def solution(mesh):
    return jax.shard_map(
        local,
        mesh=mesh,
        in_specs=(P("sx", "sy", "vel"), P(("sx", "sy"), None), P()),
        out_specs=P("sx", "sy", "vel"),
        check_vma=False,
    )
```

profile of v0, /device:TPU:56, one launch (start us, length us, event | category | flops | bytes accessed | tf_op | source)
XLA Modules:
  0.0 298.2 jit_solution(4032208354417458388)
XLA Ops:
  6.5 0.0 copy-start
  6.5 0.0 copy-start.1
  6.5 0.0 all-gather.3.cloned.1.call-start
  6.5 0.7 all-gather.3.cloned.1.call-update
  7.3 0.0 all-gather.5.cloned.1.call-start
  7.3 2.3 reshape.215
  9.7 0.1 broadcast_bitcast_fusion
  9.8 0.1 add.177
  9.9 0.0 copy-done.1
  9.9 0.7 fusion.4
  10.6 0.1 reduce_sum.56
  10.6 0.1 reduce_sum.58
  10.7 0.1 reduce_sum.60
  10.8 0.1 reduce_sum.62
  10.9 0.1 reduce_sum.64
  11.0 35.1 %all-reduce = (f32[96]{0:T(128)S(1)}, f32[96]{0:T(128)S(1)}, f32[96]{0:T(128)S(1)}, f32[96]{0:T(128)S(1)}, f32[96]{0:T(128)S(1)}) all-reduce(f32[96]{0:T(128)S(1)} %reduce_sum.64, f32[96]{0:T(128)S(1)} %reduce_sum.56, f32[96]{0:T(128)S(1)} %reduce_sum.62, f32[96]{0:T(128)S(1)} %reduce_sum.60, ...), channel_id=1, replica_groups=mesh['vel'=8,'sx'=8,'sy'=8] {'vel'}, use_global_device_ids=true, to_apply=%region_9.10 | all-reduce | flops 480 | bytes 3840 | tf_op jit(solution)/shard_map/psum | solution.py:86
  46.2 0.1 subtract_multiply_fusion
  46.2 0.1 multiply_add_fusion
  46.4 83.4 %all-gather.3.cloned.1.call-done = bf16[1024,1024]{1,0:T(8,128)(2,1)} async-done(((bf16[16,1024]{1,0:T(8,128)(2,1)}), bf16[1024,1024]{1,0:T(8,128)(2,1)}) %all-gather.3.cloned.1.call-update) | async-done | bytes 2097168 | tf_op jit(solution)/shard_map/all_gather | solution.py:111
  129.8 4.4 %fusion.20 = bf16[96,4,1024]{2,0,1:T(8,128)(2,1)} fusion(bf16[1024,1024]{1,0:T(8,128)(2,1)} %all-gather.3.cloned.1.call-done, f32[96,4,1024]{2,1,0:T(4,128)S(1)} %reshape.215, f32[96]{0:T(128)S(1)} %broadcast_multiply_fusion, f32[96,4]{0,1:T(4,128)S(1)} %subtract_multiply_fusion, f32[96,1024]{1,0:T(8,128)S(1)} %multiply_add_fusion, f32[96]{0:T(128)S(1)} %get-tuple-element.15), kind=kOutput, calls=%fused_computation.31 | convolution fusion | flops 808058880 | bytes 4851968 | tf_op jit(solution)/shard_map/czb,ab->cza/dot_general | solution.py:108
  134.1 0.0 all-gather.5.cloned.1.call-update
  134.2 0.2 slice.35
  134.4 4.6 %collective-permute-start = (bf16[1,32,4,1024]{3,2,1,0:T(4,128)(2,1)S(1)}, bf16[1,32,4,1024]{3,2,1,0:T(4,128)(2,1)S(1)}, u32[]{:S(2)}, u32[]{:S(2)}) collective-permute-start(bf16[1,32,4,1024]{3,2,1,0:T(4,128)(2,1)S(1)} %slice.35), channel_id=1, source_target_pairs={{0,8},{8,16},{16,24},{24,32},{32,40},{40,48},{48,56},{56,0},{1,9},... | collective-permute-start | bytes 786440 | tf_op jit(solution)/shard_map/ppermute | solution.py:21
  139.0 0.9 slice.38
  139.9 1.9 collective-permute-start.1
  141.8 0.6 reshape.214
  142.4 2.5 collective-permute-done
  144.9 0.1 constant_dynamic-update-slice_fusion.2
  145.0 0.4 constant_dynamic-update-slice_fusion.1
  145.4 5.9 %collective-permute-done.1 = bf16[1,32,4,1024]{3,2,1,0:T(4,128)(2,1)S(1)} collective-permute-done((bf16[1,32,4,1024]{3,2,1,0:T(4,128)(2,1)}, bf16[1,32,4,1024]{3,2,1,0:T(4,128)(2,1)S(1)}, u32[]{:S(2)}, u32[]{:S(2)}) %collective-permute-start.1) | collective-permute-done | bytes 262176 | tf_op jit(solution)/shard_map/ppermute | solution.py:24
  151.4 0.1 constant_dynamic-update-slice_fusion
  151.5 0.6 fusion.48
  152.1 1.9 collective-permute-start.2
  154.0 5.6 %collective-permute-start.3 = (bf16[5,1,4,1024]{3,2,1,0:T(4,128)(2,1)S(1)}, bf16[5,1,4,1024]{3,2,1,0:T(4,128)(2,1)S(1)}, u32[]{:S(2)}, u32[]{:S(2)}) collective-permute-start(bf16[5,1,4,1024]{3,2,1,0:T(4,128)(2,1)S(1)} %get-tuple-element.21), channel_id=1, source_target_pairs={{1,0},{2,1},{3,2},{4,3},{5,4},{6,5},{7,6},{0,7},{9,8},{10,9},{11,1... | collective-permute-start | bytes 122888 | tf_op jit(solution)/shard_map/ppermute | solution.py:24
  159.7 120.8 %all-gather.5.cloned.1.call-done = bf16[96,32,1024]{2,0,1:T(8,128)(2,1)} async-done(((bf16[96,4,1024]{2,0,1:T(8,128)(2,1)}), bf16[96,32,1024]{2,0,1:T(8,128)(2,1)}) %all-gather.5.cloned.1.call-update) | async-done | bytes 6291472 | tf_op jit(solution)/shard_map/all_gather | solution.py:118
  280.5 0.0 copy-done
  280.5 6.4 %fusion.23 = bf16[96,4,1024]{2,1,0:T(4,128)(2,1)S(1)} fusion(bf16[96,32,1024]{2,0,1:T(8,128)(2,1)} %all-gather.5.cloned.1.call-done, bf16[32,32]{1,0:T(8,128)(2,1)S(1)} %copy-done, s32[]{:T(128)S(6)} %select_n.59), kind=kOutput, calls=%fused_computation.32 | convolution fusion | flops 25559040 | bytes 7078916 | tf_op jit(solution)/shard_map/zw,cwk->czk/dot_general | solution.py:115
  286.9 0.5 convert_multiply_fusion.4
  287.3 0.0 collective-permute-done.2
  287.4 0.0 collective-permute-done.3
  287.4 2.6 add_convert_fusion
  289.9 1.5 convert_element_type.123
  (16 shorter events, 0.1 us)
Async XLA Ops:
  6.5 273.9 %copy-start = (bf16[32,32]{1,0:T(8,128)(2,1)S(1)}, bf16[32,32]{1,0:T(8,128)(2,1)}, u32[]{:S(2)}) copy-start(bf16[32,32]{1,0:T(8,128)(2,1)} %param.5) | copy-start | bytes 6148
  6.5 3.3 %copy-start.1 = (bf16[3,32,4096]{2,1,0:T(8,128)(2,1)S(1)}, bf16[3,32,4096]{2,1,0:T(8,128)(2,1)}, u32[]{:S(2)}) copy-start(bf16[3,32,4096]{2,1,0:T(8,128)(2,1)} %param.3) | copy-start | bytes 2359300
  6.5 123.3 %all-gather.3.cloned.1.call-start = ((), (), s32[]{:S(2)}) async-start(), calls=%async_computation | async-start | bytes 2129920 | tf_op jit(solution)/shard_map/all_gather | solution.py:111
  7.3 273.2 %all-gather.5.cloned.1.call-start = ((), (), s32[]{:S(2)}) async-start(), calls=%async_computation.1 | async-start | bytes 7077888 | tf_op jit(solution)/shard_map/all_gather | solution.py:118
  134.4 10.6 %collective-permute-start = (bf16[1,32,4,1024]{3,2,1,0:T(4,128)(2,1)S(1)}, bf16[1,32,4,1024]{3,2,1,0:T(4,128)(2,1)S(1)}, u32[]{:S(2)}, u32[]{:S(2)}) collective-permute-start(bf16[1,32,4,1024]{3,2,1,0:T(4,128)(2,1)S(1)} %slice.35), channel_id=1, source_target_pairs={{0,8},{8,16},{16,24},{24,32},{32,40},{40,48},{48,56},{56,0},{1,9},... | collective-permute-start | bytes 786440 | tf_op jit(solution)/shard_map/ppermute | solution.py:21
  139.9 11.5 %collective-permute-start.1 = (bf16[1,32,4,1024]{3,2,1,0:T(4,128)(2,1)}, bf16[1,32,4,1024]{3,2,1,0:T(4,128)(2,1)S(1)}, u32[]{:S(2)}, u32[]{:S(2)}) collective-permute-start(bf16[1,32,4,1024]{3,2,1,0:T(4,128)(2,1)} %slice.38), channel_id=1, source_target_pairs={{8,0},{16,8},{24,16},{32,24},{40,32},{48,40},{56,48},{0,56},{9,1},... | collective-permute-start | bytes 786440 | tf_op jit(solution)/shard_map/ppermute | solution.py:24
  152.1 135.2 %collective-permute-start.2 = (bf16[5,1,4,1024]{3,2,1,0:T(4,128)(2,1)}, bf16[5,1,4,1024]{3,2,1,0:T(4,128)(2,1)S(1)}, u32[]{:S(2)}, u32[]{:S(2)}) collective-permute-start(bf16[5,1,4,1024]{3,2,1,0:T(4,128)(2,1)} %get-tuple-element.20), channel_id=1, source_target_pairs={{0,1},{1,2},{2,3},{3,4},{4,5},{5,6},{6,7},{7,0},{8,9},{9,10},{10,1... | collective-permute-start | bytes 122888 | tf_op jit(solution)/shard_map/ppermute | solution.py:21
  154.0 133.3 %collective-permute-start.3 = (bf16[5,1,4,1024]{3,2,1,0:T(4,128)(2,1)S(1)}, bf16[5,1,4,1024]{3,2,1,0:T(4,128)(2,1)S(1)}, u32[]{:S(2)}, u32[]{:S(2)}) collective-permute-start(bf16[5,1,4,1024]{3,2,1,0:T(4,128)(2,1)S(1)} %get-tuple-element.21), channel_id=1, source_target_pairs={{1,0},{2,1},{3,2},{4,3},{5,4},{6,5},{7,6},{0,7},{9,8},{10,9},{11,1... | collective-permute-start | bytes 122888 | tf_op jit(solution)/shard_map/ppermute | solution.py:24
Sparse Core Ops, SparseCore 0:
  9.5 120.2 all-gather.2
  134.3 146.1 all-gather.4
where the time goes:
time: 300 us; the launch traced here: 298 us
  waiting for transfers between devices  213 us (71%)
  blocking collectives  35.1 us (12%)
  starting transfers between devices  14.1 us (5%)
  between operations  13.6 us (5%)
  matrix products  10.8 us (4%)
  local copies, waits for them, and re-layouts  7.24 us (2%)
  other arithmetic  3.97 us (1%)
    all_gather x1, waiting for transfers between devices, local(): lax.all_gather(mixed_plane, 'vel', axis=1, tiled=True)  121 us
    all_gather x1, waiting for transfers between devices, local(): lax.all_gather(plane_weights, ('sx', 'sy'), axis=0, tiled=True)  83.4 us
    psum x1, blocking collectives, local(): lax.psum((particle_concentration, momentum_across, momentum_along, moment...  35.1 us
    ppermute x2, starting transfers between devices, extended(): lax.ppermute(lax.slice_in_dim(block, 0, width, axis=dim), axis, backward)  7.53 us
    ppermute x2, starting transfers between devices, extended(): lax.ppermute(lax.slice_in_dim(block, block.shape[dim] - width, None, axis...  6.5 us
    dot_general x1, matrix products, local(): jnp.einsum('zw,cwk->czk', own_rows, lax.all_gather(mixed_plane, 'vel', ax...  6.4 us
  transfers between devices with their start and end apart: 6, of which 4 were waited for; matrix products, arithmetic and copies ran while one was open for 5% of the time, Pallas kernels for 0%

commit v1 on v0

v1 whole, which is shorter than its diff:
```python
import functools

import jax
import jax.numpy as jnp
from jax import lax
from jax.experimental import pallas as pl
from jax.experimental.pallas import tpu as pltpu
from jax.sharding import PartitionSpec as P

NVZ = 32
NVX = 32
NVY = 32
NXY = NVX * NVY
COURANT = 0.45
RELAX_RATE = 0.3
ROWS = 3
COLS = 32
CELLS = ROWS * COLS
PLANES = 4
GROUP = 8
BLOCK = NXY // GROUP
DATA = PLANES * CELLS
CHUNK = DATA + 16
TILE = 16
F32 = jnp.float32
BF16 = jnp.bfloat16


def speed(index, count):
    return (index.astype(F32) - (count - 1) / 2.0) * (8.0 / count)


def lane_speeds(shape, offset):
    lane = lax.broadcasted_iota(jnp.int32, shape, len(shape) - 1) + offset
    return speed(lane // NVY, NVX), speed(lane % NVY, NVY)


def vmem():
    return pl.BlockSpec(memory_space=pltpu.VMEM)


def smem():
    return pl.BlockSpec(memory_space=pltpu.SMEM)


def pack_kernel(place_ref, f_ref, send_ref, low_ref, high_ref, first_ref, last_ref):
    for v in range(GROUP):
        for p in range(PLANES):
            for r in range(ROWS):
                send_ref[v, p * CELLS + r * COLS : p * CELLS + (r + 1) * COLS, :] = f_ref[
                    r, :, p * NXY + v * BLOCK : p * NXY + (v + 1) * BLOCK
                ]
    row = lax.broadcasted_iota(jnp.int32, (16, NXY), 0)
    kind = row % 5
    vx, vy = lane_speeds((16, NXY), 0)
    squared = vx * vx + vy * vy
    rough = squared.astype(BF16).astype(F32)
    one = jnp.ones((16, NXY), F32)
    basis = jnp.where(kind == 1, vx, jnp.where(kind == 2, vy, jnp.where(kind == 4, rough, one)))
    basis = basis.astype(BF16)
    rest = jnp.where(kind == 4, squared - rough, 0.0 * one).astype(BF16)
    contract = (((1,), (1,)), ((), ()))
    column = lax.broadcasted_iota(jnp.int32, (16, CELLS), 0)
    column_kind = column % 5
    total = jnp.zeros((16, CELLS), F32)
    first_plane = place_ref[0] * PLANES
    for p in range(PLANES):
        x = jnp.concatenate([f_ref[r, :, p * NXY : (p + 1) * NXY] for r in range(ROWS)], axis=0)
        sums = lax.dot_general(basis, x, contract, preferred_element_type=F32)
        sums = sums + lax.dot_general(rest, x, contract, preferred_element_type=F32)
        density = lax.dot_general(jnp.ones((16, NXY), BF16), x, contract, preferred_element_type=F32)
        vz = speed(first_plane + p, NVZ)
        total = total + jnp.where(
            column_kind == 3, vz * density, jnp.where(column_kind == 4, sums + vz * vz * density, sums)
        )
    high = total.astype(BF16).astype(F32)
    middle = (total - high).astype(BF16).astype(F32)
    low = (total - high) - middle
    parts = jnp.where(
        column < 5, high, jnp.where(column < 10, middle, jnp.where(column < 15, low, 0.0))
    )
    parts = jnp.concatenate([parts, jnp.zeros((16, 128 - CELLS), F32)], axis=1).astype(BF16)
    for v in range(GROUP):
        send_ref[v, DATA:CHUNK, :] = parts
    for p in range(PLANES):
        half = NXY // 2
        high_ref[:, p * half : (p + 1) * half] = f_ref[ROWS - 1, :, p * NXY + half : (p + 1) * NXY]
        low_ref[:, p * half : (p + 1) * half] = f_ref[0, :, p * NXY : p * NXY + half]
    edge_row = lax.broadcasted_iota(jnp.int32, (8, PLANES * NXY), 0)
    first = jnp.zeros((8, PLANES * NXY), F32)
    last = jnp.zeros((8, PLANES * NXY), F32)
    for r in range(ROWS):
        a = f_ref[r, 0:8, :].astype(F32)[0:1, :]
        b = f_ref[r, COLS - 8 : COLS, :].astype(F32)[7:8, :]
        first = jnp.where(edge_row == r, a, first)
        last = jnp.where(edge_row == r, b, last)
    first_ref[...] = first.astype(BF16)
    last_ref[...] = last.astype(BF16)


def pack(place, f):
    return pl.pallas_call(
        pack_kernel,
        out_shape=(
            jax.ShapeDtypeStruct((GROUP, CHUNK, BLOCK), BF16),
            jax.ShapeDtypeStruct((COLS, PLANES * NXY // 2), BF16),
            jax.ShapeDtypeStruct((COLS, PLANES * NXY // 2), BF16),
            jax.ShapeDtypeStruct((8, PLANES * NXY), BF16),
            jax.ShapeDtypeStruct((8, PLANES * NXY), BF16),
        ),
        in_specs=[smem(), vmem()],
        out_specs=(vmem(),) * 5,
        name="pack",
    )(place, f)


def spread_kernel(depth_ref, out_ref):
    size = NVZ * TILE
    row = lax.broadcasted_iota(jnp.int32, (size, NVZ), 0)
    col = lax.broadcasted_iota(jnp.int32, (size, NVZ), 1)
    pick = jnp.where(row // TILE == col, 1.0, 0.0).astype(BF16)
    left = jnp.dot(pick, depth_ref[...], preferred_element_type=F32).astype(BF16)
    full = lax.dot_general(left, pick, (((1,), (1,)), ((), ())), preferred_element_type=F32)
    i = lax.broadcasted_iota(jnp.int32, (size, size), 0)
    j = lax.broadcasted_iota(jnp.int32, (size, size), 1)
    out_ref[...] = jnp.where(i % TILE == j % TILE, full, 0.0).astype(BF16)


def spread(depth_weights):
    size = NVZ * TILE
    return pl.pallas_call(
        spread_kernel,
        out_shape=jax.ShapeDtypeStruct((size, size), BF16),
        in_specs=[vmem()],
        out_specs=vmem(),
        name="spread",
    )(depth_weights)


def relax_kernel(place_ref, got_ref, mix_ref, send_ref, dev_ref):
    pieces = jnp.concatenate([got_ref[v, DATA:CHUNK, :] for v in range(GROUP)], axis=0)
    i = lax.broadcasted_iota(jnp.int32, (GROUP * 16, 128), 0) % 16
    j = lax.broadcasted_iota(jnp.int32, (GROUP * 16, 128), 1)
    pick = jnp.where((i % 5 == j) & (i < 15), 1.0, 0.0).astype(BF16)
    moments = lax.dot_general(pieces, pick, (((0,), (0,)), ((), ())), preferred_element_type=F32)
    moments = moments[:CELLS, :]
    density = moments[:, 0:1]
    ux = moments[:, 1:2] / density
    uy = moments[:, 2:3] / density
    uz = moments[:, 3:4] / density
    heat = (moments[:, 4:5] / density - (ux * ux + uy * uy + uz * uz)) / 3.0
    measure = (8.0 / NVX) * (8.0 / NVY) * (8.0 / NVZ)
    width = 2.0 * jnp.pi * heat
    scale = density * measure / (width * jnp.sqrt(width))
    inverse = -1.0 / (2.0 * heat)
    vx, vy = lane_speeds((CELLS, BLOCK), place_ref[0] * BLOCK)
    dx = vx - ux
    dy = vy - uy
    plane = scale * jnp.exp((dx * dx + dy * dy) * inverse)
    dz = speed(lax.broadcasted_iota(jnp.int32, (CELLS, 128), 1), NVZ) - uz
    depth = jnp.exp((dz * dz) * inverse)
    for w in range(NVZ):
        v, p = w // PLANES, w % PLANES
        f = got_ref[v, p * CELLS : (p + 1) * CELLS, :].astype(F32)
        deviation = (depth[:, w : w + 1] * plane - f).astype(BF16)
        for t in range(CELLS // TILE):
            dev_ref[w * TILE : (w + 1) * TILE, t * BLOCK : (t + 1) * BLOCK] = deviation[
                t * TILE : (t + 1) * TILE, :
            ]
    mixed = jnp.dot(mix_ref[...], dev_ref[...], preferred_element_type=F32).astype(BF16)
    for w in range(NVZ):
        v, p = w // PLANES, w % PLANES
        for t in range(CELLS // TILE):
            send_ref[v, p * CELLS + t * TILE : p * CELLS + (t + 1) * TILE, :] = mixed[
                w * TILE : (w + 1) * TILE, t * BLOCK : (t + 1) * BLOCK
            ]


def relax(place, got, mix):
    return pl.pallas_call(
        relax_kernel,
        out_shape=jax.ShapeDtypeStruct((GROUP, DATA, BLOCK), BF16),
        in_specs=[smem(), vmem(), vmem()],
        out_specs=vmem(),
        scratch_shapes=[pltpu.VMEM((NVZ * TILE, CELLS // TILE * BLOCK), BF16)],
        name="relax",
    )(place, got, mix)


def advance_kernel(f_ref, back_ref, weights_ref, lower_ref, upper_ref, left_ref, right_ref, out_ref):
    half = NXY // 2
    vx, vy = lane_speeds((COLS, NXY), 0)
    courant_across = COURANT / (4.0 - 4.0 / NVX)
    courant_along = COURANT / (4.0 - 4.0 / NVY)
    cx = courant_across * jnp.abs(vx)
    cy = courant_along * jnp.abs(vy)
    upwind = vy > 0.0
    col = lax.broadcasted_iota(jnp.int32, (COLS, NXY), 0)
    for p in range(PLANES):
        mixed = jnp.concatenate(
            [back_ref[v, p * CELLS : (p + 1) * CELLS, :] for v in range(GROUP)], axis=1
        )
        collision = lax.dot_general(
            mixed, weights_ref[...], (((1,), (1,)), ((), ())), preferred_element_type=F32
        )
        lanes = slice(p * NXY, (p + 1) * NXY)
        first_half = slice(p * NXY, p * NXY + half)
        second_half = slice(p * NXY + half, (p + 1) * NXY)
        packed = slice(p * half, (p + 1) * half)
        for r in range(ROWS):
            current = f_ref[r, :, lanes].astype(F32)
            above = upper_ref[:, packed] if r == ROWS - 1 else f_ref[r + 1, :, first_half]
            below = lower_ref[:, packed] if r == 0 else f_ref[r - 1, :, second_half]
            across = jnp.concatenate([above, below], axis=1).astype(F32)
            left = left_ref[:, lanes].astype(F32)[r : r + 1, :]
            right = right_ref[:, lanes].astype(F32)[r : r + 1, :]
            left = jnp.where(col == 0, left, pltpu.roll(current, 1, 0))
            right = jnp.where(col == COLS - 1, right, pltpu.roll(current, COLS - 1, 0))
            along = jnp.where(upwind, left, right)
            value = current - (cx * (current - across) + cy * (current - along))
            value = value + RELAX_RATE * collision[r * COLS : (r + 1) * COLS, :]
            out_ref[r, :, lanes] = value.astype(BF16)


def advance(f, back, weights, lower, upper, left, right):
    return pl.pallas_call(
        advance_kernel,
        out_shape=jax.ShapeDtypeStruct(f.shape, BF16),
        in_specs=[vmem()] * 7,
        out_specs=vmem(),
        compiler_params=pltpu.CompilerParams(vmem_limit_bytes=48 << 20),
        name="advance",
    )(f, back, weights, lower, upper, left, right)


def ring(axis, step):
    count = lax.axis_size(axis)
    return [(i, (i + step) % count) for i in range(count)]


def local(distribution, plane_weights, depth_weights):
    place = lax.axis_index("vel").astype(jnp.int32).reshape(1)
    send, low, high, first, last = pack(place, distribution)
    got = lax.all_to_all(send, "vel", 0, 0, tiled=True)
    shard = plane_weights.shape[0]
    count = lax.axis_size("sy")
    rows = jnp.broadcast_to(plane_weights[None], (count, shard, NXY))
    rows = lax.all_to_all(rows, "sy", 0, 0, tiled=True).reshape(count * shard, NXY)
    weights = lax.all_gather(rows, "sx", axis=0, tiled=True)
    lower = lax.ppermute(high, "sx", ring("sx", 1))
    upper = lax.ppermute(low, "sx", ring("sx", -1))
    left = lax.ppermute(last, "sy", ring("sy", 1))
    right = lax.ppermute(first, "sy", ring("sy", -1))
    mix = spread(depth_weights)
    back = lax.all_to_all(relax(place, got, mix), "vel", 0, 0, tiled=True)
    return advance(distribution, back, weights, lower, upper, left, right)


def solution(mesh):
    return jax.shard_map(
        local,
        mesh=mesh,
        in_specs=(P("sx", "sy", "vel"), P(("sx", "sy"), None), P()),
        out_specs=P("sx", "sy", "vel"),
        check_vma=False,
    )
```

time: 300 us -> 104 us (0.35)
  waiting for transfers between devices: 213 us -> 28.9 us
  blocking collectives: 35.1 us -> 16.9 us
  starting transfers between devices: 14.1 us -> 28.3 us
  Pallas kernels: 0 us -> 12.5 us
  matrix products: 10.8 us -> 0 us
  other arithmetic: 3.97 us -> 0 us
  local copies, waits for them, and re-layouts: 7.24 us -> 3.28 us
    all_gather x2 -> x1, waiting for transfers between devices: 204 us -> 0.02 us  [local(): weights = lax.all_gather(rows, 'sx', axis=0, tiled=True)]
    psum x1 -> x0, blocking collectives: 35.1 us -> none  [local(): lax.psum((particle_concentration, momentum_across, momentum_along, moment...]
    all_to_all x0 -> x2, waiting for transfers between devices: none -> 20.7 us  [the longest x1 20.7 us: local(): got = lax.all_to_all(send, 'vel', 0, 0, tiled=True)]
    all_to_all x0 -> x1, blocking collectives: none -> 16.9 us  [local(): lax.all_to_all(rows, 'sy', 0, 0, tiled=True).reshape(count * shard, NXY)]
    all_to_all x0 -> x2, starting transfers between devices: none -> 15.1 us  [the longest x1 10 us: local(): got = lax.all_to_all(send, 'vel', 0, 0, tiled=True)]
    pallas_call x0 -> x4, Pallas kernels: none -> 12.5 us  [the longest x1 4 us: advance(): pl.pallas_call(advance_kernel, out_shape=jax.ShapeDtypeStruct(f.shape, BF...]
    dot_general x2 -> x0, matrix products: 10.8 us -> none  [the longest x1 6.4 us: local(): jnp.einsum('zw,cwk->czk', own_rows, lax.all_gather(mixed_plane, 'vel', ax...]
    convert_element_type x2 -> x0, local copies, waits for them, and re-layouts: 3.75 us -> none  [the longest x1 2.29 us: local(): current = lattice.astype(jnp.float32)]
  transfers between devices with their start and end apart: 6 -> 7, of which waited for: 4 -> 2; matrix products, arithmetic and copies ran while one was open for 5% -> 0% of each run, Pallas kernels for 0% -> 8%
where the time goes in v1:
time: 104 us; the launch traced here: 103 us
  waiting for transfers between devices  28.9 us (28%)
  starting transfers between devices  28.3 us (27%)
  blocking collectives  16.9 us (16%)
  between operations  13.5 us (13%)
  Pallas kernels  12.5 us (12%)
  local copies, waits for them, and re-layouts  3.28 us (3%)
    all_to_all x1, waiting for transfers between devices, local(): got = lax.all_to_all(send, 'vel', 0, 0, tiled=True)  20.7 us
    all_to_all x1, blocking collectives, local(): lax.all_to_all(rows, 'sy', 0, 0, tiled=True).reshape(count * shard, NXY)  16.9 us
    all_to_all x1, starting transfers between devices, local(): got = lax.all_to_all(send, 'vel', 0, 0, tiled=True)  10 us
    ppermute x1, waiting for transfers between devices, local(): left = lax.ppermute(last, 'sy', ring('sy', 1))  8.14 us
    ppermute x1, starting transfers between devices, local(): right = lax.ppermute(first, 'sy', ring('sy', -1))  5.44 us
    all_to_all x1, starting transfers between devices, local(): back = lax.all_to_all(relax(place, got, mix), 'vel', 0, 0, tiled=True)  5.08 us
    pallas_call x1, Pallas kernels, advance(): pl.pallas_call(advance_kernel, out_shape=jax.ShapeDtypeStruct(f.shape, BF...  4 us
    ppermute x1, starting transfers between devices, local(): upper = lax.ppermute(low, 'sx', ring('sx', -1))  3.92 us
  transfers between devices with their start and end apart: 7, of which 2 were waited for; matrix products, arithmetic and copies ran while one was open for 0% of the time, Pallas kernels for 8%

profile of v1, /device:TPU:56, one launch (start us, length us, event | category | flops | bytes accessed | tf_op | source)
XLA Modules:
  0.0 103.4 jit_solution(772574211557193147)
XLA Ops:
  6.5 0.0 all-gather.2.cloned.1.call-start
  6.5 0.8 broadcast_in_dim.2
  7.3 16.9 %all_to_all.15 = bf16[8,16,1024]{2,1,0:T(8,128)(2,1)} all-to-all(bf16[8,16,1024]{2,1,0:T(8,128)(2,1)S(1)} %broadcast_in_dim.2), channel_id=1, replica_groups=mesh['vel'=8,'sx'=8,'sy'=8] {'sy'}, dimensions={0} | all-to-all | bytes 524288 | tf_op jit(solution)/shard_map/all_to_all | solution.py:248
  24.2 0.0 all-gather.2.cloned.1.call-update
  24.3 2.9 %pack.1 = (bf16[8,400,128]{2,1,0:T(8,128)(2,1)}, bf16[32,2048]{1,0:T(8,128)(2,1)}, bf16[32,2048]{1,0:T(8,128)(2,1)}, bf16[8,4096]{1,0:T(8,128)(2,1)}, bf16[8,4096]{1,0:T(8,128)(2,1)}) custom-call(s32[1]{0:T(128)} %bitcast.place_ref, bf16[3,32,4096]{2,1,0:T(8,128)(2,1)} %f_ref.3), custom_call_target="tpu_custom_call" | custom-call | tf_op jit(solution)/shard_map/pack/pallas_call | solution.py:102
  27.2 10.0 %all-to-all-start = ((bf16[8,400,128]{2,1,0:T(8,128)(2,1)}), bf16[8,400,128]{2,1,0:T(8,128)(2,1)S(1)}, u32[]{:S(2)}, u32[]{:S(2)}) async-start(bf16[8,400,128]{2,1,0:T(8,128)(2,1)} %get-tuple-element.10), calls=%async_computation | async-start | bytes 1638400 | tf_op jit(solution)/shard_map/all_to_all | solution.py:244
  37.2 0.0 copy-start.4
  37.2 0.0 copy-start.3
  37.3 0.0 copy-start.6
  37.3 0.0 copy-start.5
  37.3 0.0 copy-start
  37.3 2.0 %spread.1.mix_ref = bf16[512,512]{1,0:T(8,128)(2,1)} custom-call(bf16[32,32]{1,0:T(8,128)(2,1)} %depth_ref.1), custom_call_target="tpu_custom_call" | custom-call | tf_op jit(solution)/shard_map/spread/pallas_call | solution.py:131
  39.3 20.7 %all-to-all-done.got_ref = bf16[8,400,128]{2,1,0:T(8,128)(2,1)S(1)} async-done(((bf16[8,400,128]{2,1,0:T(8,128)(2,1)}), bf16[8,400,128]{2,1,0:T(8,128)(2,1)S(1)}, u32[]{:S(2)}, u32[]{:S(2)}) %all-to-all-start) | async-done | bytes 819232 | tf_op jit(solution)/shard_map/all_to_all | solution.py:244
  59.9 0.0 copy-start.2
  59.9 0.9 copy-done.2
  60.8 3.6 %relax.1 = bf16[8,384,128]{2,1,0:T(8,128)(2,1)} custom-call(s32[1]{0:T(128)} %bitcast.place_ref, bf16[8,400,128]{2,1,0:T(8,128)(2,1)} %copy-done.2, bf16[512,512]{1,0:T(8,128)(2,1)} %spread.1.mix_ref), custom_call_target="tpu_custom_call" | custom-call | tf_op jit(solution)/shard_map/relax/pallas_call | solution.py:180
  64.4 5.1 %all-to-all-start.1 = ((bf16[8,384,128]{2,1,0:T(8,128)(2,1)}), bf16[8,384,128]{2,1,0:T(8,128)(2,1)S(1)}, u32[]{:S(2)}, u32[]{:S(2)}) async-start(bf16[8,384,128]{2,1,0:T(8,128)(2,1)} %relax.1), calls=%async_computation.1 | async-start | bytes 1572864 | tf_op jit(solution)/shard_map/all_to_all | solution.py:255
  69.5 0.0 copy-done.4
  69.5 1.9 %collective-permute-start = (bf16[32,2048]{1,0:T(8,128)(2,1)S(1)}, bf16[32,2048]{1,0:T(8,128)(2,1)S(1)}, u32[]{:S(2)}, u32[]{:S(2)}) collective-permute-start(bf16[32,2048]{1,0:T(8,128)(2,1)S(1)} %copy-done.4), channel_id=1, source_target_pairs={{0,8},{8,16},{16,24},{24,32},{32,40},{40,48},{48,56},{56,0},{1,9},... | collective-permute-start | bytes 393224 | tf_op jit(solution)/shard_map/ppermute | solution.py:250
  71.4 0.0 copy-done.3
  71.5 3.9 %collective-permute-start.1 = (bf16[32,2048]{1,0:T(8,128)(2,1)S(1)}, bf16[32,2048]{1,0:T(8,128)(2,1)S(1)}, u32[]{:S(2)}, u32[]{:S(2)}) collective-permute-start(bf16[32,2048]{1,0:T(8,128)(2,1)S(1)} %copy-done.3), channel_id=1, source_target_pairs={{0,56},{8,0},{16,8},{24,16},{32,24},{40,32},{48,40},{56,48},{1,57}... | collective-permute-start | bytes 393224 | tf_op jit(solution)/shard_map/ppermute | solution.py:251
  75.4 0.0 copy-done.6
  75.4 1.9 %collective-permute-start.2 = (bf16[8,4096]{1,0:T(8,128)(2,1)S(1)}, bf16[8,4096]{1,0:T(8,128)(2,1)S(1)}, u32[]{:S(2)}, u32[]{:S(2)}) collective-permute-start(bf16[8,4096]{1,0:T(8,128)(2,1)S(1)} %copy-done.6), channel_id=1, source_target_pairs={{0,1},{1,2},{2,3},{3,4},{4,5},{5,6},{6,7},{7,0},{8,9},{9,10},{10,1... | collective-permute-start | bytes 196616 | tf_op jit(solution)/shard_map/ppermute | solution.py:252
  77.3 0.0 copy-done.5
  77.3 5.4 %collective-permute-start.3 = (bf16[8,4096]{1,0:T(8,128)(2,1)S(1)}, bf16[8,4096]{1,0:T(8,128)(2,1)S(1)}, u32[]{:S(2)}, u32[]{:S(2)}) collective-permute-start(bf16[8,4096]{1,0:T(8,128)(2,1)S(1)} %copy-done.5), channel_id=1, source_target_pairs={{0,7},{1,0},{2,1},{3,2},{4,3},{5,4},{6,5},{7,6},{8,15},{9,8},{10,9... | collective-permute-start | bytes 196616 | tf_op jit(solution)/shard_map/ppermute | solution.py:253
  82.8 8.1 %collective-permute-done.2.left_ref = bf16[8,4096]{1,0:T(8,128)(2,1)S(1)} collective-permute-done((bf16[8,4096]{1,0:T(8,128)(2,1)S(1)}, bf16[8,4096]{1,0:T(8,128)(2,1)S(1)}, u32[]{:S(2)}, u32[]{:S(2)}) %collective-permute-start.2) | collective-permute-done | bytes 65568 | tf_op jit(solution)/shard_map/ppermute | solution.py:252
  90.9 0.0 collective-permute-done.3.right_ref
  90.9 0.0 collective-permute-done.lower_ref
  90.9 0.0 collective-permute-done.1.upper_ref
  90.9 0.0 all-to-all-done.1.back_ref
  90.9 0.0 all-gather.2.cloned.1.call-done.weights_ref
  91.0 0.0 copy-done
  91.0 0.0 copy-start.1
  91.0 1.6 %copy-done.1 = bf16[1024,1024]{1,0:T(8,128)(2,1)S(1)} copy-done((bf16[1024,1024]{1,0:T(8,128)(2,1)S(1)}, bf16[1024,1024]{1,0:T(8,128)(2,1)}, u32[]{:S(2)}) %copy-start.1) | copy-done | bytes 2097176
  92.6 4.0 %advance.1 = bf16[3,32,4096]{2,1,0:T(8,128)(2,1)} custom-call(bf16[3,32,4096]{2,1,0:T(8,128)(2,1)S(1)} %copy-done, bf16[8,384,128]{2,1,0:T(8,128)(2,1)S(1)} %all-to-all-done.1.back_ref, bf16[1024,1024]{1,0:T(8,128)(2,1)S(1)} %copy-done.1, bf16[32,2048]{1,0:T(8,128)(2,1)S(1)} %collective-permute-done.lower_ref, ...), custom_call_target="tpu_custom_call" | custom-call | tf_op jit(solution)/shard_map/advance/pallas_call | solution.py:226
Async XLA Ops:
  6.5 84.4 %all-gather.2.cloned.1.call-start = ((), (), s32[]{:S(2)}) async-start(), calls=%async_computation.3 | async-start | bytes 2359296 | tf_op jit(solution)/shard_map/all_gather | solution.py:249
  27.2 32.7 %all-to-all-start = ((bf16[8,400,128]{2,1,0:T(8,128)(2,1)}), bf16[8,400,128]{2,1,0:T(8,128)(2,1)S(1)}, u32[]{:S(2)}, u32[]{:S(2)}) async-start(bf16[8,400,128]{2,1,0:T(8,128)(2,1)} %get-tuple-element.10), calls=%async_computation | async-start | bytes 1638400 | tf_op jit(solution)/shard_map/all_to_all | solution.py:244
  37.2 32.3 %copy-start.4 = (bf16[32,2048]{1,0:T(8,128)(2,1)S(1)}, bf16[32,2048]{1,0:T(8,128)(2,1)}, u32[]{:S(2)}) copy-start(bf16[32,2048]{1,0:T(8,128)(2,1)} %get-tuple-element.11) | copy-start | bytes 393220
  37.2 34.2 %copy-start.3 = (bf16[32,2048]{1,0:T(8,128)(2,1)S(1)}, bf16[32,2048]{1,0:T(8,128)(2,1)}, u32[]{:S(2)}) copy-start(bf16[32,2048]{1,0:T(8,128)(2,1)} %get-tuple-element.12) | copy-start | bytes 393220
  37.3 38.1 %copy-start.6 = (bf16[8,4096]{1,0:T(8,128)(2,1)S(1)}, bf16[8,4096]{1,0:T(8,128)(2,1)}, u32[]{:S(2)}) copy-start(bf16[8,4096]{1,0:T(8,128)(2,1)} %get-tuple-element.13) | copy-start | bytes 196612
  37.3 40.1 %copy-start.5 = (bf16[8,4096]{1,0:T(8,128)(2,1)S(1)}, bf16[8,4096]{1,0:T(8,128)(2,1)}, u32[]{:S(2)}) copy-start(bf16[8,4096]{1,0:T(8,128)(2,1)} %get-tuple-element.14) | copy-start | bytes 196612
  37.3 53.7 %copy-start = (bf16[3,32,4096]{2,1,0:T(8,128)(2,1)S(1)}, bf16[3,32,4096]{2,1,0:T(8,128)(2,1)}, u32[]{:S(2)}) copy-start(bf16[3,32,4096]{2,1,0:T(8,128)(2,1)} %f_ref.3) | copy-start | bytes 2359300
  59.9 0.9 copy-start.2
  64.4 26.5 %all-to-all-start.1 = ((bf16[8,384,128]{2,1,0:T(8,128)(2,1)}), bf16[8,384,128]{2,1,0:T(8,128)(2,1)S(1)}, u32[]{:S(2)}, u32[]{:S(2)}) async-start(bf16[8,384,128]{2,1,0:T(8,128)(2,1)} %relax.1), calls=%async_computation.1 | async-start | bytes 1572864 | tf_op jit(solution)/shard_map/all_to_all | solution.py:255
  69.5 21.4 %collective-permute-start = (bf16[32,2048]{1,0:T(8,128)(2,1)S(1)}, bf16[32,2048]{1,0:T(8,128)(2,1)S(1)}, u32[]{:S(2)}, u32[]{:S(2)}) collective-permute-start(bf16[32,2048]{1,0:T(8,128)(2,1)S(1)} %copy-done.4), channel_id=1, source_target_pairs={{0,8},{8,16},{16,24},{24,32},{32,40},{40,48},{48,56},{56,0},{1,9},... | collective-permute-start | bytes 393224 | tf_op jit(solution)/shard_map/ppermute | solution.py:250
  71.5 19.5 %collective-permute-start.1 = (bf16[32,2048]{1,0:T(8,128)(2,1)S(1)}, bf16[32,2048]{1,0:T(8,128)(2,1)S(1)}, u32[]{:S(2)}, u32[]{:S(2)}) collective-permute-start(bf16[32,2048]{1,0:T(8,128)(2,1)S(1)} %copy-done.3), channel_id=1, source_target_pairs={{0,56},{8,0},{16,8},{24,16},{32,24},{40,32},{48,40},{56,48},{1,57}... | collective-permute-start | bytes 393224 | tf_op jit(solution)/shard_map/ppermute | solution.py:251
  75.4 15.5 %collective-permute-start.2 = (bf16[8,4096]{1,0:T(8,128)(2,1)S(1)}, bf16[8,4096]{1,0:T(8,128)(2,1)S(1)}, u32[]{:S(2)}, u32[]{:S(2)}) collective-permute-start(bf16[8,4096]{1,0:T(8,128)(2,1)S(1)} %copy-done.6), channel_id=1, source_target_pairs={{0,1},{1,2},{2,3},{3,4},{4,5},{5,6},{6,7},{7,0},{8,9},{9,10},{10,1... | collective-permute-start | bytes 196616 | tf_op jit(solution)/shard_map/ppermute | solution.py:252
  77.3 13.6 %collective-permute-start.3 = (bf16[8,4096]{1,0:T(8,128)(2,1)S(1)}, bf16[8,4096]{1,0:T(8,128)(2,1)S(1)}, u32[]{:S(2)}, u32[]{:S(2)}) collective-permute-start(bf16[8,4096]{1,0:T(8,128)(2,1)S(1)} %copy-done.5), channel_id=1, source_target_pairs={{0,7},{1,0},{2,1},{3,2},{4,3},{5,4},{6,5},{7,6},{8,15},{9,8},{10,9... | collective-permute-start | bytes 196616 | tf_op jit(solution)/shard_map/ppermute | solution.py:253
  91.0 1.6 %copy-start.1 = (bf16[1024,1024]{1,0:T(8,128)(2,1)S(1)}, bf16[1024,1024]{1,0:T(8,128)(2,1)}, u32[]{:S(2)}) copy-start(bf16[1024,1024]{1,0:T(8,128)(2,1)} %all-gather.2.cloned.1.call-done.weights_ref) | copy-start | bytes 6291460
Sparse Core Ops, SparseCore 0:
  24.4 44.0 all-gather.1

commit v2 on v1

v2 whole, which is shorter than its diff:
```python
import jax
import jax.numpy as jnp
import numpy as np
from jax import lax
from jax.experimental import pallas as pl
from jax.experimental.pallas import tpu as pltpu
from jax.sharding import PartitionSpec as P

NVZ = 32
NVX = 32
NVY = 32
NXY = NVX * NVY
COURANT = 0.45
RELAX_RATE = 0.3
ROWS = 3
COLS = 32
CELLS = ROWS * COLS
PLANES = 4
GROUP = 8
BLOCK = NXY // GROUP
DATA = PLANES * CELLS
CHUNK = DATA + 16
TILE = 16
F32 = jnp.float32
BF16 = jnp.bfloat16


def speed(index, count):
    return (index.astype(F32) - (count - 1) / 2.0) * (8.0 / count)


def lane_speeds(shape, offset):
    lane = lax.broadcasted_iota(jnp.int32, shape, len(shape) - 1) + offset
    return speed(lane // NVY, NVX), speed(lane % NVY, NVY)


def vmem():
    return pl.BlockSpec(memory_space=pltpu.VMEM)


def smem():
    return pl.BlockSpec(memory_space=pltpu.SMEM)


def moment_basis():
    lane = np.arange(NXY)
    vx = (lane // NVY - (NVX - 1) / 2.0) * (8.0 / NVX)
    vy = (lane % NVY - (NVY - 1) / 2.0) * (8.0 / NVY)
    squared = (vx * vx + vy * vy).astype(np.float32)
    rough = squared.astype(BF16).astype(np.float32)
    basis = np.zeros((NXY, 128), np.float32)
    for part in range(3):
        basis[:, part * 5] = 1.0
        basis[:, part * 5 + 1] = vx
        basis[:, part * 5 + 2] = vy
        basis[:, part * 5 + 3] = 1.0
        basis[:, part * 5 + 4] = rough
        basis[:, 16 + part * 5 + 4] = squared - rough
        basis[:, 32 + part * 5 + 4] = 1.0
    return basis.astype(BF16)


def pack_kernel(place_ref, f_ref, basis_ref, send_ref):
    lane = lax.broadcasted_iota(jnp.int32, (1, 128), 1)
    first_plane = place_ref[0] * PLANES
    total = jnp.zeros((CELLS, 128), F32)
    for p in range(PLANES):
        x = jnp.concatenate([f_ref[r, :, p * NXY : (p + 1) * NXY] for r in range(ROWS)], axis=0)
        sums = jnp.dot(x, basis_ref[...], preferred_element_type=F32)
        vz = speed(first_plane + p, NVZ)
        factor = jnp.where(lane >= 32, vz * vz, jnp.where((lane < 16) & (lane % 5 == 3), vz, 1.0))
        total = total + sums * factor
        for v in range(GROUP):
            send_ref[v, p * CELLS : (p + 1) * CELLS, :] = x[:, v * BLOCK : (v + 1) * BLOCK]
    total = jnp.transpose(total)
    total = (total[0:16, :] + total[16:32, :]) + total[32:48, :]
    column = lax.broadcasted_iota(jnp.int32, (16, CELLS), 0)
    high = total.astype(BF16).astype(F32)
    middle = (total - high).astype(BF16).astype(F32)
    low = (total - high) - middle
    parts = jnp.where(
        column < 5, high, jnp.where(column < 10, middle, jnp.where(column < 15, low, 0.0))
    )
    parts = jnp.concatenate([parts, jnp.zeros((16, 128 - CELLS), F32)], axis=1).astype(BF16)
    for v in range(GROUP):
        send_ref[v, DATA:CHUNK, :] = parts


def pack(place, f):
    return pl.pallas_call(
        pack_kernel,
        out_shape=jax.ShapeDtypeStruct((GROUP, CHUNK, BLOCK), BF16),
        in_specs=[smem(), vmem(), vmem()],
        out_specs=vmem(),
        name="pack",
    )(place, f, jnp.asarray(moment_basis()))


def edges_kernel(core_ref, f_ref, low_ref, high_ref, inner_ref, outer_ref):
    half = NXY // 2
    for p in range(PLANES):
        rows = slice(p // 2 * COLS, (p // 2 + 1) * COLS)
        lanes = slice(p % 2 * half, (p % 2 + 1) * half)
        high_ref[rows, lanes] = f_ref[ROWS - 1, :, p * NXY + half : (p + 1) * NXY]
        low_ref[rows, lanes] = f_ref[0, :, p * NXY : p * NXY + half]
    edge_row = lax.broadcasted_iota(jnp.int32, (16, NXY), 0)
    first = jnp.zeros((16, NXY), F32)
    last = jnp.zeros((16, NXY), F32)
    for r in range(ROWS):
        for p in range(PLANES):
            lanes = slice(p * NXY, (p + 1) * NXY)
            a = f_ref[r, 0:8, lanes].astype(F32)[0:1, :]
            b = f_ref[r, COLS - 8 : COLS, lanes].astype(F32)[7:8, :]
            first = jnp.where(edge_row == r * PLANES + p, a, first)
            last = jnp.where(edge_row == r * PLANES + p, b, last)
    core = core_ref[0]
    inner_ref[...] = jnp.where(core == 0, last, first).astype(BF16)
    outer_ref[...] = jnp.where(core == 0, first, last).astype(BF16)


def edges(core, f):
    row = jax.ShapeDtypeStruct((2 * COLS, NXY), BF16)
    column = jax.ShapeDtypeStruct((16, NXY), BF16)
    return pl.pallas_call(
        edges_kernel,
        out_shape=(row, row, column, column),
        in_specs=[smem(), vmem()],
        out_specs=(vmem(),) * 4,
        name="edges",
    )(core, f)


def assemble_kernel(where_ref, own_ref, other_ref, out_ref, rows_ref):
    core, z, y = where_ref[0], where_ref[1], where_ref[2]
    far = jnp.where(y % 2 == 0, y + 6, y + 2)
    for m, base in enumerate((y, y + 1, y + 7, far)):
        for i in range(2):
            for j in range(4):
                place = ((base + 4 * i) % 8 * 4 + jnp.bitwise_xor(z, j)) * 2
                block = slice((m * 8 + i * 4 + j) * 16, (m * 8 + i * 4 + j + 1) * 16)
                rows_ref[place + core] = own_ref[block, :]
                rows_ref[place + 1 - core] = other_ref[block, :]
    out_ref[...] = jnp.transpose(rows_ref[...].reshape(NXY, NXY))


def assemble(where, own, other):
    return pl.pallas_call(
        assemble_kernel,
        out_shape=jax.ShapeDtypeStruct((NXY, NXY), BF16),
        in_specs=[smem(), vmem(), vmem()],
        out_specs=vmem(),
        scratch_shapes=[pltpu.VMEM((NXY // 16, 16, NXY), BF16)],
        compiler_params=pltpu.CompilerParams(vmem_limit_bytes=32 << 20),
        name="assemble",
    )(where, own, other)


def spread_kernel(depth_ref, out_ref):
    size = NVZ * TILE
    row = lax.broadcasted_iota(jnp.int32, (size, NVZ), 0)
    col = lax.broadcasted_iota(jnp.int32, (size, NVZ), 1)
    pick = jnp.where(row // TILE == col, 1.0, 0.0).astype(BF16)
    left = jnp.dot(pick, depth_ref[...], preferred_element_type=F32).astype(BF16)
    full = lax.dot_general(left, pick, (((1,), (1,)), ((), ())), preferred_element_type=F32)
    i = lax.broadcasted_iota(jnp.int32, (size, size), 0)
    j = lax.broadcasted_iota(jnp.int32, (size, size), 1)
    out_ref[...] = jnp.where(i % TILE == j % TILE, full, 0.0).astype(BF16)


def spread(depth_weights):
    size = NVZ * TILE
    return pl.pallas_call(
        spread_kernel,
        out_shape=jax.ShapeDtypeStruct((size, size), BF16),
        in_specs=[vmem()],
        out_specs=vmem(),
        name="spread",
    )(depth_weights)


def relax_kernel(place_ref, got_ref, mix_ref, send_ref, dev_ref):
    pieces = jnp.concatenate([got_ref[v, DATA:CHUNK, :] for v in range(GROUP)], axis=0)
    i = lax.broadcasted_iota(jnp.int32, (GROUP * 16, 128), 0) % 16
    j = lax.broadcasted_iota(jnp.int32, (GROUP * 16, 128), 1)
    pick = jnp.where((i % 5 == j) & (i < 15), 1.0, 0.0).astype(BF16)
    moments = lax.dot_general(pieces, pick, (((0,), (0,)), ((), ())), preferred_element_type=F32)
    moments = moments[:CELLS, :]
    density = moments[:, 0:1]
    ux = moments[:, 1:2] / density
    uy = moments[:, 2:3] / density
    uz = moments[:, 3:4] / density
    heat = (moments[:, 4:5] / density - (ux * ux + uy * uy + uz * uz)) / 3.0
    measure = (8.0 / NVX) * (8.0 / NVY) * (8.0 / NVZ)
    width = 2.0 * jnp.pi * heat
    scale = density * measure / (width * jnp.sqrt(width))
    inverse = -1.0 / (2.0 * heat)
    vx, vy = lane_speeds((CELLS, BLOCK), place_ref[0] * BLOCK)
    dx = vx - ux
    dy = vy - uy
    plane = scale * jnp.exp((dx * dx + dy * dy) * inverse)
    dz = speed(lax.broadcasted_iota(jnp.int32, (CELLS, 128), 1), NVZ) - uz
    depth = jnp.exp((dz * dz) * inverse)
    for w in range(NVZ):
        v, p = w // PLANES, w % PLANES
        f = got_ref[v, p * CELLS : (p + 1) * CELLS, :].astype(F32)
        deviation = (depth[:, w : w + 1] * plane - f).astype(BF16)
        for t in range(CELLS // TILE):
            dev_ref[w * TILE : (w + 1) * TILE, t * BLOCK : (t + 1) * BLOCK] = deviation[
                t * TILE : (t + 1) * TILE, :
            ]
    mixed = jnp.dot(mix_ref[...], dev_ref[...], preferred_element_type=F32).astype(BF16)
    for w in range(NVZ):
        v, p = w // PLANES, w % PLANES
        for t in range(CELLS // TILE):
            send_ref[v, p * CELLS + t * TILE : p * CELLS + (t + 1) * TILE, :] = mixed[
                w * TILE : (w + 1) * TILE, t * BLOCK : (t + 1) * BLOCK
            ]


def relax(place, got, mix):
    return pl.pallas_call(
        relax_kernel,
        out_shape=jax.ShapeDtypeStruct((GROUP, DATA, BLOCK), BF16),
        in_specs=[smem(), vmem(), vmem()],
        out_specs=vmem(),
        scratch_shapes=[pltpu.VMEM((NVZ * TILE, CELLS // TILE * BLOCK), BF16)],
        name="relax",
    )(place, got, mix)


def advance_kernel(
    core_ref, f_ref, back_ref, weights_ref, lower_ref, upper_ref, inner_ref, outer_ref, out_ref, mixed_ref
):
    half = NXY // 2
    vx, vy = lane_speeds((COLS, NXY), 0)
    courant_across = COURANT / (4.0 - 4.0 / NVX)
    courant_along = COURANT / (4.0 - 4.0 / NVY)
    cx = courant_across * jnp.abs(vx)
    cy = courant_along * jnp.abs(vy)
    upwind = vy > 0.0
    inner = inner_ref[...].astype(F32)
    outer = outer_ref[...].astype(F32)
    core = core_ref[0]
    left_edge = jnp.where(core == 0, outer, inner)
    right_edge = jnp.where(core == 0, inner, outer)
    col = lax.broadcasted_iota(jnp.int32, (COLS, NXY), 0)
    mixed = jnp.concatenate([back_ref[v] for v in range(GROUP)], axis=1)
    mixed_ref[...] = jnp.dot(mixed, weights_ref[...], preferred_element_type=F32)
    for p in range(PLANES):
        lanes = slice(p * NXY, (p + 1) * NXY)
        first_half = slice(p * NXY, p * NXY + half)
        second_half = slice(p * NXY + half, (p + 1) * NXY)
        rows = slice(p // 2 * COLS, (p // 2 + 1) * COLS)
        packed = slice(p % 2 * half, (p % 2 + 1) * half)
        for r in range(ROWS):
            current = f_ref[r, :, lanes].astype(F32)
            above = upper_ref[rows, packed] if r == ROWS - 1 else f_ref[r + 1, :, first_half]
            below = lower_ref[rows, packed] if r == 0 else f_ref[r - 1, :, second_half]
            across = jnp.concatenate([above, below], axis=1).astype(F32)
            left = left_edge[r * PLANES + p : r * PLANES + p + 1, :]
            right = right_edge[r * PLANES + p : r * PLANES + p + 1, :]
            left = jnp.where(col == 0, left, pltpu.roll(current, 1, 0))
            right = jnp.where(col == COLS - 1, right, pltpu.roll(current, COLS - 1, 0))
            along = jnp.where(upwind, left, right)
            value = current - (cx * (current - across) + cy * (current - along))
            start = p * CELLS + r * COLS
            value = value + RELAX_RATE * mixed_ref[start : start + COLS, :]
            out_ref[r, :, lanes] = value.astype(BF16)


def advance(core, f, back, weights, lower, upper, inner, outer):
    return pl.pallas_call(
        advance_kernel,
        out_shape=jax.ShapeDtypeStruct(f.shape, BF16),
        in_specs=[smem()] + [vmem()] * 7,
        out_specs=vmem(),
        scratch_shapes=[pltpu.VMEM((DATA, NXY), F32)],
        compiler_params=pltpu.CompilerParams(vmem_limit_bytes=48 << 20),
        name="advance",
    )(core, f, back, weights, lower, upper, inner, outer)


def ring(axis, step):
    count = lax.axis_size(axis)
    return [(i, (i + step) % count) for i in range(count)]


def local(distribution, plane_weights, depth_weights):
    place = lax.axis_index("vel").astype(jnp.int32).reshape(1)
    along = lax.axis_index("sy").astype(jnp.int32)
    core = jnp.bitwise_and(along, 1).reshape(1)
    where = jnp.stack([jnp.bitwise_and(along, 1), along >> 1, lax.axis_index("sx").astype(jnp.int32)])
    send = pack(place, distribution)
    got = lax.all_to_all(send, "vel", 0, 0, tiled=True)
    mix = spread(depth_weights)
    low, high, inner, outer = edges(core, distribution)
    flip = lambda bit: [(i, i ^ bit) for i in range(8)]
    held = jnp.concatenate([plane_weights, lax.ppermute(plane_weights, "sy", flip(2))])
    held = jnp.concatenate([held, lax.ppermute(held, "sy", flip(4))])
    held = jnp.concatenate([held, lax.ppermute(held, "sx", flip(4))])
    size = held.shape[0]
    above = lax.ppermute(jnp.concatenate([held, low]), "sx", ring("sx", -1))
    below = lax.ppermute(jnp.concatenate([held, high]), "sx", ring("sx", 1))
    across = lax.ppermute(held, "sx", [(i, (i + 2) % 8 if i % 2 == 0 else (i - 2) % 8) for i in range(8)])
    outer = lax.ppermute(outer, "sy", [(i, (i + 1) % 8 if i % 2 else (i - 1) % 8) for i in range(8)])
    own = jnp.concatenate([held, above[:size], below[:size], across, inner])
    other = lax.ppermute(own, "sy", flip(1))
    weights = assemble(where, own, other)
    back = lax.all_to_all(relax(place, got, mix), "vel", 0, 0, tiled=True)
    return advance(
        core, distribution, back, weights, below[size:], above[size:], other[4 * size :], outer
    )


def solution(mesh):
    return jax.shard_map(
        local,
        mesh=mesh,
        in_specs=(P("sx", "sy", "vel"), P(("sx", "sy"), None), P()),
        out_specs=P("sx", "sy", "vel"),
        check_vma=False,
    )
```

time: 104 us -> 109 us (1.048)
  the two profiles are of different devices: /device:TPU:56 before, /device:TPU:8 now
where the time goes in v2:
time: 109 us; the launch traced here: 108 us
  starting transfers between devices  54.3 us (50%)
  waiting for transfers between devices  29.6 us (27%)
  Pallas kernels  14.9 us (14%)
  local copies, waits for them, and re-layouts  8.37 us (8%)
    ppermute x1, waiting for transfers between devices, local(): held = jnp.concatenate([held, lax.ppermute(held, 'sy', flip(4))])  16.8 us
    all_to_all x1, starting transfers between devices, local(): got = lax.all_to_all(send, 'vel', 0, 0, tiled=True)  12 us
    all_to_all x1, starting transfers between devices, local(): back = lax.all_to_all(relax(place, got, mix), 'vel', 0, 0, tiled=True)  7.56 us
    ppermute x1, waiting for transfers between devices, local(): held = jnp.concatenate([held, lax.ppermute(held, 'sx', flip(4))])  7 us
    ppermute x1, starting transfers between devices, local(): held = jnp.concatenate([held, lax.ppermute(held, 'sx', flip(4))])  6.83 us
    unnamed x32, local copies, waits for them, and re-layouts  6.51 us
    ppermute x1, starting transfers between devices, local(): lax.ppermute(held, 'sx', [(i, (i + 2) % 8 if i % 2 == 0 else (i - 2) % 8)...  6.24 us
    ppermute x1, starting transfers between devices, local(): lax.ppermute(outer, 'sy', [(i, (i + 1) % 8 if i % 2 else (i - 1) % 8) for...  5.26 us
  transfers between devices with their start and end apart: 10, of which 4 were waited for; matrix products, arithmetic and copies ran while one was open for 3% of the time, Pallas kernels for 10%

profile of v2, /device:TPU:8, one launch (start us, length us, event | category | flops | bytes accessed | tf_op | source)
XLA Modules:
  0.0 108.4 jit_solution(10611164692312272385)
XLA Ops:
  0.0 4.3 %collective-permute-start = (bf16[16,1024]{1,0:T(8,128)(2,1)}, bf16[16,1024]{1,0:T(8,128)(2,1)S(1)}, u32[]{:S(2)}, u32[]{:S(2)}) collective-permute-start(bf16[16,1024]{1,0:T(8,128)(2,1)} %param.5), channel_id=1, source_target_pairs={{0,2},{1,3},{2,0},{3,1},{4,6},{5,7},{6,4},{7,5},{8,10},{9,11},{10,... | collective-permute-start | bytes 98312 | tf_op jit(solution)/shard_map/ppermute | solution.py:298
  4.3 2.5 %pack.1 = bf16[8,400,128]{2,1,0:T(8,128)(2,1)} custom-call(s32[1]{0:T(128)} %bitcast.1.place_ref, bf16[3,32,4096]{2,1,0:T(8,128)(2,1)} %f_ref.5, bf16[1024,128]{1,0:T(8,128)(2,1)} %constant.15.clone.basis_ref), custom_call_target="tpu_custom_call" | custom-call | tf_op jit(solution)/shard_map/pack/pallas_call | solution.py:90
  6.8 12.0 %all-to-all-start = ((bf16[8,400,128]{2,1,0:T(8,128)(2,1)}), bf16[8,400,128]{2,1,0:T(8,128)(2,1)S(1)}, u32[]{:S(2)}, u32[]{:S(2)}) async-start(bf16[8,400,128]{2,1,0:T(8,128)(2,1)} %pack.1), calls=%async_computation | async-start | bytes 1638400 | tf_op jit(solution)/shard_map/all_to_all | solution.py:294
  18.8 1.9 %edges.1 = (bf16[64,1024]{1,0:T(8,128)(2,1)}, bf16[64,1024]{1,0:T(8,128)(2,1)}, bf16[16,1024]{1,0:T(8,128)(2,1)}, bf16[16,1024]{1,0:T(8,128)(2,1)}) custom-call(s32[1]{0:T(128)} %bitcast.core_ref, bf16[3,32,4096]{2,1,0:T(8,128)(2,1)} %f_ref.5), custom_call_target="tpu_custom_call" | custom-call | tf_op jit(solution)/shard_map/edges/pallas_call | solution.py:124
  20.7 0.0 collective-permute-done
  20.7 0.0 copy-done.6
  20.7 0.0 copy-start.8
  20.7 4.4 %collective-permute-start.1 = (bf16[32,1024]{1,0:T(8,128)(2,1)S(1)}, bf16[32,1024]{1,0:T(8,128)(2,1)S(1)}, u32[]{:S(2)}, u32[]{:S(2)}) collective-permute-start(bf16[32,1024]{1,0:T(8,128)(2,1)S(1)} %pad_maximum_fusion.2), channel_id=1, source_target_pairs={{0,4},{1,5},{2,6},{3,7},{4,0},{5,1},{6,2},{7,3},{8,12},{9,13},{10,... | collective-permute-start | bytes 196616 | tf_op jit(solution)/shard_map/ppermute | solution.py:299
  25.1 16.8 %collective-permute-done.1 = bf16[32,1024]{1,0:T(8,128)(2,1)S(1)} collective-permute-done((bf16[32,1024]{1,0:T(8,128)(2,1)S(1)}, bf16[32,1024]{1,0:T(8,128)(2,1)S(1)}, u32[]{:S(2)}, u32[]{:S(2)}) %collective-permute-start.1) | collective-permute-done | bytes 65568 | tf_op jit(solution)/shard_map/ppermute | solution.py:299
  42.0 6.8 %collective-permute-start.2 = (bf16[64,1024]{1,0:T(8,128)(2,1)S(1)}, bf16[64,1024]{1,0:T(8,128)(2,1)S(1)}, u32[]{:S(2)}, u32[]{:S(2)}) collective-permute-start(bf16[64,1024]{1,0:T(8,128)(2,1)S(1)} %pad_maximum_fusion.1), channel_id=1, source_target_pairs={{0,32},{8,40},{16,48},{24,56},{32,0},{40,8},{48,16},{56,24},{1,33}... | collective-permute-start | bytes 393224 | tf_op jit(solution)/shard_map/ppermute | solution.py:300
  48.9 7.0 %collective-permute-done.2 = bf16[64,1024]{1,0:T(8,128)(2,1)S(1)} collective-permute-done((bf16[64,1024]{1,0:T(8,128)(2,1)S(1)}, bf16[64,1024]{1,0:T(8,128)(2,1)S(1)}, u32[]{:S(2)}, u32[]{:S(2)}) %collective-permute-start.2) | collective-permute-done | bytes 131104 | tf_op jit(solution)/shard_map/ppermute | solution.py:300
  55.9 0.0 copy-done.9
  55.9 1.9 %collective-permute-start.3 = (bf16[192,1024]{1,0:T(8,128)(2,1)S(1)}, bf16[192,1024]{1,0:T(8,128)(2,1)S(1)}, u32[]{:S(2)}, u32[]{:S(2)}) collective-permute-start(bf16[192,1024]{1,0:T(8,128)(2,1)S(1)} %constant_dynamic-update-slice_fusion), channel_id=1, source_target_pairs={{0,56},{8,0},{16,8},{24,16},{32,24},{40,32},{48,40},{56,48},{1,57}... | collective-permute-start | bytes 1179656 | tf_op jit(solution)/shard_map/ppermute | solution.py:302
  57.9 0.0 copy-done.8
  57.9 3.9 %collective-permute-start.4 = (bf16[192,1024]{1,0:T(8,128)(2,1)S(1)}, bf16[192,1024]{1,0:T(8,128)(2,1)}, u32[]{:S(2)}, u32[]{:S(2)}) collective-permute-start(bf16[192,1024]{1,0:T(8,128)(2,1)S(1)} %constant_dynamic-update-slice_fusion.5), channel_id=1, source_target_pairs={{0,8},{8,16},{16,24},{24,32},{32,40},{40,48},{48,56},{56,0},{1,9},... | collective-permute-start | bytes 1179656 | tf_op jit(solution)/shard_map/ppermute | solution.py:303
  61.8 1.9 %spread.1.mix_ref = bf16[512,512]{1,0:T(8,128)(2,1)} custom-call(bf16[32,32]{1,0:T(8,128)(2,1)} %depth_ref.1), custom_call_target="tpu_custom_call" | custom-call | tf_op jit(solution)/shard_map/spread/pallas_call | solution.py:172
  63.8 0.7 pad_maximum_fusion
  64.5 6.2 %collective-permute-start.5 = (bf16[128,1024]{1,0:T(8,128)(2,1)}, bf16[128,1024]{1,0:T(8,128)(2,1)S(1)}, u32[]{:S(2)}, u32[]{:S(2)}) collective-permute-start(bf16[128,1024]{1,0:T(8,128)(2,1)} %pad_maximum_fusion), channel_id=1, source_target_pairs={{0,16},{8,56},{16,32},{24,8},{32,48},{40,24},{48,0},{56,40},{1,17}... | collective-permute-start | bytes 786440 | tf_op jit(solution)/shard_map/ppermute | solution.py:304
  70.7 0.0 collective-permute-done.3
  70.7 0.0 copy-start.7
  70.8 0.0 all-to-all-done.got_ref
  70.8 0.0 copy-start.5
  70.8 1.0 copy-done.5
  71.8 3.6 %relax.1 = bf16[8,384,128]{2,1,0:T(8,128)(2,1)} custom-call(s32[1]{0:T(128)} %bitcast.1.place_ref, bf16[8,400,128]{2,1,0:T(8,128)(2,1)} %copy-done.5, bf16[512,512]{1,0:T(8,128)(2,1)} %spread.1.mix_ref), custom_call_target="tpu_custom_call" | custom-call | tf_op jit(solution)/shard_map/relax/pallas_call | solution.py:221
  75.3 0.0 copy-done.7
  75.3 7.6 %all-to-all-start.1 = ((bf16[8,384,128]{2,1,0:T(8,128)(2,1)}), bf16[8,384,128]{2,1,0:T(8,128)(2,1)}, u32[]{:S(2)}, u32[]{:S(2)}) async-start(bf16[8,384,128]{2,1,0:T(8,128)(2,1)} %relax.1), calls=%async_computation.1 | async-start | bytes 1572864 | tf_op jit(solution)/shard_map/all_to_all | solution.py:309
  82.9 0.0 collective-permute-done.4
  82.9 1.0 slice_dynamic-update-slice_fusion
  83.9 0.0 collective-permute-done.5
  83.9 0.0 copy-done.10
  83.9 1.9 %collective-permute-start.6 = (bf16[528,1024]{1,0:T(8,128)(2,1)S(1)}, bf16[528,1024]{1,0:T(8,128)(2,1)S(1)}, u32[]{:S(2)}, u32[]{:S(2)}) collective-permute-start(bf16[528,1024]{1,0:T(8,128)(2,1)S(1)} %constant_dynamic-update-slice_fusion.10.own_ref), channel_id=1, source_target_pairs={{0,1},{1,0},{2,3},{3,2},{4,5},{5,4},{6,7},{7,6},{8,9},{9,8},{10,11... | collective-permute-start | bytes 3244040 | tf_op jit(solution)/shard_map/ppermute | solution.py:307
  85.9 0.0 copy-start.3
  85.9 1.0 copy-done.3
  86.9 0.0 copy-done.11
  86.9 5.3 %collective-permute-start.7 = (bf16[16,1024]{1,0:T(8,128)(2,1)S(1)}, bf16[16,1024]{1,0:T(8,128)(2,1)S(1)}, u32[]{:S(2)}, u32[]{:S(2)}) collective-permute-start(bf16[16,1024]{1,0:T(8,128)(2,1)S(1)} %copy-done.11), channel_id=1, source_target_pairs={{0,7},{1,2},{2,1},{3,4},{4,3},{5,6},{6,5},{7,0},{8,15},{9,10},{10,... | collective-permute-start | bytes 98312 | tf_op jit(solution)/shard_map/ppermute | solution.py:305
  92.2 0.1 pad_add_fusion.where_ref
  92.2 0.9 slice.22.lower_ref
  93.2 0.9 slice.23.upper_ref
  94.1 0.0 collective-permute-done.6.other_ref
  94.1 0.0 copy-start.1
  94.1 1.0 copy-done.1
  95.1 1.2 %copy-done.2 = bf16[528,1024]{1,0:T(8,128)(2,1)S(1)} copy-done((bf16[528,1024]{1,0:T(8,128)(2,1)S(1)}, bf16[528,1024]{1,0:T(8,128)(2,1)}, u32[]{:S(2)}) %copy-start.2) | copy-done | bytes 1081368
  96.3 1.2 %copy-done.4 = bf16[528,1024]{1,0:T(8,128)(2,1)S(1)} copy-done((bf16[528,1024]{1,0:T(8,128)(2,1)S(1)}, bf16[528,1024]{1,0:T(8,128)(2,1)}, u32[]{:S(2)}) %copy-start.4) | copy-done | bytes 1081368
  97.6 1.3 %assemble.1.weights_ref = bf16[1024,1024]{1,0:T(8,128)(2,1)S(1)} custom-call(s32[3]{0:T(128)S(1)} %pad_add_fusion.where_ref, bf16[528,1024]{1,0:T(8,128)(2,1)S(1)} %copy-done.4, bf16[528,1024]{1,0:T(8,128)(2,1)S(1)} %copy-done.2), custom_call_target="tpu_custom_call" | custom-call | tf_op jit(solution)/shard_map/assemble/pallas_call | solution.py:147
  98.9 0.6 collective-permute-done.7.outer_ref
  99.5 5.1 %all-to-all-done.1.back_ref = bf16[8,384,128]{2,1,0:T(8,128)(2,1)} async-done(((bf16[8,384,128]{2,1,0:T(8,128)(2,1)}), bf16[8,384,128]{2,1,0:T(8,128)(2,1)}, u32[]{:S(2)}, u32[]{:S(2)}) %all-to-all-start.1) | async-done | bytes 786464 | tf_op jit(solution)/shard_map/all_to_all | solution.py:309
  104.7 0.0 copy-done
  104.7 3.7 %advance.1 = bf16[3,32,4096]{2,1,0:T(8,128)(2,1)} custom-call(s32[1]{0:T(128)} %bitcast.core_ref, bf16[3,32,4096]{2,1,0:T(8,128)(2,1)S(1)} %copy-done, bf16[8,384,128]{2,1,0:T(8,128)(2,1)} %all-to-all-done.1.back_ref, bf16[1024,1024]{1,0:T(8,128)(2,1)S(1)} %assemble.1.weights_ref, bf16[64,1024]{1,0:T(8,128)(2,1)S(1)} %slice.22.lower_ref, ...), custom_call_target="tpu_custom_call" | custom-call | tf_op jit(solution)/shard_map/advance/pallas_call | solution.py:272
  (20 shorter events, 0.2 us)
Async XLA Ops:
  0.0 20.7 %collective-permute-start = (bf16[16,1024]{1,0:T(8,128)(2,1)}, bf16[16,1024]{1,0:T(8,128)(2,1)S(1)}, u32[]{:S(2)}, u32[]{:S(2)}) collective-permute-start(bf16[16,1024]{1,0:T(8,128)(2,1)} %param.5), channel_id=1, source_target_pairs={{0,2},{1,3},{2,0},{3,1},{4,6},{5,7},{6,4},{7,5},{8,10},{9,11},{10,... | collective-permute-start | bytes 98312 | tf_op jit(solution)/shard_map/ppermute | solution.py:298
  6.8 13.8 %copy-start.6 = (bf16[16,1024]{1,0:T(8,128)(2,1)S(1)}, bf16[16,1024]{1,0:T(8,128)(2,1)}, u32[]{:S(2)}) copy-start(bf16[16,1024]{1,0:T(8,128)(2,1)} %param.5) | copy-start | bytes 98308
  6.8 64.0 %all-to-all-start = ((bf16[8,400,128]{2,1,0:T(8,128)(2,1)}), bf16[8,400,128]{2,1,0:T(8,128)(2,1)S(1)}, u32[]{:S(2)}, u32[]{:S(2)}) async-start(bf16[8,400,128]{2,1,0:T(8,128)(2,1)} %pack.1), calls=%async_computation | async-start | bytes 1638400 | tf_op jit(solution)/shard_map/all_to_all | solution.py:294
  20.7 35.3 %copy-start.9 = (bf16[64,1024]{1,0:T(8,128)(2,1)S(1)}, bf16[64,1024]{1,0:T(8,128)(2,1)}, u32[]{:S(2)}) copy-start(bf16[64,1024]{1,0:T(8,128)(2,1)} %get-tuple-element.9) | copy-start | bytes 393220
  20.7 37.2 %copy-start.8 = (bf16[64,1024]{1,0:T(8,128)(2,1)S(1)}, bf16[64,1024]{1,0:T(8,128)(2,1)}, u32[]{:S(2)}) copy-start(bf16[64,1024]{1,0:T(8,128)(2,1)} %get-tuple-element.10) | copy-start | bytes 393220
  20.7 21.3 %collective-permute-start.1 = (bf16[32,1024]{1,0:T(8,128)(2,1)S(1)}, bf16[32,1024]{1,0:T(8,128)(2,1)S(1)}, u32[]{:S(2)}, u32[]{:S(2)}) collective-permute-start(bf16[32,1024]{1,0:T(8,128)(2,1)S(1)} %pad_maximum_fusion.2), channel_id=1, source_target_pairs={{0,4},{1,5},{2,6},{3,7},{4,0},{5,1},{6,2},{7,3},{8,12},{9,13},{10,... | collective-permute-start | bytes 196616 | tf_op jit(solution)/shard_map/ppermute | solution.py:299
  42.0 13.9 %collective-permute-start.2 = (bf16[64,1024]{1,0:T(8,128)(2,1)S(1)}, bf16[64,1024]{1,0:T(8,128)(2,1)S(1)}, u32[]{:S(2)}, u32[]{:S(2)}) collective-permute-start(bf16[64,1024]{1,0:T(8,128)(2,1)S(1)} %pad_maximum_fusion.1), channel_id=1, source_target_pairs={{0,32},{8,40},{16,48},{24,56},{32,0},{40,8},{48,16},{56,24},{1,33}... | collective-permute-start | bytes 393224 | tf_op jit(solution)/shard_map/ppermute | solution.py:300
  55.9 14.8 %collective-permute-start.3 = (bf16[192,1024]{1,0:T(8,128)(2,1)S(1)}, bf16[192,1024]{1,0:T(8,128)(2,1)S(1)}, u32[]{:S(2)}, u32[]{:S(2)}) collective-permute-start(bf16[192,1024]{1,0:T(8,128)(2,1)S(1)} %constant_dynamic-update-slice_fusion), channel_id=1, source_target_pairs={{0,56},{8,0},{16,8},{24,16},{32,24},{40,32},{48,40},{56,48},{1,57}... | collective-permute-start | bytes 1179656 | tf_op jit(solution)/shard_map/ppermute | solution.py:302
  57.9 25.0 %collective-permute-start.4 = (bf16[192,1024]{1,0:T(8,128)(2,1)S(1)}, bf16[192,1024]{1,0:T(8,128)(2,1)}, u32[]{:S(2)}, u32[]{:S(2)}) collective-permute-start(bf16[192,1024]{1,0:T(8,128)(2,1)S(1)} %constant_dynamic-update-slice_fusion.5), channel_id=1, source_target_pairs={{0,8},{8,16},{16,24},{24,32},{32,40},{40,48},{48,56},{56,0},{1,9},... | collective-permute-start | bytes 1179656 | tf_op jit(solution)/shard_map/ppermute | solution.py:303
  64.5 19.4 %collective-permute-start.5 = (bf16[128,1024]{1,0:T(8,128)(2,1)}, bf16[128,1024]{1,0:T(8,128)(2,1)S(1)}, u32[]{:S(2)}, u32[]{:S(2)}) collective-permute-start(bf16[128,1024]{1,0:T(8,128)(2,1)} %pad_maximum_fusion), channel_id=1, source_target_pairs={{0,16},{8,56},{16,32},{24,8},{32,48},{40,24},{48,0},{56,40},{1,17}... | collective-permute-start | bytes 786440 | tf_op jit(solution)/shard_map/ppermute | solution.py:304
  70.7 4.6 %copy-start.7 = (bf16[192,1024]{1,0:T(8,128)(2,1)}, bf16[192,1024]{1,0:T(8,128)(2,1)S(1)}, u32[]{:S(2)}) copy-start(bf16[192,1024]{1,0:T(8,128)(2,1)S(1)} %collective-permute-done.3) | copy-start | bytes 1179652
  70.8 1.0 copy-start.5
  75.3 8.6 %copy-start.10 = (bf16[16,1024]{1,0:T(8,128)(2,1)S(1)}, bf16[16,1024]{1,0:T(8,128)(2,1)}, u32[]{:S(2)}) copy-start(bf16[16,1024]{1,0:T(8,128)(2,1)} %get-tuple-element.11) | copy-start | bytes 98308
  75.3 11.5 %copy-start.11 = (bf16[16,1024]{1,0:T(8,128)(2,1)S(1)}, bf16[16,1024]{1,0:T(8,128)(2,1)}, u32[]{:S(2)}) copy-start(bf16[16,1024]{1,0:T(8,128)(2,1)} %get-tuple-element.12) | copy-start | bytes 98308
  75.3 29.3 %all-to-all-start.1 = ((bf16[8,384,128]{2,1,0:T(8,128)(2,1)}), bf16[8,384,128]{2,1,0:T(8,128)(2,1)}, u32[]{:S(2)}, u32[]{:S(2)}) async-start(bf16[8,384,128]{2,1,0:T(8,128)(2,1)} %relax.1), calls=%async_computation.1 | async-start | bytes 1572864 | tf_op jit(solution)/shard_map/all_to_all | solution.py:309
  83.9 10.1 %collective-permute-start.6 = (bf16[528,1024]{1,0:T(8,128)(2,1)S(1)}, bf16[528,1024]{1,0:T(8,128)(2,1)S(1)}, u32[]{:S(2)}, u32[]{:S(2)}) collective-permute-start(bf16[528,1024]{1,0:T(8,128)(2,1)S(1)} %constant_dynamic-update-slice_fusion.10.own_ref), channel_id=1, source_target_pairs={{0,1},{1,0},{2,3},{3,2},{4,5},{5,4},{6,7},{7,6},{8,9},{9,8},{10,11... | collective-permute-start | bytes 3244040 | tf_op jit(solution)/shard_map/ppermute | solution.py:307
  85.9 1.0 copy-start.3
  86.9 12.7 %collective-permute-start.7 = (bf16[16,1024]{1,0:T(8,128)(2,1)S(1)}, bf16[16,1024]{1,0:T(8,128)(2,1)S(1)}, u32[]{:S(2)}, u32[]{:S(2)}) collective-permute-start(bf16[16,1024]{1,0:T(8,128)(2,1)S(1)} %copy-done.11), channel_id=1, source_target_pairs={{0,7},{1,2},{2,1},{3,4},{4,3},{5,6},{6,5},{7,0},{8,15},{9,10},{10,... | collective-permute-start | bytes 98312 | tf_op jit(solution)/shard_map/ppermute | solution.py:305
  94.1 1.0 copy-start.1
  95.1 1.2 %copy-start.2 = (bf16[528,1024]{1,0:T(8,128)(2,1)S(1)}, bf16[528,1024]{1,0:T(8,128)(2,1)}, u32[]{:S(2)}) copy-start(bf16[528,1024]{1,0:T(8,128)(2,1)} %copy-done.1) | copy-start | bytes 3244036
  96.3 1.2 %copy-start.4 = (bf16[528,1024]{1,0:T(8,128)(2,1)S(1)}, bf16[528,1024]{1,0:T(8,128)(2,1)}, u32[]{:S(2)}) copy-start(bf16[528,1024]{1,0:T(8,128)(2,1)} %copy-done.3) | copy-start | bytes 3244036
  97.6 7.1 %copy-start = (bf16[3,32,4096]{2,1,0:T(8,128)(2,1)S(1)}, bf16[3,32,4096]{2,1,0:T(8,128)(2,1)}, u32[]{:S(2)}) copy-start(bf16[3,32,4096]{2,1,0:T(8,128)(2,1)} %f_ref.5) | copy-start | bytes 2359300

commit v3 on v2

--- a/solution.py
+++ b/solution.py
@@ -21,6 +21,7 @@
 DATA = PLANES * CELLS
 CHUNK = DATA + 16
 TILE = 16
+LIMIT = 16 << 20
 F32 = jnp.float32
 BF16 = jnp.bfloat16
 
@@ -92,6 +93,7 @@
         out_shape=jax.ShapeDtypeStruct((GROUP, CHUNK, BLOCK), BF16),
         in_specs=[smem(), vmem(), vmem()],
         out_specs=vmem(),
+        compiler_params=pltpu.CompilerParams(vmem_limit_bytes=LIMIT),
         name="pack",
     )(place, f, jnp.asarray(moment_basis()))
 
@@ -126,11 +128,12 @@
         out_shape=(row, row, column, column),
         in_specs=[smem(), vmem()],
         out_specs=(vmem(),) * 4,
+        compiler_params=pltpu.CompilerParams(vmem_limit_bytes=LIMIT),
         name="edges",
     )(core, f)
 
 
-def assemble_kernel(where_ref, own_ref, other_ref, out_ref, rows_ref):
+def assemble_kernel(where_ref, own_ref, other_ref, out_ref, inner_ref, rows_ref):
     core, z, y = where_ref[0], where_ref[1], where_ref[2]
     far = jnp.where(y % 2 == 0, y + 6, y + 2)
     for m, base in enumerate((y, y + 1, y + 7, far)):
@@ -140,17 +143,21 @@
                 block = slice((m * 8 + i * 4 + j) * 16, (m * 8 + i * 4 + j + 1) * 16)
                 rows_ref[place + core] = own_ref[block, :]
                 rows_ref[place + 1 - core] = other_ref[block, :]
+    inner_ref[...] = other_ref[NXY // 2 : NXY // 2 + 16, :]
     out_ref[...] = jnp.transpose(rows_ref[...].reshape(NXY, NXY))
 
 
 def assemble(where, own, other):
     return pl.pallas_call(
         assemble_kernel,
-        out_shape=jax.ShapeDtypeStruct((NXY, NXY), BF16),
+        out_shape=(
+            jax.ShapeDtypeStruct((NXY, NXY), BF16),
+            jax.ShapeDtypeStruct((16, NXY), BF16),
+        ),
         in_specs=[smem(), vmem(), vmem()],
-        out_specs=vmem(),
+        out_specs=(vmem(), vmem()),
         scratch_shapes=[pltpu.VMEM((NXY // 16, 16, NXY), BF16)],
-        compiler_params=pltpu.CompilerParams(vmem_limit_bytes=32 << 20),
+        compiler_params=pltpu.CompilerParams(vmem_limit_bytes=LIMIT),
         name="assemble",
     )(where, own, other)
 
@@ -174,6 +181,7 @@
         out_shape=jax.ShapeDtypeStruct((size, size), BF16),
         in_specs=[vmem()],
         out_specs=vmem(),
+        compiler_params=pltpu.CompilerParams(vmem_limit_bytes=LIMIT),
         name="spread",
     )(depth_weights)
 
@@ -224,6 +232,7 @@
         in_specs=[smem(), vmem(), vmem()],
         out_specs=vmem(),
         scratch_shapes=[pltpu.VMEM((NVZ * TILE, CELLS // TILE * BLOCK), BF16)],
+        compiler_params=pltpu.CompilerParams(vmem_limit_bytes=LIMIT),
         name="relax",
     )(place, got, mix)
 
@@ -238,6 +247,7 @@
     cx = courant_across * jnp.abs(vx)
     cy = courant_along * jnp.abs(vy)
     upwind = vy > 0.0
+    edge = lower_ref.shape[0] - 2 * COLS
     inner = inner_ref[...].astype(F32)
     outer = outer_ref[...].astype(F32)
     core = core_ref[0]
@@ -250,7 +260,7 @@
         lanes = slice(p * NXY, (p + 1) * NXY)
         first_half = slice(p * NXY, p * NXY + half)
         second_half = slice(p * NXY + half, (p + 1) * NXY)
-        rows = slice(p // 2 * COLS, (p // 2 + 1) * COLS)
+        rows = slice(edge + p // 2 * COLS, edge + (p // 2 + 1) * COLS)
         packed = slice(p % 2 * half, (p % 2 + 1) * half)
         for r in range(ROWS):
             current = f_ref[r, :, lanes].astype(F32)
@@ -275,7 +285,7 @@
         in_specs=[smem()] + [vmem()] * 7,
         out_specs=vmem(),
         scratch_shapes=[pltpu.VMEM((DATA, NXY), F32)],
-        compiler_params=pltpu.CompilerParams(vmem_limit_bytes=48 << 20),
+        compiler_params=pltpu.CompilerParams(vmem_limit_bytes=LIMIT),
         name="advance",
     )(core, f, back, weights, lower, upper, inner, outer)
 
@@ -290,13 +300,15 @@
     along = lax.axis_index("sy").astype(jnp.int32)
     core = jnp.bitwise_and(along, 1).reshape(1)
     where = jnp.stack([jnp.bitwise_and(along, 1), along >> 1, lax.axis_index("sx").astype(jnp.int32)])
+    flip = lambda bit: [(i, i ^ bit) for i in range(8)]
     send = pack(place, distribution)
+    held = jnp.concatenate([plane_weights, lax.ppermute(plane_weights, "sy", flip(2))])
+    send, held = lax.optimization_barrier((send, held))
+    held = jnp.concatenate([held, lax.ppermute(held, "sy", flip(4))])
+    send, held = lax.optimization_barrier((send, held))
     got = lax.all_to_all(send, "vel", 0, 0, tiled=True)
     mix = spread(depth_weights)
     low, high, inner, outer = edges(core, distribution)
-    flip = lambda bit: [(i, i ^ bit) for i in range(8)]
-    held = jnp.concatenate([plane_weights, lax.ppermute(plane_weights, "sy", flip(2))])
-    held = jnp.concatenate([held, lax.ppermute(held, "sy", flip(4))])
     held = jnp.concatenate([held, lax.ppermute(held, "sx", flip(4))])
     size = held.shape[0]
     above = lax.ppermute(jnp.concatenate([held, low]), "sx", ring("sx", -1))
@@ -305,10 +317,10 @@
     outer = lax.ppermute(outer, "sy", [(i, (i + 1) % 8 if i % 2 else (i - 1) % 8) for i in range(8)])
     own = jnp.concatenate([held, above[:size], below[:size], across, inner])
     other = lax.ppermute(own, "sy", flip(1))
-    weights = assemble(where, own, other)
+    weights, inner = assemble(where, own, other)
     back = lax.all_to_all(relax(place, got, mix), "vel", 0, 0, tiled=True)
     return advance(
-        core, distribution, back, weights, below[size:], above[size:], other[4 * size :], outer
+        core, distribution, back, weights, below, above, inner, outer
     )
 
 

time: 109 us -> 92.4 us (0.85)
  the two profiles are of different devices: /device:TPU:8 before, /device:TPU:136 now
where the time goes in v3:
time: 92.4 us; the launch traced here: 91.7 us
  starting transfers between devices  49.8 us (54%)
  waiting for transfers between devices  22.6 us (24%)
  Pallas kernels  9.74 us (11%)
  local copies, waits for them, and re-layouts  7.73 us (8%)
  other arithmetic  1.63 us (2%)
    all_to_all x1, waiting for transfers between devices, local(): back = lax.all_to_all(relax(place, got, mix), 'vel', 0, 0, tiled=True)  12.2 us
    all_to_all x1, starting transfers between devices, local(): got = lax.all_to_all(send, 'vel', 0, 0, tiled=True)  10.1 us
    all_to_all x1, starting transfers between devices, local(): back = lax.all_to_all(relax(place, got, mix), 'vel', 0, 0, tiled=True)  9.73 us
    unnamed x23, local copies, waits for them, and re-layouts  7.73 us
    ppermute x1, starting transfers between devices, local(): lax.ppermute(held, 'sx', [(i, (i + 2) % 8 if i % 2 == 0 else (i - 2) % 8)...  6.97 us
    ppermute x1, starting transfers between devices, local(): held = jnp.concatenate([held, lax.ppermute(held, 'sx', flip(4))])  6.83 us
    ppermute x1, waiting for transfers between devices, local(): held = jnp.concatenate([held, lax.ppermute(held, 'sy', flip(4))])  5.13 us
    ppermute x1, waiting for transfers between devices, local(): held = jnp.concatenate([held, lax.ppermute(held, 'sx', flip(4))])  4.5 us
  transfers between devices with their start and end apart: 10, of which 4 were waited for; matrix products, arithmetic and copies ran while one was open for 4% of the time, Pallas kernels for 7%

profile of v3, /device:TPU:136, one launch (start us, length us, event | category | flops | bytes accessed | tf_op | source)
XLA Modules:
  0.0 91.7 jit_solution(14814455458398474882)
XLA Ops:
  0.0 4.3 %collective-permute-start = (bf16[16,1024]{1,0:T(8,128)(2,1)}, bf16[16,1024]{1,0:T(8,128)(2,1)S(1)}, u32[]{:S(2)}, u32[]{:S(2)}) collective-permute-start(bf16[16,1024]{1,0:T(8,128)(2,1)} %param.5), channel_id=1, source_target_pairs={{0,2},{1,3},{2,0},{3,1},{4,6},{5,7},{6,4},{7,5},{8,10},{9,11},{10,... | collective-permute-start | bytes 98312 | tf_op jit(solution)/shard_map/ppermute | solution.py:305
  4.3 0.0 copy-start
  4.3 1.1 %copy-done = bf16[3,32,4096]{2,1,0:T(8,128)(2,1)S(1)} copy-done((bf16[3,32,4096]{2,1,0:T(8,128)(2,1)S(1)}, bf16[3,32,4096]{2,1,0:T(8,128)(2,1)}, u32[]{:S(2)}) %copy-start) | copy-done | bytes 786456
  5.4 0.0 copy-start.6
  5.4 0.9 %copy-done.6 = bf16[1024,128]{1,0:T(8,128)(2,1)S(1)} copy-done((bf16[1024,128]{1,0:T(8,128)(2,1)S(1)}, bf16[1024,128]{1,0:T(8,128)(2,1)}, u32[]{:S(2)}) %copy-start.6) | copy-done | bytes 262168
  6.4 0.0 copy-start.8
  6.4 1.3 %pack.1 = bf16[8,400,128]{2,1,0:T(8,128)(2,1)} custom-call(s32[1]{0:T(128)} %bitcast.1.place_ref, bf16[3,32,4096]{2,1,0:T(8,128)(2,1)S(1)} %copy-done, bf16[1024,128]{1,0:T(8,128)(2,1)S(1)} %copy-done.6), custom_call_target="tpu_custom_call" | custom-call | tf_op jit(solution)/shard_map/pack/pallas_call | solution.py:91
  7.7 0.0 copy-start.1
  7.7 0.0 collective-permute-done
  7.7 0.0 copy-done.8
  7.7 2.1 %collective-permute-start.1 = (bf16[32,1024]{1,0:T(8,128)(2,1)S(1)}, bf16[32,1024]{1,0:T(8,128)(2,1)S(1)}, u32[]{:S(2)}, u32[]{:S(2)}) collective-permute-start(bf16[32,1024]{1,0:T(8,128)(2,1)S(1)} %pad_maximum_fusion.5), channel_id=1, source_target_pairs={{0,4},{1,5},{2,6},{3,7},{4,0},{5,1},{6,2},{7,3},{8,12},{9,13},{10,... | collective-permute-start | bytes 196616 | tf_op jit(solution)/shard_map/ppermute | solution.py:307
  9.8 5.1 %collective-permute-done.1 = bf16[32,1024]{1,0:T(8,128)(2,1)S(1)} collective-permute-done((bf16[32,1024]{1,0:T(8,128)(2,1)S(1)}, bf16[32,1024]{1,0:T(8,128)(2,1)S(1)}, u32[]{:S(2)}, u32[]{:S(2)}) %collective-permute-start.1) | collective-permute-done | bytes 65568 | tf_op jit(solution)/shard_map/ppermute | solution.py:307
  14.9 10.1 %all-to-all-start = ((bf16[8,400,128]{2,1,0:T(8,128)(2,1)}), bf16[8,400,128]{2,1,0:T(8,128)(2,1)S(1)}, u32[]{:S(2)}, u32[]{:S(2)}) async-start(bf16[8,400,128]{2,1,0:T(8,128)(2,1)} %pack.1), calls=%async_computation | async-start | bytes 1638400 | tf_op jit(solution)/shard_map/all_to_all | solution.py:309
  25.0 6.8 %collective-permute-start.2 = (bf16[64,1024]{1,0:T(8,128)(2,1)S(1)}, bf16[64,1024]{1,0:T(8,128)(2,1)S(1)}, u32[]{:S(2)}, u32[]{:S(2)}) collective-permute-start(bf16[64,1024]{1,0:T(8,128)(2,1)S(1)} %pad_maximum_fusion.4), channel_id=1, source_target_pairs={{0,32},{8,40},{16,48},{24,56},{32,0},{40,8},{48,16},{56,24},{1,33}... | collective-permute-start | bytes 393224 | tf_op jit(solution)/shard_map/ppermute | solution.py:312
  31.8 0.0 copy-done.1
  31.8 0.1 edges.1
  31.9 4.5 %collective-permute-done.2 = bf16[64,1024]{1,0:T(8,128)(2,1)S(1)} collective-permute-done((bf16[64,1024]{1,0:T(8,128)(2,1)S(1)}, bf16[64,1024]{1,0:T(8,128)(2,1)S(1)}, u32[]{:S(2)}, u32[]{:S(2)}) %collective-permute-start.2) | collective-permute-done | bytes 131104 | tf_op jit(solution)/shard_map/ppermute | solution.py:312
  36.4 0.8 pad_maximum_fusion.2
  37.3 3.2 %collective-permute-start.3 = (bf16[192,1024]{1,0:T(8,128)(2,1)S(1)}, bf16[192,1024]{1,0:T(8,128)(2,1)S(1)}, u32[]{:S(2)}, u32[]{:S(2)}) collective-permute-start(bf16[192,1024]{1,0:T(8,128)(2,1)S(1)} %get-tuple-element.26), channel_id=1, source_target_pairs={{0,56},{8,0},{16,8},{24,16},{32,24},{40,32},{48,40},{56,48},{1,57}... | collective-permute-start | bytes 1179656 | tf_op jit(solution)/shard_map/ppermute | solution.py:314
  40.4 0.0 copy-done.7
  40.4 0.4 spread.1.mix_ref
  40.9 2.9 %collective-permute-start.4 = (bf16[192,1024]{1,0:T(8,128)(2,1)}, bf16[192,1024]{1,0:T(8,128)(2,1)}, u32[]{:S(2)}, u32[]{:S(2)}) collective-permute-start(bf16[192,1024]{1,0:T(8,128)(2,1)} %get-tuple-element.25), channel_id=1, source_target_pairs={{0,8},{8,16},{16,24},{24,32},{32,40},{40,48},{48,56},{56,0},{1,9},... | collective-permute-start | bytes 1179656 | tf_op jit(solution)/shard_map/ppermute | solution.py:315
  43.7 0.7 pad_maximum_fusion.3
  44.5 7.0 %collective-permute-start.5 = (bf16[128,1024]{1,0:T(8,128)(2,1)}, bf16[128,1024]{1,0:T(8,128)(2,1)}, u32[]{:S(2)}, u32[]{:S(2)}) collective-permute-start(bf16[128,1024]{1,0:T(8,128)(2,1)} %pad_maximum_fusion.3), channel_id=1, source_target_pairs={{0,16},{8,56},{16,32},{24,8},{32,48},{40,24},{48,0},{56,40},{1,17}... | collective-permute-start | bytes 786440 | tf_op jit(solution)/shard_map/ppermute | solution.py:316
  51.5 0.0 collective-permute-done.3.upper_ref
  51.5 0.0 copy-start.4
  51.5 0.7 copy-done.4
  52.2 0.0 all-to-all-done.got_ref
  52.2 2.3 %relax.1 = bf16[8,384,128]{2,1,0:T(8,128)(2,1)} custom-call(s32[1]{0:T(128)} %bitcast.1.place_ref, bf16[8,400,128]{2,1,0:T(8,128)(2,1)S(1)} %all-to-all-done.got_ref, bf16[512,512]{1,0:T(8,128)(2,1)S(1)} %spread.1.mix_ref), custom_call_target="tpu_custom_call" | custom-call | tf_op jit(solution)/shard_map/relax/pallas_call | solution.py:229
  54.5 9.7 %all-to-all-start.1 = ((bf16[8,384,128]{2,1,0:T(8,128)(2,1)}), bf16[8,384,128]{2,1,0:T(8,128)(2,1)S(1)}, u32[]{:S(2)}, u32[]{:S(2)}) async-start(bf16[8,384,128]{2,1,0:T(8,128)(2,1)} %relax.1), calls=%async_computation.1 | async-start | bytes 1572864 | tf_op jit(solution)/shard_map/all_to_all | solution.py:321
  64.3 0.0 collective-permute-done.4.lower_ref
  64.3 1.0 %slice_dynamic-update-slice_fusion = bf16[528,1024]{1,0:T(8,128)(2,1)S(1)} fusion(bf16[528,1024]{1,0:T(8,128)(2,1)S(1)} %slice_dynamic-update-slice_fusion.1, bf16[192,1024]{1,0:T(8,128)(2,1)} %collective-permute-done.4.lower_ref), kind=kLoop, calls=%fused_computation.3 | loop fusion | bytes 524288
  65.3 0.0 collective-permute-done.5
  65.3 1.0 %constant_dynamic-update-slice_fusion.1 = bf16[528,1024]{1,0:T(8,128)(2,1)S(1)} fusion(bf16[528,1024]{1,0:T(8,128)(2,1)S(1)} %slice_dynamic-update-slice_fusion, bf16[128,1024]{1,0:T(8,128)(2,1)} %collective-permute-done.5), kind=kLoop, calls=%fused_computation.9 | loop fusion | bytes 524288
  66.2 1.9 %collective-permute-start.6 = (bf16[528,1024]{1,0:T(8,128)(2,1)S(1)}, bf16[528,1024]{1,0:T(8,128)(2,1)}, u32[]{:S(2)}, u32[]{:S(2)}) collective-permute-start(bf16[528,1024]{1,0:T(8,128)(2,1)S(1)} %constant_dynamic-update-slice_fusion.own_ref), channel_id=1, source_target_pairs={{0,1},{1,0},{2,3},{3,2},{4,5},{5,4},{6,7},{7,6},{8,9},{9,8},{10,11... | collective-permute-start | bytes 3244040 | tf_op jit(solution)/shard_map/ppermute | solution.py:319
  68.2 1.9 %collective-permute-start.7 = (bf16[16,1024]{1,0:T(8,128)(2,1)S(1)}, bf16[16,1024]{1,0:T(8,128)(2,1)S(1)}, u32[]{:S(2)}, u32[]{:S(2)}) collective-permute-start(bf16[16,1024]{1,0:T(8,128)(2,1)S(1)} %get-tuple-element.24), channel_id=1, source_target_pairs={{0,7},{1,2},{2,1},{3,4},{4,3},{5,6},{6,5},{7,0},{8,15},{9,10},{10,... | collective-permute-start | bytes 98312 | tf_op jit(solution)/shard_map/ppermute | solution.py:317
  70.1 0.1 pad_add_fusion.where_ref
  70.2 0.0 copy-start.5
  70.2 0.8 collective-permute-done.6.other_ref
  71.0 2.0 %assemble.1 = (bf16[1024,1024]{1,0:T(8,128)(2,1)S(1)}, bf16[16,1024]{1,0:T(8,128)(2,1)S(1)}) custom-call(s32[3]{0:T(128)S(1)} %pad_add_fusion.where_ref, bf16[528,1024]{1,0:T(8,128)(2,1)S(1)} %constant_dynamic-update-slice_fusion.own_ref, bf16[528,1024]{1,0:T(8,128)(2,1)} %collective-permute-done.6.other_ref), custom_call_target="tpu_custom_call" | custom-call | tf_op jit(solution)/shard_map/assemble/pallas_call | solution.py:151
  73.0 0.0 copy-start.2
  73.0 1.3 %copy-done.2 = bf16[1024,1024]{1,0:T(8,128)(2,1)} copy-done((bf16[1024,1024]{1,0:T(8,128)(2,1)}, bf16[1024,1024]{1,0:T(8,128)(2,1)S(1)}, u32[]{:S(2)}) %copy-start.2) | copy-done | bytes 2097176
  74.3 0.0 collective-permute-done.7.outer_ref
  74.4 12.2 %all-to-all-done.1.back_ref = bf16[8,384,128]{2,1,0:T(8,128)(2,1)S(1)} async-done(((bf16[8,384,128]{2,1,0:T(8,128)(2,1)}), bf16[8,384,128]{2,1,0:T(8,128)(2,1)S(1)}, u32[]{:S(2)}, u32[]{:S(2)}) %all-to-all-start.1) | async-done | bytes 786464 | tf_op jit(solution)/shard_map/all_to_all | solution.py:321
  86.5 0.0 copy-done.5
  86.5 0.0 copy-start.3
  86.5 1.6 %copy-done.3 = bf16[1024,1024]{1,0:T(8,128)(2,1)S(1)} copy-done((bf16[1024,1024]{1,0:T(8,128)(2,1)S(1)}, bf16[1024,1024]{1,0:T(8,128)(2,1)}, u32[]{:S(2)}) %copy-start.3) | copy-done | bytes 2097176
  88.1 3.6 %advance.1 = bf16[3,32,4096]{2,1,0:T(8,128)(2,1)} custom-call(s32[1]{0:T(128)} %bitcast.core_ref, bf16[3,32,4096]{2,1,0:T(8,128)(2,1)S(1)} %copy-done.1, bf16[8,384,128]{2,1,0:T(8,128)(2,1)S(1)} %all-to-all-done.1.back_ref, bf16[1024,1024]{1,0:T(8,128)(2,1)S(1)} %copy-done.3, bf16[192,1024]{1,0:T(8,128)(2,1)} %collective-permute-done.4.lower_ref, ...), custom_call_target="tpu_custom_call" | custom-call | tf_op jit(solution)/shard_map/advance/pallas_call | solution.py:282
  (7 shorter events, 0.1 us)
Async XLA Ops:
  0.0 7.7 %collective-permute-start = (bf16[16,1024]{1,0:T(8,128)(2,1)}, bf16[16,1024]{1,0:T(8,128)(2,1)S(1)}, u32[]{:S(2)}, u32[]{:S(2)}) collective-permute-start(bf16[16,1024]{1,0:T(8,128)(2,1)} %param.5), channel_id=1, source_target_pairs={{0,2},{1,3},{2,0},{3,1},{4,6},{5,7},{6,4},{7,5},{8,10},{9,11},{10,... | collective-permute-start | bytes 98312 | tf_op jit(solution)/shard_map/ppermute | solution.py:305
  4.3 1.1 %copy-start = (bf16[3,32,4096]{2,1,0:T(8,128)(2,1)S(1)}, bf16[3,32,4096]{2,1,0:T(8,128)(2,1)}, u32[]{:S(2)}) copy-start(bf16[3,32,4096]{2,1,0:T(8,128)(2,1)} %f_ref.5) | copy-start | bytes 2359300
  5.4 0.9 %copy-start.6 = (bf16[1024,128]{1,0:T(8,128)(2,1)S(1)}, bf16[1024,128]{1,0:T(8,128)(2,1)}, u32[]{:S(2)}) copy-start(bf16[1024,128]{1,0:T(8,128)(2,1)} %constant.15.clone.basis_ref) | copy-start | bytes 786436
  6.4 1.3 %copy-start.8 = (bf16[16,1024]{1,0:T(8,128)(2,1)S(1)}, bf16[16,1024]{1,0:T(8,128)(2,1)}, u32[]{:S(2)}) copy-start(bf16[16,1024]{1,0:T(8,128)(2,1)} %param.5) | copy-start | bytes 98308
  7.7 24.1 %copy-start.1 = (bf16[3,32,4096]{2,1,0:T(8,128)(2,1)S(1)}, bf16[3,32,4096]{2,1,0:T(8,128)(2,1)}, u32[]{:S(2)}) copy-start(bf16[3,32,4096]{2,1,0:T(8,128)(2,1)} %f_ref.5) | copy-start | bytes 2359300
  7.7 7.2 %collective-permute-start.1 = (bf16[32,1024]{1,0:T(8,128)(2,1)S(1)}, bf16[32,1024]{1,0:T(8,128)(2,1)S(1)}, u32[]{:S(2)}, u32[]{:S(2)}) collective-permute-start(bf16[32,1024]{1,0:T(8,128)(2,1)S(1)} %pad_maximum_fusion.5), channel_id=1, source_target_pairs={{0,4},{1,5},{2,6},{3,7},{4,0},{5,1},{6,2},{7,3},{8,12},{9,13},{10,... | collective-permute-start | bytes 196616 | tf_op jit(solution)/shard_map/ppermute | solution.py:307
  14.9 37.3 %all-to-all-start = ((bf16[8,400,128]{2,1,0:T(8,128)(2,1)}), bf16[8,400,128]{2,1,0:T(8,128)(2,1)S(1)}, u32[]{:S(2)}, u32[]{:S(2)}) async-start(bf16[8,400,128]{2,1,0:T(8,128)(2,1)} %pack.1), calls=%async_computation | async-start | bytes 1638400 | tf_op jit(solution)/shard_map/all_to_all | solution.py:309
  25.0 15.5 %copy-start.7 = (bf16[32,32]{1,0:T(8,128)(2,1)S(1)}, bf16[32,32]{1,0:T(8,128)(2,1)}, u32[]{:S(2)}) copy-start(bf16[32,32]{1,0:T(8,128)(2,1)} %depth_ref.1) | copy-start | bytes 6148
  25.0 11.5 %collective-permute-start.2 = (bf16[64,1024]{1,0:T(8,128)(2,1)S(1)}, bf16[64,1024]{1,0:T(8,128)(2,1)S(1)}, u32[]{:S(2)}, u32[]{:S(2)}) collective-permute-start(bf16[64,1024]{1,0:T(8,128)(2,1)S(1)} %pad_maximum_fusion.4), channel_id=1, source_target_pairs={{0,32},{8,40},{16,48},{24,56},{32,0},{40,8},{48,16},{56,24},{1,33}... | collective-permute-start | bytes 393224 | tf_op jit(solution)/shard_map/ppermute | solution.py:312
  37.3 14.2 %collective-permute-start.3 = (bf16[192,1024]{1,0:T(8,128)(2,1)S(1)}, bf16[192,1024]{1,0:T(8,128)(2,1)S(1)}, u32[]{:S(2)}, u32[]{:S(2)}) collective-permute-start(bf16[192,1024]{1,0:T(8,128)(2,1)S(1)} %get-tuple-element.26), channel_id=1, source_target_pairs={{0,56},{8,0},{16,8},{24,16},{32,24},{40,32},{48,40},{56,48},{1,57}... | collective-permute-start | bytes 1179656 | tf_op jit(solution)/shard_map/ppermute | solution.py:314
  40.9 23.4 %collective-permute-start.4 = (bf16[192,1024]{1,0:T(8,128)(2,1)}, bf16[192,1024]{1,0:T(8,128)(2,1)}, u32[]{:S(2)}, u32[]{:S(2)}) collective-permute-start(bf16[192,1024]{1,0:T(8,128)(2,1)} %get-tuple-element.25), channel_id=1, source_target_pairs={{0,8},{8,16},{16,24},{24,32},{32,40},{40,48},{48,56},{56,0},{1,9},... | collective-permute-start | bytes 1179656 | tf_op jit(solution)/shard_map/ppermute | solution.py:315
  44.5 20.8 %collective-permute-start.5 = (bf16[128,1024]{1,0:T(8,128)(2,1)}, bf16[128,1024]{1,0:T(8,128)(2,1)}, u32[]{:S(2)}, u32[]{:S(2)}) collective-permute-start(bf16[128,1024]{1,0:T(8,128)(2,1)} %pad_maximum_fusion.3), channel_id=1, source_target_pairs={{0,16},{8,56},{16,32},{24,8},{32,48},{40,24},{48,0},{56,40},{1,17}... | collective-permute-start | bytes 786440 | tf_op jit(solution)/shard_map/ppermute | solution.py:316
  51.5 0.8 copy-start.4
  54.5 32.0 %all-to-all-start.1 = ((bf16[8,384,128]{2,1,0:T(8,128)(2,1)}), bf16[8,384,128]{2,1,0:T(8,128)(2,1)S(1)}, u32[]{:S(2)}, u32[]{:S(2)}) async-start(bf16[8,384,128]{2,1,0:T(8,128)(2,1)} %relax.1), calls=%async_computation.1 | async-start | bytes 1572864 | tf_op jit(solution)/shard_map/all_to_all | solution.py:321
  66.2 4.7 %collective-permute-start.6 = (bf16[528,1024]{1,0:T(8,128)(2,1)S(1)}, bf16[528,1024]{1,0:T(8,128)(2,1)}, u32[]{:S(2)}, u32[]{:S(2)}) collective-permute-start(bf16[528,1024]{1,0:T(8,128)(2,1)S(1)} %constant_dynamic-update-slice_fusion.own_ref), channel_id=1, source_target_pairs={{0,1},{1,0},{2,3},{3,2},{4,5},{5,4},{6,7},{7,6},{8,9},{9,8},{10,11... | collective-permute-start | bytes 3244040 | tf_op jit(solution)/shard_map/ppermute | solution.py:319
  68.2 6.2 %collective-permute-start.7 = (bf16[16,1024]{1,0:T(8,128)(2,1)S(1)}, bf16[16,1024]{1,0:T(8,128)(2,1)S(1)}, u32[]{:S(2)}, u32[]{:S(2)}) collective-permute-start(bf16[16,1024]{1,0:T(8,128)(2,1)S(1)} %get-tuple-element.24), channel_id=1, source_target_pairs={{0,7},{1,2},{2,1},{3,4},{4,3},{5,6},{6,5},{7,0},{8,15},{9,10},{10,... | collective-permute-start | bytes 98312 | tf_op jit(solution)/shard_map/ppermute | solution.py:317
  70.2 16.3 %copy-start.5 = (bf16[192,1024]{1,0:T(8,128)(2,1)S(1)}, bf16[192,1024]{1,0:T(8,128)(2,1)}, u32[]{:S(2)}) copy-start(bf16[192,1024]{1,0:T(8,128)(2,1)} %copy-done.4) | copy-start | bytes 1179652
  73.0 1.3 %copy-start.2 = (bf16[1024,1024]{1,0:T(8,128)(2,1)}, bf16[1024,1024]{1,0:T(8,128)(2,1)S(1)}, u32[]{:S(2)}) copy-start(bf16[1024,1024]{1,0:T(8,128)(2,1)S(1)} %get-tuple-element.22.weights_ref) | copy-start | bytes 6291460
  86.5 1.6 %copy-start.3 = (bf16[1024,1024]{1,0:T(8,128)(2,1)S(1)}, bf16[1024,1024]{1,0:T(8,128)(2,1)}, u32[]{:S(2)}) copy-start(bf16[1024,1024]{1,0:T(8,128)(2,1)} %copy-done.2) | copy-start | bytes 6291460

commit v4 on v3

--- a/solution.py
+++ b/solution.py
@@ -39,6 +39,10 @@
     return pl.BlockSpec(memory_space=pltpu.VMEM)
 
 
+def hbm():
+    return pl.BlockSpec(memory_space=pltpu.HBM)
+
+
 def smem():
     return pl.BlockSpec(memory_space=pltpu.SMEM)
 
@@ -61,18 +65,35 @@
     return basis.astype(BF16)
 
 
-def pack_kernel(place_ref, f_ref, basis_ref, send_ref):
+def pack_kernel(place_ref, f_ref, basis_ref, send_ref, x_ref, base_ref, out_ref, in_sem, base_sem, out_sem):
+    def load(p):
+        lanes = pl.ds(p * NXY, NXY)
+        return pltpu.make_async_copy(f_ref.at[:, :, lanes], x_ref.at[p], in_sem.at[p])
+
+    def store(p):
+        rows = pl.ds(p * CELLS, CELLS)
+        return pltpu.make_async_copy(out_ref.at[:, rows, :], send_ref.at[:, rows, :], out_sem.at[p])
+
+    base = pltpu.make_async_copy(basis_ref, base_ref, base_sem)
+    load(0).start()
+    base.start()
+    for p in range(1, PLANES):
+        load(p).start()
     lane = lax.broadcasted_iota(jnp.int32, (1, 128), 1)
     first_plane = place_ref[0] * PLANES
     total = jnp.zeros((CELLS, 128), F32)
     for p in range(PLANES):
-        x = jnp.concatenate([f_ref[r, :, p * NXY : (p + 1) * NXY] for r in range(ROWS)], axis=0)
-        sums = jnp.dot(x, basis_ref[...], preferred_element_type=F32)
+        load(p).wait()
+        x = x_ref[p].reshape(CELLS, NXY)
+        for v in range(GROUP):
+            out_ref[v, p * CELLS : (p + 1) * CELLS, :] = x[:, v * BLOCK : (v + 1) * BLOCK]
+        store(p).start()
+        if p == 0:
+            base.wait()
+        sums = jnp.dot(x, base_ref[...], preferred_element_type=F32)
         vz = speed(first_plane + p, NVZ)
         factor = jnp.where(lane >= 32, vz * vz, jnp.where((lane < 16) & (lane % 5 == 3), vz, 1.0))
         total = total + sums * factor
-        for v in range(GROUP):
-            send_ref[v, p * CELLS : (p + 1) * CELLS, :] = x[:, v * BLOCK : (v + 1) * BLOCK]
     total = jnp.transpose(total)
     total = (total[0:16, :] + total[16:32, :]) + total[32:48, :]
     column = lax.broadcasted_iota(jnp.int32, (16, CELLS), 0)
@@ -84,18 +105,36 @@
     )
     parts = jnp.concatenate([parts, jnp.zeros((16, 128 - CELLS), F32)], axis=1).astype(BF16)
     for v in range(GROUP):
-        send_ref[v, DATA:CHUNK, :] = parts
+        out_ref[v, DATA:CHUNK, :] = parts
+    tail = pl.ds(DATA, CHUNK - DATA)
+    last = pltpu.make_async_copy(
+        out_ref.at[:, tail, :], send_ref.at[:, tail, :], out_sem.at[PLANES]
+    )
+    last.start()
+    for p in range(PLANES):
+        store(p).wait()
+    last.wait()
 
 
 def pack(place, f):
+    basis = jnp.asarray(moment_basis())
+    f, basis = (pltpu.with_memory_space_constraint(x, pltpu.HBM) for x in (f, basis))
     return pl.pallas_call(
         pack_kernel,
         out_shape=jax.ShapeDtypeStruct((GROUP, CHUNK, BLOCK), BF16),
-        in_specs=[smem(), vmem(), vmem()],
-        out_specs=vmem(),
+        in_specs=[smem(), hbm(), hbm()],
+        out_specs=hbm(),
+        scratch_shapes=[
+            pltpu.VMEM((PLANES, ROWS, COLS, NXY), BF16),
+            pltpu.VMEM((NXY, 128), BF16),
+            pltpu.VMEM((GROUP, CHUNK, BLOCK), BF16),
+            pltpu.SemaphoreType.DMA((PLANES,)),
+            pltpu.SemaphoreType.DMA(()),
+            pltpu.SemaphoreType.DMA((PLANES + 1,)),
+        ],
         compiler_params=pltpu.CompilerParams(vmem_limit_bytes=LIMIT),
         name="pack",
-    )(place, f, jnp.asarray(moment_basis()))
+    )(place, f, basis)
 
 
 def edges_kernel(core_ref, f_ref, low_ref, high_ref, inner_ref, outer_ref):
@@ -133,30 +172,67 @@
     )(core, f)
 
 
-def assemble_kernel(where_ref, own_ref, other_ref, out_ref, inner_ref, rows_ref):
+def join_kernel(held_ref, above_ref, below_ref, across_ref, inner_ref, out_ref, sem):
+    size = held_ref.shape[0]
+    copies = []
+    for m, ref in enumerate((held_ref, above_ref, below_ref, across_ref)):
+        copies.append(
+            pltpu.make_async_copy(
+                ref.at[pl.ds(0, size)], out_ref.at[pl.ds(m * size, size)], sem.at[m]
+            )
+        )
+    copies.append(
+        pltpu.make_async_copy(inner_ref, out_ref.at[pl.ds(4 * size, 16)], sem.at[4])
+    )
+    for copy in copies:
+        copy.start()
+    for copy in copies:
+        copy.wait()
+
+
+def join(held, above, below, across, inner):
+    return pl.pallas_call(
+        join_kernel,
+        out_shape=jax.ShapeDtypeStruct((4 * held.shape[0] + 16, NXY), BF16),
+        in_specs=[hbm()] * 5,
+        out_specs=hbm(),
+        scratch_shapes=[pltpu.SemaphoreType.DMA((5,))],
+        compiler_params=pltpu.CompilerParams(vmem_limit_bytes=LIMIT),
+        name="join",
+    )(held, above, below, across, inner)
+
+
+def assemble_kernel(where_ref, own_ref, other_ref, out_hbm, inner_hbm, rows_ref, turned_ref, sem):
+    half = NXY // 2
+    edge = pltpu.make_async_copy(other_ref.at[pl.ds(half, 16)], inner_hbm, sem.at[1])
+    edge.start()
     core, z, y = where_ref[0], where_ref[1], where_ref[2]
     far = jnp.where(y % 2 == 0, y + 6, y + 2)
     for m, base in enumerate((y, y + 1, y + 7, far)):
         for i in range(2):
             for j in range(4):
                 place = ((base + 4 * i) % 8 * 4 + jnp.bitwise_xor(z, j)) * 2
-                block = slice((m * 8 + i * 4 + j) * 16, (m * 8 + i * 4 + j + 1) * 16)
+                block = slice((m * 8 + j * 2 + i) * 16, (m * 8 + j * 2 + i + 1) * 16)
                 rows_ref[place + core] = own_ref[block, :]
                 rows_ref[place + 1 - core] = other_ref[block, :]
-    inner_ref[...] = other_ref[NXY // 2 : NXY // 2 + 16, :]
-    out_ref[...] = jnp.transpose(rows_ref[...].reshape(NXY, NXY))
+    turned_ref[...] = jnp.transpose(rows_ref[...].reshape(NXY, NXY))
+    copy = pltpu.make_async_copy(turned_ref, out_hbm, sem.at[0])
+    copy.start()
+    edge.wait()
+    copy.wait()
 
 
 def assemble(where, own, other):
     return pl.pallas_call(
         assemble_kernel,
-        out_shape=(
-            jax.ShapeDtypeStruct((NXY, NXY), BF16),
-            jax.ShapeDtypeStruct((16, NXY), BF16),
-        ),
+        out_shape=(pltpu.HBM((NXY, NXY), BF16), jax.ShapeDtypeStruct((16, NXY), BF16)),
         in_specs=[smem(), vmem(), vmem()],
-        out_specs=(vmem(), vmem()),
-        scratch_shapes=[pltpu.VMEM((NXY // 16, 16, NXY), BF16)],
+        out_specs=(hbm(), hbm()),
+        scratch_shapes=[
+            pltpu.VMEM((NXY // 16, 16, NXY), BF16),
+            pltpu.VMEM((NXY, NXY), BF16),
+            pltpu.SemaphoreType.DMA((2,)),
+        ],
         compiler_params=pltpu.CompilerParams(vmem_limit_bytes=LIMIT),
         name="assemble",
     )(where, own, other)
@@ -238,8 +314,41 @@
 
 
 def advance_kernel(
-    core_ref, f_ref, back_ref, weights_ref, lower_ref, upper_ref, inner_ref, outer_ref, out_ref, mixed_ref
+    core_ref,
+    f_hbm,
+    back_hbm,
+    weights_hbm,
+    below_hbm,
+    above_hbm,
+    inner_hbm,
+    outer_hbm,
+    out_hbm,
+    f_ref,
+    back_ref,
+    weights_ref,
+    lower_ref,
+    upper_ref,
+    inner_ref,
+    outer_ref,
+    moved_ref,
+    out_ref,
+    sem,
+    out_sem,
 ):
+    edge = pl.ds(below_hbm.shape[0] - 2 * COLS, 2 * COLS)
+    first = [
+        pltpu.make_async_copy(below_hbm.at[edge], lower_ref, sem.at[0]),
+        pltpu.make_async_copy(above_hbm.at[edge], upper_ref, sem.at[1]),
+        pltpu.make_async_copy(inner_hbm, inner_ref, sem.at[2]),
+        pltpu.make_async_copy(outer_hbm, outer_ref, sem.at[3]),
+        pltpu.make_async_copy(f_hbm, f_ref, sem.at[4]),
+    ]
+    second = [
+        pltpu.make_async_copy(back_hbm, back_ref, sem.at[5]),
+        pltpu.make_async_copy(weights_hbm, weights_ref, sem.at[6]),
+    ]
+    for copy in first + second:
+        copy.start()
     half = NXY // 2
     vx, vy = lane_speeds((COLS, NXY), 0)
     courant_across = COURANT / (4.0 - 4.0 / NVX)
@@ -247,20 +356,19 @@
     cx = courant_across * jnp.abs(vx)
     cy = courant_along * jnp.abs(vy)
     upwind = vy > 0.0
-    edge = lower_ref.shape[0] - 2 * COLS
+    col = lax.broadcasted_iota(jnp.int32, (COLS, NXY), 0)
+    core = core_ref[0]
+    for copy in first:
+        copy.wait()
     inner = inner_ref[...].astype(F32)
     outer = outer_ref[...].astype(F32)
-    core = core_ref[0]
     left_edge = jnp.where(core == 0, outer, inner)
     right_edge = jnp.where(core == 0, inner, outer)
-    col = lax.broadcasted_iota(jnp.int32, (COLS, NXY), 0)
-    mixed = jnp.concatenate([back_ref[v] for v in range(GROUP)], axis=1)
-    mixed_ref[...] = jnp.dot(mixed, weights_ref[...], preferred_element_type=F32)
     for p in range(PLANES):
         lanes = slice(p * NXY, (p + 1) * NXY)
         first_half = slice(p * NXY, p * NXY + half)
         second_half = slice(p * NXY + half, (p + 1) * NXY)
-        rows = slice(edge + p // 2 * COLS, edge + (p // 2 + 1) * COLS)
+        rows = slice(p // 2 * COLS, (p // 2 + 1) * COLS)
         packed = slice(p % 2 * half, (p % 2 + 1) * half)
         for r in range(ROWS):
             current = f_ref[r, :, lanes].astype(F32)
@@ -272,22 +380,54 @@
             left = jnp.where(col == 0, left, pltpu.roll(current, 1, 0))
             right = jnp.where(col == COLS - 1, right, pltpu.roll(current, COLS - 1, 0))
             along = jnp.where(upwind, left, right)
-            value = current - (cx * (current - across) + cy * (current - along))
             start = p * CELLS + r * COLS
-            value = value + RELAX_RATE * mixed_ref[start : start + COLS, :]
-            out_ref[r, :, lanes] = value.astype(BF16)
-
-
-def advance(core, f, back, weights, lower, upper, inner, outer):
+            moved_ref[start : start + COLS, :] = current - (
+                cx * (current - across) + cy * (current - along)
+            )
+    for copy in second:
+        copy.wait()
+    mixed = jnp.concatenate([back_ref[v] for v in range(GROUP)], axis=1)
+    collision = jnp.dot(mixed, weights_ref[...], preferred_element_type=F32)
+    stores = []
+    for p in range(PLANES):
+        for r in range(ROWS):
+            start = p * CELLS + r * COLS
+            value = moved_ref[start : start + COLS, :] + RELAX_RATE * collision[start : start + COLS, :]
+            out_ref[r, :, p * NXY : (p + 1) * NXY] = value.astype(BF16)
+        lanes = pl.ds(p * NXY, NXY)
+        stores.append(
+            pltpu.make_async_copy(
+                out_ref.at[:, :, lanes], out_hbm.at[:, :, lanes], out_sem.at[p]
+            )
+        )
+        stores[-1].start()
+    for copy in stores:
+        copy.wait()
+
+
+def advance(core, f, back, weights, below, above, inner, outer):
+    weights = pltpu.with_memory_space_constraint(weights, pltpu.HBM)
     return pl.pallas_call(
         advance_kernel,
         out_shape=jax.ShapeDtypeStruct(f.shape, BF16),
-        in_specs=[smem()] + [vmem()] * 7,
-        out_specs=vmem(),
-        scratch_shapes=[pltpu.VMEM((DATA, NXY), F32)],
+        in_specs=[smem()] + [hbm()] * 7,
+        out_specs=hbm(),
+        scratch_shapes=[
+            pltpu.VMEM(f.shape, BF16),
+            pltpu.VMEM(back.shape, BF16),
+            pltpu.VMEM(weights.shape, BF16),
+            pltpu.VMEM((2 * COLS, NXY), BF16),
+            pltpu.VMEM((2 * COLS, NXY), BF16),
+            pltpu.VMEM(inner.shape, BF16),
+            pltpu.VMEM(outer.shape, BF16),
+            pltpu.VMEM((DATA, NXY), F32),
+            pltpu.VMEM(f.shape, BF16),
+            pltpu.SemaphoreType.DMA((7,)),
+            pltpu.SemaphoreType.DMA((PLANES,)),
+        ],
         compiler_params=pltpu.CompilerParams(vmem_limit_bytes=LIMIT),
         name="advance",
-    )(core, f, back, weights, lower, upper, inner, outer)
+    )(core, f, back, weights, below, above, inner, outer)
 
 
 def ring(axis, step):
@@ -301,21 +441,20 @@
     core = jnp.bitwise_and(along, 1).reshape(1)
     where = jnp.stack([jnp.bitwise_and(along, 1), along >> 1, lax.axis_index("sx").astype(jnp.int32)])
     flip = lambda bit: [(i, i ^ bit) for i in range(8)]
-    send = pack(place, distribution)
-    held = jnp.concatenate([plane_weights, lax.ppermute(plane_weights, "sy", flip(2))])
-    send, held = lax.optimization_barrier((send, held))
-    held = jnp.concatenate([held, lax.ppermute(held, "sy", flip(4))])
-    send, held = lax.optimization_barrier((send, held))
+    pair = jnp.concatenate([plane_weights, lax.ppermute(plane_weights, "sx", flip(4))])
+    low, high, inner, outer = edges(core, distribution)
+    mix = spread(depth_weights)
+    spot, pair = lax.optimization_barrier((place, pair))
+    held = jnp.concatenate(
+        [pair] + [lax.ppermute(pair, "sy", flip(2 * step)) for step in (1, 2, 3)]
+    )
+    send, held = lax.optimization_barrier((pack(spot, distribution), held))
     got = lax.all_to_all(send, "vel", 0, 0, tiled=True)
-    mix = spread(depth_weights)
-    low, high, inner, outer = edges(core, distribution)
-    held = jnp.concatenate([held, lax.ppermute(held, "sx", flip(4))])
-    size = held.shape[0]
     above = lax.ppermute(jnp.concatenate([held, low]), "sx", ring("sx", -1))
     below = lax.ppermute(jnp.concatenate([held, high]), "sx", ring("sx", 1))
     across = lax.ppermute(held, "sx", [(i, (i + 2) % 8 if i % 2 == 0 else (i - 2) % 8) for i in range(8)])
     outer = lax.ppermute(outer, "sy", [(i, (i + 1) % 8 if i % 2 else (i - 1) % 8) for i in range(8)])
-    own = jnp.concatenate([held, above[:size], below[:size], across, inner])
+    own = join(held, above, below, across, inner)
     other = lax.ppermute(own, "sy", flip(1))
     weights, inner = assemble(where, own, other)
     back = lax.all_to_all(relax(place, got, mix), "vel", 0, 0, tiled=True)

time: 92.4 us -> 92.7 us (level)
  the two profiles are of different devices: /device:TPU:136 before, /device:TPU:56 now
where the time goes in v4:
time: 92.7 us; the launch traced here: 91 us
  starting transfers between devices  54.1 us (58%)
  waiting for transfers between devices  20.7 us (22%)
  Pallas kernels  14 us (15%)
  other arithmetic  1.85 us (2%)
    ppermute x3, starting transfers between devices, local(): lax.ppermute(pair, 'sy', flip(2 * step))  12.3 us
    ppermute x1, starting transfers between devices, local(): lax.ppermute(outer, 'sy', [(i, (i + 1) % 8 if i % 2 else (i - 1) % 8) for...  11.8 us
    all_to_all x1, starting transfers between devices, local(): got = lax.all_to_all(send, 'vel', 0, 0, tiled=True)  10.1 us
    all_to_all x1, waiting for transfers between devices, local(): got = lax.all_to_all(send, 'vel', 0, 0, tiled=True)  8 us
    ppermute x1, waiting for transfers between devices, local(): lax.ppermute(held, 'sx', [(i, (i + 2) % 8 if i % 2 == 0 else (i - 2) % 8)...  6.36 us
    ppermute x1, waiting for transfers between devices, local(): lax.ppermute(plane_weights, 'sx', flip(4))  5.55 us
    ppermute x1, starting transfers between devices, local(): lax.ppermute(plane_weights, 'sx', flip(4))  4.7 us
    ppermute x1, starting transfers between devices, local(): lax.ppermute(held, 'sx', [(i, (i + 2) % 8 if i % 2 == 0 else (i - 2) % 8)...  4.01 us
  transfers between devices with their start and end apart: 11, of which 4 were waited for; matrix products, arithmetic and copies ran while one was open for 1% of the time, Pallas kernels for 11%

profile of v4, /device:TPU:56, one launch (start us, length us, event | category | flops | bytes accessed | tf_op | source)
XLA Modules:
  0.0 91.0 jit_solution(15352392929583376)
XLA Ops:
  0.0 4.7 %collective-permute-start = (bf16[16,1024]{1,0:T(8,128)(2,1)}, bf16[16,1024]{1,0:T(8,128)(2,1)S(1)}, u32[]{:S(2)}, u32[]{:S(2)}) collective-permute-start(bf16[16,1024]{1,0:T(8,128)(2,1)} %param.5), channel_id=1, source_target_pairs={{0,32},{8,40},{16,48},{24,56},{32,0},{40,8},{48,16},{56,24},{1,33}... | collective-permute-start | bytes 98312 | tf_op jit(solution)/shard_map/ppermute | solution.py:444
  4.7 5.5 %collective-permute-done = bf16[16,1024]{1,0:T(8,128)(2,1)S(1)} collective-permute-done((bf16[16,1024]{1,0:T(8,128)(2,1)}, bf16[16,1024]{1,0:T(8,128)(2,1)S(1)}, u32[]{:S(2)}, u32[]{:S(2)}) %collective-permute-start) | collective-permute-done | bytes 32800 | tf_op jit(solution)/shard_map/ppermute | solution.py:444
  10.3 0.8 pad_maximum_fusion.3
  11.0 7.9 %collective-permute-start.3 = (bf16[32,1024]{1,0:T(8,128)(2,1)S(1)}, bf16[32,1024]{1,0:T(8,128)(2,1)S(1)}, u32[]{:S(2)}, u32[]{:S(2)}) collective-permute-start(bf16[32,1024]{1,0:T(8,128)(2,1)S(1)} %pad_maximum_fusion.3), channel_id=1, source_target_pairs={{0,6},{1,7},{2,4},{3,5},{4,2},{5,3},{6,0},{7,1},{8,14},{9,15},{10,... | collective-permute-start | bytes 196616 | tf_op jit(solution)/shard_map/ppermute | solution.py:449
  18.9 1.9 %collective-permute-start.2 = (bf16[32,1024]{1,0:T(8,128)(2,1)S(1)}, bf16[32,1024]{1,0:T(8,128)(2,1)S(1)}, u32[]{:S(2)}, u32[]{:S(2)}) collective-permute-start(bf16[32,1024]{1,0:T(8,128)(2,1)S(1)} %pad_maximum_fusion.3), channel_id=1, source_target_pairs={{0,4},{1,5},{2,6},{3,7},{4,0},{5,1},{6,2},{7,3},{8,12},{9,13},{10,... | collective-permute-start | bytes 196616 | tf_op jit(solution)/shard_map/ppermute | solution.py:449
  20.9 2.5 %collective-permute-start.1 = (bf16[32,1024]{1,0:T(8,128)(2,1)S(1)}, bf16[32,1024]{1,0:T(8,128)(2,1)S(1)}, u32[]{:S(2)}, u32[]{:S(2)}) collective-permute-start(bf16[32,1024]{1,0:T(8,128)(2,1)S(1)} %pad_maximum_fusion.3), channel_id=1, source_target_pairs={{0,2},{1,3},{2,0},{3,1},{4,6},{5,7},{6,4},{7,5},{8,10},{9,11},{10,... | collective-permute-start | bytes 196616 | tf_op jit(solution)/shard_map/ppermute | solution.py:449
  23.3 2.8 %pack.1 = bf16[8,400,128]{2,1,0:T(8,128)(2,1)} custom-call(s32[1]{0:T(128)} %bitcast.1.place_ref, bf16[3,32,4096]{2,1,0:T(8,128)(2,1)} %f_hbm.1, bf16[1024,128]{1,0:T(8,128)(2,1)} %constant.15.clone.basis_ref), custom_call_target="tpu_custom_call" | custom-call | tf_op jit(solution)/shard_map/pack/pallas_call | solution.py:122
  26.2 0.0 copy-start
  26.2 0.0 collective-permute-done.3
  26.2 0.0 collective-permute-done.2
  26.2 0.8 collective-permute-done.1
  27.0 10.1 %all-to-all-start = ((bf16[8,400,128]{2,1,0:T(8,128)(2,1)}), bf16[8,400,128]{2,1,0:T(8,128)(2,1)S(1)}, u32[]{:S(2)}, u32[]{:S(2)}) async-start(bf16[8,400,128]{2,1,0:T(8,128)(2,1)} %pack.1), calls=%async_computation | async-start | bytes 1638400 | tf_op jit(solution)/shard_map/all_to_all | solution.py:452
  37.1 0.0 copy-start.1
  37.1 0.0 copy-done
  37.1 0.1 edges.1
  37.2 1.0 %pad_maximum_fusion = (bf16[192,1024]{1,0:T(8,128)(2,1)}, bf16[192,1024]{1,0:T(8,128)(2,1)}) fusion(bf16[128,1024]{1,0:T(8,128)(2,1)S(1)} %pad_maximum_fusion.2.held_ref, bf16[64,1024]{1,0:T(8,128)(2,1)S(1)} %get-tuple-element.20, bf16[64,1024]{1,0:T(8,128)(2,1)S(1)} %get-tuple-element.19), kind=kLoop, calls=%fused_computation | loop fusion | flops 1376256 | bytes 1310720 | tf_op jit(solution)/shard_map/concatenate | solution.py:454
  38.2 1.9 %collective-permute-start.5 = (bf16[192,1024]{1,0:T(8,128)(2,1)}, bf16[192,1024]{1,0:T(8,128)(2,1)S(1)}, u32[]{:S(2)}, u32[]{:S(2)}) collective-permute-start(bf16[192,1024]{1,0:T(8,128)(2,1)} %get-tuple-element.25), channel_id=1, source_target_pairs={{0,8},{8,16},{16,24},{24,32},{32,40},{40,48},{48,56},{56,0},{1,9},... | collective-permute-start | bytes 1179656 | tf_op jit(solution)/shard_map/ppermute | solution.py:454
  40.1 3.9 %collective-permute-start.4 = (bf16[192,1024]{1,0:T(8,128)(2,1)}, bf16[192,1024]{1,0:T(8,128)(2,1)}, u32[]{:S(2)}, u32[]{:S(2)}) collective-permute-start(bf16[192,1024]{1,0:T(8,128)(2,1)} %get-tuple-element.26), channel_id=1, source_target_pairs={{0,56},{8,0},{16,8},{24,16},{32,24},{40,32},{48,40},{56,48},{1,57}... | collective-permute-start | bytes 1179656 | tf_op jit(solution)/shard_map/ppermute | solution.py:453
  44.1 0.0 copy-done.1
  44.1 0.4 spread.1.mix_ref
  44.5 8.0 %all-to-all-done.got_ref = bf16[8,400,128]{2,1,0:T(8,128)(2,1)S(1)} async-done(((bf16[8,400,128]{2,1,0:T(8,128)(2,1)}), bf16[8,400,128]{2,1,0:T(8,128)(2,1)S(1)}, u32[]{:S(2)}, u32[]{:S(2)}) %all-to-all-start) | async-done | bytes 819232 | tf_op jit(solution)/shard_map/all_to_all | solution.py:452
  52.5 2.3 %relax.1 = bf16[8,384,128]{2,1,0:T(8,128)(2,1)} custom-call(s32[1]{0:T(128)} %bitcast.1.place_ref, bf16[8,400,128]{2,1,0:T(8,128)(2,1)S(1)} %all-to-all-done.got_ref, bf16[512,512]{1,0:T(8,128)(2,1)S(1)} %spread.1.mix_ref), custom_call_target="tpu_custom_call" | custom-call | tf_op jit(solution)/shard_map/relax/pallas_call | solution.py:305
  54.8 3.5 %all-to-all-start.1 = ((bf16[8,384,128]{2,1,0:T(8,128)(2,1)}), bf16[8,384,128]{2,1,0:T(8,128)(2,1)S(1)}, u32[]{:S(2)}, u32[]{:S(2)}) async-start(bf16[8,384,128]{2,1,0:T(8,128)(2,1)} %relax.1), calls=%async_computation.1 | async-start | bytes 1572864 | tf_op jit(solution)/shard_map/all_to_all | solution.py:460
  58.3 4.0 %collective-permute-start.6 = (bf16[128,1024]{1,0:T(8,128)(2,1)S(1)}, bf16[128,1024]{1,0:T(8,128)(2,1)S(1)}, u32[]{:S(2)}, u32[]{:S(2)}) collective-permute-start(bf16[128,1024]{1,0:T(8,128)(2,1)S(1)} %pad_maximum_fusion.2.held_ref), channel_id=1, source_target_pairs={{0,16},{8,56},{16,32},{24,8},{32,48},{40,24},{48,0},{56,40},{1,17}... | collective-permute-start | bytes 786440 | tf_op jit(solution)/shard_map/ppermute | solution.py:455
  62.3 6.4 %collective-permute-done.6.across_ref = bf16[128,1024]{1,0:T(8,128)(2,1)S(1)} collective-permute-done((bf16[128,1024]{1,0:T(8,128)(2,1)S(1)}, bf16[128,1024]{1,0:T(8,128)(2,1)S(1)}, u32[]{:S(2)}, u32[]{:S(2)}) %collective-permute-start.6) | collective-permute-done | bytes 262176 | tf_op jit(solution)/shard_map/ppermute | solution.py:455
  68.7 0.0 collective-permute-done.5.below_ref.below_hbm
  68.7 0.0 collective-permute-done.4.above_ref.above_hbm
  68.7 1.0 %join.1.own_ref = bf16[528,1024]{1,0:T(8,128)(2,1)S(1)} custom-call(bf16[128,1024]{1,0:T(8,128)(2,1)S(1)} %pad_maximum_fusion.2.held_ref, bf16[192,1024]{1,0:T(8,128)(2,1)} %collective-permute-done.4.above_ref.above_hbm, bf16[192,1024]{1,0:T(8,128)(2,1)S(1)} %collective-permute-done.5.below_ref.below_hbm, ...), custom_call_target="tpu_custom_call" | custom-call | tf_op jit(solution)/shard_map/join/pallas_call | solution.py:194
  69.7 1.9 %collective-permute-start.7 = (bf16[528,1024]{1,0:T(8,128)(2,1)S(1)}, bf16[528,1024]{1,0:T(8,128)(2,1)}, u32[]{:S(2)}, u32[]{:S(2)}) collective-permute-start(bf16[528,1024]{1,0:T(8,128)(2,1)S(1)} %join.1.own_ref), channel_id=1, source_target_pairs={{0,1},{1,0},{2,3},{3,2},{4,5},{5,4},{6,7},{7,6},{8,9},{9,8},{10,11... | collective-permute-start | bytes 3244040 | tf_op jit(solution)/shard_map/ppermute | solution.py:458
  71.7 11.8 %collective-permute-start.8 = (bf16[16,1024]{1,0:T(8,128)(2,1)S(1)}, bf16[16,1024]{1,0:T(8,128)(2,1)S(1)}, u32[]{:S(2)}, u32[]{:S(2)}) collective-permute-start(bf16[16,1024]{1,0:T(8,128)(2,1)S(1)} %get-tuple-element.24), channel_id=1, source_target_pairs={{0,7},{1,2},{2,1},{3,4},{4,3},{5,6},{6,5},{7,0},{8,15},{9,10},{10,... | collective-permute-start | bytes 98312 | tf_op jit(solution)/shard_map/ppermute | solution.py:456
  83.5 0.1 pad_add_fusion.where_ref
  83.6 0.0 collective-permute-done.7.other_ref
  83.6 3.4 %assemble.1 = (bf16[1024,1024]{1,0:T(8,128)(2,1)}, bf16[16,1024]{1,0:T(8,128)(2,1)S(1)}) custom-call(s32[3]{0:T(128)S(1)} %pad_add_fusion.where_ref, bf16[528,1024]{1,0:T(8,128)(2,1)S(1)} %join.1.own_ref, bf16[528,1024]{1,0:T(8,128)(2,1)} %collective-permute-done.7.other_ref), custom_call_target="tpu_custom_call" | custom-call | tf_op jit(solution)/shard_map/assemble/pallas_call | solution.py:226
  87.0 0.0 collective-permute-done.8.outer_hbm
  87.0 0.0 all-to-all-done.1.back_hbm
  87.0 3.9 %advance.1 = bf16[3,32,4096]{2,1,0:T(8,128)(2,1)} custom-call(s32[1]{0:T(128)} %bitcast.core_ref, bf16[3,32,4096]{2,1,0:T(8,128)(2,1)S(1)} %copy-done, bf16[8,384,128]{2,1,0:T(8,128)(2,1)S(1)} %all-to-all-done.1.back_hbm, bf16[1024,1024]{1,0:T(8,128)(2,1)} %get-tuple-element.22.weights_hbm, bf16[192,1024]{1,0:T(8,128)(2,1)S(1)} %collective-permute-done.5.below_ref.below_hbm, ...), custom_call_target="tpu_custom_call" | custom-call | tf_op jit(solution)/shard_map/advance/pallas_call | solution.py:410
  (1 shorter events, 0.0 us)
Async XLA Ops:
  0.0 10.3 %collective-permute-start = (bf16[16,1024]{1,0:T(8,128)(2,1)}, bf16[16,1024]{1,0:T(8,128)(2,1)S(1)}, u32[]{:S(2)}, u32[]{:S(2)}) collective-permute-start(bf16[16,1024]{1,0:T(8,128)(2,1)} %param.5), channel_id=1, source_target_pairs={{0,32},{8,40},{16,48},{24,56},{32,0},{40,8},{48,16},{56,24},{1,33}... | collective-permute-start | bytes 98312 | tf_op jit(solution)/shard_map/ppermute | solution.py:444
  11.0 15.2 %collective-permute-start.3 = (bf16[32,1024]{1,0:T(8,128)(2,1)S(1)}, bf16[32,1024]{1,0:T(8,128)(2,1)S(1)}, u32[]{:S(2)}, u32[]{:S(2)}) collective-permute-start(bf16[32,1024]{1,0:T(8,128)(2,1)S(1)} %pad_maximum_fusion.3), channel_id=1, source_target_pairs={{0,6},{1,7},{2,4},{3,5},{4,2},{5,3},{6,0},{7,1},{8,14},{9,15},{10,... | collective-permute-start | bytes 196616 | tf_op jit(solution)/shard_map/ppermute | solution.py:449
  18.9 7.3 %collective-permute-start.2 = (bf16[32,1024]{1,0:T(8,128)(2,1)S(1)}, bf16[32,1024]{1,0:T(8,128)(2,1)S(1)}, u32[]{:S(2)}, u32[]{:S(2)}) collective-permute-start(bf16[32,1024]{1,0:T(8,128)(2,1)S(1)} %pad_maximum_fusion.3), channel_id=1, source_target_pairs={{0,4},{1,5},{2,6},{3,7},{4,0},{5,1},{6,2},{7,3},{8,12},{9,13},{10,... | collective-permute-start | bytes 196616 | tf_op jit(solution)/shard_map/ppermute | solution.py:449
  20.9 6.2 %collective-permute-start.1 = (bf16[32,1024]{1,0:T(8,128)(2,1)S(1)}, bf16[32,1024]{1,0:T(8,128)(2,1)S(1)}, u32[]{:S(2)}, u32[]{:S(2)}) collective-permute-start(bf16[32,1024]{1,0:T(8,128)(2,1)S(1)} %pad_maximum_fusion.3), channel_id=1, source_target_pairs={{0,2},{1,3},{2,0},{3,1},{4,6},{5,7},{6,4},{7,5},{8,10},{9,11},{10,... | collective-permute-start | bytes 196616 | tf_op jit(solution)/shard_map/ppermute | solution.py:449
  26.2 10.9 %copy-start = (bf16[3,32,4096]{2,1,0:T(8,128)(2,1)S(1)}, bf16[3,32,4096]{2,1,0:T(8,128)(2,1)}, u32[]{:S(2)}) copy-start(bf16[3,32,4096]{2,1,0:T(8,128)(2,1)} %f_hbm.1) | copy-start | bytes 2359300
  27.0 25.4 %all-to-all-start = ((bf16[8,400,128]{2,1,0:T(8,128)(2,1)}), bf16[8,400,128]{2,1,0:T(8,128)(2,1)S(1)}, u32[]{:S(2)}, u32[]{:S(2)}) async-start(bf16[8,400,128]{2,1,0:T(8,128)(2,1)} %pack.1), calls=%async_computation | async-start | bytes 1638400 | tf_op jit(solution)/shard_map/all_to_all | solution.py:452
  37.1 7.0 %copy-start.1 = (bf16[32,32]{1,0:T(8,128)(2,1)S(1)}, bf16[32,32]{1,0:T(8,128)(2,1)}, u32[]{:S(2)}) copy-start(bf16[32,32]{1,0:T(8,128)(2,1)} %depth_ref.1) | copy-start | bytes 6148
  38.2 30.5 %collective-permute-start.5 = (bf16[192,1024]{1,0:T(8,128)(2,1)}, bf16[192,1024]{1,0:T(8,128)(2,1)S(1)}, u32[]{:S(2)}, u32[]{:S(2)}) collective-permute-start(bf16[192,1024]{1,0:T(8,128)(2,1)} %get-tuple-element.25), channel_id=1, source_target_pairs={{0,8},{8,16},{16,24},{24,32},{32,40},{40,48},{48,56},{56,0},{1,9},... | collective-permute-start | bytes 1179656 | tf_op jit(solution)/shard_map/ppermute | solution.py:454
  40.1 28.6 %collective-permute-start.4 = (bf16[192,1024]{1,0:T(8,128)(2,1)}, bf16[192,1024]{1,0:T(8,128)(2,1)}, u32[]{:S(2)}, u32[]{:S(2)}) collective-permute-start(bf16[192,1024]{1,0:T(8,128)(2,1)} %get-tuple-element.26), channel_id=1, source_target_pairs={{0,56},{8,0},{16,8},{24,16},{32,24},{40,32},{48,40},{56,48},{1,57}... | collective-permute-start | bytes 1179656 | tf_op jit(solution)/shard_map/ppermute | solution.py:453
  54.8 32.3 %all-to-all-start.1 = ((bf16[8,384,128]{2,1,0:T(8,128)(2,1)}), bf16[8,384,128]{2,1,0:T(8,128)(2,1)S(1)}, u32[]{:S(2)}, u32[]{:S(2)}) async-start(bf16[8,384,128]{2,1,0:T(8,128)(2,1)} %relax.1), calls=%async_computation.1 | async-start | bytes 1572864 | tf_op jit(solution)/shard_map/all_to_all | solution.py:460
  58.3 10.4 %collective-permute-start.6 = (bf16[128,1024]{1,0:T(8,128)(2,1)S(1)}, bf16[128,1024]{1,0:T(8,128)(2,1)S(1)}, u32[]{:S(2)}, u32[]{:S(2)}) collective-permute-start(bf16[128,1024]{1,0:T(8,128)(2,1)S(1)} %pad_maximum_fusion.2.held_ref), channel_id=1, source_target_pairs={{0,16},{8,56},{16,32},{24,8},{32,48},{40,24},{48,0},{56,40},{1,17}... | collective-permute-start | bytes 786440 | tf_op jit(solution)/shard_map/ppermute | solution.py:455
  69.7 13.8 %collective-permute-start.7 = (bf16[528,1024]{1,0:T(8,128)(2,1)S(1)}, bf16[528,1024]{1,0:T(8,128)(2,1)}, u32[]{:S(2)}, u32[]{:S(2)}) collective-permute-start(bf16[528,1024]{1,0:T(8,128)(2,1)S(1)} %join.1.own_ref), channel_id=1, source_target_pairs={{0,1},{1,0},{2,3},{3,2},{4,5},{5,4},{6,7},{7,6},{8,9},{9,8},{10,11... | collective-permute-start | bytes 3244040 | tf_op jit(solution)/shard_map/ppermute | solution.py:458
  71.7 15.3 %collective-permute-start.8 = (bf16[16,1024]{1,0:T(8,128)(2,1)S(1)}, bf16[16,1024]{1,0:T(8,128)(2,1)S(1)}, u32[]{:S(2)}, u32[]{:S(2)}) collective-permute-start(bf16[16,1024]{1,0:T(8,128)(2,1)S(1)} %get-tuple-element.24), channel_id=1, source_target_pairs={{0,7},{1,2},{2,1},{3,4},{4,3},{5,6},{6,5},{7,0},{8,15},{9,10},{10,... | collective-permute-start | bytes 98312 | tf_op jit(solution)/shard_map/ppermute | solution.py:456

commit v5 on v4

--- a/solution.py
+++ b/solution.py
@@ -172,72 +172,6 @@
     )(core, f)
 
 
-def join_kernel(held_ref, above_ref, below_ref, across_ref, inner_ref, out_ref, sem):
-    size = held_ref.shape[0]
-    copies = []
-    for m, ref in enumerate((held_ref, above_ref, below_ref, across_ref)):
-        copies.append(
-            pltpu.make_async_copy(
-                ref.at[pl.ds(0, size)], out_ref.at[pl.ds(m * size, size)], sem.at[m]
-            )
-        )
-    copies.append(
-        pltpu.make_async_copy(inner_ref, out_ref.at[pl.ds(4 * size, 16)], sem.at[4])
-    )
-    for copy in copies:
-        copy.start()
-    for copy in copies:
-        copy.wait()
-
-
-def join(held, above, below, across, inner):
-    return pl.pallas_call(
-        join_kernel,
-        out_shape=jax.ShapeDtypeStruct((4 * held.shape[0] + 16, NXY), BF16),
-        in_specs=[hbm()] * 5,
-        out_specs=hbm(),
-        scratch_shapes=[pltpu.SemaphoreType.DMA((5,))],
-        compiler_params=pltpu.CompilerParams(vmem_limit_bytes=LIMIT),
-        name="join",
-    )(held, above, below, across, inner)
-
-
-def assemble_kernel(where_ref, own_ref, other_ref, out_hbm, inner_hbm, rows_ref, turned_ref, sem):
-    half = NXY // 2
-    edge = pltpu.make_async_copy(other_ref.at[pl.ds(half, 16)], inner_hbm, sem.at[1])
-    edge.start()
-    core, z, y = where_ref[0], where_ref[1], where_ref[2]
-    far = jnp.where(y % 2 == 0, y + 6, y + 2)
-    for m, base in enumerate((y, y + 1, y + 7, far)):
-        for i in range(2):
-            for j in range(4):
-                place = ((base + 4 * i) % 8 * 4 + jnp.bitwise_xor(z, j)) * 2
-                block = slice((m * 8 + j * 2 + i) * 16, (m * 8 + j * 2 + i + 1) * 16)
-                rows_ref[place + core] = own_ref[block, :]
-                rows_ref[place + 1 - core] = other_ref[block, :]
-    turned_ref[...] = jnp.transpose(rows_ref[...].reshape(NXY, NXY))
-    copy = pltpu.make_async_copy(turned_ref, out_hbm, sem.at[0])
-    copy.start()
-    edge.wait()
-    copy.wait()
-
-
-def assemble(where, own, other):
-    return pl.pallas_call(
-        assemble_kernel,
-        out_shape=(pltpu.HBM((NXY, NXY), BF16), jax.ShapeDtypeStruct((16, NXY), BF16)),
-        in_specs=[smem(), vmem(), vmem()],
-        out_specs=(hbm(), hbm()),
-        scratch_shapes=[
-            pltpu.VMEM((NXY // 16, 16, NXY), BF16),
-            pltpu.VMEM((NXY, NXY), BF16),
-            pltpu.SemaphoreType.DMA((2,)),
-        ],
-        compiler_params=pltpu.CompilerParams(vmem_limit_bytes=LIMIT),
-        name="assemble",
-    )(where, own, other)
-
-
 def spread_kernel(depth_ref, out_ref):
     size = NVZ * TILE
     row = lax.broadcasted_iota(jnp.int32, (size, NVZ), 0)
@@ -335,10 +269,9 @@
     sem,
     out_sem,
 ):
-    edge = pl.ds(below_hbm.shape[0] - 2 * COLS, 2 * COLS)
     first = [
-        pltpu.make_async_copy(below_hbm.at[edge], lower_ref, sem.at[0]),
-        pltpu.make_async_copy(above_hbm.at[edge], upper_ref, sem.at[1]),
+        pltpu.make_async_copy(below_hbm, lower_ref, sem.at[0]),
+        pltpu.make_async_copy(above_hbm, upper_ref, sem.at[1]),
         pltpu.make_async_copy(inner_hbm, inner_ref, sem.at[2]),
         pltpu.make_async_copy(outer_hbm, outer_ref, sem.at[3]),
         pltpu.make_async_copy(f_hbm, f_ref, sem.at[4]),
@@ -387,7 +320,9 @@
     for copy in second:
         copy.wait()
     mixed = jnp.concatenate([back_ref[v] for v in range(GROUP)], axis=1)
-    collision = jnp.dot(mixed, weights_ref[...], preferred_element_type=F32)
+    collision = lax.dot_general(
+        mixed, weights_ref[...], (((1,), (1,)), ((), ())), preferred_element_type=F32
+    )
     stores = []
     for p in range(PLANES):
         for r in range(ROWS):
@@ -437,30 +372,24 @@
 
 def local(distribution, plane_weights, depth_weights):
     place = lax.axis_index("vel").astype(jnp.int32).reshape(1)
-    along = lax.axis_index("sy").astype(jnp.int32)
-    core = jnp.bitwise_and(along, 1).reshape(1)
-    where = jnp.stack([jnp.bitwise_and(along, 1), along >> 1, lax.axis_index("sx").astype(jnp.int32)])
-    flip = lambda bit: [(i, i ^ bit) for i in range(8)]
-    pair = jnp.concatenate([plane_weights, lax.ppermute(plane_weights, "sx", flip(4))])
+    core = jnp.bitwise_and(lax.axis_index("sy").astype(jnp.int32), 1).reshape(1)
+    shard, width = plane_weights.shape
+    count = lax.axis_size("sy")
+    rows = jnp.broadcast_to(plane_weights[None], (count, shard, width))
+    rows = lax.all_to_all(rows, "sy", 0, 0, tiled=True).reshape(count * shard, width)
+    send, rows = lax.optimization_barrier((pack(place, distribution), rows))
+    weights = lax.all_gather(rows, "sx", axis=0, tiled=True)
+    got = lax.all_to_all(send, "vel", 0, 0, tiled=True)
     low, high, inner, outer = edges(core, distribution)
     mix = spread(depth_weights)
-    spot, pair = lax.optimization_barrier((place, pair))
-    held = jnp.concatenate(
-        [pair] + [lax.ppermute(pair, "sy", flip(2 * step)) for step in (1, 2, 3)]
+    above = lax.ppermute(low, "sx", ring("sx", -1))
+    below = lax.ppermute(high, "sx", ring("sx", 1))
+    inner = lax.ppermute(inner, "sy", [(i, i ^ 1) for i in range(count)])
+    outer = lax.ppermute(
+        outer, "sy", [(i, (i + 1) % count if i % 2 else (i - 1) % count) for i in range(count)]
     )
-    send, held = lax.optimization_barrier((pack(spot, distribution), held))
-    got = lax.all_to_all(send, "vel", 0, 0, tiled=True)
-    above = lax.ppermute(jnp.concatenate([held, low]), "sx", ring("sx", -1))
-    below = lax.ppermute(jnp.concatenate([held, high]), "sx", ring("sx", 1))
-    across = lax.ppermute(held, "sx", [(i, (i + 2) % 8 if i % 2 == 0 else (i - 2) % 8) for i in range(8)])
-    outer = lax.ppermute(outer, "sy", [(i, (i + 1) % 8 if i % 2 else (i - 1) % 8) for i in range(8)])
-    own = join(held, above, below, across, inner)
-    other = lax.ppermute(own, "sy", flip(1))
-    weights, inner = assemble(where, own, other)
     back = lax.all_to_all(relax(place, got, mix), "vel", 0, 0, tiled=True)
-    return advance(
-        core, distribution, back, weights, below, above, inner, outer
-    )
+    return advance(core, distribution, back, weights, below, above, inner, outer)
 
 
 def solution(mesh):

time: 92.7 us -> 98.2 us (1.059)
  the two profiles are of different devices: /device:TPU:56 before, /device:TPU:2 now
where the time goes in v5:
time: 98.2 us; the launch traced here: 97.6 us
  starting transfers between devices  36.9 us (38%)
  waiting for transfers between devices  35.4 us (36%)
  between operations  13.5 us (14%)
  Pallas kernels  9.66 us (10%)
  local copies, waits for them, and re-layouts  2.19 us (2%)
    all_to_all x1, waiting for transfers between devices, local(): got = lax.all_to_all(send, 'vel', 0, 0, tiled=True)  19.7 us
    all_to_all x1, starting transfers between devices, local(): got = lax.all_to_all(send, 'vel', 0, 0, tiled=True)  10.6 us
    ppermute x1, waiting for transfers between devices, local(): lax.ppermute(outer, 'sy', [(i, (i + 1) % count if i % 2 else (i - 1) % co...  8.86 us
    all_to_all x1, starting transfers between devices, local(): back = lax.all_to_all(relax(place, got, mix), 'vel', 0, 0, tiled=True)  7.71 us
    all_to_all x1, starting transfers between devices, local(): lax.all_to_all(rows, 'sy', 0, 0, tiled=True).reshape(count * shard, width)  7.4 us
    all_to_all x1, waiting for transfers between devices, local(): lax.all_to_all(rows, 'sy', 0, 0, tiled=True).reshape(count * shard, width)  6.85 us
    pallas_call x1, Pallas kernels, advance(): pl.pallas_call(advance_kernel, out_shape=jax.ShapeDtypeStruct(f.shape, BF...  4.04 us
    ppermute x1, starting transfers between devices, local(): above = lax.ppermute(low, 'sx', ring('sx', -1))  3.81 us
  transfers between devices with their start and end apart: 8, of which 3 were waited for; matrix products, arithmetic and copies ran while one was open for 0% of the time, Pallas kernels for 6%

profile of v5, /device:TPU:2, one launch (start us, length us, event | category | flops | bytes accessed | tf_op | source)
XLA Modules:
  0.0 97.6 jit_solution(230840740188338410)
XLA Ops:
  6.5 1.5 %broadcast_in_dim.2 = bf16[8,16,1024]{2,1,0:T(8,128)(2,1)} broadcast(bf16[16,1024]{1,0:T(8,128)(2,1)} %param.5), dimensions={1,2} | broadcast | bytes 294912 | tf_op jit(solution)/shard_map/broadcast_in_dim | solution.py:378
  8.0 0.0 copy-start.1
  8.0 7.4 %all-to-all-start = ((bf16[8,16,1024]{2,1,0:T(8,128)(2,1)}), bf16[8,16,1024]{2,1,0:T(8,128)(2,1)S(1)}, u32[]{:S(2)}, u32[]{:S(2)}) async-start(bf16[8,16,1024]{2,1,0:T(8,128)(2,1)} %broadcast_in_dim.2), calls=%async_computation | async-start | bytes 524288 | tf_op jit(solution)/shard_map/all_to_all | solution.py:379
  15.4 0.0 all-gather.2.cloned.1.call-start
  15.5 2.8 %pack.1 = bf16[8,400,128]{2,1,0:T(8,128)(2,1)} custom-call(s32[1]{0:T(128)} %bitcast.1.place_ref, bf16[3,32,4096]{2,1,0:T(8,128)(2,1)} %f_hbm.1, bf16[1024,128]{1,0:T(8,128)(2,1)} %constant.12.clone.basis_ref), custom_call_target="tpu_custom_call" | custom-call | tf_op jit(solution)/shard_map/pack/pallas_call | solution.py:122
  18.3 6.8 %all-to-all-done = bf16[8,16,1024]{2,1,0:T(8,128)(2,1)S(1)} async-done(((bf16[8,16,1024]{2,1,0:T(8,128)(2,1)}), bf16[8,16,1024]{2,1,0:T(8,128)(2,1)S(1)}, u32[]{:S(2)}, u32[]{:S(2)}) %all-to-all-start) | async-done | bytes 262176 | tf_op jit(solution)/shard_map/all_to_all | solution.py:379
  25.2 0.0 copy-start.2
  25.2 0.7 copy-done.2
  25.9 0.0 all-gather.2.cloned.1.call-update
  25.9 10.6 %all-to-all-start.1 = ((bf16[8,400,128]{2,1,0:T(8,128)(2,1)}), bf16[8,400,128]{2,1,0:T(8,128)(2,1)S(1)}, u32[]{:S(2)}, u32[]{:S(2)}) async-start(bf16[8,400,128]{2,1,0:T(8,128)(2,1)} %pack.1), calls=%async_computation.1 | async-start | bytes 1638400 | tf_op jit(solution)/shard_map/all_to_all | solution.py:382
  36.5 0.0 copy-done.1
  36.5 0.0 copy-start
  36.5 0.4 spread.1.mix_ref
  36.9 19.7 %all-to-all-done.1.got_ref = bf16[8,400,128]{2,1,0:T(8,128)(2,1)S(1)} async-done(((bf16[8,400,128]{2,1,0:T(8,128)(2,1)}), bf16[8,400,128]{2,1,0:T(8,128)(2,1)S(1)}, u32[]{:S(2)}, u32[]{:S(2)}) %all-to-all-start.1) | async-done | bytes 819232 | tf_op jit(solution)/shard_map/all_to_all | solution.py:382
  56.6 2.3 %relax.1 = bf16[8,384,128]{2,1,0:T(8,128)(2,1)} custom-call(s32[1]{0:T(128)} %bitcast.1.place_ref, bf16[8,400,128]{2,1,0:T(8,128)(2,1)S(1)} %all-to-all-done.1.got_ref, bf16[512,512]{1,0:T(8,128)(2,1)S(1)} %spread.1.mix_ref), custom_call_target="tpu_custom_call" | custom-call | tf_op jit(solution)/shard_map/relax/pallas_call | solution.py:239
  58.8 7.7 %all-to-all-start.2 = ((bf16[8,384,128]{2,1,0:T(8,128)(2,1)}), bf16[8,384,128]{2,1,0:T(8,128)(2,1)S(1)}, u32[]{:S(2)}, u32[]{:S(2)}) async-start(bf16[8,384,128]{2,1,0:T(8,128)(2,1)} %relax.1), calls=%async_computation.2 | async-start | bytes 1572864 | tf_op jit(solution)/shard_map/all_to_all | solution.py:391
  66.6 0.0 copy-done
  66.6 0.1 edges.1
  66.7 3.5 %collective-permute-start = (bf16[64,1024]{1,0:T(8,128)(2,1)S(1)}, bf16[64,1024]{1,0:T(8,128)(2,1)S(1)}, u32[]{:S(2)}, u32[]{:S(2)}) collective-permute-start(bf16[64,1024]{1,0:T(8,128)(2,1)S(1)} %get-tuple-element.13), channel_id=1, source_target_pairs={{0,8},{8,16},{16,24},{24,32},{32,40},{40,48},{48,56},{56,0},{1,9},... | collective-permute-start | bytes 393224 | tf_op jit(solution)/shard_map/ppermute | solution.py:386
  70.1 3.8 %collective-permute-start.1 = (bf16[64,1024]{1,0:T(8,128)(2,1)S(1)}, bf16[64,1024]{1,0:T(8,128)(2,1)S(1)}, u32[]{:S(2)}, u32[]{:S(2)}) collective-permute-start(bf16[64,1024]{1,0:T(8,128)(2,1)S(1)} %get-tuple-element.14), channel_id=1, source_target_pairs={{0,56},{8,0},{16,8},{24,16},{32,24},{40,32},{48,40},{56,48},{1,57}... | collective-permute-start | bytes 393224 | tf_op jit(solution)/shard_map/ppermute | solution.py:385
  74.0 1.9 %collective-permute-start.2 = (bf16[16,1024]{1,0:T(8,128)(2,1)S(1)}, bf16[16,1024]{1,0:T(8,128)(2,1)S(1)}, u32[]{:S(2)}, u32[]{:S(2)}) collective-permute-start(bf16[16,1024]{1,0:T(8,128)(2,1)S(1)} %get-tuple-element.15), channel_id=1, source_target_pairs={{0,1},{1,0},{2,3},{3,2},{4,5},{5,4},{6,7},{7,6},{8,9},{9,8},{10,11... | collective-permute-start | bytes 98312 | tf_op jit(solution)/shard_map/ppermute | solution.py:387
  75.9 1.9 %collective-permute-start.3 = (bf16[16,1024]{1,0:T(8,128)(2,1)S(1)}, bf16[16,1024]{1,0:T(8,128)(2,1)S(1)}, u32[]{:S(2)}, u32[]{:S(2)}) collective-permute-start(bf16[16,1024]{1,0:T(8,128)(2,1)S(1)} %get-tuple-element.16), channel_id=1, source_target_pairs={{0,7},{1,2},{2,1},{3,4},{4,3},{5,6},{6,5},{7,0},{8,15},{9,10},{10,... | collective-permute-start | bytes 98312 | tf_op jit(solution)/shard_map/ppermute | solution.py:388
  77.8 0.0 collective-permute-done.2.inner_hbm
  77.8 8.9 %collective-permute-done.3.outer_hbm = bf16[16,1024]{1,0:T(8,128)(2,1)S(1)} collective-permute-done((bf16[16,1024]{1,0:T(8,128)(2,1)S(1)}, bf16[16,1024]{1,0:T(8,128)(2,1)S(1)}, u32[]{:S(2)}, u32[]{:S(2)}) %collective-permute-start.3) | collective-permute-done | bytes 32800 | tf_op jit(solution)/shard_map/ppermute | solution.py:388
  86.7 0.0 collective-permute-done.below_hbm
  86.7 0.0 collective-permute-done.1.above_hbm
  86.7 0.0 all-to-all-done.2.back_hbm
  86.7 0.0 all-gather.2.cloned.1.call-done.weights_hbm
  86.7 4.0 %advance.1 = bf16[3,32,4096]{2,1,0:T(8,128)(2,1)} custom-call(s32[1]{0:T(128)} %bitcast.core_ref, bf16[3,32,4096]{2,1,0:T(8,128)(2,1)S(1)} %copy-done, bf16[8,384,128]{2,1,0:T(8,128)(2,1)S(1)} %all-to-all-done.2.back_hbm, bf16[1024,1024]{1,0:T(8,128)(2,1)} %all-gather.2.cloned.1.call-done.weights_hbm, bf16[64,1024]{1,0:T(8,128)(2,1)S(1)} %collective-permute-done.below_hbm, ...), custom_call_target="tpu_custom_call" | custom-call | tf_op jit(solution)/shard_map/advance/pallas_call | solution.py:345
Async XLA Ops:
  8.0 28.5 %copy-start.1 = (bf16[32,32]{1,0:T(8,128)(2,1)S(1)}, bf16[32,32]{1,0:T(8,128)(2,1)}, u32[]{:S(2)}) copy-start(bf16[32,32]{1,0:T(8,128)(2,1)} %depth_ref.1) | copy-start | bytes 6148
  8.0 17.1 %all-to-all-start = ((bf16[8,16,1024]{2,1,0:T(8,128)(2,1)}), bf16[8,16,1024]{2,1,0:T(8,128)(2,1)S(1)}, u32[]{:S(2)}, u32[]{:S(2)}) async-start(bf16[8,16,1024]{2,1,0:T(8,128)(2,1)} %broadcast_in_dim.2), calls=%async_computation | async-start | bytes 524288 | tf_op jit(solution)/shard_map/all_to_all | solution.py:379
  15.4 71.3 %all-gather.2.cloned.1.call-start = ((), (), s32[]{:S(2)}) async-start(), calls=%async_computation.3 | async-start | bytes 2359296 | tf_op jit(solution)/shard_map/all_gather | solution.py:381
  25.2 0.7 copy-start.2
  25.9 30.7 %all-to-all-start.1 = ((bf16[8,400,128]{2,1,0:T(8,128)(2,1)}), bf16[8,400,128]{2,1,0:T(8,128)(2,1)S(1)}, u32[]{:S(2)}, u32[]{:S(2)}) async-start(bf16[8,400,128]{2,1,0:T(8,128)(2,1)} %pack.1), calls=%async_computation.1 | async-start | bytes 1638400 | tf_op jit(solution)/shard_map/all_to_all | solution.py:382
  36.5 30.1 %copy-start = (bf16[3,32,4096]{2,1,0:T(8,128)(2,1)S(1)}, bf16[3,32,4096]{2,1,0:T(8,128)(2,1)}, u32[]{:S(2)}) copy-start(bf16[3,32,4096]{2,1,0:T(8,128)(2,1)} %f_hbm.1) | copy-start | bytes 2359300
  58.8 27.9 %all-to-all-start.2 = ((bf16[8,384,128]{2,1,0:T(8,128)(2,1)}), bf16[8,384,128]{2,1,0:T(8,128)(2,1)S(1)}, u32[]{:S(2)}, u32[]{:S(2)}) async-start(bf16[8,384,128]{2,1,0:T(8,128)(2,1)} %relax.1), calls=%async_computation.2 | async-start | bytes 1572864 | tf_op jit(solution)/shard_map/all_to_all | solution.py:391
  66.7 20.0 %collective-permute-start = (bf16[64,1024]{1,0:T(8,128)(2,1)S(1)}, bf16[64,1024]{1,0:T(8,128)(2,1)S(1)}, u32[]{:S(2)}, u32[]{:S(2)}) collective-permute-start(bf16[64,1024]{1,0:T(8,128)(2,1)S(1)} %get-tuple-element.13), channel_id=1, source_target_pairs={{0,8},{8,16},{16,24},{24,32},{32,40},{40,48},{48,56},{56,0},{1,9},... | collective-permute-start | bytes 393224 | tf_op jit(solution)/shard_map/ppermute | solution.py:386
  70.1 16.6 %collective-permute-start.1 = (bf16[64,1024]{1,0:T(8,128)(2,1)S(1)}, bf16[64,1024]{1,0:T(8,128)(2,1)S(1)}, u32[]{:S(2)}, u32[]{:S(2)}) collective-permute-start(bf16[64,1024]{1,0:T(8,128)(2,1)S(1)} %get-tuple-element.14), channel_id=1, source_target_pairs={{0,56},{8,0},{16,8},{24,16},{32,24},{40,32},{48,40},{56,48},{1,57}... | collective-permute-start | bytes 393224 | tf_op jit(solution)/shard_map/ppermute | solution.py:385
  74.0 3.9 %collective-permute-start.2 = (bf16[16,1024]{1,0:T(8,128)(2,1)S(1)}, bf16[16,1024]{1,0:T(8,128)(2,1)S(1)}, u32[]{:S(2)}, u32[]{:S(2)}) collective-permute-start(bf16[16,1024]{1,0:T(8,128)(2,1)S(1)} %get-tuple-element.15), channel_id=1, source_target_pairs={{0,1},{1,0},{2,3},{3,2},{4,5},{5,4},{6,7},{7,6},{8,9},{9,8},{10,11... | collective-permute-start | bytes 98312 | tf_op jit(solution)/shard_map/ppermute | solution.py:387
  75.9 10.8 %collective-permute-start.3 = (bf16[16,1024]{1,0:T(8,128)(2,1)S(1)}, bf16[16,1024]{1,0:T(8,128)(2,1)S(1)}, u32[]{:S(2)}, u32[]{:S(2)}) collective-permute-start(bf16[16,1024]{1,0:T(8,128)(2,1)S(1)} %get-tuple-element.16), channel_id=1, source_target_pairs={{0,7},{1,2},{2,1},{3,4},{4,3},{5,6},{6,5},{7,0},{8,15},{9,10},{10,... | collective-permute-start | bytes 98312 | tf_op jit(solution)/shard_map/ppermute | solution.py:388
Sparse Core Ops, SparseCore 0:
  26.0 46.0 all-gather.1

commit v6 on v4

--- a/solution.py
+++ b/solution.py
@@ -137,39 +137,74 @@
     )(place, f, basis)
 
 
-def edges_kernel(core_ref, f_ref, low_ref, high_ref, inner_ref, outer_ref):
-    half = NXY // 2
-    for p in range(PLANES):
-        rows = slice(p // 2 * COLS, (p // 2 + 1) * COLS)
-        lanes = slice(p % 2 * half, (p % 2 + 1) * half)
-        high_ref[rows, lanes] = f_ref[ROWS - 1, :, p * NXY + half : (p + 1) * NXY]
-        low_ref[rows, lanes] = f_ref[0, :, p * NXY : p * NXY + half]
+def columns_kernel(core_ref, f_hbm, shard_hbm, pack_ref, inner_ref, first_ref, last_ref, sem):
+    shard = shard_hbm.shape[0]
+    copies = [
+        pltpu.make_async_copy(f_hbm.at[:, pl.ds(0, 8), :], first_ref, sem.at[0]),
+        pltpu.make_async_copy(f_hbm.at[:, pl.ds(COLS - 8, 8), :], last_ref, sem.at[1]),
+        pltpu.make_async_copy(shard_hbm, pack_ref.at[pl.ds(0, shard)], sem.at[2]),
+    ]
+    for copy in copies:
+        copy.start()
     edge_row = lax.broadcasted_iota(jnp.int32, (16, NXY), 0)
     first = jnp.zeros((16, NXY), F32)
     last = jnp.zeros((16, NXY), F32)
+    for copy in copies:
+        copy.wait()
     for r in range(ROWS):
         for p in range(PLANES):
             lanes = slice(p * NXY, (p + 1) * NXY)
-            a = f_ref[r, 0:8, lanes].astype(F32)[0:1, :]
-            b = f_ref[r, COLS - 8 : COLS, lanes].astype(F32)[7:8, :]
+            a = first_ref[r, :, lanes].astype(F32)[0:1, :]
+            b = last_ref[r, :, lanes].astype(F32)[7:8, :]
             first = jnp.where(edge_row == r * PLANES + p, a, first)
             last = jnp.where(edge_row == r * PLANES + p, b, last)
     core = core_ref[0]
     inner_ref[...] = jnp.where(core == 0, last, first).astype(BF16)
-    outer_ref[...] = jnp.where(core == 0, first, last).astype(BF16)
-
-
-def edges(core, f):
-    row = jax.ShapeDtypeStruct((2 * COLS, NXY), BF16)
-    column = jax.ShapeDtypeStruct((16, NXY), BF16)
+    pack_ref[shard : shard + 16, :] = jnp.where(core == 0, first, last).astype(BF16)
+
+
+def columns(core, f, shard):
+    f, shard = (pltpu.with_memory_space_constraint(x, pltpu.HBM) for x in (f, shard))
+    return pl.pallas_call(
+        columns_kernel,
+        out_shape=(
+            jax.ShapeDtypeStruct((shard.shape[0] + 16, NXY), BF16),
+            jax.ShapeDtypeStruct((16, NXY), BF16),
+        ),
+        in_specs=[smem(), hbm(), hbm()],
+        out_specs=(vmem(), vmem()),
+        scratch_shapes=[
+            pltpu.VMEM((ROWS, 8, PLANES * NXY), BF16),
+            pltpu.VMEM((ROWS, 8, PLANES * NXY), BF16),
+            pltpu.SemaphoreType.DMA((3,)),
+        ],
+        compiler_params=pltpu.CompilerParams(vmem_limit_bytes=LIMIT),
+        name="columns",
+    )(core, f, shard)
+
+
+def edges_kernel(held_ref, f_ref, low_ref, high_ref):
+    half = NXY // 2
+    size = held_ref.shape[0]
+    low_ref[0:size, :] = held_ref[...]
+    high_ref[0:size, :] = held_ref[...]
+    for p in range(PLANES):
+        rows = slice(size + p // 2 * COLS, size + (p // 2 + 1) * COLS)
+        lanes = slice(p % 2 * half, (p % 2 + 1) * half)
+        high_ref[rows, lanes] = f_ref[ROWS - 1, :, p * NXY + half : (p + 1) * NXY]
+        low_ref[rows, lanes] = f_ref[0, :, p * NXY : p * NXY + half]
+
+
+def edges(held, f):
+    row = jax.ShapeDtypeStruct((held.shape[0] + 2 * COLS, NXY), BF16)
     return pl.pallas_call(
         edges_kernel,
-        out_shape=(row, row, column, column),
-        in_specs=[smem(), vmem()],
-        out_specs=(vmem(),) * 4,
+        out_shape=(row, row),
+        in_specs=[vmem(), vmem()],
+        out_specs=(vmem(), vmem()),
         compiler_params=pltpu.CompilerParams(vmem_limit_bytes=LIMIT),
         name="edges",
-    )(core, f)
+    )(held, f)
 
 
 def join_kernel(held_ref, above_ref, below_ref, across_ref, inner_ref, out_ref, sem):
@@ -206,15 +241,17 @@
     half = NXY // 2
     edge = pltpu.make_async_copy(other_ref.at[pl.ds(half, 16)], inner_hbm, sem.at[1])
     edge.start()
-    core, z, y = where_ref[0], where_ref[1], where_ref[2]
+    mine, y = where_ref[0], where_ref[1]
     far = jnp.where(y % 2 == 0, y + 6, y + 2)
-    for m, base in enumerate((y, y + 1, y + 7, far)):
-        for i in range(2):
-            for j in range(4):
-                place = ((base + 4 * i) % 8 * 4 + jnp.bitwise_xor(z, j)) * 2
-                block = slice((m * 8 + j * 2 + i) * 16, (m * 8 + j * 2 + i + 1) * 16)
-                rows_ref[place + core] = own_ref[block, :]
-                rows_ref[place + 1 - core] = other_ref[block, :]
+    for side, ref in ((mine, own_ref), (jnp.bitwise_xor(mine, 1), other_ref)):
+        turn = jnp.bitwise_xor(side, 4)
+        step = jnp.where(side % 2 == 1, 1, 7)
+        places = (side, (side + step) % 8, turn, (turn + step) % 8)
+        for m, base in enumerate((y, y + 1, y + 7, far)):
+            for i in range(2):
+                for j in range(4):
+                    block = slice((m * 8 + i * 4 + j) * 16, (m * 8 + i * 4 + j + 1) * 16)
+                    rows_ref[(base + 4 * i) % 8 * 8 + places[j]] = ref[block, :]
     turned_ref[...] = jnp.transpose(rows_ref[...].reshape(NXY, NXY))
     copy = pltpu.make_async_copy(turned_ref, out_hbm, sem.at[0])
     copy.start()
@@ -340,7 +377,7 @@
         pltpu.make_async_copy(below_hbm.at[edge], lower_ref, sem.at[0]),
         pltpu.make_async_copy(above_hbm.at[edge], upper_ref, sem.at[1]),
         pltpu.make_async_copy(inner_hbm, inner_ref, sem.at[2]),
-        pltpu.make_async_copy(outer_hbm, outer_ref, sem.at[3]),
+        pltpu.make_async_copy(outer_hbm.at[pl.ds(outer_hbm.shape[0] - 16, 16)], outer_ref, sem.at[3]),
         pltpu.make_async_copy(f_hbm, f_ref, sem.at[4]),
     ]
     second = [
@@ -419,7 +456,7 @@
             pltpu.VMEM((2 * COLS, NXY), BF16),
             pltpu.VMEM((2 * COLS, NXY), BF16),
             pltpu.VMEM(inner.shape, BF16),
-            pltpu.VMEM(outer.shape, BF16),
+            pltpu.VMEM((16, NXY), BF16),
             pltpu.VMEM((DATA, NXY), F32),
             pltpu.VMEM(f.shape, BF16),
             pltpu.SemaphoreType.DMA((7,)),
@@ -439,28 +476,25 @@
     place = lax.axis_index("vel").astype(jnp.int32).reshape(1)
     along = lax.axis_index("sy").astype(jnp.int32)
     core = jnp.bitwise_and(along, 1).reshape(1)
-    where = jnp.stack([jnp.bitwise_and(along, 1), along >> 1, lax.axis_index("sx").astype(jnp.int32)])
+    where = jnp.stack([along, lax.axis_index("sx").astype(jnp.int32)])
     flip = lambda bit: [(i, i ^ bit) for i in range(8)]
-    pair = jnp.concatenate([plane_weights, lax.ppermute(plane_weights, "sx", flip(4))])
-    low, high, inner, outer = edges(core, distribution)
+    bundle, inner = columns(core, distribution, plane_weights)
+    outer = lax.ppermute(bundle, "sy", [(i, (i + 1) % 8 if i % 2 else (i - 1) % 8) for i in range(8)])
+    held = jnp.concatenate([plane_weights, outer[: plane_weights.shape[0]]])
+    held = jnp.concatenate([held, lax.ppermute(held, "sy", flip(4))])
+    send, held = lax.optimization_barrier((pack(place, distribution), held))
+    got = lax.all_to_all(send, "vel", 0, 0, tiled=True)
+    held = jnp.concatenate([held, lax.ppermute(held, "sx", flip(4))])
+    low, high = edges(held, distribution)
     mix = spread(depth_weights)
-    spot, pair = lax.optimization_barrier((place, pair))
-    held = jnp.concatenate(
-        [pair] + [lax.ppermute(pair, "sy", flip(2 * step)) for step in (1, 2, 3)]
-    )
-    send, held = lax.optimization_barrier((pack(spot, distribution), held))
-    got = lax.all_to_all(send, "vel", 0, 0, tiled=True)
-    above = lax.ppermute(jnp.concatenate([held, low]), "sx", ring("sx", -1))
-    below = lax.ppermute(jnp.concatenate([held, high]), "sx", ring("sx", 1))
+    above = lax.ppermute(low, "sx", ring("sx", -1))
+    below = lax.ppermute(high, "sx", ring("sx", 1))
     across = lax.ppermute(held, "sx", [(i, (i + 2) % 8 if i % 2 == 0 else (i - 2) % 8) for i in range(8)])
-    outer = lax.ppermute(outer, "sy", [(i, (i + 1) % 8 if i % 2 else (i - 1) % 8) for i in range(8)])
     own = join(held, above, below, across, inner)
     other = lax.ppermute(own, "sy", flip(1))
     weights, inner = assemble(where, own, other)
     back = lax.all_to_all(relax(place, got, mix), "vel", 0, 0, tiled=True)
-    return advance(
-        core, distribution, back, weights, below, above, inner, outer
-    )
+    return advance(core, distribution, back, weights, below, above, inner, outer)
 
 
 def solution(mesh):

time: 92.7 us -> 91 us (0.982)
  the two profiles are of different devices: /device:TPU:56 before, /device:TPU:64 now
where the time goes in v6:
time: 91 us; the launch traced here: 90.2 us
  starting transfers between devices  46.5 us (51%)
  waiting for transfers between devices  26.8 us (29%)
  Pallas kernels  15.9 us (17%)
    all_to_all x1, starting transfers between devices, local(): got = lax.all_to_all(send, 'vel', 0, 0, tiled=True)  10.7 us
    ppermute x1, starting transfers between devices, local(): held = jnp.concatenate([held, lax.ppermute(held, 'sx', flip(4))])  7.73 us
    ppermute x1, waiting for transfers between devices, local(): lax.ppermute(held, 'sx', [(i, (i + 2) % 8 if i % 2 == 0 else (i - 2) % 8)...  7.67 us
    ppermute x1, starting transfers between devices, local(): above = lax.ppermute(low, 'sx', ring('sx', -1))  7.53 us
    ppermute x1, starting transfers between devices, local(): held = jnp.concatenate([held, lax.ppermute(held, 'sy', flip(4))])  6.08 us
    all_to_all x1, starting transfers between devices, local(): back = lax.all_to_all(relax(place, got, mix), 'vel', 0, 0, tiled=True)  5.33 us
    ppermute x1, waiting for transfers between devices, local(): held = jnp.concatenate([held, lax.ppermute(held, 'sx', flip(4))])  4.33 us
    all_to_all x1, waiting for transfers between devices, local(): back = lax.all_to_all(relax(place, got, mix), 'vel', 0, 0, tiled=True)  4.24 us
  transfers between devices with their start and end apart: 9, of which 6 were waited for; matrix products, arithmetic and copies ran while one was open for 0% of the time, Pallas kernels for 12%

profile of v6, /device:TPU:64, one launch (start us, length us, event | category | flops | bytes accessed | tf_op | source)
XLA Modules:
  0.0 90.2 jit_solution(325997864332150837)
XLA Ops:
  0.0 1.1 %columns.1 = (bf16[32,1024]{1,0:T(8,128)(2,1)S(1)}, bf16[16,1024]{1,0:T(8,128)(2,1)S(1)}) custom-call(s32[1]{0:T(128)} %bitcast.core_ref, bf16[3,32,4096]{2,1,0:T(8,128)(2,1)} %f_hbm.3, bf16[16,1024]{1,0:T(8,128)(2,1)} %shard_hbm.1), custom_call_target="tpu_custom_call" | custom-call | tf_op jit(solution)/shard_map/columns/pallas_call | solution.py:168
  1.1 0.0 copy-start.2
  1.2 1.9 %collective-permute-start = (bf16[32,1024]{1,0:T(8,128)(2,1)S(1)}, bf16[32,1024]{1,0:T(8,128)(2,1)S(1)}, u32[]{:S(2)}, u32[]{:S(2)}) collective-permute-start(bf16[32,1024]{1,0:T(8,128)(2,1)S(1)} %get-tuple-element.13), channel_id=1, source_target_pairs={{0,7},{1,2},{2,1},{3,4},{4,3},{5,6},{6,5},{7,0},{8,15},{9,10},{10,... | collective-permute-start | bytes 196616 | tf_op jit(solution)/shard_map/ppermute | solution.py:482
  3.1 3.7 %collective-permute-done.outer_hbm = bf16[32,1024]{1,0:T(8,128)(2,1)S(1)} collective-permute-done((bf16[32,1024]{1,0:T(8,128)(2,1)S(1)}, bf16[32,1024]{1,0:T(8,128)(2,1)S(1)}, u32[]{:S(2)}, u32[]{:S(2)}) %collective-permute-start) | collective-permute-done | bytes 65568 | tf_op jit(solution)/shard_map/ppermute | solution.py:482
  6.7 0.8 pad_maximum_fusion.1
  7.5 6.1 %collective-permute-start.1 = (bf16[32,1024]{1,0:T(8,128)(2,1)S(1)}, bf16[32,1024]{1,0:T(8,128)(2,1)S(1)}, u32[]{:S(2)}, u32[]{:S(2)}) collective-permute-start(bf16[32,1024]{1,0:T(8,128)(2,1)S(1)} %pad_maximum_fusion.1), channel_id=1, source_target_pairs={{0,4},{1,5},{2,6},{3,7},{4,0},{5,1},{6,2},{7,3},{8,12},{9,13},{10,... | collective-permute-start | bytes 196616 | tf_op jit(solution)/shard_map/ppermute | solution.py:484
  13.6 2.8 %pack.1 = bf16[8,400,128]{2,1,0:T(8,128)(2,1)} custom-call(s32[1]{0:T(128)} %bitcast.1.place_ref, bf16[3,32,4096]{2,1,0:T(8,128)(2,1)} %f_hbm.3, bf16[1024,128]{1,0:T(8,128)(2,1)} %constant.15.clone.basis_ref), custom_call_target="tpu_custom_call" | custom-call | tf_op jit(solution)/shard_map/pack/pallas_call | solution.py:122
  16.4 0.0 collective-permute-done.1
  16.4 0.0 copy-done.2
  16.5 0.0 copy-start
  16.5 10.7 %all-to-all-start = ((bf16[8,400,128]{2,1,0:T(8,128)(2,1)}), bf16[8,400,128]{2,1,0:T(8,128)(2,1)S(1)}, u32[]{:S(2)}, u32[]{:S(2)}) async-start(bf16[8,400,128]{2,1,0:T(8,128)(2,1)} %pack.1), calls=%async_computation | async-start | bytes 1638400 | tf_op jit(solution)/shard_map/all_to_all | solution.py:486
  27.1 0.0 copy-start.1
  27.1 7.7 %collective-permute-start.2 = (bf16[64,1024]{1,0:T(8,128)(2,1)S(1)}, bf16[64,1024]{1,0:T(8,128)(2,1)S(1)}, u32[]{:S(2)}, u32[]{:S(2)}) collective-permute-start(bf16[64,1024]{1,0:T(8,128)(2,1)S(1)} %pad_maximum_fusion), channel_id=1, source_target_pairs={{0,32},{8,40},{16,48},{24,56},{32,0},{40,8},{48,16},{56,24},{1,33}... | collective-permute-start | bytes 393224 | tf_op jit(solution)/shard_map/ppermute | solution.py:487
  34.9 4.3 %collective-permute-done.2 = bf16[64,1024]{1,0:T(8,128)(2,1)S(1)} collective-permute-done((bf16[64,1024]{1,0:T(8,128)(2,1)S(1)}, bf16[64,1024]{1,0:T(8,128)(2,1)S(1)}, u32[]{:S(2)}, u32[]{:S(2)}) %collective-permute-start.2) | collective-permute-done | bytes 131104 | tf_op jit(solution)/shard_map/ppermute | solution.py:487
  39.2 0.0 copy-done
  39.3 0.9 %edges.1 = (bf16[192,1024]{1,0:T(8,128)(2,1)}, bf16[192,1024]{1,0:T(8,128)(2,1)}) custom-call(bf16[128,1024]{1,0:T(8,128)(2,1)S(1)} %constant_dynamic-update-slice_fusion.held_ref, bf16[3,32,4096]{2,1,0:T(8,128)(2,1)S(1)} %copy-done), custom_call_target="tpu_custom_call" | custom-call | tf_op jit(solution)/shard_map/edges/pallas_call | solution.py:200
  40.2 7.5 %collective-permute-start.3 = (bf16[192,1024]{1,0:T(8,128)(2,1)}, bf16[192,1024]{1,0:T(8,128)(2,1)S(1)}, u32[]{:S(2)}, u32[]{:S(2)}) collective-permute-start(bf16[192,1024]{1,0:T(8,128)(2,1)} %get-tuple-element.16), channel_id=1, source_target_pairs={{0,56},{8,0},{16,8},{24,16},{32,24},{40,32},{48,40},{56,48},{1,57}... | collective-permute-start | bytes 1179656 | tf_op jit(solution)/shard_map/ppermute | solution.py:490
  47.7 1.9 %collective-permute-start.4 = (bf16[192,1024]{1,0:T(8,128)(2,1)}, bf16[192,1024]{1,0:T(8,128)(2,1)}, u32[]{:S(2)}, u32[]{:S(2)}) collective-permute-start(bf16[192,1024]{1,0:T(8,128)(2,1)} %get-tuple-element.17), channel_id=1, source_target_pairs={{0,8},{8,16},{16,24},{24,32},{32,40},{40,48},{48,56},{56,0},{1,9},... | collective-permute-start | bytes 1179656 | tf_op jit(solution)/shard_map/ppermute | solution.py:491
  49.7 0.0 copy-done.1
  49.7 0.4 spread.1.mix_ref
  50.1 4.1 %all-to-all-done.got_ref = bf16[8,400,128]{2,1,0:T(8,128)(2,1)S(1)} async-done(((bf16[8,400,128]{2,1,0:T(8,128)(2,1)}), bf16[8,400,128]{2,1,0:T(8,128)(2,1)S(1)}, u32[]{:S(2)}, u32[]{:S(2)}) %all-to-all-start) | async-done | bytes 819232 | tf_op jit(solution)/shard_map/all_to_all | solution.py:486
  54.2 2.3 %relax.1 = bf16[8,384,128]{2,1,0:T(8,128)(2,1)} custom-call(s32[1]{0:T(128)} %bitcast.1.place_ref, bf16[8,400,128]{2,1,0:T(8,128)(2,1)S(1)} %all-to-all-done.got_ref, bf16[512,512]{1,0:T(8,128)(2,1)S(1)} %spread.1.mix_ref), custom_call_target="tpu_custom_call" | custom-call | tf_op jit(solution)/shard_map/relax/pallas_call | solution.py:342
  56.5 5.3 %all-to-all-start.1 = ((bf16[8,384,128]{2,1,0:T(8,128)(2,1)}), bf16[8,384,128]{2,1,0:T(8,128)(2,1)S(1)}, u32[]{:S(2)}, u32[]{:S(2)}) async-start(bf16[8,384,128]{2,1,0:T(8,128)(2,1)} %relax.1), calls=%async_computation.1 | async-start | bytes 1572864 | tf_op jit(solution)/shard_map/all_to_all | solution.py:496
  61.8 3.4 %collective-permute-start.5 = (bf16[128,1024]{1,0:T(8,128)(2,1)S(1)}, bf16[128,1024]{1,0:T(8,128)(2,1)S(1)}, u32[]{:S(2)}, u32[]{:S(2)}) collective-permute-start(bf16[128,1024]{1,0:T(8,128)(2,1)S(1)} %constant_dynamic-update-slice_fusion.held_ref), channel_id=1, source_target_pairs={{0,16},{8,56},{16,32},{24,8},{32,48},{40,24},{48,0},{56,40},{1,17}... | collective-permute-start | bytes 786440 | tf_op jit(solution)/shard_map/ppermute | solution.py:492
  65.3 7.7 %collective-permute-done.5.across_ref = bf16[128,1024]{1,0:T(8,128)(2,1)S(1)} collective-permute-done((bf16[128,1024]{1,0:T(8,128)(2,1)S(1)}, bf16[128,1024]{1,0:T(8,128)(2,1)S(1)}, u32[]{:S(2)}, u32[]{:S(2)}) %collective-permute-start.5) | collective-permute-done | bytes 262176 | tf_op jit(solution)/shard_map/ppermute | solution.py:492
  73.0 0.0 collective-permute-done.3.above_ref.above_hbm
  73.0 0.0 collective-permute-done.4.below_ref.below_hbm
  73.0 1.0 %join.1.own_ref = bf16[528,1024]{1,0:T(8,128)(2,1)S(1)} custom-call(bf16[128,1024]{1,0:T(8,128)(2,1)S(1)} %constant_dynamic-update-slice_fusion.held_ref, bf16[192,1024]{1,0:T(8,128)(2,1)S(1)} %collective-permute-done.3.above_ref.above_hbm, bf16[192,1024]{1,0:T(8,128)(2,1)} %collective-permute-done.4.below_ref.below_hbm, ...), custom_call_target="tpu_custom_call" | custom-call | tf_op jit(solution)/shard_map/join/pallas_call | solution.py:229
  74.0 1.9 %collective-permute-start.6 = (bf16[528,1024]{1,0:T(8,128)(2,1)S(1)}, bf16[528,1024]{1,0:T(8,128)(2,1)}, u32[]{:S(2)}, u32[]{:S(2)}) collective-permute-start(bf16[528,1024]{1,0:T(8,128)(2,1)S(1)} %join.1.own_ref), channel_id=1, source_target_pairs={{0,1},{1,0},{2,3},{3,2},{4,5},{5,4},{6,7},{7,6},{8,9},{9,8},{10,11... | collective-permute-start | bytes 3244040 | tf_op jit(solution)/shard_map/ppermute | solution.py:494
  75.9 0.1 pad_add_fusion.where_ref
  76.0 2.7 %collective-permute-done.6.other_ref = bf16[528,1024]{1,0:T(8,128)(2,1)} collective-permute-done((bf16[528,1024]{1,0:T(8,128)(2,1)S(1)}, bf16[528,1024]{1,0:T(8,128)(2,1)}, u32[]{:S(2)}, u32[]{:S(2)}) %collective-permute-start.6) | collective-permute-done | bytes 1081376 | tf_op jit(solution)/shard_map/ppermute | solution.py:494
  78.7 3.4 %assemble.1 = (bf16[1024,1024]{1,0:T(8,128)(2,1)}, bf16[16,1024]{1,0:T(8,128)(2,1)S(1)}) custom-call(s32[2]{0:T(128)S(1)} %pad_add_fusion.where_ref, bf16[528,1024]{1,0:T(8,128)(2,1)S(1)} %join.1.own_ref, bf16[528,1024]{1,0:T(8,128)(2,1)} %collective-permute-done.6.other_ref), custom_call_target="tpu_custom_call" | custom-call | tf_op jit(solution)/shard_map/assemble/pallas_call | solution.py:263
  82.2 4.2 %all-to-all-done.1.back_hbm = bf16[8,384,128]{2,1,0:T(8,128)(2,1)S(1)} async-done(((bf16[8,384,128]{2,1,0:T(8,128)(2,1)}), bf16[8,384,128]{2,1,0:T(8,128)(2,1)S(1)}, u32[]{:S(2)}, u32[]{:S(2)}) %all-to-all-start.1) | async-done | bytes 786464 | tf_op jit(solution)/shard_map/all_to_all | solution.py:496
  86.4 3.8 %advance.1 = bf16[3,32,4096]{2,1,0:T(8,128)(2,1)} custom-call(s32[1]{0:T(128)} %bitcast.core_ref, bf16[3,32,4096]{2,1,0:T(8,128)(2,1)S(1)} %copy-done, bf16[8,384,128]{2,1,0:T(8,128)(2,1)S(1)} %all-to-all-done.1.back_hbm, bf16[1024,1024]{1,0:T(8,128)(2,1)} %get-tuple-element.19.weights_hbm, bf16[192,1024]{1,0:T(8,128)(2,1)} %collective-permute-done.4.below_ref.below_hbm, ...), custom_call_target="tpu_custom_call" | custom-call | tf_op jit(solution)/shard_map/advance/pallas_call | solution.py:447
  (4 shorter events, 0.0 us)
Async XLA Ops:
  1.1 15.3 %copy-start.2 = (bf16[16,1024]{1,0:T(8,128)(2,1)S(1)}, bf16[16,1024]{1,0:T(8,128)(2,1)}, u32[]{:S(2)}) copy-start(bf16[16,1024]{1,0:T(8,128)(2,1)} %shard_hbm.1) | copy-start | bytes 98308
  1.2 5.6 %collective-permute-start = (bf16[32,1024]{1,0:T(8,128)(2,1)S(1)}, bf16[32,1024]{1,0:T(8,128)(2,1)S(1)}, u32[]{:S(2)}, u32[]{:S(2)}) collective-permute-start(bf16[32,1024]{1,0:T(8,128)(2,1)S(1)} %get-tuple-element.13), channel_id=1, source_target_pairs={{0,7},{1,2},{2,1},{3,4},{4,3},{5,6},{6,5},{7,0},{8,15},{9,10},{10,... | collective-permute-start | bytes 196616 | tf_op jit(solution)/shard_map/ppermute | solution.py:482
  7.5 8.9 %collective-permute-start.1 = (bf16[32,1024]{1,0:T(8,128)(2,1)S(1)}, bf16[32,1024]{1,0:T(8,128)(2,1)S(1)}, u32[]{:S(2)}, u32[]{:S(2)}) collective-permute-start(bf16[32,1024]{1,0:T(8,128)(2,1)S(1)} %pad_maximum_fusion.1), channel_id=1, source_target_pairs={{0,4},{1,5},{2,6},{3,7},{4,0},{5,1},{6,2},{7,3},{8,12},{9,13},{10,... | collective-permute-start | bytes 196616 | tf_op jit(solution)/shard_map/ppermute | solution.py:484
  16.5 22.8 %copy-start = (bf16[3,32,4096]{2,1,0:T(8,128)(2,1)S(1)}, bf16[3,32,4096]{2,1,0:T(8,128)(2,1)}, u32[]{:S(2)}) copy-start(bf16[3,32,4096]{2,1,0:T(8,128)(2,1)} %f_hbm.3) | copy-start | bytes 2359300
  16.5 37.7 %all-to-all-start = ((bf16[8,400,128]{2,1,0:T(8,128)(2,1)}), bf16[8,400,128]{2,1,0:T(8,128)(2,1)S(1)}, u32[]{:S(2)}, u32[]{:S(2)}) async-start(bf16[8,400,128]{2,1,0:T(8,128)(2,1)} %pack.1), calls=%async_computation | async-start | bytes 1638400 | tf_op jit(solution)/shard_map/all_to_all | solution.py:486
  27.1 22.5 %copy-start.1 = (bf16[32,32]{1,0:T(8,128)(2,1)S(1)}, bf16[32,32]{1,0:T(8,128)(2,1)}, u32[]{:S(2)}) copy-start(bf16[32,32]{1,0:T(8,128)(2,1)} %depth_ref.1) | copy-start | bytes 6148
  27.1 12.1 %collective-permute-start.2 = (bf16[64,1024]{1,0:T(8,128)(2,1)S(1)}, bf16[64,1024]{1,0:T(8,128)(2,1)S(1)}, u32[]{:S(2)}, u32[]{:S(2)}) collective-permute-start(bf16[64,1024]{1,0:T(8,128)(2,1)S(1)} %pad_maximum_fusion), channel_id=1, source_target_pairs={{0,32},{8,40},{16,48},{24,56},{32,0},{40,8},{48,16},{56,24},{1,33}... | collective-permute-start | bytes 393224 | tf_op jit(solution)/shard_map/ppermute | solution.py:487
  40.2 32.8 %collective-permute-start.3 = (bf16[192,1024]{1,0:T(8,128)(2,1)}, bf16[192,1024]{1,0:T(8,128)(2,1)S(1)}, u32[]{:S(2)}, u32[]{:S(2)}) collective-permute-start(bf16[192,1024]{1,0:T(8,128)(2,1)} %get-tuple-element.16), channel_id=1, source_target_pairs={{0,56},{8,0},{16,8},{24,16},{32,24},{40,32},{48,40},{56,48},{1,57}... | collective-permute-start | bytes 1179656 | tf_op jit(solution)/shard_map/ppermute | solution.py:490
  47.7 25.2 %collective-permute-start.4 = (bf16[192,1024]{1,0:T(8,128)(2,1)}, bf16[192,1024]{1,0:T(8,128)(2,1)}, u32[]{:S(2)}, u32[]{:S(2)}) collective-permute-start(bf16[192,1024]{1,0:T(8,128)(2,1)} %get-tuple-element.17), channel_id=1, source_target_pairs={{0,8},{8,16},{16,24},{24,32},{32,40},{40,48},{48,56},{56,0},{1,9},... | collective-permute-start | bytes 1179656 | tf_op jit(solution)/shard_map/ppermute | solution.py:491
  56.5 29.9 %all-to-all-start.1 = ((bf16[8,384,128]{2,1,0:T(8,128)(2,1)}), bf16[8,384,128]{2,1,0:T(8,128)(2,1)S(1)}, u32[]{:S(2)}, u32[]{:S(2)}) async-start(bf16[8,384,128]{2,1,0:T(8,128)(2,1)} %relax.1), calls=%async_computation.1 | async-start | bytes 1572864 | tf_op jit(solution)/shard_map/all_to_all | solution.py:496
  61.8 11.1 %collective-permute-start.5 = (bf16[128,1024]{1,0:T(8,128)(2,1)S(1)}, bf16[128,1024]{1,0:T(8,128)(2,1)S(1)}, u32[]{:S(2)}, u32[]{:S(2)}) collective-permute-start(bf16[128,1024]{1,0:T(8,128)(2,1)S(1)} %constant_dynamic-update-slice_fusion.held_ref), channel_id=1, source_target_pairs={{0,16},{8,56},{16,32},{24,8},{32,48},{40,24},{48,0},{56,40},{1,17}... | collective-permute-start | bytes 786440 | tf_op jit(solution)/shard_map/ppermute | solution.py:492
  74.0 4.7 %collective-permute-start.6 = (bf16[528,1024]{1,0:T(8,128)(2,1)S(1)}, bf16[528,1024]{1,0:T(8,128)(2,1)}, u32[]{:S(2)}, u32[]{:S(2)}) collective-permute-start(bf16[528,1024]{1,0:T(8,128)(2,1)S(1)} %join.1.own_ref), channel_id=1, source_target_pairs={{0,1},{1,0},{2,3},{3,2},{4,5},{5,4},{6,7},{7,6},{8,9},{9,8},{10,11... | collective-permute-start | bytes 3244040 | tf_op jit(solution)/shard_map/ppermute | solution.py:494

commit v7 on v6

--- a/solution.py
+++ b/solution.py
@@ -207,17 +207,18 @@
     )(held, f)
 
 
-def join_kernel(held_ref, above_ref, below_ref, across_ref, inner_ref, out_ref, sem):
-    size = held_ref.shape[0]
+def join_kernel(*refs):
+    *parts, inner_ref, out_ref, sem = refs
+    size = (out_ref.shape[0] - 16) // len(parts)
     copies = []
-    for m, ref in enumerate((held_ref, above_ref, below_ref, across_ref)):
+    for m, ref in enumerate(parts):
         copies.append(
             pltpu.make_async_copy(
                 ref.at[pl.ds(0, size)], out_ref.at[pl.ds(m * size, size)], sem.at[m]
             )
         )
     copies.append(
-        pltpu.make_async_copy(inner_ref, out_ref.at[pl.ds(4 * size, 16)], sem.at[4])
+        pltpu.make_async_copy(inner_ref, out_ref.at[pl.ds(len(parts) * size, 16)], sem.at[len(parts)])
     )
     for copy in copies:
         copy.start()
@@ -225,16 +226,16 @@
         copy.wait()
 
 
-def join(held, above, below, across, inner):
+def join(parts, inner):
     return pl.pallas_call(
         join_kernel,
-        out_shape=jax.ShapeDtypeStruct((4 * held.shape[0] + 16, NXY), BF16),
-        in_specs=[hbm()] * 5,
+        out_shape=jax.ShapeDtypeStruct((len(parts) * parts[0].shape[0] + 16, NXY), BF16),
+        in_specs=[hbm()] * (len(parts) + 1),
         out_specs=hbm(),
-        scratch_shapes=[pltpu.SemaphoreType.DMA((5,))],
+        scratch_shapes=[pltpu.SemaphoreType.DMA((len(parts) + 1,))],
         compiler_params=pltpu.CompilerParams(vmem_limit_bytes=LIMIT),
         name="join",
-    )(held, above, below, across, inner)
+    )(*parts, inner)
 
 
 def assemble_kernel(where_ref, own_ref, other_ref, out_hbm, inner_hbm, rows_ref, turned_ref, sem):
@@ -242,16 +243,14 @@
     edge = pltpu.make_async_copy(other_ref.at[pl.ds(half, 16)], inner_hbm, sem.at[1])
     edge.start()
     mine, y = where_ref[0], where_ref[1]
-    far = jnp.where(y % 2 == 0, y + 6, y + 2)
     for side, ref in ((mine, own_ref), (jnp.bitwise_xor(mine, 1), other_ref)):
         turn = jnp.bitwise_xor(side, 4)
         step = jnp.where(side % 2 == 1, 1, 7)
         places = (side, (side + step) % 8, turn, (turn + step) % 8)
-        for m, base in enumerate((y, y + 1, y + 7, far)):
-            for i in range(2):
-                for j in range(4):
-                    block = slice((m * 8 + i * 4 + j) * 16, (m * 8 + i * 4 + j + 1) * 16)
-                    rows_ref[(base + 4 * i) % 8 * 8 + places[j]] = ref[block, :]
+        for m, away in enumerate((0, 1, 7, 2, 6, 3, 5, 4)):
+            for j in range(4):
+                block = slice((m * 4 + j) * 16, (m * 4 + j + 1) * 16)
+                rows_ref[(y + away) % 8 * 8 + places[j]] = ref[block, :]
     turned_ref[...] = jnp.transpose(rows_ref[...].reshape(NXY, NXY))
     copy = pltpu.make_async_copy(turned_ref, out_hbm, sem.at[0])
     copy.start()
@@ -484,16 +483,17 @@
     held = jnp.concatenate([held, lax.ppermute(held, "sy", flip(4))])
     send, held = lax.optimization_barrier((pack(place, distribution), held))
     got = lax.all_to_all(send, "vel", 0, 0, tiled=True)
-    held = jnp.concatenate([held, lax.ppermute(held, "sx", flip(4))])
+    far = [lax.ppermute(held, "sx", ring("sx", -away)) for away in (2, 6, 3, 5, 4)]
     low, high = edges(held, distribution)
     mix = spread(depth_weights)
     above = lax.ppermute(low, "sx", ring("sx", -1))
     below = lax.ppermute(high, "sx", ring("sx", 1))
-    across = lax.ppermute(held, "sx", [(i, (i + 2) % 8 if i % 2 == 0 else (i - 2) % 8) for i in range(8)])
-    own = join(held, above, below, across, inner)
+    send = relax(place, got, mix)
+    send, *far = lax.optimization_barrier((send, *far))
+    own = join([held, above, below] + far, inner)
     other = lax.ppermute(own, "sy", flip(1))
     weights, inner = assemble(where, own, other)
-    back = lax.all_to_all(relax(place, got, mix), "vel", 0, 0, tiled=True)
+    back = lax.all_to_all(send, "vel", 0, 0, tiled=True)
     return advance(core, distribution, back, weights, below, above, inner, outer)
 
 

time: 91 us -> 102 us (1.12)
  the two profiles are of different devices: /device:TPU:64 before, /device:TPU:67 now
where the time goes in v7:
time: 102 us
  starting transfers between devices  65.7 us (64%)
  Pallas kernels  15.6 us (15%)
  waiting for transfers between devices  15.5 us (15%)
  local copies, waits for them, and re-layouts  3.65 us (4%)
    ppermute x5, starting transfers between devices, local(): lax.ppermute(held, 'sx', ring('sx', -away))  23.1 us
    all_to_all x1, starting transfers between devices, local(): got = lax.all_to_all(send, 'vel', 0, 0, tiled=True)  10 us
    all_to_all x1, starting transfers between devices, local(): back = lax.all_to_all(send, 'vel', 0, 0, tiled=True)  9.05 us
    ppermute x1, starting transfers between devices, local(): held = jnp.concatenate([held, lax.ppermute(held, 'sy', flip(4))])  6.68 us
    ppermute x1, starting transfers between devices, local(): above = lax.ppermute(low, 'sx', ring('sx', -1))  5.73 us
    ppermute x1, waiting for transfers between devices, local(): below = lax.ppermute(high, 'sx', ring('sx', 1))  5.05 us
    ppermute x1, starting transfers between devices, local(): other = lax.ppermute(own, 'sy', flip(1))  4.64 us
    ppermute x1, starting transfers between devices, local(): lax.ppermute(bundle, 'sy', [(i, (i + 1) % 8 if i % 2 else (i - 1) % 8) fo...  4.56 us
  transfers between devices with their start and end apart: 12, of which 6 were waited for; matrix products, arithmetic and copies ran while one was open for 0% of the time, Pallas kernels for 10%

profile of v7, /device:TPU:67, one launch (start us, length us, event | category | flops | bytes accessed | tf_op | source)
XLA Modules:
  0.0 101.6 jit_solution(14891962780023983652)
XLA Ops:
  0.0 1.1 %columns.1 = (bf16[32,1024]{1,0:T(8,128)(2,1)S(1)}, bf16[16,1024]{1,0:T(8,128)(2,1)S(1)}) custom-call(s32[1]{0:T(128)} %bitcast.core_ref, bf16[3,32,4096]{2,1,0:T(8,128)(2,1)} %f_hbm.3, bf16[16,1024]{1,0:T(8,128)(2,1)} %shard_hbm.1), custom_call_target="tpu_custom_call" | custom-call | tf_op jit(solution)/shard_map/columns/pallas_call | solution.py:168
  1.1 0.0 copy-start.10
  1.2 4.6 %collective-permute-start = (bf16[32,1024]{1,0:T(8,128)(2,1)S(1)}, bf16[32,1024]{1,0:T(8,128)(2,1)S(1)}, u32[]{:S(2)}, u32[]{:S(2)}) collective-permute-start(bf16[32,1024]{1,0:T(8,128)(2,1)S(1)} %get-tuple-element.19), channel_id=1, source_target_pairs={{0,7},{1,2},{2,1},{3,4},{4,3},{5,6},{6,5},{7,0},{8,15},{9,10},{10,... | collective-permute-start | bytes 196616 | tf_op jit(solution)/shard_map/ppermute | solution.py:481
  5.7 1.9 %collective-permute-done.outer_hbm = bf16[32,1024]{1,0:T(8,128)(2,1)S(1)} collective-permute-done((bf16[32,1024]{1,0:T(8,128)(2,1)S(1)}, bf16[32,1024]{1,0:T(8,128)(2,1)S(1)}, u32[]{:S(2)}, u32[]{:S(2)}) %collective-permute-start) | collective-permute-done | bytes 65568 | tf_op jit(solution)/shard_map/ppermute | solution.py:481
  7.7 0.8 pad_maximum_fusion.1
  8.4 6.7 %collective-permute-start.1 = (bf16[32,1024]{1,0:T(8,128)(2,1)S(1)}, bf16[32,1024]{1,0:T(8,128)(2,1)S(1)}, u32[]{:S(2)}, u32[]{:S(2)}) collective-permute-start(bf16[32,1024]{1,0:T(8,128)(2,1)S(1)} %pad_maximum_fusion.1), channel_id=1, source_target_pairs={{0,4},{1,5},{2,6},{3,7},{4,0},{5,1},{6,2},{7,3},{8,12},{9,13},{10,... | collective-permute-start | bytes 196616 | tf_op jit(solution)/shard_map/ppermute | solution.py:483
  15.1 2.8 %pack.1 = bf16[8,400,128]{2,1,0:T(8,128)(2,1)} custom-call(s32[1]{0:T(128)} %bitcast.1.place_ref, bf16[3,32,4096]{2,1,0:T(8,128)(2,1)} %f_hbm.3, bf16[1024,128]{1,0:T(8,128)(2,1)} %constant.15.clone.basis_ref), custom_call_target="tpu_custom_call" | custom-call | tf_op jit(solution)/shard_map/pack/pallas_call | solution.py:122
  18.0 0.0 copy-start.9
  18.0 0.0 collective-permute-done.1
  18.0 0.0 copy-done.10
  18.0 10.0 %all-to-all-start = ((bf16[8,400,128]{2,1,0:T(8,128)(2,1)}), bf16[8,400,128]{2,1,0:T(8,128)(2,1)S(1)}, u32[]{:S(2)}, u32[]{:S(2)}) async-start(bf16[8,400,128]{2,1,0:T(8,128)(2,1)} %pack.1), calls=%async_computation | async-start | bytes 1638400 | tf_op jit(solution)/shard_map/all_to_all | solution.py:485
  28.0 7.4 %collective-permute-start.6 = (bf16[64,1024]{1,0:T(8,128)(2,1)S(1)}, bf16[64,1024]{1,0:T(8,128)(2,1)S(1)}, u32[]{:S(2)}, u32[]{:S(2)}) collective-permute-start(bf16[64,1024]{1,0:T(8,128)(2,1)S(1)} %pad_maximum_fusion.held_ref.refs_0_), channel_id=1, source_target_pairs={{0,32},{8,40},{16,48},{24,56},{32,0},{40,8},{48,16},{56,24},{1,33}... | collective-permute-start | bytes 393224 | tf_op jit(solution)/shard_map/ppermute | solution.py:486
  35.5 2.5 %collective-permute-start.5 = (bf16[64,1024]{1,0:T(8,128)(2,1)S(1)}, bf16[64,1024]{1,0:T(8,128)(2,1)S(1)}, u32[]{:S(2)}, u32[]{:S(2)}) collective-permute-start(bf16[64,1024]{1,0:T(8,128)(2,1)S(1)} %pad_maximum_fusion.held_ref.refs_0_), channel_id=1, source_target_pairs={{0,24},{8,32},{16,40},{24,48},{32,56},{40,0},{48,8},{56,16},{1,25}... | collective-permute-start | bytes 393224 | tf_op jit(solution)/shard_map/ppermute | solution.py:486
  38.0 5.8 %collective-permute-start.4 = (bf16[64,1024]{1,0:T(8,128)(2,1)S(1)}, bf16[64,1024]{1,0:T(8,128)(2,1)S(1)}, u32[]{:S(2)}, u32[]{:S(2)}) collective-permute-start(bf16[64,1024]{1,0:T(8,128)(2,1)S(1)} %pad_maximum_fusion.held_ref.refs_0_), channel_id=1, source_target_pairs={{0,40},{8,48},{16,56},{24,0},{32,8},{40,16},{48,24},{56,32},{1,41}... | collective-permute-start | bytes 393224 | tf_op jit(solution)/shard_map/ppermute | solution.py:486
  43.8 2.4 %collective-permute-start.3 = (bf16[64,1024]{1,0:T(8,128)(2,1)S(1)}, bf16[64,1024]{1,0:T(8,128)(2,1)S(1)}, u32[]{:S(2)}, u32[]{:S(2)}) collective-permute-start(bf16[64,1024]{1,0:T(8,128)(2,1)S(1)} %pad_maximum_fusion.held_ref.refs_0_), channel_id=1, source_target_pairs={{0,16},{8,24},{16,32},{24,40},{32,48},{40,56},{48,0},{56,8},{1,17}... | collective-permute-start | bytes 393224 | tf_op jit(solution)/shard_map/ppermute | solution.py:486
  46.2 5.0 %collective-permute-start.2 = (bf16[64,1024]{1,0:T(8,128)(2,1)S(1)}, bf16[64,1024]{1,0:T(8,128)(2,1)S(1)}, u32[]{:S(2)}, u32[]{:S(2)}) collective-permute-start(bf16[64,1024]{1,0:T(8,128)(2,1)S(1)} %pad_maximum_fusion.held_ref.refs_0_), channel_id=1, source_target_pairs={{0,48},{8,56},{16,0},{24,8},{32,16},{40,24},{48,32},{56,40},{1,49}... | collective-permute-start | bytes 393224 | tf_op jit(solution)/shard_map/ppermute | solution.py:486
  51.2 0.0 copy-done.9
  51.2 0.4 spread.1.mix_ref
  51.6 0.1 all-to-all-done.got_ref
  51.7 2.3 %relax.1 = bf16[8,384,128]{2,1,0:T(8,128)(2,1)} custom-call(s32[1]{0:T(128)} %bitcast.1.place_ref, bf16[8,400,128]{2,1,0:T(8,128)(2,1)S(1)} %all-to-all-done.got_ref, bf16[512,512]{1,0:T(8,128)(2,1)S(1)} %spread.1.mix_ref), custom_call_target="tpu_custom_call" | custom-call | tf_op jit(solution)/shard_map/relax/pallas_call | solution.py:341
  54.0 0.0 collective-permute-done.6.refs_7_
  54.0 0.0 collective-permute-done.5.refs_6_
  54.0 0.0 copy-start.1
  54.0 0.0 collective-permute-done.4.refs_5_
  54.0 0.0 copy-start.3
  54.0 0.0 collective-permute-done.3.refs_4_
  54.0 0.0 copy-start.5
  54.0 3.9 %collective-permute-done.2.refs_3_ = bf16[64,1024]{1,0:T(8,128)(2,1)S(1)} collective-permute-done((bf16[64,1024]{1,0:T(8,128)(2,1)S(1)}, bf16[64,1024]{1,0:T(8,128)(2,1)S(1)}, u32[]{:S(2)}, u32[]{:S(2)}) %collective-permute-start.2) | collective-permute-done | bytes 131104 | tf_op jit(solution)/shard_map/ppermute | solution.py:486
  58.0 9.1 %all-to-all-start.1 = ((bf16[8,384,128]{2,1,0:T(8,128)(2,1)}), bf16[8,384,128]{2,1,0:T(8,128)(2,1)S(1)}, u32[]{:S(2)}, u32[]{:S(2)}) async-start(bf16[8,384,128]{2,1,0:T(8,128)(2,1)} %relax.1), calls=%async_computation.1 | async-start | bytes 1572864 | tf_op jit(solution)/shard_map/all_to_all | solution.py:496
  67.0 0.0 copy-done
  67.1 0.0 copy-done.1
  67.1 0.0 copy-done.3
  67.1 0.0 copy-done.5
  67.1 5.7 %collective-permute-start.7 = (bf16[128,1024]{1,0:T(8,128)(2,1)S(1)}, bf16[128,1024]{1,0:T(8,128)(2,1)S(1)}, u32[]{:S(2)}, u32[]{:S(2)}) collective-permute-start(bf16[128,1024]{1,0:T(8,128)(2,1)S(1)} %get-tuple-element.23), channel_id=1, source_target_pairs={{0,56},{8,0},{16,8},{24,16},{32,24},{40,32},{48,40},{56,48},{1,57}... | collective-permute-start | bytes 786440 | tf_op jit(solution)/shard_map/ppermute | solution.py:489
  72.8 1.9 %collective-permute-start.8 = (bf16[128,1024]{1,0:T(8,128)(2,1)S(1)}, bf16[128,1024]{1,0:T(8,128)(2,1)S(1)}, u32[]{:S(2)}, u32[]{:S(2)}) collective-permute-start(bf16[128,1024]{1,0:T(8,128)(2,1)S(1)} %get-tuple-element.24), channel_id=1, source_target_pairs={{0,8},{8,16},{16,24},{24,32},{32,40},{40,48},{48,56},{56,0},{1,9},... | collective-permute-start | bytes 786440 | tf_op jit(solution)/shard_map/ppermute | solution.py:490
  74.8 2.1 %collective-permute-done.7.refs_1_.above_hbm = bf16[128,1024]{1,0:T(8,128)(2,1)S(1)} collective-permute-done((bf16[128,1024]{1,0:T(8,128)(2,1)S(1)}, bf16[128,1024]{1,0:T(8,128)(2,1)S(1)}, u32[]{:S(2)}, u32[]{:S(2)}) %collective-permute-start.7) | collective-permute-done | bytes 262176 | tf_op jit(solution)/shard_map/ppermute | solution.py:489
  76.9 5.0 %collective-permute-done.8.refs_2_.below_hbm = bf16[128,1024]{1,0:T(8,128)(2,1)S(1)} collective-permute-done((bf16[128,1024]{1,0:T(8,128)(2,1)S(1)}, bf16[128,1024]{1,0:T(8,128)(2,1)S(1)}, u32[]{:S(2)}, u32[]{:S(2)}) %collective-permute-start.8) | collective-permute-done | bytes 262176 | tf_op jit(solution)/shard_map/ppermute | solution.py:490
  81.9 0.9 copy-done.2
  82.8 0.9 copy-done.4
  83.8 0.9 copy-done.6
  84.7 0.9 copy-done.8
  85.6 1.5 %join.1.own_ref = bf16[528,1024]{1,0:T(8,128)(2,1)S(1)} custom-call(bf16[64,1024]{1,0:T(8,128)(2,1)S(1)} %pad_maximum_fusion.held_ref.refs_0_, bf16[128,1024]{1,0:T(8,128)(2,1)S(1)} %collective-permute-done.7.refs_1_.above_hbm, bf16[128,1024]{1,0:T(8,128)(2,1)S(1)} %collective-permute-done.8.refs_2_.below_hbm, bf16[64,1024]{1,0:T(8,128)(2,1)S(1)} %copy-done.8, ...), custom_call_target="tpu_custom_call" | custom-call | tf_op jit(solution)/shard_map/join/pallas_call | solution.py:230
  87.0 4.6 %collective-permute-start.9 = (bf16[528,1024]{1,0:T(8,128)(2,1)S(1)}, bf16[528,1024]{1,0:T(8,128)(2,1)}, u32[]{:S(2)}, u32[]{:S(2)}) collective-permute-start(bf16[528,1024]{1,0:T(8,128)(2,1)S(1)} %join.1.own_ref), channel_id=1, source_target_pairs={{0,1},{1,0},{2,3},{3,2},{4,5},{5,4},{6,7},{7,6},{8,9},{9,8},{10,11... | collective-permute-start | bytes 3244040 | tf_op jit(solution)/shard_map/ppermute | solution.py:494
  91.7 0.1 pad_add_fusion.where_ref
  91.7 2.4 %collective-permute-done.9.other_ref = bf16[528,1024]{1,0:T(8,128)(2,1)} collective-permute-done((bf16[528,1024]{1,0:T(8,128)(2,1)S(1)}, bf16[528,1024]{1,0:T(8,128)(2,1)}, u32[]{:S(2)}, u32[]{:S(2)}) %collective-permute-start.9) | collective-permute-done | bytes 1081376 | tf_op jit(solution)/shard_map/ppermute | solution.py:494
  94.1 3.4 %assemble.1 = (bf16[1024,1024]{1,0:T(8,128)(2,1)}, bf16[16,1024]{1,0:T(8,128)(2,1)S(1)}) custom-call(s32[2]{0:T(128)S(1)} %pad_add_fusion.where_ref, bf16[528,1024]{1,0:T(8,128)(2,1)S(1)} %join.1.own_ref, bf16[528,1024]{1,0:T(8,128)(2,1)} %collective-permute-done.9.other_ref), custom_call_target="tpu_custom_call" | custom-call | tf_op jit(solution)/shard_map/assemble/pallas_call | solution.py:262
  97.5 0.0 all-to-all-done.1.back_hbm
  97.6 4.0 %advance.1 = bf16[3,32,4096]{2,1,0:T(8,128)(2,1)} custom-call(s32[1]{0:T(128)} %bitcast.core_ref, bf16[3,32,4096]{2,1,0:T(8,128)(2,1)S(1)} %copy-done, bf16[8,384,128]{2,1,0:T(8,128)(2,1)S(1)} %all-to-all-done.1.back_hbm, bf16[1024,1024]{1,0:T(8,128)(2,1)} %get-tuple-element.31.weights_hbm, bf16[128,1024]{1,0:T(8,128)(2,1)S(1)} %collective-permute-done.8.refs_2_.below_hbm, ...), custom_call_target="tpu_custom_call" | custom-call | tf_op jit(solution)/shard_map/advance/pallas_call | solution.py:446
  (10 shorter events, 0.1 us)
Async XLA Ops:
  1.1 16.8 %copy-start.10 = (bf16[16,1024]{1,0:T(8,128)(2,1)S(1)}, bf16[16,1024]{1,0:T(8,128)(2,1)}, u32[]{:S(2)}) copy-start(bf16[16,1024]{1,0:T(8,128)(2,1)} %shard_hbm.1) | copy-start | bytes 98308
  1.2 6.5 %collective-permute-start = (bf16[32,1024]{1,0:T(8,128)(2,1)S(1)}, bf16[32,1024]{1,0:T(8,128)(2,1)S(1)}, u32[]{:S(2)}, u32[]{:S(2)}) collective-permute-start(bf16[32,1024]{1,0:T(8,128)(2,1)S(1)} %get-tuple-element.19), channel_id=1, source_target_pairs={{0,7},{1,2},{2,1},{3,4},{4,3},{5,6},{6,5},{7,0},{8,15},{9,10},{10,... | collective-permute-start | bytes 196616 | tf_op jit(solution)/shard_map/ppermute | solution.py:481
  8.4 9.5 %collective-permute-start.1 = (bf16[32,1024]{1,0:T(8,128)(2,1)S(1)}, bf16[32,1024]{1,0:T(8,128)(2,1)S(1)}, u32[]{:S(2)}, u32[]{:S(2)}) collective-permute-start(bf16[32,1024]{1,0:T(8,128)(2,1)S(1)} %pad_maximum_fusion.1), channel_id=1, source_target_pairs={{0,4},{1,5},{2,6},{3,7},{4,0},{5,1},{6,2},{7,3},{8,12},{9,13},{10,... | collective-permute-start | bytes 196616 | tf_op jit(solution)/shard_map/ppermute | solution.py:483
  18.0 33.2 %copy-start.9 = (bf16[32,32]{1,0:T(8,128)(2,1)S(1)}, bf16[32,32]{1,0:T(8,128)(2,1)}, u32[]{:S(2)}) copy-start(bf16[32,32]{1,0:T(8,128)(2,1)} %depth_ref.1) | copy-start | bytes 6148
  18.0 33.7 %all-to-all-start = ((bf16[8,400,128]{2,1,0:T(8,128)(2,1)}), bf16[8,400,128]{2,1,0:T(8,128)(2,1)S(1)}, u32[]{:S(2)}, u32[]{:S(2)}) async-start(bf16[8,400,128]{2,1,0:T(8,128)(2,1)} %pack.1), calls=%async_computation | async-start | bytes 1638400 | tf_op jit(solution)/shard_map/all_to_all | solution.py:485
  28.0 25.9 %collective-permute-start.6 = (bf16[64,1024]{1,0:T(8,128)(2,1)S(1)}, bf16[64,1024]{1,0:T(8,128)(2,1)S(1)}, u32[]{:S(2)}, u32[]{:S(2)}) collective-permute-start(bf16[64,1024]{1,0:T(8,128)(2,1)S(1)} %pad_maximum_fusion.held_ref.refs_0_), channel_id=1, source_target_pairs={{0,32},{8,40},{16,48},{24,56},{32,0},{40,8},{48,16},{56,24},{1,33}... | collective-permute-start | bytes 393224 | tf_op jit(solution)/shard_map/ppermute | solution.py:486
  35.5 18.5 %collective-permute-start.5 = (bf16[64,1024]{1,0:T(8,128)(2,1)S(1)}, bf16[64,1024]{1,0:T(8,128)(2,1)S(1)}, u32[]{:S(2)}, u32[]{:S(2)}) collective-permute-start(bf16[64,1024]{1,0:T(8,128)(2,1)S(1)} %pad_maximum_fusion.held_ref.refs_0_), channel_id=1, source_target_pairs={{0,24},{8,32},{16,40},{24,48},{32,56},{40,0},{48,8},{56,16},{1,25}... | collective-permute-start | bytes 393224 | tf_op jit(solution)/shard_map/ppermute | solution.py:486
  38.0 16.0 %collective-permute-start.4 = (bf16[64,1024]{1,0:T(8,128)(2,1)S(1)}, bf16[64,1024]{1,0:T(8,128)(2,1)S(1)}, u32[]{:S(2)}, u32[]{:S(2)}) collective-permute-start(bf16[64,1024]{1,0:T(8,128)(2,1)S(1)} %pad_maximum_fusion.held_ref.refs_0_), channel_id=1, source_target_pairs={{0,40},{8,48},{16,56},{24,0},{32,8},{40,16},{48,24},{56,32},{1,41}... | collective-permute-start | bytes 393224 | tf_op jit(solution)/shard_map/ppermute | solution.py:486
  43.8 10.2 %collective-permute-start.3 = (bf16[64,1024]{1,0:T(8,128)(2,1)S(1)}, bf16[64,1024]{1,0:T(8,128)(2,1)S(1)}, u32[]{:S(2)}, u32[]{:S(2)}) collective-permute-start(bf16[64,1024]{1,0:T(8,128)(2,1)S(1)} %pad_maximum_fusion.held_ref.refs_0_), channel_id=1, source_target_pairs={{0,16},{8,24},{16,32},{24,40},{32,48},{40,56},{48,0},{56,8},{1,17}... | collective-permute-start | bytes 393224 | tf_op jit(solution)/shard_map/ppermute | solution.py:486
  46.2 11.7 %collective-permute-start.2 = (bf16[64,1024]{1,0:T(8,128)(2,1)S(1)}, bf16[64,1024]{1,0:T(8,128)(2,1)S(1)}, u32[]{:S(2)}, u32[]{:S(2)}) collective-permute-start(bf16[64,1024]{1,0:T(8,128)(2,1)S(1)} %pad_maximum_fusion.held_ref.refs_0_), channel_id=1, source_target_pairs={{0,48},{8,56},{16,0},{24,8},{32,16},{40,24},{48,32},{56,40},{1,49}... | collective-permute-start | bytes 393224 | tf_op jit(solution)/shard_map/ppermute | solution.py:486
  54.0 13.1 %copy-start = (bf16[3,32,4096]{2,1,0:T(8,128)(2,1)S(1)}, bf16[3,32,4096]{2,1,0:T(8,128)(2,1)}, u32[]{:S(2)}) copy-start(bf16[3,32,4096]{2,1,0:T(8,128)(2,1)} %f_hbm.3) | copy-start | bytes 2359300
  54.0 13.1 %copy-start.1 = (bf16[64,1024]{1,0:T(8,128)(2,1)}, bf16[64,1024]{1,0:T(8,128)(2,1)S(1)}, u32[]{:S(2)}) copy-start(bf16[64,1024]{1,0:T(8,128)(2,1)S(1)} %collective-permute-done.5.refs_6_) | copy-start | bytes 393220
  54.0 13.1 %copy-start.3 = (bf16[64,1024]{1,0:T(8,128)(2,1)}, bf16[64,1024]{1,0:T(8,128)(2,1)S(1)}, u32[]{:S(2)}) copy-start(bf16[64,1024]{1,0:T(8,128)(2,1)S(1)} %collective-permute-done.4.refs_5_) | copy-start | bytes 393220
  54.0 13.1 %copy-start.5 = (bf16[64,1024]{1,0:T(8,128)(2,1)}, bf16[64,1024]{1,0:T(8,128)(2,1)S(1)}, u32[]{:S(2)}) copy-start(bf16[64,1024]{1,0:T(8,128)(2,1)S(1)} %collective-permute-done.3.refs_4_) | copy-start | bytes 393220
  58.0 9.1 %copy-start.7 = (bf16[64,1024]{1,0:T(8,128)(2,1)}, bf16[64,1024]{1,0:T(8,128)(2,1)S(1)}, u32[]{:S(2)}) copy-start(bf16[64,1024]{1,0:T(8,128)(2,1)S(1)} %collective-permute-done.2.refs_3_) | copy-start | bytes 393220
  58.0 39.6 %all-to-all-start.1 = ((bf16[8,384,128]{2,1,0:T(8,128)(2,1)}), bf16[8,384,128]{2,1,0:T(8,128)(2,1)S(1)}, u32[]{:S(2)}, u32[]{:S(2)}) async-start(bf16[8,384,128]{2,1,0:T(8,128)(2,1)} %relax.1), calls=%async_computation.1 | async-start | bytes 1572864 | tf_op jit(solution)/shard_map/all_to_all | solution.py:496
  67.1 9.8 %collective-permute-start.7 = (bf16[128,1024]{1,0:T(8,128)(2,1)S(1)}, bf16[128,1024]{1,0:T(8,128)(2,1)S(1)}, u32[]{:S(2)}, u32[]{:S(2)}) collective-permute-start(bf16[128,1024]{1,0:T(8,128)(2,1)S(1)} %get-tuple-element.23), channel_id=1, source_target_pairs={{0,56},{8,0},{16,8},{24,16},{32,24},{40,32},{48,40},{56,48},{1,57}... | collective-permute-start | bytes 786440 | tf_op jit(solution)/shard_map/ppermute | solution.py:489
  72.8 9.1 %collective-permute-start.8 = (bf16[128,1024]{1,0:T(8,128)(2,1)S(1)}, bf16[128,1024]{1,0:T(8,128)(2,1)S(1)}, u32[]{:S(2)}, u32[]{:S(2)}) collective-permute-start(bf16[128,1024]{1,0:T(8,128)(2,1)S(1)} %get-tuple-element.24), channel_id=1, source_target_pairs={{0,8},{8,16},{16,24},{24,32},{32,40},{40,48},{48,56},{56,0},{1,9},... | collective-permute-start | bytes 786440 | tf_op jit(solution)/shard_map/ppermute | solution.py:490
  81.9 0.9 copy-start.2
  82.8 0.9 copy-start.4
  83.7 0.9 copy-start.6
  84.7 0.9 copy-start.8
  87.0 7.1 %collective-permute-start.9 = (bf16[528,1024]{1,0:T(8,128)(2,1)S(1)}, bf16[528,1024]{1,0:T(8,128)(2,1)}, u32[]{:S(2)}, u32[]{:S(2)}) collective-permute-start(bf16[528,1024]{1,0:T(8,128)(2,1)S(1)} %join.1.own_ref), channel_id=1, source_target_pairs={{0,1},{1,0},{2,3},{3,2},{4,5},{5,4},{6,7},{7,6},{8,9},{9,8},{10,11... | collective-permute-start | bytes 3244040 | tf_op jit(solution)/shard_map/ppermute | solution.py:494

commit v8 on v5

--- a/solution.py
+++ b/solution.py
@@ -137,13 +137,21 @@
     )(place, f, basis)
 
 
-def edges_kernel(core_ref, f_ref, low_ref, high_ref, inner_ref, outer_ref):
+def edges_kernel(
+    core_ref, f_ref, low_hbm, high_hbm, inner_ref, outer_ref, low_ref, high_ref, sem
+):
     half = NXY // 2
     for p in range(PLANES):
         rows = slice(p // 2 * COLS, (p // 2 + 1) * COLS)
         lanes = slice(p % 2 * half, (p % 2 + 1) * half)
         high_ref[rows, lanes] = f_ref[ROWS - 1, :, p * NXY + half : (p + 1) * NXY]
         low_ref[rows, lanes] = f_ref[0, :, p * NXY : p * NXY + half]
+    copies = [
+        pltpu.make_async_copy(low_ref, low_hbm, sem.at[0]),
+        pltpu.make_async_copy(high_ref, high_hbm, sem.at[1]),
+    ]
+    for copy in copies:
+        copy.start()
     edge_row = lax.broadcasted_iota(jnp.int32, (16, NXY), 0)
     first = jnp.zeros((16, NXY), F32)
     last = jnp.zeros((16, NXY), F32)
@@ -157,19 +165,80 @@
     core = core_ref[0]
     inner_ref[...] = jnp.where(core == 0, last, first).astype(BF16)
     outer_ref[...] = jnp.where(core == 0, first, last).astype(BF16)
+    for copy in copies:
+        copy.wait()
 
 
 def edges(core, f):
-    row = jax.ShapeDtypeStruct((2 * COLS, NXY), BF16)
+    row = pltpu.HBM((2 * COLS, NXY), BF16)
     column = jax.ShapeDtypeStruct((16, NXY), BF16)
     return pl.pallas_call(
         edges_kernel,
         out_shape=(row, row, column, column),
         in_specs=[smem(), vmem()],
-        out_specs=(vmem(),) * 4,
+        out_specs=(hbm(), hbm(), vmem(), vmem()),
+        scratch_shapes=[
+            pltpu.VMEM((2 * COLS, NXY), BF16),
+            pltpu.VMEM((2 * COLS, NXY), BF16),
+            pltpu.SemaphoreType.DMA((2,)),
+        ],
         compiler_params=pltpu.CompilerParams(vmem_limit_bytes=LIMIT),
         name="edges",
     )(core, f)
+
+
+def spray_kernel(place_ref, shard_ref, out_ref):
+    start = place_ref[0] // 2 * 2 * BLOCK
+    for core in range(2):
+        offset = pl.multiple_of(start + core * BLOCK, BLOCK)
+        part = shard_ref[:, pl.ds(offset, BLOCK)]
+        for d in range(core, out_ref.shape[0], 2):
+            out_ref[d] = part
+
+
+def spray(place, shard, count):
+    return pl.pallas_call(
+        spray_kernel,
+        out_shape=jax.ShapeDtypeStruct((count, shard.shape[0], BLOCK), BF16),
+        in_specs=[smem(), vmem()],
+        out_specs=vmem(),
+        compiler_params=pltpu.CompilerParams(vmem_limit_bytes=LIMIT),
+        name="spray",
+    )(place, shard)
+
+
+def join_kernel(*refs):
+    *parts, inner_ref, out_ref, sem = refs
+    size = parts[0].shape[0]
+    copies = [
+        pltpu.make_async_copy(ref, out_ref.at[pl.ds(m * size, size)], sem.at[m])
+        for m, ref in enumerate(parts)
+    ]
+    for lane in range(NXY // BLOCK):
+        rows = pl.ds(len(parts) * size + lane * 16, 16)
+        copies.append(
+            pltpu.make_async_copy(
+                inner_ref.at[:, pl.ds(lane * BLOCK, BLOCK)], out_ref.at[rows], sem.at[len(parts) + lane]
+            )
+        )
+    for copy in copies:
+        copy.start()
+    for copy in copies:
+        copy.wait()
+
+
+def join(parts, inner):
+    size = parts[0].shape[0]
+    lanes = NXY // BLOCK
+    return pl.pallas_call(
+        join_kernel,
+        out_shape=pltpu.HBM((len(parts) * size + lanes * 16, BLOCK), BF16),
+        in_specs=[hbm()] * (len(parts) + 1),
+        out_specs=hbm(),
+        scratch_shapes=[pltpu.SemaphoreType.DMA((len(parts) + lanes,))],
+        compiler_params=pltpu.CompilerParams(vmem_limit_bytes=LIMIT),
+        name="join",
+    )(*parts, inner)
 
 
 def spread_kernel(depth_ref, out_ref):
@@ -251,10 +320,10 @@
     core_ref,
     f_hbm,
     back_hbm,
-    weights_hbm,
+    own_hbm,
+    other_hbm,
     below_hbm,
     above_hbm,
-    inner_hbm,
     outer_hbm,
     out_hbm,
     f_ref,
@@ -272,14 +341,31 @@
     first = [
         pltpu.make_async_copy(below_hbm, lower_ref, sem.at[0]),
         pltpu.make_async_copy(above_hbm, upper_ref, sem.at[1]),
-        pltpu.make_async_copy(inner_hbm, inner_ref, sem.at[2]),
         pltpu.make_async_copy(outer_hbm, outer_ref, sem.at[3]),
         pltpu.make_async_copy(f_hbm, f_ref, sem.at[4]),
     ]
-    second = [
-        pltpu.make_async_copy(back_hbm, back_ref, sem.at[5]),
-        pltpu.make_async_copy(weights_hbm, weights_ref, sem.at[6]),
-    ]
+    second = [pltpu.make_async_copy(back_hbm, back_ref, sem.at[5])]
+    core, place = core_ref[0], core_ref[1]
+    for m in range(4):
+        column = jnp.bitwise_xor(place // 2, m) * 2
+        block = pl.ds(m * NXY, NXY)
+        second.append(
+            pltpu.make_async_copy(own_hbm.at[block], weights_ref.at[column + core], sem.at[6 + m])
+        )
+        second.append(
+            pltpu.make_async_copy(
+                other_hbm.at[block], weights_ref.at[column + 1 - core], sem.at[10 + m]
+            )
+        )
+    lanes_of = NXY // BLOCK
+    for lane in range(lanes_of):
+        first.append(
+            pltpu.make_async_copy(
+                other_hbm.at[pl.ds(4 * NXY + lane * 16, 16)],
+                inner_ref.at[:, pl.ds(lane * BLOCK, BLOCK)],
+                sem.at[14 + lane],
+            )
+        )
     for copy in first + second:
         copy.start()
     half = NXY // 2
@@ -290,7 +376,6 @@
     cy = courant_along * jnp.abs(vy)
     upwind = vy > 0.0
     col = lax.broadcasted_iota(jnp.int32, (COLS, NXY), 0)
-    core = core_ref[0]
     for copy in first:
         copy.wait()
     inner = inner_ref[...].astype(F32)
@@ -320,8 +405,9 @@
     for copy in second:
         copy.wait()
     mixed = jnp.concatenate([back_ref[v] for v in range(GROUP)], axis=1)
+    weights = jnp.concatenate([weights_ref[v] for v in range(GROUP)], axis=1)
     collision = lax.dot_general(
-        mixed, weights_ref[...], (((1,), (1,)), ((), ())), preferred_element_type=F32
+        mixed, weights, (((1,), (1,)), ((), ())), preferred_element_type=F32
     )
     stores = []
     for p in range(PLANES):
@@ -340,8 +426,8 @@
         copy.wait()
 
 
-def advance(core, f, back, weights, below, above, inner, outer):
-    weights = pltpu.with_memory_space_constraint(weights, pltpu.HBM)
+def advance(where, f, back, own, other, below, above, outer):
+    own, other = (pltpu.with_memory_space_constraint(x, pltpu.HBM) for x in (own, other))
     return pl.pallas_call(
         advance_kernel,
         out_shape=jax.ShapeDtypeStruct(f.shape, BF16),
@@ -350,19 +436,19 @@
         scratch_shapes=[
             pltpu.VMEM(f.shape, BF16),
             pltpu.VMEM(back.shape, BF16),
-            pltpu.VMEM(weights.shape, BF16),
+            pltpu.VMEM((GROUP, NXY, BLOCK), BF16),
             pltpu.VMEM((2 * COLS, NXY), BF16),
             pltpu.VMEM((2 * COLS, NXY), BF16),
-            pltpu.VMEM(inner.shape, BF16),
-            pltpu.VMEM(outer.shape, BF16),
+            pltpu.VMEM((16, NXY), BF16),
+            pltpu.VMEM((16, NXY), BF16),
             pltpu.VMEM((DATA, NXY), F32),
             pltpu.VMEM(f.shape, BF16),
-            pltpu.SemaphoreType.DMA((7,)),
+            pltpu.SemaphoreType.DMA((14 + NXY // BLOCK,)),
             pltpu.SemaphoreType.DMA((PLANES,)),
         ],
         compiler_params=pltpu.CompilerParams(vmem_limit_bytes=LIMIT),
         name="advance",
-    )(core, f, back, weights, below, above, inner, outer)
+    )(where, f, back, own, other, below, above, outer)
 
 
 def ring(axis, step):
@@ -373,23 +459,28 @@
 def local(distribution, plane_weights, depth_weights):
     place = lax.axis_index("vel").astype(jnp.int32).reshape(1)
     core = jnp.bitwise_and(lax.axis_index("sy").astype(jnp.int32), 1).reshape(1)
+    where = jnp.concatenate([core, place])
     shard, width = plane_weights.shape
     count = lax.axis_size("sy")
-    rows = jnp.broadcast_to(plane_weights[None], (count, shard, width))
-    rows = lax.all_to_all(rows, "sy", 0, 0, tiled=True).reshape(count * shard, width)
-    send, rows = lax.optimization_barrier((pack(place, distribution), rows))
-    weights = lax.all_gather(rows, "sx", axis=0, tiled=True)
+    flip = lambda bit: [(i, i ^ bit) for i in range(8)]
+    columns = lax.all_to_all(
+        spray(place, plane_weights, width // shard), ("sx", "sy"), 0, 0, tiled=True
+    ).reshape(width, BLOCK)
+    send, columns = lax.optimization_barrier((pack(place, distribution), columns))
     got = lax.all_to_all(send, "vel", 0, 0, tiled=True)
+    far = [lax.ppermute(columns, "vel", flip(2 * step)) for step in (1, 2, 3)]
     low, high, inner, outer = edges(core, distribution)
-    mix = spread(depth_weights)
-    above = lax.ppermute(low, "sx", ring("sx", -1))
-    below = lax.ppermute(high, "sx", ring("sx", 1))
-    inner = lax.ppermute(inner, "sy", [(i, i ^ 1) for i in range(count)])
     outer = lax.ppermute(
         outer, "sy", [(i, (i + 1) % count if i % 2 else (i - 1) % count) for i in range(count)]
     )
-    back = lax.all_to_all(relax(place, got, mix), "vel", 0, 0, tiled=True)
-    return advance(core, distribution, back, weights, below, above, inner, outer)
+    send = relax(place, got, spread(depth_weights))
+    send, outer, *far = lax.optimization_barrier((send, outer, *far))
+    own = join([columns] + far, inner)
+    other = lax.ppermute(own, "sy", flip(1))
+    above = lax.ppermute(low, "sx", ring("sx", -1))
+    below = lax.ppermute(high, "sx", ring("sx", 1))
+    back = lax.all_to_all(send, "vel", 0, 0, tiled=True)
+    return advance(where, distribution, back, own, other, below, above, outer)
 
 
 def solution(mesh):

time: 98.2 us -> 98.5 us (level)
  the two profiles are of different devices: /device:TPU:2 before, /device:TPU:73 now
where the time goes in v8:
time: 98.5 us; the launch traced here: 97.8 us
  starting transfers between devices  48.4 us (49%)
  waiting for transfers between devices  35.6 us (36%)
  Pallas kernels  12.8 us (13%)
    all_to_all x1, starting transfers between devices, local(): lax.all_to_all(spray(place, plane_weights, width // shard), ('sx', 'sy'),...  12.9 us
    all_to_all x1, waiting for transfers between devices, local(): back = lax.all_to_all(send, 'vel', 0, 0, tiled=True)  11.5 us
    all_to_all x1, waiting for transfers between devices, local(): got = lax.all_to_all(send, 'vel', 0, 0, tiled=True)  11.5 us
    all_to_all x1, starting transfers between devices, local(): got = lax.all_to_all(send, 'vel', 0, 0, tiled=True)  9.9 us
    all_to_all x1, waiting for transfers between devices, local(): lax.all_to_all(spray(place, plane_weights, width // shard), ('sx', 'sy'),...  9.07 us
    ppermute x3, starting transfers between devices, local(): far = [lax.ppermute(columns, 'vel', flip(2 * step)) for step in (1, 2, 3)]  8.98 us
    pallas_call x1, Pallas kernels, advance(): pl.pallas_call(advance_kernel, out_shape=jax.ShapeDtypeStruct(f.shape, BF...  4.74 us
    ppermute x1, starting transfers between devices, local(): lax.ppermute(outer, 'sy', [(i, (i + 1) % count if i % 2 else (i - 1) % co...  4.3 us
  transfers between devices with their start and end apart: 10, of which 5 were waited for; matrix products, arithmetic and copies ran while one was open for 0% of the time, Pallas kernels for 8%

profile of v8, /device:TPU:73, one launch (start us, length us, event | category | flops | bytes accessed | tf_op | source)
XLA Modules:
  0.0 97.8 jit_solution(7598461990217154315)
XLA Ops:
  0.0 0.0 copy-start.1
  0.0 0.8 copy-done.1
  0.8 0.7 spray.1
  1.5 12.9 %all-to-all-start = ((bf16[64,16,128]{2,1,0:T(8,128)(2,1)}), bf16[64,16,128]{2,1,0:T(8,128)(2,1)S(1)}, u32[]{:S(2)}, u32[]{:S(2)}) async-start(bf16[64,16,128]{2,1,0:T(8,128)(2,1)} %spray.1), calls=%async_computation | async-start | bytes 524288 | tf_op jit(solution)/shard_map/all_to_all | solution.py:466
  14.4 2.8 %pack.1 = bf16[8,400,128]{2,1,0:T(8,128)(2,1)} custom-call(s32[1]{0:T(128)} %bitcast.1.place_ref, bf16[3,32,4096]{2,1,0:T(8,128)(2,1)} %f_hbm.1, bf16[1024,128]{1,0:T(8,128)(2,1)} %constant.12.clone.basis_ref), custom_call_target="tpu_custom_call" | custom-call | tf_op jit(solution)/shard_map/pack/pallas_call | solution.py:122
  17.3 0.0 copy-start
  17.3 9.1 %all-to-all-done = bf16[64,16,128]{2,1,0:T(8,128)(2,1)S(1)} async-done(((bf16[64,16,128]{2,1,0:T(8,128)(2,1)}), bf16[64,16,128]{2,1,0:T(8,128)(2,1)S(1)}, u32[]{:S(2)}, u32[]{:S(2)}) %all-to-all-start) | async-done | bytes 262176 | tf_op jit(solution)/shard_map/all_to_all | solution.py:466
  26.4 0.0 copy-start.2
  26.4 9.9 %all-to-all-start.1 = ((bf16[8,400,128]{2,1,0:T(8,128)(2,1)}), bf16[8,400,128]{2,1,0:T(8,128)(2,1)S(1)}, u32[]{:S(2)}, u32[]{:S(2)}) async-start(bf16[8,400,128]{2,1,0:T(8,128)(2,1)} %pack.1), calls=%async_computation.1 | async-start | bytes 1638400 | tf_op jit(solution)/shard_map/all_to_all | solution.py:470
  36.3 4.6 %collective-permute-start.3 = (bf16[1024,128]{1,0:T(8,128)(2,1)S(1)}, bf16[1024,128]{1,0:T(8,128)(2,1)S(1)}, u32[]{:S(2)}, u32[]{:S(2)}) collective-permute-start(bf16[1024,128]{1,0:T(8,128)(2,1)S(1)} %bitcast.3), channel_id=1, source_target_pairs={{0,384},{64,448},{128,256},{192,320},{256,128},{320,192},{384,0},{... | collective-permute-start | bytes 786440 | tf_op jit(solution)/shard_map/ppermute | solution.py:471
  40.8 2.5 %collective-permute-start.2 = (bf16[1024,128]{1,0:T(8,128)(2,1)S(1)}, bf16[1024,128]{1,0:T(8,128)(2,1)S(1)}, u32[]{:S(2)}, u32[]{:S(2)}) collective-permute-start(bf16[1024,128]{1,0:T(8,128)(2,1)S(1)} %bitcast.4), channel_id=1, source_target_pairs={{0,256},{64,320},{128,384},{192,448},{256,0},{320,64},{384,128},{4... | collective-permute-start | bytes 786440 | tf_op jit(solution)/shard_map/ppermute | solution.py:471
  43.3 1.9 %collective-permute-start.1 = (bf16[1024,128]{1,0:T(8,128)(2,1)S(1)}, bf16[1024,128]{1,0:T(8,128)(2,1)S(1)}, u32[]{:S(2)}, u32[]{:S(2)}) collective-permute-start(bf16[1024,128]{1,0:T(8,128)(2,1)S(1)} %bitcast.5), channel_id=1, source_target_pairs={{0,128},{64,192},{128,0},{192,64},{256,384},{320,448},{384,256},{4... | collective-permute-start | bytes 786440 | tf_op jit(solution)/shard_map/ppermute | solution.py:471
  45.3 0.0 copy-done
  45.3 0.7 edges.1
  46.0 4.3 %collective-permute-start = (bf16[16,1024]{1,0:T(8,128)(2,1)S(1)}, bf16[16,1024]{1,0:T(8,128)(2,1)S(1)}, u32[]{:S(2)}, u32[]{:S(2)}) collective-permute-start(bf16[16,1024]{1,0:T(8,128)(2,1)S(1)} %get-tuple-element.17), channel_id=1, source_target_pairs={{0,7},{1,2},{2,1},{3,4},{4,3},{5,6},{6,5},{7,0},{8,15},{9,10},{10,... | collective-permute-start | bytes 98312 | tf_op jit(solution)/shard_map/ppermute | solution.py:473
  50.3 0.0 copy-done.2
  50.3 0.4 spread.1.mix_ref
  50.7 11.5 %all-to-all-done.1.got_ref = bf16[8,400,128]{2,1,0:T(8,128)(2,1)S(1)} async-done(((bf16[8,400,128]{2,1,0:T(8,128)(2,1)}), bf16[8,400,128]{2,1,0:T(8,128)(2,1)S(1)}, u32[]{:S(2)}, u32[]{:S(2)}) %all-to-all-start.1) | async-done | bytes 819232 | tf_op jit(solution)/shard_map/all_to_all | solution.py:470
  62.3 2.3 %relax.1 = bf16[8,384,128]{2,1,0:T(8,128)(2,1)} custom-call(s32[1]{0:T(128)} %bitcast.1.place_ref, bf16[8,400,128]{2,1,0:T(8,128)(2,1)S(1)} %all-to-all-done.1.got_ref, bf16[512,512]{1,0:T(8,128)(2,1)S(1)} %spread.1.mix_ref), custom_call_target="tpu_custom_call" | custom-call | tf_op jit(solution)/shard_map/relax/pallas_call | solution.py:308
  64.6 0.0 collective-permute-done.outer_hbm
  64.6 0.0 collective-permute-done.3.refs_3_
  64.6 0.0 collective-permute-done.2.refs_2_
  64.6 0.0 collective-permute-done.1.refs_1_
  64.6 3.6 %all-to-all-start.2 = ((bf16[8,384,128]{2,1,0:T(8,128)(2,1)}), bf16[8,384,128]{2,1,0:T(8,128)(2,1)S(1)}, u32[]{:S(2)}, u32[]{:S(2)}) async-start(bf16[8,384,128]{2,1,0:T(8,128)(2,1)} %relax.1), calls=%async_computation.2 | async-start | bytes 1572864 | tf_op jit(solution)/shard_map/all_to_all | solution.py:482
  68.1 0.0 copy-start.4
  68.2 0.0 copy-start.3
  68.2 1.1 %join.1.own_hbm = bf16[4224,128]{1,0:T(8,128)(2,1)} custom-call(bf16[1024,128]{1,0:T(8,128)(2,1)S(1)} %bitcast.6, bf16[1024,128]{1,0:T(8,128)(2,1)S(1)} %collective-permute-done.1.refs_1_, bf16[1024,128]{1,0:T(8,128)(2,1)S(1)} %collective-permute-done.2.refs_2_, bf16[1024,128]{1,0:T(8,128)(2,1)S(1)} %collective-permute-done.3.refs_3_, ...), custom_call_target="tpu_custom_call" | custom-call | tf_op jit(solution)/shard_map/join/pallas_call | solution.py:233
  69.3 3.4 %collective-permute-start.4 = (bf16[4224,128]{1,0:T(8,128)(2,1)}, bf16[4224,128]{1,0:T(8,128)(2,1)}, u32[]{:S(2)}, u32[]{:S(2)}) collective-permute-start(bf16[4224,128]{1,0:T(8,128)(2,1)} %join.1.own_hbm), channel_id=1, source_target_pairs={{0,1},{1,0},{2,3},{3,2},{4,5},{5,4},{6,7},{7,6},{8,9},{9,8},{10,11... | collective-permute-start | bytes 3244040 | tf_op jit(solution)/shard_map/ppermute | solution.py:479
  72.7 0.0 copy-done.4
  72.7 2.1 %collective-permute-start.5 = (bf16[64,1024]{1,0:T(8,128)(2,1)S(1)}, bf16[64,1024]{1,0:T(8,128)(2,1)S(1)}, u32[]{:S(2)}, u32[]{:S(2)}) collective-permute-start(bf16[64,1024]{1,0:T(8,128)(2,1)S(1)} %copy-done.4), channel_id=1, source_target_pairs={{0,8},{8,16},{16,24},{24,32},{32,40},{40,48},{48,56},{56,0},{1,9},... | collective-permute-start | bytes 393224 | tf_op jit(solution)/shard_map/ppermute | solution.py:481
  74.9 0.0 copy-done.3
  74.9 3.2 %collective-permute-start.6 = (bf16[64,1024]{1,0:T(8,128)(2,1)S(1)}, bf16[64,1024]{1,0:T(8,128)(2,1)S(1)}, u32[]{:S(2)}, u32[]{:S(2)}) collective-permute-start(bf16[64,1024]{1,0:T(8,128)(2,1)S(1)} %copy-done.3), channel_id=1, source_target_pairs={{0,56},{8,0},{16,8},{24,16},{32,24},{40,32},{48,40},{56,48},{1,57}... | collective-permute-start | bytes 393224 | tf_op jit(solution)/shard_map/ppermute | solution.py:480
  78.0 0.1 pad_add_fusion.core_ref
  78.1 1.6 %collective-permute-done.5.below_hbm = bf16[64,1024]{1,0:T(8,128)(2,1)S(1)} collective-permute-done((bf16[64,1024]{1,0:T(8,128)(2,1)S(1)}, bf16[64,1024]{1,0:T(8,128)(2,1)S(1)}, u32[]{:S(2)}, u32[]{:S(2)}) %collective-permute-start.5) | collective-permute-done | bytes 131104 | tf_op jit(solution)/shard_map/ppermute | solution.py:481
  79.7 1.8 %collective-permute-done.6.above_hbm = bf16[64,1024]{1,0:T(8,128)(2,1)S(1)} collective-permute-done((bf16[64,1024]{1,0:T(8,128)(2,1)S(1)}, bf16[64,1024]{1,0:T(8,128)(2,1)S(1)}, u32[]{:S(2)}, u32[]{:S(2)}) %collective-permute-start.6) | collective-permute-done | bytes 131104 | tf_op jit(solution)/shard_map/ppermute | solution.py:480
  81.6 0.0 collective-permute-done.4.other_hbm
  81.6 11.5 %all-to-all-done.2.back_hbm = bf16[8,384,128]{2,1,0:T(8,128)(2,1)S(1)} async-done(((bf16[8,384,128]{2,1,0:T(8,128)(2,1)}), bf16[8,384,128]{2,1,0:T(8,128)(2,1)S(1)}, u32[]{:S(2)}, u32[]{:S(2)}) %all-to-all-start.2) | async-done | bytes 786464 | tf_op jit(solution)/shard_map/all_to_all | solution.py:482
  93.1 4.7 %advance.1 = bf16[3,32,4096]{2,1,0:T(8,128)(2,1)} custom-call(s32[2]{0:T(128)S(1)} %pad_add_fusion.core_ref, bf16[3,32,4096]{2,1,0:T(8,128)(2,1)S(1)} %copy-done, bf16[8,384,128]{2,1,0:T(8,128)(2,1)S(1)} %all-to-all-done.2.back_hbm, bf16[4224,128]{1,0:T(8,128)(2,1)} %join.1.own_hbm, bf16[4224,128]{1,0:T(8,128)(2,1)} %collective-permute-done.4.other_hbm, ...), custom_call_target="tpu_custom_call" | custom-call | tf_op jit(solution)/shard_map/advance/pallas_call | solution.py:431
Async XLA Ops:
  0.0 0.8 copy-start.1
  1.5 24.9 %all-to-all-start = ((bf16[64,16,128]{2,1,0:T(8,128)(2,1)}), bf16[64,16,128]{2,1,0:T(8,128)(2,1)S(1)}, u32[]{:S(2)}, u32[]{:S(2)}) async-start(bf16[64,16,128]{2,1,0:T(8,128)(2,1)} %spray.1), calls=%async_computation | async-start | bytes 524288 | tf_op jit(solution)/shard_map/all_to_all | solution.py:466
  17.3 28.0 %copy-start = (bf16[3,32,4096]{2,1,0:T(8,128)(2,1)S(1)}, bf16[3,32,4096]{2,1,0:T(8,128)(2,1)}, u32[]{:S(2)}) copy-start(bf16[3,32,4096]{2,1,0:T(8,128)(2,1)} %f_hbm.1) | copy-start | bytes 2359300
  26.4 24.0 %copy-start.2 = (bf16[32,32]{1,0:T(8,128)(2,1)S(1)}, bf16[32,32]{1,0:T(8,128)(2,1)}, u32[]{:S(2)}) copy-start(bf16[32,32]{1,0:T(8,128)(2,1)} %depth_ref.1) | copy-start | bytes 6148
  26.4 35.9 %all-to-all-start.1 = ((bf16[8,400,128]{2,1,0:T(8,128)(2,1)}), bf16[8,400,128]{2,1,0:T(8,128)(2,1)S(1)}, u32[]{:S(2)}, u32[]{:S(2)}) async-start(bf16[8,400,128]{2,1,0:T(8,128)(2,1)} %pack.1), calls=%async_computation.1 | async-start | bytes 1638400 | tf_op jit(solution)/shard_map/all_to_all | solution.py:470
  36.3 28.3 %collective-permute-start.3 = (bf16[1024,128]{1,0:T(8,128)(2,1)S(1)}, bf16[1024,128]{1,0:T(8,128)(2,1)S(1)}, u32[]{:S(2)}, u32[]{:S(2)}) collective-permute-start(bf16[1024,128]{1,0:T(8,128)(2,1)S(1)} %bitcast.3), channel_id=1, source_target_pairs={{0,384},{64,448},{128,256},{192,320},{256,128},{320,192},{384,0},{... | collective-permute-start | bytes 786440 | tf_op jit(solution)/shard_map/ppermute | solution.py:471
  40.8 23.7 %collective-permute-start.2 = (bf16[1024,128]{1,0:T(8,128)(2,1)S(1)}, bf16[1024,128]{1,0:T(8,128)(2,1)S(1)}, u32[]{:S(2)}, u32[]{:S(2)}) collective-permute-start(bf16[1024,128]{1,0:T(8,128)(2,1)S(1)} %bitcast.4), channel_id=1, source_target_pairs={{0,256},{64,320},{128,384},{192,448},{256,0},{320,64},{384,128},{4... | collective-permute-start | bytes 786440 | tf_op jit(solution)/shard_map/ppermute | solution.py:471
  43.3 21.2 %collective-permute-start.1 = (bf16[1024,128]{1,0:T(8,128)(2,1)S(1)}, bf16[1024,128]{1,0:T(8,128)(2,1)S(1)}, u32[]{:S(2)}, u32[]{:S(2)}) collective-permute-start(bf16[1024,128]{1,0:T(8,128)(2,1)S(1)} %bitcast.5), channel_id=1, source_target_pairs={{0,128},{64,192},{128,0},{192,64},{256,384},{320,448},{384,256},{4... | collective-permute-start | bytes 786440 | tf_op jit(solution)/shard_map/ppermute | solution.py:471
  46.0 18.5 %collective-permute-start = (bf16[16,1024]{1,0:T(8,128)(2,1)S(1)}, bf16[16,1024]{1,0:T(8,128)(2,1)S(1)}, u32[]{:S(2)}, u32[]{:S(2)}) collective-permute-start(bf16[16,1024]{1,0:T(8,128)(2,1)S(1)} %get-tuple-element.17), channel_id=1, source_target_pairs={{0,7},{1,2},{2,1},{3,4},{4,3},{5,6},{6,5},{7,0},{8,15},{9,10},{10,... | collective-permute-start | bytes 98312 | tf_op jit(solution)/shard_map/ppermute | solution.py:473
  64.6 28.5 %all-to-all-start.2 = ((bf16[8,384,128]{2,1,0:T(8,128)(2,1)}), bf16[8,384,128]{2,1,0:T(8,128)(2,1)S(1)}, u32[]{:S(2)}, u32[]{:S(2)}) async-start(bf16[8,384,128]{2,1,0:T(8,128)(2,1)} %relax.1), calls=%async_computation.2 | async-start | bytes 1572864 | tf_op jit(solution)/shard_map/all_to_all | solution.py:482
  68.1 4.6 %copy-start.4 = (bf16[64,1024]{1,0:T(8,128)(2,1)S(1)}, bf16[64,1024]{1,0:T(8,128)(2,1)}, u32[]{:S(2)}) copy-start(bf16[64,1024]{1,0:T(8,128)(2,1)} %get-tuple-element.24) | copy-start | bytes 393220
  68.2 6.7 %copy-start.3 = (bf16[64,1024]{1,0:T(8,128)(2,1)S(1)}, bf16[64,1024]{1,0:T(8,128)(2,1)}, u32[]{:S(2)}) copy-start(bf16[64,1024]{1,0:T(8,128)(2,1)} %get-tuple-element.25) | copy-start | bytes 393220
  69.3 12.3 %collective-permute-start.4 = (bf16[4224,128]{1,0:T(8,128)(2,1)}, bf16[4224,128]{1,0:T(8,128)(2,1)}, u32[]{:S(2)}, u32[]{:S(2)}) collective-permute-start(bf16[4224,128]{1,0:T(8,128)(2,1)} %join.1.own_hbm), channel_id=1, source_target_pairs={{0,1},{1,0},{2,3},{3,2},{4,5},{5,4},{6,7},{7,6},{8,9},{9,8},{10,11... | collective-permute-start | bytes 3244040 | tf_op jit(solution)/shard_map/ppermute | solution.py:479
  72.7 7.0 %collective-permute-start.5 = (bf16[64,1024]{1,0:T(8,128)(2,1)S(1)}, bf16[64,1024]{1,0:T(8,128)(2,1)S(1)}, u32[]{:S(2)}, u32[]{:S(2)}) collective-permute-start(bf16[64,1024]{1,0:T(8,128)(2,1)S(1)} %copy-done.4), channel_id=1, source_target_pairs={{0,8},{8,16},{16,24},{24,32},{32,40},{40,48},{48,56},{56,0},{1,9},... | collective-permute-start | bytes 393224 | tf_op jit(solution)/shard_map/ppermute | solution.py:481
  74.9 6.7 %collective-permute-start.6 = (bf16[64,1024]{1,0:T(8,128)(2,1)S(1)}, bf16[64,1024]{1,0:T(8,128)(2,1)S(1)}, u32[]{:S(2)}, u32[]{:S(2)}) collective-permute-start(bf16[64,1024]{1,0:T(8,128)(2,1)S(1)} %copy-done.3), channel_id=1, source_target_pairs={{0,56},{8,0},{16,8},{24,16},{32,24},{40,32},{48,40},{56,48},{1,57}... | collective-permute-start | bytes 393224 | tf_op jit(solution)/shard_map/ppermute | solution.py:480

commit v9 on v4

--- a/solution.py
+++ b/solution.py
@@ -137,10 +137,13 @@
     )(place, f, basis)
 
 
-def edges_kernel(core_ref, f_ref, low_ref, high_ref, inner_ref, outer_ref):
+def edges_kernel(core_ref, held_ref, f_ref, low_ref, high_ref, inner_ref, outer_ref):
     half = NXY // 2
+    size = held_ref.shape[0]
+    low_ref[0:size, :] = held_ref[...]
+    high_ref[0:size, :] = held_ref[...]
     for p in range(PLANES):
-        rows = slice(p // 2 * COLS, (p // 2 + 1) * COLS)
+        rows = slice(size + p // 2 * COLS, size + (p // 2 + 1) * COLS)
         lanes = slice(p % 2 * half, (p % 2 + 1) * half)
         high_ref[rows, lanes] = f_ref[ROWS - 1, :, p * NXY + half : (p + 1) * NXY]
         low_ref[rows, lanes] = f_ref[0, :, p * NXY : p * NXY + half]
@@ -159,17 +162,17 @@
     outer_ref[...] = jnp.where(core == 0, first, last).astype(BF16)
 
 
-def edges(core, f):
-    row = jax.ShapeDtypeStruct((2 * COLS, NXY), BF16)
+def edges(core, held, f):
+    row = jax.ShapeDtypeStruct((held.shape[0] + 2 * COLS, NXY), BF16)
     column = jax.ShapeDtypeStruct((16, NXY), BF16)
     return pl.pallas_call(
         edges_kernel,
         out_shape=(row, row, column, column),
-        in_specs=[smem(), vmem()],
+        in_specs=[smem(), vmem(), vmem()],
         out_specs=(vmem(),) * 4,
         compiler_params=pltpu.CompilerParams(vmem_limit_bytes=LIMIT),
         name="edges",
-    )(core, f)
+    )(core, held, f)
 
 
 def join_kernel(held_ref, above_ref, below_ref, across_ref, inner_ref, out_ref, sem):
@@ -206,15 +209,15 @@
     half = NXY // 2
     edge = pltpu.make_async_copy(other_ref.at[pl.ds(half, 16)], inner_hbm, sem.at[1])
     edge.start()
-    core, z, y = where_ref[0], where_ref[1], where_ref[2]
+    mine, y = where_ref[0], where_ref[1]
     far = jnp.where(y % 2 == 0, y + 6, y + 2)
-    for m, base in enumerate((y, y + 1, y + 7, far)):
-        for i in range(2):
-            for j in range(4):
-                place = ((base + 4 * i) % 8 * 4 + jnp.bitwise_xor(z, j)) * 2
-                block = slice((m * 8 + j * 2 + i) * 16, (m * 8 + j * 2 + i + 1) * 16)
-                rows_ref[place + core] = own_ref[block, :]
-                rows_ref[place + 1 - core] = other_ref[block, :]
+    for side, ref in ((mine, own_ref), (jnp.bitwise_xor(mine, 1), other_ref)):
+        places = [jnp.bitwise_xor(side, 2 * step) for step in range(4)]
+        for m, base in enumerate((y, y + 1, y + 7, far)):
+            for i in range(2):
+                for j in range(4):
+                    block = slice((m * 8 + i * 4 + j) * 16, (m * 8 + i * 4 + j + 1) * 16)
+                    rows_ref[(base + 4 * i) % 8 * 8 + places[j]] = ref[block, :]
     turned_ref[...] = jnp.transpose(rows_ref[...].reshape(NXY, NXY))
     copy = pltpu.make_async_copy(turned_ref, out_hbm, sem.at[0])
     copy.start()
@@ -340,7 +343,7 @@
         pltpu.make_async_copy(below_hbm.at[edge], lower_ref, sem.at[0]),
         pltpu.make_async_copy(above_hbm.at[edge], upper_ref, sem.at[1]),
         pltpu.make_async_copy(inner_hbm, inner_ref, sem.at[2]),
-        pltpu.make_async_copy(outer_hbm, outer_ref, sem.at[3]),
+        pltpu.make_async_copy(outer_hbm.at[pl.ds(outer_hbm.shape[0] - 16, 16)], outer_ref, sem.at[3]),
         pltpu.make_async_copy(f_hbm, f_ref, sem.at[4]),
     ]
     second = [
@@ -419,7 +422,7 @@
             pltpu.VMEM((2 * COLS, NXY), BF16),
             pltpu.VMEM((2 * COLS, NXY), BF16),
             pltpu.VMEM(inner.shape, BF16),
-            pltpu.VMEM(outer.shape, BF16),
+            pltpu.VMEM((16, NXY), BF16),
             pltpu.VMEM((DATA, NXY), F32),
             pltpu.VMEM(f.shape, BF16),
             pltpu.SemaphoreType.DMA((7,)),
@@ -439,28 +442,26 @@
     place = lax.axis_index("vel").astype(jnp.int32).reshape(1)
     along = lax.axis_index("sy").astype(jnp.int32)
     core = jnp.bitwise_and(along, 1).reshape(1)
-    where = jnp.stack([jnp.bitwise_and(along, 1), along >> 1, lax.axis_index("sx").astype(jnp.int32)])
+    where = jnp.stack([along, lax.axis_index("sx").astype(jnp.int32)])
     flip = lambda bit: [(i, i ^ bit) for i in range(8)]
-    pair = jnp.concatenate([plane_weights, lax.ppermute(plane_weights, "sx", flip(4))])
-    low, high, inner, outer = edges(core, distribution)
-    mix = spread(depth_weights)
-    spot, pair = lax.optimization_barrier((place, pair))
-    held = jnp.concatenate(
-        [pair] + [lax.ppermute(pair, "sy", flip(2 * step)) for step in (1, 2, 3)]
-    )
-    send, held = lax.optimization_barrier((pack(spot, distribution), held))
+    held = jnp.concatenate([plane_weights, lax.ppermute(plane_weights, "sy", flip(2))])
+    held = jnp.concatenate([held, lax.ppermute(held, "sy", flip(4))])
+    send, held = lax.optimization_barrier((pack(place, distribution), held))
     got = lax.all_to_all(send, "vel", 0, 0, tiled=True)
-    above = lax.ppermute(jnp.concatenate([held, low]), "sx", ring("sx", -1))
-    below = lax.ppermute(jnp.concatenate([held, high]), "sx", ring("sx", 1))
+    held = jnp.concatenate([held, lax.ppermute(held, "sx", flip(4))])
+    low, high, inner, outer = edges(core, held, distribution)
+    above = lax.ppermute(low, "sx", ring("sx", -1))
+    below = lax.ppermute(high, "sx", ring("sx", 1))
     across = lax.ppermute(held, "sx", [(i, (i + 2) % 8 if i % 2 == 0 else (i - 2) % 8) for i in range(8)])
     outer = lax.ppermute(outer, "sy", [(i, (i + 1) % 8 if i % 2 else (i - 1) % 8) for i in range(8)])
+    send = relax(place, got, spread(depth_weights))
+    across = pltpu.with_memory_space_constraint(across, pltpu.HBM)
+    send, across = lax.optimization_barrier((send, across))
     own = join(held, above, below, across, inner)
     other = lax.ppermute(own, "sy", flip(1))
     weights, inner = assemble(where, own, other)
-    back = lax.all_to_all(relax(place, got, mix), "vel", 0, 0, tiled=True)
-    return advance(
-        core, distribution, back, weights, below, above, inner, outer
-    )
+    back = lax.all_to_all(send, "vel", 0, 0, tiled=True)
+    return advance(core, distribution, back, weights, below, above, inner, outer)
 
 
 def solution(mesh):

time: 92.7 us -> 90.4 us (0.975)
  the two profiles are of different devices: /device:TPU:56 before, /device:TPU:80 now
where the time goes in v9:
time: 90.4 us; the launch traced here: 89.7 us
  starting transfers between devices  50.1 us (55%)
  waiting for transfers between devices  23 us (25%)
  Pallas kernels  14.9 us (16%)
    all_to_all x1, starting transfers between devices, local(): got = lax.all_to_all(send, 'vel', 0, 0, tiled=True)  10.2 us
    all_to_all x1, starting transfers between devices, local(): back = lax.all_to_all(send, 'vel', 0, 0, tiled=True)  9.66 us
    all_to_all x1, waiting for transfers between devices, local(): back = lax.all_to_all(send, 'vel', 0, 0, tiled=True)  7.86 us
    ppermute x1, waiting for transfers between devices, local(): held = jnp.concatenate([held, lax.ppermute(held, 'sx', flip(4))])  6.13 us
    ppermute x1, starting transfers between devices, local(): held = jnp.concatenate([held, lax.ppermute(held, 'sy', flip(4))])  6.08 us
    ppermute x1, starting transfers between devices, local(): held = jnp.concatenate([held, lax.ppermute(held, 'sx', flip(4))])  5.94 us
    ppermute x1, starting transfers between devices, local(): lax.ppermute(held, 'sx', [(i, (i + 2) % 8 if i % 2 == 0 else (i - 2) % 8)...  5.84 us
    ppermute x1, waiting for transfers between devices, local(): lax.ppermute(outer, 'sy', [(i, (i + 1) % 8 if i % 2 else (i - 1) % 8) for...  4.71 us
  transfers between devices with their start and end apart: 10, of which 5 were waited for; matrix products, arithmetic and copies ran while one was open for 0% of the time, Pallas kernels for 12%

profile of v9, /device:TPU:80, one launch (start us, length us, event | category | flops | bytes accessed | tf_op | source)
XLA Modules:
  0.0 89.7 jit_solution(13844504130803434450)
XLA Ops:
  0.0 0.0 copy-start.3
  0.0 2.0 %collective-permute-start = (bf16[16,1024]{1,0:T(8,128)(2,1)}, bf16[16,1024]{1,0:T(8,128)(2,1)S(1)}, u32[]{:S(2)}, u32[]{:S(2)}) collective-permute-start(bf16[16,1024]{1,0:T(8,128)(2,1)} %param.5), channel_id=1, source_target_pairs={{0,2},{1,3},{2,0},{3,1},{4,6},{5,7},{6,4},{7,5},{8,10},{9,11},{10,... | collective-permute-start | bytes 98312 | tf_op jit(solution)/shard_map/ppermute | solution.py:447
  2.0 4.1 %collective-permute-done = bf16[16,1024]{1,0:T(8,128)(2,1)S(1)} collective-permute-done((bf16[16,1024]{1,0:T(8,128)(2,1)}, bf16[16,1024]{1,0:T(8,128)(2,1)S(1)}, u32[]{:S(2)}, u32[]{:S(2)}) %collective-permute-start) | collective-permute-done | bytes 32800 | tf_op jit(solution)/shard_map/ppermute | solution.py:447
  6.1 0.8 pad_maximum_fusion.1
  6.9 6.1 %collective-permute-start.1 = (bf16[32,1024]{1,0:T(8,128)(2,1)S(1)}, bf16[32,1024]{1,0:T(8,128)(2,1)S(1)}, u32[]{:S(2)}, u32[]{:S(2)}) collective-permute-start(bf16[32,1024]{1,0:T(8,128)(2,1)S(1)} %pad_maximum_fusion.1), channel_id=1, source_target_pairs={{0,4},{1,5},{2,6},{3,7},{4,0},{5,1},{6,2},{7,3},{8,12},{9,13},{10,... | collective-permute-start | bytes 196616 | tf_op jit(solution)/shard_map/ppermute | solution.py:448
  13.0 2.8 %pack.1 = bf16[8,400,128]{2,1,0:T(8,128)(2,1)} custom-call(s32[1]{0:T(128)} %bitcast.1.place_ref, bf16[3,32,4096]{2,1,0:T(8,128)(2,1)} %f_hbm.1, bf16[1024,128]{1,0:T(8,128)(2,1)} %constant.15.clone.basis_ref), custom_call_target="tpu_custom_call" | custom-call | tf_op jit(solution)/shard_map/pack/pallas_call | solution.py:122
  15.8 0.0 collective-permute-done.1
  15.9 0.0 copy-done.3
  15.9 0.0 copy-start
  15.9 10.2 %all-to-all-start = ((bf16[8,400,128]{2,1,0:T(8,128)(2,1)}), bf16[8,400,128]{2,1,0:T(8,128)(2,1)S(1)}, u32[]{:S(2)}, u32[]{:S(2)}) async-start(bf16[8,400,128]{2,1,0:T(8,128)(2,1)} %pack.1), calls=%async_computation | async-start | bytes 1638400 | tf_op jit(solution)/shard_map/all_to_all | solution.py:450
  26.1 0.0 copy-start.1
  26.1 5.9 %collective-permute-start.2 = (bf16[64,1024]{1,0:T(8,128)(2,1)S(1)}, bf16[64,1024]{1,0:T(8,128)(2,1)S(1)}, u32[]{:S(2)}, u32[]{:S(2)}) collective-permute-start(bf16[64,1024]{1,0:T(8,128)(2,1)S(1)} %pad_maximum_fusion), channel_id=1, source_target_pairs={{0,32},{8,40},{16,48},{24,56},{32,0},{40,8},{48,16},{56,24},{1,33}... | collective-permute-start | bytes 393224 | tf_op jit(solution)/shard_map/ppermute | solution.py:451
  32.1 6.1 %collective-permute-done.2 = bf16[64,1024]{1,0:T(8,128)(2,1)S(1)} collective-permute-done((bf16[64,1024]{1,0:T(8,128)(2,1)S(1)}, bf16[64,1024]{1,0:T(8,128)(2,1)S(1)}, u32[]{:S(2)}, u32[]{:S(2)}) %collective-permute-start.2) | collective-permute-done | bytes 131104 | tf_op jit(solution)/shard_map/ppermute | solution.py:451
  38.2 5.8 %collective-permute-start.3 = (bf16[128,1024]{1,0:T(8,128)(2,1)S(1)}, bf16[128,1024]{1,0:T(8,128)(2,1)S(1)}, u32[]{:S(2)}, u32[]{:S(2)}) collective-permute-start(bf16[128,1024]{1,0:T(8,128)(2,1)S(1)} %constant_dynamic-update-slice_fusion.held_ref), channel_id=1, source_target_pairs={{0,16},{8,56},{16,32},{24,8},{32,48},{40,24},{48,0},{56,40},{1,17}... | collective-permute-start | bytes 786440 | tf_op jit(solution)/shard_map/ppermute | solution.py:455
  44.1 0.0 copy-done
  44.1 1.0 %edges.1 = (bf16[192,1024]{1,0:T(8,128)(2,1)}, bf16[192,1024]{1,0:T(8,128)(2,1)}, bf16[16,1024]{1,0:T(8,128)(2,1)S(1)}, bf16[16,1024]{1,0:T(8,128)(2,1)S(1)}) custom-call(s32[1]{0:T(128)} %bitcast.core_ref, bf16[128,1024]{1,0:T(8,128)(2,1)S(1)} %constant_dynamic-update-slice_fusion.held_ref, bf16[3,32,4096]{2,1,0:T(8,128)(2,1)S(1)} %copy-done), custom_call_target="tpu_custom_call" | custom-call | tf_op jit(solution)/shard_map/edges/pallas_call | solution.py:168
  45.0 1.9 %collective-permute-start.4 = (bf16[192,1024]{1,0:T(8,128)(2,1)}, bf16[192,1024]{1,0:T(8,128)(2,1)S(1)}, u32[]{:S(2)}, u32[]{:S(2)}) collective-permute-start(bf16[192,1024]{1,0:T(8,128)(2,1)} %get-tuple-element.18), channel_id=1, source_target_pairs={{0,56},{8,0},{16,8},{24,16},{32,24},{40,32},{48,40},{56,48},{1,57}... | collective-permute-start | bytes 1179656 | tf_op jit(solution)/shard_map/ppermute | solution.py:453
  46.9 3.9 %collective-permute-start.5 = (bf16[192,1024]{1,0:T(8,128)(2,1)}, bf16[192,1024]{1,0:T(8,128)(2,1)}, u32[]{:S(2)}, u32[]{:S(2)}) collective-permute-start(bf16[192,1024]{1,0:T(8,128)(2,1)} %get-tuple-element.19), channel_id=1, source_target_pairs={{0,8},{8,16},{16,24},{24,32},{32,40},{40,48},{48,56},{56,0},{1,9},... | collective-permute-start | bytes 1179656 | tf_op jit(solution)/shard_map/ppermute | solution.py:454
  50.9 0.0 copy-done.1
  50.9 0.4 spread.1.mix_ref
  51.3 0.0 all-to-all-done.got_ref
  51.3 2.3 %relax.1 = bf16[8,384,128]{2,1,0:T(8,128)(2,1)} custom-call(s32[1]{0:T(128)} %bitcast.1.place_ref, bf16[8,400,128]{2,1,0:T(8,128)(2,1)S(1)} %all-to-all-done.got_ref, bf16[512,512]{1,0:T(8,128)(2,1)S(1)} %spread.1.mix_ref), custom_call_target="tpu_custom_call" | custom-call | tf_op jit(solution)/shard_map/relax/pallas_call | solution.py:308
  53.6 0.0 collective-permute-done.3.across_ref
  53.6 0.0 copy-start.2
  53.6 0.7 copy-done.2
  54.3 9.7 %all-to-all-start.1 = ((bf16[8,384,128]{2,1,0:T(8,128)(2,1)}), bf16[8,384,128]{2,1,0:T(8,128)(2,1)S(1)}, u32[]{:S(2)}, u32[]{:S(2)}) async-start(bf16[8,384,128]{2,1,0:T(8,128)(2,1)} %relax.1), calls=%async_computation.1 | async-start | bytes 1572864 | tf_op jit(solution)/shard_map/all_to_all | solution.py:463
  63.9 0.0 collective-permute-done.4.above_ref.above_hbm
  63.9 0.0 collective-permute-done.5.below_ref.below_hbm
  64.0 1.1 %join.1.own_ref = bf16[528,1024]{1,0:T(8,128)(2,1)S(1)} custom-call(bf16[128,1024]{1,0:T(8,128)(2,1)S(1)} %constant_dynamic-update-slice_fusion.held_ref, bf16[192,1024]{1,0:T(8,128)(2,1)S(1)} %collective-permute-done.4.above_ref.above_hbm, bf16[192,1024]{1,0:T(8,128)(2,1)} %collective-permute-done.5.below_ref.below_hbm, bf16[128,1024]{1,0:T(8,128)(2,1)} %copy-done.2, ...), custom_call_target="tpu_custom_call" | custom-call | tf_op jit(solution)/shard_map/join/pallas_call | solution.py:197
  65.1 1.9 %collective-permute-start.6 = (bf16[528,1024]{1,0:T(8,128)(2,1)S(1)}, bf16[528,1024]{1,0:T(8,128)(2,1)}, u32[]{:S(2)}, u32[]{:S(2)}) collective-permute-start(bf16[528,1024]{1,0:T(8,128)(2,1)S(1)} %join.1.own_ref), channel_id=1, source_target_pairs={{0,1},{1,0},{2,3},{3,2},{4,5},{5,4},{6,7},{7,6},{8,9},{9,8},{10,11... | collective-permute-start | bytes 3244040 | tf_op jit(solution)/shard_map/ppermute | solution.py:461
  67.0 2.6 %collective-permute-start.7 = (bf16[16,1024]{1,0:T(8,128)(2,1)S(1)}, bf16[16,1024]{1,0:T(8,128)(2,1)S(1)}, u32[]{:S(2)}, u32[]{:S(2)}) collective-permute-start(bf16[16,1024]{1,0:T(8,128)(2,1)S(1)} %get-tuple-element.24), channel_id=1, source_target_pairs={{0,7},{1,2},{2,1},{3,4},{4,3},{5,6},{6,5},{7,0},{8,15},{9,10},{10,... | collective-permute-start | bytes 98312 | tf_op jit(solution)/shard_map/ppermute | solution.py:456
  69.6 0.1 pad_add_fusion.where_ref
  69.7 0.1 collective-permute-done.6.other_ref
  69.8 3.4 %assemble.1 = (bf16[1024,1024]{1,0:T(8,128)(2,1)}, bf16[16,1024]{1,0:T(8,128)(2,1)S(1)}) custom-call(s32[2]{0:T(128)S(1)} %pad_add_fusion.where_ref, bf16[528,1024]{1,0:T(8,128)(2,1)S(1)} %join.1.own_ref, bf16[528,1024]{1,0:T(8,128)(2,1)} %collective-permute-done.6.other_ref), custom_call_target="tpu_custom_call" | custom-call | tf_op jit(solution)/shard_map/assemble/pallas_call | solution.py:229
  73.3 4.7 %collective-permute-done.7.outer_hbm = bf16[16,1024]{1,0:T(8,128)(2,1)S(1)} collective-permute-done((bf16[16,1024]{1,0:T(8,128)(2,1)S(1)}, bf16[16,1024]{1,0:T(8,128)(2,1)S(1)}, u32[]{:S(2)}, u32[]{:S(2)}) %collective-permute-start.7) | collective-permute-done | bytes 32800 | tf_op jit(solution)/shard_map/ppermute | solution.py:456
  78.0 7.9 %all-to-all-done.1.back_hbm = bf16[8,384,128]{2,1,0:T(8,128)(2,1)S(1)} async-done(((bf16[8,384,128]{2,1,0:T(8,128)(2,1)}), bf16[8,384,128]{2,1,0:T(8,128)(2,1)S(1)}, u32[]{:S(2)}, u32[]{:S(2)}) %all-to-all-start.1) | async-done | bytes 786464 | tf_op jit(solution)/shard_map/all_to_all | solution.py:463
  85.8 3.8 %advance.1 = bf16[3,32,4096]{2,1,0:T(8,128)(2,1)} custom-call(s32[1]{0:T(128)} %bitcast.core_ref, bf16[3,32,4096]{2,1,0:T(8,128)(2,1)S(1)} %copy-done, bf16[8,384,128]{2,1,0:T(8,128)(2,1)S(1)} %all-to-all-done.1.back_hbm, bf16[1024,1024]{1,0:T(8,128)(2,1)} %get-tuple-element.22.weights_hbm, bf16[192,1024]{1,0:T(8,128)(2,1)} %collective-permute-done.5.below_ref.below_hbm, ...), custom_call_target="tpu_custom_call" | custom-call | tf_op jit(solution)/shard_map/advance/pallas_call | solution.py:413
  (3 shorter events, 0.0 us)
Async XLA Ops:
  0.0 15.9 %copy-start.3 = (bf16[16,1024]{1,0:T(8,128)(2,1)S(1)}, bf16[16,1024]{1,0:T(8,128)(2,1)}, u32[]{:S(2)}) copy-start(bf16[16,1024]{1,0:T(8,128)(2,1)} %param.5) | copy-start | bytes 98308
  0.0 6.1 %collective-permute-start = (bf16[16,1024]{1,0:T(8,128)(2,1)}, bf16[16,1024]{1,0:T(8,128)(2,1)S(1)}, u32[]{:S(2)}, u32[]{:S(2)}) collective-permute-start(bf16[16,1024]{1,0:T(8,128)(2,1)} %param.5), channel_id=1, source_target_pairs={{0,2},{1,3},{2,0},{3,1},{4,6},{5,7},{6,4},{7,5},{8,10},{9,11},{10,... | collective-permute-start | bytes 98312 | tf_op jit(solution)/shard_map/ppermute | solution.py:447
  6.9 8.9 %collective-permute-start.1 = (bf16[32,1024]{1,0:T(8,128)(2,1)S(1)}, bf16[32,1024]{1,0:T(8,128)(2,1)S(1)}, u32[]{:S(2)}, u32[]{:S(2)}) collective-permute-start(bf16[32,1024]{1,0:T(8,128)(2,1)S(1)} %pad_maximum_fusion.1), channel_id=1, source_target_pairs={{0,4},{1,5},{2,6},{3,7},{4,0},{5,1},{6,2},{7,3},{8,12},{9,13},{10,... | collective-permute-start | bytes 196616 | tf_op jit(solution)/shard_map/ppermute | solution.py:448
  15.9 28.2 %copy-start = (bf16[3,32,4096]{2,1,0:T(8,128)(2,1)S(1)}, bf16[3,32,4096]{2,1,0:T(8,128)(2,1)}, u32[]{:S(2)}) copy-start(bf16[3,32,4096]{2,1,0:T(8,128)(2,1)} %f_hbm.1) | copy-start | bytes 2359300
  15.9 35.4 %all-to-all-start = ((bf16[8,400,128]{2,1,0:T(8,128)(2,1)}), bf16[8,400,128]{2,1,0:T(8,128)(2,1)S(1)}, u32[]{:S(2)}, u32[]{:S(2)}) async-start(bf16[8,400,128]{2,1,0:T(8,128)(2,1)} %pack.1), calls=%async_computation | async-start | bytes 1638400 | tf_op jit(solution)/shard_map/all_to_all | solution.py:450
  26.1 24.8 %copy-start.1 = (bf16[32,32]{1,0:T(8,128)(2,1)S(1)}, bf16[32,32]{1,0:T(8,128)(2,1)}, u32[]{:S(2)}) copy-start(bf16[32,32]{1,0:T(8,128)(2,1)} %depth_ref.1) | copy-start | bytes 6148
  26.1 12.1 %collective-permute-start.2 = (bf16[64,1024]{1,0:T(8,128)(2,1)S(1)}, bf16[64,1024]{1,0:T(8,128)(2,1)S(1)}, u32[]{:S(2)}, u32[]{:S(2)}) collective-permute-start(bf16[64,1024]{1,0:T(8,128)(2,1)S(1)} %pad_maximum_fusion), channel_id=1, source_target_pairs={{0,32},{8,40},{16,48},{24,56},{32,0},{40,8},{48,16},{56,24},{1,33}... | collective-permute-start | bytes 393224 | tf_op jit(solution)/shard_map/ppermute | solution.py:451
  38.2 15.4 %collective-permute-start.3 = (bf16[128,1024]{1,0:T(8,128)(2,1)S(1)}, bf16[128,1024]{1,0:T(8,128)(2,1)S(1)}, u32[]{:S(2)}, u32[]{:S(2)}) collective-permute-start(bf16[128,1024]{1,0:T(8,128)(2,1)S(1)} %constant_dynamic-update-slice_fusion.held_ref), channel_id=1, source_target_pairs={{0,16},{8,56},{16,32},{24,8},{32,48},{40,24},{48,0},{56,40},{1,17}... | collective-permute-start | bytes 786440 | tf_op jit(solution)/shard_map/ppermute | solution.py:455
  45.0 18.9 %collective-permute-start.4 = (bf16[192,1024]{1,0:T(8,128)(2,1)}, bf16[192,1024]{1,0:T(8,128)(2,1)S(1)}, u32[]{:S(2)}, u32[]{:S(2)}) collective-permute-start(bf16[192,1024]{1,0:T(8,128)(2,1)} %get-tuple-element.18), channel_id=1, source_target_pairs={{0,56},{8,0},{16,8},{24,16},{32,24},{40,32},{48,40},{56,48},{1,57}... | collective-permute-start | bytes 1179656 | tf_op jit(solution)/shard_map/ppermute | solution.py:453
  46.9 17.0 %collective-permute-start.5 = (bf16[192,1024]{1,0:T(8,128)(2,1)}, bf16[192,1024]{1,0:T(8,128)(2,1)}, u32[]{:S(2)}, u32[]{:S(2)}) collective-permute-start(bf16[192,1024]{1,0:T(8,128)(2,1)} %get-tuple-element.19), channel_id=1, source_target_pairs={{0,8},{8,16},{16,24},{24,32},{32,40},{40,48},{48,56},{56,0},{1,9},... | collective-permute-start | bytes 1179656 | tf_op jit(solution)/shard_map/ppermute | solution.py:454
  53.6 0.7 copy-start.2
  54.3 31.5 %all-to-all-start.1 = ((bf16[8,384,128]{2,1,0:T(8,128)(2,1)}), bf16[8,384,128]{2,1,0:T(8,128)(2,1)S(1)}, u32[]{:S(2)}, u32[]{:S(2)}) async-start(bf16[8,384,128]{2,1,0:T(8,128)(2,1)} %relax.1), calls=%async_computation.1 | async-start | bytes 1572864 | tf_op jit(solution)/shard_map/all_to_all | solution.py:463
  65.1 4.7 %collective-permute-start.6 = (bf16[528,1024]{1,0:T(8,128)(2,1)S(1)}, bf16[528,1024]{1,0:T(8,128)(2,1)}, u32[]{:S(2)}, u32[]{:S(2)}) collective-permute-start(bf16[528,1024]{1,0:T(8,128)(2,1)S(1)} %join.1.own_ref), channel_id=1, source_target_pairs={{0,1},{1,0},{2,3},{3,2},{4,5},{5,4},{6,7},{7,6},{8,9},{9,8},{10,11... | collective-permute-start | bytes 3244040 | tf_op jit(solution)/shard_map/ppermute | solution.py:461
  67.0 11.0 %collective-permute-start.7 = (bf16[16,1024]{1,0:T(8,128)(2,1)S(1)}, bf16[16,1024]{1,0:T(8,128)(2,1)S(1)}, u32[]{:S(2)}, u32[]{:S(2)}) collective-permute-start(bf16[16,1024]{1,0:T(8,128)(2,1)S(1)} %get-tuple-element.24), channel_id=1, source_target_pairs={{0,7},{1,2},{2,1},{3,4},{4,3},{5,6},{6,5},{7,0},{8,15},{9,10},{10,... | collective-permute-start | bytes 98312 | tf_op jit(solution)/shard_map/ppermute | solution.py:456

commit v10 on v9

--- a/solution.py
+++ b/solution.py
@@ -455,8 +455,6 @@
     across = lax.ppermute(held, "sx", [(i, (i + 2) % 8 if i % 2 == 0 else (i - 2) % 8) for i in range(8)])
     outer = lax.ppermute(outer, "sy", [(i, (i + 1) % 8 if i % 2 else (i - 1) % 8) for i in range(8)])
     send = relax(place, got, spread(depth_weights))
-    across = pltpu.with_memory_space_constraint(across, pltpu.HBM)
-    send, across = lax.optimization_barrier((send, across))
     own = join(held, above, below, across, inner)
     other = lax.ppermute(own, "sy", flip(1))
     weights, inner = assemble(where, own, other)

time: 90.4 us -> 87.8 us (0.971)
  the two profiles are of different devices: /device:TPU:80 before, /device:TPU:56 now
where the time goes in v10:
time: 87.8 us; the launch traced here: 86.3 us
  starting transfers between devices  52.7 us (60%)
  waiting for transfers between devices  17.8 us (20%)
  Pallas kernels  14.8 us (17%)
    all_to_all x1, starting transfers between devices, local(): got = lax.all_to_all(send, 'vel', 0, 0, tiled=True)  10.7 us
    all_to_all x1, starting transfers between devices, local(): back = lax.all_to_all(send, 'vel', 0, 0, tiled=True)  9.73 us
    ppermute x1, waiting for transfers between devices, local(): lax.ppermute(held, 'sx', [(i, (i + 2) % 8 if i % 2 == 0 else (i - 2) % 8)...  8.22 us
    ppermute x1, waiting for transfers between devices, local(): held = jnp.concatenate([held, lax.ppermute(held, 'sx', flip(4))])  7.43 us
    ppermute x1, starting transfers between devices, local(): held = jnp.concatenate([held, lax.ppermute(held, 'sy', flip(4))])  6.08 us
    ppermute x1, starting transfers between devices, local(): lax.ppermute(outer, 'sy', [(i, (i + 1) % 8 if i % 2 else (i - 1) % 8) for...  5.92 us
    ppermute x1, starting transfers between devices, local(): held = jnp.concatenate([held, lax.ppermute(held, 'sx', flip(4))])  4.71 us
    ppermute x1, starting transfers between devices, local(): lax.ppermute(plane_weights, 'sy', flip(2))  4.4 us
  transfers between devices with their start and end apart: 10, of which 3 were waited for; matrix products, arithmetic and copies ran while one was open for 0% of the time, Pallas kernels for 13%

profile of v10, /device:TPU:56, one launch (start us, length us, event | category | flops | bytes accessed | tf_op | source)
XLA Modules:
  0.0 86.3 jit_solution(9896484477445710047)
XLA Ops:
  0.0 0.0 copy-start.2
  0.0 4.4 %collective-permute-start = (bf16[16,1024]{1,0:T(8,128)(2,1)}, bf16[16,1024]{1,0:T(8,128)(2,1)S(1)}, u32[]{:S(2)}, u32[]{:S(2)}) collective-permute-start(bf16[16,1024]{1,0:T(8,128)(2,1)} %param.5), channel_id=1, source_target_pairs={{0,2},{1,3},{2,0},{3,1},{4,6},{5,7},{6,4},{7,5},{8,10},{9,11},{10,... | collective-permute-start | bytes 98312 | tf_op jit(solution)/shard_map/ppermute | solution.py:447
  4.4 2.1 %collective-permute-done = bf16[16,1024]{1,0:T(8,128)(2,1)S(1)} collective-permute-done((bf16[16,1024]{1,0:T(8,128)(2,1)}, bf16[16,1024]{1,0:T(8,128)(2,1)S(1)}, u32[]{:S(2)}, u32[]{:S(2)}) %collective-permute-start) | collective-permute-done | bytes 32800 | tf_op jit(solution)/shard_map/ppermute | solution.py:447
  6.5 0.8 pad_maximum_fusion.1
  7.3 6.1 %collective-permute-start.1 = (bf16[32,1024]{1,0:T(8,128)(2,1)S(1)}, bf16[32,1024]{1,0:T(8,128)(2,1)S(1)}, u32[]{:S(2)}, u32[]{:S(2)}) collective-permute-start(bf16[32,1024]{1,0:T(8,128)(2,1)S(1)} %pad_maximum_fusion.1), channel_id=1, source_target_pairs={{0,4},{1,5},{2,6},{3,7},{4,0},{5,1},{6,2},{7,3},{8,12},{9,13},{10,... | collective-permute-start | bytes 196616 | tf_op jit(solution)/shard_map/ppermute | solution.py:448
  13.4 2.8 %pack.1 = bf16[8,400,128]{2,1,0:T(8,128)(2,1)} custom-call(s32[1]{0:T(128)} %bitcast.1.place_ref, bf16[3,32,4096]{2,1,0:T(8,128)(2,1)} %f_hbm.1, bf16[1024,128]{1,0:T(8,128)(2,1)} %constant.15.clone.basis_ref), custom_call_target="tpu_custom_call" | custom-call | tf_op jit(solution)/shard_map/pack/pallas_call | solution.py:122
  16.2 0.0 collective-permute-done.1
  16.2 0.0 copy-done.2
  16.2 0.0 copy-start
  16.2 10.7 %all-to-all-start = ((bf16[8,400,128]{2,1,0:T(8,128)(2,1)}), bf16[8,400,128]{2,1,0:T(8,128)(2,1)S(1)}, u32[]{:S(2)}, u32[]{:S(2)}) async-start(bf16[8,400,128]{2,1,0:T(8,128)(2,1)} %pack.1), calls=%async_computation | async-start | bytes 1638400 | tf_op jit(solution)/shard_map/all_to_all | solution.py:450
  27.0 0.0 copy-start.1
  27.0 4.7 %collective-permute-start.2 = (bf16[64,1024]{1,0:T(8,128)(2,1)S(1)}, bf16[64,1024]{1,0:T(8,128)(2,1)S(1)}, u32[]{:S(2)}, u32[]{:S(2)}) collective-permute-start(bf16[64,1024]{1,0:T(8,128)(2,1)S(1)} %pad_maximum_fusion), channel_id=1, source_target_pairs={{0,32},{8,40},{16,48},{24,56},{32,0},{40,8},{48,16},{56,24},{1,33}... | collective-permute-start | bytes 393224 | tf_op jit(solution)/shard_map/ppermute | solution.py:451
  31.7 7.4 %collective-permute-done.2 = bf16[64,1024]{1,0:T(8,128)(2,1)S(1)} collective-permute-done((bf16[64,1024]{1,0:T(8,128)(2,1)S(1)}, bf16[64,1024]{1,0:T(8,128)(2,1)S(1)}, u32[]{:S(2)}, u32[]{:S(2)}) %collective-permute-start.2) | collective-permute-done | bytes 131104 | tf_op jit(solution)/shard_map/ppermute | solution.py:451
  39.2 0.0 copy-done
  39.2 1.0 %edges.1 = (bf16[192,1024]{1,0:T(8,128)(2,1)}, bf16[192,1024]{1,0:T(8,128)(2,1)}, bf16[16,1024]{1,0:T(8,128)(2,1)S(1)}, bf16[16,1024]{1,0:T(8,128)(2,1)S(1)}) custom-call(s32[1]{0:T(128)} %bitcast.core_ref, bf16[128,1024]{1,0:T(8,128)(2,1)S(1)} %constant_dynamic-update-slice_fusion.held_ref, bf16[3,32,4096]{2,1,0:T(8,128)(2,1)S(1)} %copy-done), custom_call_target="tpu_custom_call" | custom-call | tf_op jit(solution)/shard_map/edges/pallas_call | solution.py:168
  40.1 2.8 %collective-permute-start.3 = (bf16[192,1024]{1,0:T(8,128)(2,1)}, bf16[192,1024]{1,0:T(8,128)(2,1)S(1)}, u32[]{:S(2)}, u32[]{:S(2)}) collective-permute-start(bf16[192,1024]{1,0:T(8,128)(2,1)} %get-tuple-element.15), channel_id=1, source_target_pairs={{0,56},{8,0},{16,8},{24,16},{32,24},{40,32},{48,40},{56,48},{1,57}... | collective-permute-start | bytes 1179656 | tf_op jit(solution)/shard_map/ppermute | solution.py:453
  42.9 4.3 %collective-permute-start.4 = (bf16[192,1024]{1,0:T(8,128)(2,1)}, bf16[192,1024]{1,0:T(8,128)(2,1)}, u32[]{:S(2)}, u32[]{:S(2)}) collective-permute-start(bf16[192,1024]{1,0:T(8,128)(2,1)} %get-tuple-element.16), channel_id=1, source_target_pairs={{0,8},{8,16},{16,24},{24,32},{32,40},{40,48},{48,56},{56,0},{1,9},... | collective-permute-start | bytes 1179656 | tf_op jit(solution)/shard_map/ppermute | solution.py:454
  47.2 0.0 copy-done.1
  47.2 0.4 spread.1.mix_ref
  47.6 0.0 all-to-all-done.got_ref
  47.6 2.3 %relax.1 = bf16[8,384,128]{2,1,0:T(8,128)(2,1)} custom-call(s32[1]{0:T(128)} %bitcast.1.place_ref, bf16[8,400,128]{2,1,0:T(8,128)(2,1)S(1)} %all-to-all-done.got_ref, bf16[512,512]{1,0:T(8,128)(2,1)S(1)} %spread.1.mix_ref), custom_call_target="tpu_custom_call" | custom-call | tf_op jit(solution)/shard_map/relax/pallas_call | solution.py:308
  49.9 9.7 %all-to-all-start.1 = ((bf16[8,384,128]{2,1,0:T(8,128)(2,1)}), bf16[8,384,128]{2,1,0:T(8,128)(2,1)S(1)}, u32[]{:S(2)}, u32[]{:S(2)}) async-start(bf16[8,384,128]{2,1,0:T(8,128)(2,1)} %relax.1), calls=%async_computation.1 | async-start | bytes 1572864 | tf_op jit(solution)/shard_map/all_to_all | solution.py:461
  59.6 2.1 %collective-permute-start.5 = (bf16[128,1024]{1,0:T(8,128)(2,1)S(1)}, bf16[128,1024]{1,0:T(8,128)(2,1)S(1)}, u32[]{:S(2)}, u32[]{:S(2)}) collective-permute-start(bf16[128,1024]{1,0:T(8,128)(2,1)S(1)} %constant_dynamic-update-slice_fusion.held_ref), channel_id=1, source_target_pairs={{0,16},{8,56},{16,32},{24,8},{32,48},{40,24},{48,0},{56,40},{1,17}... | collective-permute-start | bytes 786440 | tf_op jit(solution)/shard_map/ppermute | solution.py:455
  61.8 8.2 %collective-permute-done.5.across_ref = bf16[128,1024]{1,0:T(8,128)(2,1)S(1)} collective-permute-done((bf16[128,1024]{1,0:T(8,128)(2,1)S(1)}, bf16[128,1024]{1,0:T(8,128)(2,1)S(1)}, u32[]{:S(2)}, u32[]{:S(2)}) %collective-permute-start.5) | collective-permute-done | bytes 262176 | tf_op jit(solution)/shard_map/ppermute | solution.py:455
  70.0 0.0 collective-permute-done.3.above_ref.above_hbm
  70.0 0.0 collective-permute-done.4.below_ref.below_hbm
  70.0 1.0 %join.1.own_ref = bf16[528,1024]{1,0:T(8,128)(2,1)S(1)} custom-call(bf16[128,1024]{1,0:T(8,128)(2,1)S(1)} %constant_dynamic-update-slice_fusion.held_ref, bf16[192,1024]{1,0:T(8,128)(2,1)S(1)} %collective-permute-done.3.above_ref.above_hbm, bf16[192,1024]{1,0:T(8,128)(2,1)} %collective-permute-done.4.below_ref.below_hbm, ...), custom_call_target="tpu_custom_call" | custom-call | tf_op jit(solution)/shard_map/join/pallas_call | solution.py:197
  71.1 1.9 %collective-permute-start.6 = (bf16[528,1024]{1,0:T(8,128)(2,1)S(1)}, bf16[528,1024]{1,0:T(8,128)(2,1)}, u32[]{:S(2)}, u32[]{:S(2)}) collective-permute-start(bf16[528,1024]{1,0:T(8,128)(2,1)S(1)} %join.1.own_ref), channel_id=1, source_target_pairs={{0,1},{1,0},{2,3},{3,2},{4,5},{5,4},{6,7},{7,6},{8,9},{9,8},{10,11... | collective-permute-start | bytes 3244040 | tf_op jit(solution)/shard_map/ppermute | solution.py:459
  73.0 5.9 %collective-permute-start.7 = (bf16[16,1024]{1,0:T(8,128)(2,1)S(1)}, bf16[16,1024]{1,0:T(8,128)(2,1)S(1)}, u32[]{:S(2)}, u32[]{:S(2)}) collective-permute-start(bf16[16,1024]{1,0:T(8,128)(2,1)S(1)} %get-tuple-element.20), channel_id=1, source_target_pairs={{0,7},{1,2},{2,1},{3,4},{4,3},{5,6},{6,5},{7,0},{8,15},{9,10},{10,... | collective-permute-start | bytes 98312 | tf_op jit(solution)/shard_map/ppermute | solution.py:456
  78.9 0.1 pad_add_fusion.where_ref
  79.0 0.0 collective-permute-done.6.other_ref
  79.0 3.4 %assemble.1 = (bf16[1024,1024]{1,0:T(8,128)(2,1)}, bf16[16,1024]{1,0:T(8,128)(2,1)S(1)}) custom-call(s32[2]{0:T(128)S(1)} %pad_add_fusion.where_ref, bf16[528,1024]{1,0:T(8,128)(2,1)S(1)} %join.1.own_ref, bf16[528,1024]{1,0:T(8,128)(2,1)} %collective-permute-done.6.other_ref), custom_call_target="tpu_custom_call" | custom-call | tf_op jit(solution)/shard_map/assemble/pallas_call | solution.py:229
  82.4 0.0 collective-permute-done.7.outer_hbm
  82.4 0.0 all-to-all-done.1.back_hbm
  82.5 3.9 %advance.1 = bf16[3,32,4096]{2,1,0:T(8,128)(2,1)} custom-call(s32[1]{0:T(128)} %bitcast.core_ref, bf16[3,32,4096]{2,1,0:T(8,128)(2,1)S(1)} %copy-done, bf16[8,384,128]{2,1,0:T(8,128)(2,1)S(1)} %all-to-all-done.1.back_hbm, bf16[1024,1024]{1,0:T(8,128)(2,1)} %get-tuple-element.18.weights_hbm, bf16[192,1024]{1,0:T(8,128)(2,1)} %collective-permute-done.4.below_ref.below_hbm, ...), custom_call_target="tpu_custom_call" | custom-call | tf_op jit(solution)/shard_map/advance/pallas_call | solution.py:413
  (3 shorter events, 0.0 us)
Async XLA Ops:
  0.0 16.2 %copy-start.2 = (bf16[16,1024]{1,0:T(8,128)(2,1)S(1)}, bf16[16,1024]{1,0:T(8,128)(2,1)}, u32[]{:S(2)}) copy-start(bf16[16,1024]{1,0:T(8,128)(2,1)} %param.5) | copy-start | bytes 98308
  0.0 6.5 %collective-permute-start = (bf16[16,1024]{1,0:T(8,128)(2,1)}, bf16[16,1024]{1,0:T(8,128)(2,1)S(1)}, u32[]{:S(2)}, u32[]{:S(2)}) collective-permute-start(bf16[16,1024]{1,0:T(8,128)(2,1)} %param.5), channel_id=1, source_target_pairs={{0,2},{1,3},{2,0},{3,1},{4,6},{5,7},{6,4},{7,5},{8,10},{9,11},{10,... | collective-permute-start | bytes 98312 | tf_op jit(solution)/shard_map/ppermute | solution.py:447
  7.3 8.9 %collective-permute-start.1 = (bf16[32,1024]{1,0:T(8,128)(2,1)S(1)}, bf16[32,1024]{1,0:T(8,128)(2,1)S(1)}, u32[]{:S(2)}, u32[]{:S(2)}) collective-permute-start(bf16[32,1024]{1,0:T(8,128)(2,1)S(1)} %pad_maximum_fusion.1), channel_id=1, source_target_pairs={{0,4},{1,5},{2,6},{3,7},{4,0},{5,1},{6,2},{7,3},{8,12},{9,13},{10,... | collective-permute-start | bytes 196616 | tf_op jit(solution)/shard_map/ppermute | solution.py:448
  16.2 22.9 %copy-start = (bf16[3,32,4096]{2,1,0:T(8,128)(2,1)S(1)}, bf16[3,32,4096]{2,1,0:T(8,128)(2,1)}, u32[]{:S(2)}) copy-start(bf16[3,32,4096]{2,1,0:T(8,128)(2,1)} %f_hbm.1) | copy-start | bytes 2359300
  16.2 31.4 %all-to-all-start = ((bf16[8,400,128]{2,1,0:T(8,128)(2,1)}), bf16[8,400,128]{2,1,0:T(8,128)(2,1)S(1)}, u32[]{:S(2)}, u32[]{:S(2)}) async-start(bf16[8,400,128]{2,1,0:T(8,128)(2,1)} %pack.1), calls=%async_computation | async-start | bytes 1638400 | tf_op jit(solution)/shard_map/all_to_all | solution.py:450
  27.0 20.2 %copy-start.1 = (bf16[32,32]{1,0:T(8,128)(2,1)S(1)}, bf16[32,32]{1,0:T(8,128)(2,1)}, u32[]{:S(2)}) copy-start(bf16[32,32]{1,0:T(8,128)(2,1)} %depth_ref.1) | copy-start | bytes 6148
  27.0 12.2 %collective-permute-start.2 = (bf16[64,1024]{1,0:T(8,128)(2,1)S(1)}, bf16[64,1024]{1,0:T(8,128)(2,1)S(1)}, u32[]{:S(2)}, u32[]{:S(2)}) collective-permute-start(bf16[64,1024]{1,0:T(8,128)(2,1)S(1)} %pad_maximum_fusion), channel_id=1, source_target_pairs={{0,32},{8,40},{16,48},{24,56},{32,0},{40,8},{48,16},{56,24},{1,33}... | collective-permute-start | bytes 393224 | tf_op jit(solution)/shard_map/ppermute | solution.py:451
  40.1 29.9 %collective-permute-start.3 = (bf16[192,1024]{1,0:T(8,128)(2,1)}, bf16[192,1024]{1,0:T(8,128)(2,1)S(1)}, u32[]{:S(2)}, u32[]{:S(2)}) collective-permute-start(bf16[192,1024]{1,0:T(8,128)(2,1)} %get-tuple-element.15), channel_id=1, source_target_pairs={{0,56},{8,0},{16,8},{24,16},{32,24},{40,32},{48,40},{56,48},{1,57}... | collective-permute-start | bytes 1179656 | tf_op jit(solution)/shard_map/ppermute | solution.py:453
  42.9 27.1 %collective-permute-start.4 = (bf16[192,1024]{1,0:T(8,128)(2,1)}, bf16[192,1024]{1,0:T(8,128)(2,1)}, u32[]{:S(2)}, u32[]{:S(2)}) collective-permute-start(bf16[192,1024]{1,0:T(8,128)(2,1)} %get-tuple-element.16), channel_id=1, source_target_pairs={{0,8},{8,16},{16,24},{24,32},{32,40},{40,48},{48,56},{56,0},{1,9},... | collective-permute-start | bytes 1179656 | tf_op jit(solution)/shard_map/ppermute | solution.py:454
  49.9 32.5 %all-to-all-start.1 = ((bf16[8,384,128]{2,1,0:T(8,128)(2,1)}), bf16[8,384,128]{2,1,0:T(8,128)(2,1)S(1)}, u32[]{:S(2)}, u32[]{:S(2)}) async-start(bf16[8,384,128]{2,1,0:T(8,128)(2,1)} %relax.1), calls=%async_computation.1 | async-start | bytes 1572864 | tf_op jit(solution)/shard_map/all_to_all | solution.py:461
  59.6 10.4 %collective-permute-start.5 = (bf16[128,1024]{1,0:T(8,128)(2,1)S(1)}, bf16[128,1024]{1,0:T(8,128)(2,1)S(1)}, u32[]{:S(2)}, u32[]{:S(2)}) collective-permute-start(bf16[128,1024]{1,0:T(8,128)(2,1)S(1)} %constant_dynamic-update-slice_fusion.held_ref), channel_id=1, source_target_pairs={{0,16},{8,56},{16,32},{24,8},{32,48},{40,24},{48,0},{56,40},{1,17}... | collective-permute-start | bytes 786440 | tf_op jit(solution)/shard_map/ppermute | solution.py:455
  71.1 7.9 %collective-permute-start.6 = (bf16[528,1024]{1,0:T(8,128)(2,1)S(1)}, bf16[528,1024]{1,0:T(8,128)(2,1)}, u32[]{:S(2)}, u32[]{:S(2)}) collective-permute-start(bf16[528,1024]{1,0:T(8,128)(2,1)S(1)} %join.1.own_ref), channel_id=1, source_target_pairs={{0,1},{1,0},{2,3},{3,2},{4,5},{5,4},{6,7},{7,6},{8,9},{9,8},{10,11... | collective-permute-start | bytes 3244040 | tf_op jit(solution)/shard_map/ppermute | solution.py:459
  73.0 9.4 %collective-permute-start.7 = (bf16[16,1024]{1,0:T(8,128)(2,1)S(1)}, bf16[16,1024]{1,0:T(8,128)(2,1)S(1)}, u32[]{:S(2)}, u32[]{:S(2)}) collective-permute-start(bf16[16,1024]{1,0:T(8,128)(2,1)S(1)} %get-tuple-element.20), channel_id=1, source_target_pairs={{0,7},{1,2},{2,1},{3,4},{4,3},{5,6},{6,5},{7,0},{8,15},{9,10},{10,... | collective-permute-start | bytes 98312 | tf_op jit(solution)/shard_map/ppermute | solution.py:456

commit v11 on v10

--- a/solution.py
+++ b/solution.py
@@ -196,49 +196,13 @@
 def join(held, above, below, across, inner):
     return pl.pallas_call(
         join_kernel,
-        out_shape=jax.ShapeDtypeStruct((4 * held.shape[0] + 16, NXY), BF16),
+        out_shape=pltpu.HBM((4 * held.shape[0] + 16, NXY), BF16),
         in_specs=[hbm()] * 5,
         out_specs=hbm(),
         scratch_shapes=[pltpu.SemaphoreType.DMA((5,))],
         compiler_params=pltpu.CompilerParams(vmem_limit_bytes=LIMIT),
         name="join",
     )(held, above, below, across, inner)
-
-
-def assemble_kernel(where_ref, own_ref, other_ref, out_hbm, inner_hbm, rows_ref, turned_ref, sem):
-    half = NXY // 2
-    edge = pltpu.make_async_copy(other_ref.at[pl.ds(half, 16)], inner_hbm, sem.at[1])
-    edge.start()
-    mine, y = where_ref[0], where_ref[1]
-    far = jnp.where(y % 2 == 0, y + 6, y + 2)
-    for side, ref in ((mine, own_ref), (jnp.bitwise_xor(mine, 1), other_ref)):
-        places = [jnp.bitwise_xor(side, 2 * step) for step in range(4)]
-        for m, base in enumerate((y, y + 1, y + 7, far)):
-            for i in range(2):
-                for j in range(4):
-                    block = slice((m * 8 + i * 4 + j) * 16, (m * 8 + i * 4 + j + 1) * 16)
-                    rows_ref[(base + 4 * i) % 8 * 8 + places[j]] = ref[block, :]
-    turned_ref[...] = jnp.transpose(rows_ref[...].reshape(NXY, NXY))
-    copy = pltpu.make_async_copy(turned_ref, out_hbm, sem.at[0])
-    copy.start()
-    edge.wait()
-    copy.wait()
-
-
-def assemble(where, own, other):
-    return pl.pallas_call(
-        assemble_kernel,
-        out_shape=(pltpu.HBM((NXY, NXY), BF16), jax.ShapeDtypeStruct((16, NXY), BF16)),
-        in_specs=[smem(), vmem(), vmem()],
-        out_specs=(hbm(), hbm()),
-        scratch_shapes=[
-            pltpu.VMEM((NXY // 16, 16, NXY), BF16),
-            pltpu.VMEM((NXY, NXY), BF16),
-            pltpu.SemaphoreType.DMA((2,)),
-        ],
-        compiler_params=pltpu.CompilerParams(vmem_limit_bytes=LIMIT),
-        name="assemble",
-    )(where, own, other)
 
 
 def spread_kernel(depth_ref, out_ref):
@@ -317,13 +281,13 @@
 
 
 def advance_kernel(
-    core_ref,
+    where_ref,
     f_hbm,
     back_hbm,
-    weights_hbm,
+    own_hbm,
+    other_hbm,
     below_hbm,
     above_hbm,
-    inner_hbm,
     outer_hbm,
     out_hbm,
     f_ref,
@@ -342,14 +306,25 @@
     first = [
         pltpu.make_async_copy(below_hbm.at[edge], lower_ref, sem.at[0]),
         pltpu.make_async_copy(above_hbm.at[edge], upper_ref, sem.at[1]),
-        pltpu.make_async_copy(inner_hbm, inner_ref, sem.at[2]),
+        pltpu.make_async_copy(other_hbm.at[pl.ds(NXY // 2, 16)], inner_ref, sem.at[2]),
         pltpu.make_async_copy(outer_hbm.at[pl.ds(outer_hbm.shape[0] - 16, 16)], outer_ref, sem.at[3]),
         pltpu.make_async_copy(f_hbm, f_ref, sem.at[4]),
     ]
-    second = [
-        pltpu.make_async_copy(back_hbm, back_ref, sem.at[5]),
-        pltpu.make_async_copy(weights_hbm, weights_ref, sem.at[6]),
-    ]
+    second = [pltpu.make_async_copy(back_hbm, back_ref, sem.at[5])]
+    mine, y = where_ref[0], where_ref[1]
+    far = jnp.where(y % 2 == 0, y + 6, y + 2)
+    for side, ref in ((mine, own_hbm), (jnp.bitwise_xor(mine, 1), other_hbm)):
+        for m, base in enumerate((y, y + 1, y + 7, far)):
+            for i in range(2):
+                row = (base + 4 * i) % 8 * 8
+                for j in range(4):
+                    block = pl.ds((m * 8 + i * 4 + j) * 16, 16)
+                    place = row + jnp.bitwise_xor(side, 2 * j)
+                    second.append(
+                        pltpu.make_async_copy(
+                            ref.at[block], weights_ref.at[place], sem.at[5 + len(second)]
+                        )
+                    )
     for copy in first + second:
         copy.start()
     half = NXY // 2
@@ -360,7 +335,7 @@
     cy = courant_along * jnp.abs(vy)
     upwind = vy > 0.0
     col = lax.broadcasted_iota(jnp.int32, (COLS, NXY), 0)
-    core = core_ref[0]
+    core = mine % 2
     for copy in first:
         copy.wait()
     inner = inner_ref[...].astype(F32)
@@ -390,7 +365,10 @@
     for copy in second:
         copy.wait()
     mixed = jnp.concatenate([back_ref[v] for v in range(GROUP)], axis=1)
-    collision = jnp.dot(mixed, weights_ref[...], preferred_element_type=F32)
+    weights = weights_ref[...].reshape(NXY, NXY)
+    collision = lax.dot_general(
+        mixed, weights, (((1,), (1,)), ((), ())), preferred_element_type=F32
+    )
     stores = []
     for p in range(PLANES):
         for r in range(ROWS):
@@ -408,8 +386,8 @@
         copy.wait()
 
 
-def advance(core, f, back, weights, below, above, inner, outer):
-    weights = pltpu.with_memory_space_constraint(weights, pltpu.HBM)
+def advance(where, f, back, own, other, below, above, outer):
+    own, other = (pltpu.with_memory_space_constraint(x, pltpu.HBM) for x in (own, other))
     return pl.pallas_call(
         advance_kernel,
         out_shape=jax.ShapeDtypeStruct(f.shape, BF16),
@@ -418,19 +396,19 @@
         scratch_shapes=[
             pltpu.VMEM(f.shape, BF16),
             pltpu.VMEM(back.shape, BF16),
-            pltpu.VMEM(weights.shape, BF16),
+            pltpu.VMEM((NXY // 16, 16, NXY), BF16),
             pltpu.VMEM((2 * COLS, NXY), BF16),
             pltpu.VMEM((2 * COLS, NXY), BF16),
-            pltpu.VMEM(inner.shape, BF16),
+            pltpu.VMEM((16, NXY), BF16),
             pltpu.VMEM((16, NXY), BF16),
             pltpu.VMEM((DATA, NXY), F32),
             pltpu.VMEM(f.shape, BF16),
-            pltpu.SemaphoreType.DMA((7,)),
+            pltpu.SemaphoreType.DMA((6 + NXY // 16,)),
             pltpu.SemaphoreType.DMA((PLANES,)),
         ],
         compiler_params=pltpu.CompilerParams(vmem_limit_bytes=LIMIT),
         name="advance",
-    )(core, f, back, weights, below, above, inner, outer)
+    )(where, f, back, own, other, below, above, outer)
 
 
 def ring(axis, step):
@@ -457,9 +435,8 @@
     send = relax(place, got, spread(depth_weights))
     own = join(held, above, below, across, inner)
     other = lax.ppermute(own, "sy", flip(1))
-    weights, inner = assemble(where, own, other)
     back = lax.all_to_all(send, "vel", 0, 0, tiled=True)
-    return advance(core, distribution, back, weights, below, above, inner, outer)
+    return advance(where, distribution, back, own, other, below, above, outer)
 
 
 def solution(mesh):

time: 87.8 us -> 87.3 us (level)
  Pallas kernels: 14.8 us -> 12.8 us
  waiting for transfers between devices: 17.8 us -> 19.4 us
    pallas_call x2 -> x1, Pallas kernels: 4.46 us -> 1.04 us  [join(): pl.pallas_call(join_kernel, out_shape=pltpu.HBM((4 * held.shape[0] + 16,...]
    ppermute x1, waiting for transfers between devices: 0.01 us -> 1.64 us  [local(): lax.ppermute(outer, 'sy', [(i, (i + 1) % 8 if i % 2 else (i - 1) % 8) for...]
    pallas_call x1, Pallas kernels: 3.86 us -> 5.23 us  [advance(): pl.pallas_call(advance_kernel, out_shape=jax.ShapeDtypeStruct(f.shape, BF...]
  transfers between devices with their start and end apart: 10 -> 10, of which waited for: 3 -> 4; matrix products, arithmetic and copies ran while one was open for 0% -> 0% of each run, Pallas kernels for 13% -> 9%
where the time goes in v11:
time: 87.3 us; the launch traced here: 85.9 us
  starting transfers between devices  52.7 us (60%)
  waiting for transfers between devices  19.4 us (22%)
  Pallas kernels  12.8 us (15%)
    all_to_all x1, starting transfers between devices, local(): got = lax.all_to_all(send, 'vel', 0, 0, tiled=True)  10.7 us
    all_to_all x1, starting transfers between devices, local(): back = lax.all_to_all(send, 'vel', 0, 0, tiled=True)  9.73 us
    ppermute x1, waiting for transfers between devices, local(): lax.ppermute(held, 'sx', [(i, (i + 2) % 8 if i % 2 == 0 else (i - 2) % 8)...  8.22 us
    ppermute x1, waiting for transfers between devices, local(): held = jnp.concatenate([held, lax.ppermute(held, 'sx', flip(4))])  7.43 us
    ppermute x1, starting transfers between devices, local(): held = jnp.concatenate([held, lax.ppermute(held, 'sy', flip(4))])  6.08 us
    ppermute x1, starting transfers between devices, local(): lax.ppermute(outer, 'sy', [(i, (i + 1) % 8 if i % 2 else (i - 1) % 8) for...  5.91 us
    pallas_call x1, Pallas kernels, advance(): pl.pallas_call(advance_kernel, out_shape=jax.ShapeDtypeStruct(f.shape, BF...  5.23 us
    ppermute x1, starting transfers between devices, local(): held = jnp.concatenate([held, lax.ppermute(held, 'sx', flip(4))])  4.71 us
  transfers between devices with their start and end apart: 10, of which 4 were waited for; matrix products, arithmetic and copies ran while one was open for 0% of the time, Pallas kernels for 9%

profile of v11, /device:TPU:56, one launch (start us, length us, event | category | flops | bytes accessed | tf_op | source)
XLA Modules:
  0.0 85.9 jit_solution(17592191990401430026)
XLA Ops:
  0.0 0.0 copy-start.2
  0.0 4.4 %collective-permute-start = (bf16[16,1024]{1,0:T(8,128)(2,1)}, bf16[16,1024]{1,0:T(8,128)(2,1)S(1)}, u32[]{:S(2)}, u32[]{:S(2)}) collective-permute-start(bf16[16,1024]{1,0:T(8,128)(2,1)} %param.5), channel_id=1, source_target_pairs={{0,2},{1,3},{2,0},{3,1},{4,6},{5,7},{6,4},{7,5},{8,10},{9,11},{10,... | collective-permute-start | bytes 98312 | tf_op jit(solution)/shard_map/ppermute | solution.py:425
  4.4 2.1 %collective-permute-done = bf16[16,1024]{1,0:T(8,128)(2,1)S(1)} collective-permute-done((bf16[16,1024]{1,0:T(8,128)(2,1)}, bf16[16,1024]{1,0:T(8,128)(2,1)S(1)}, u32[]{:S(2)}, u32[]{:S(2)}) %collective-permute-start) | collective-permute-done | bytes 32800 | tf_op jit(solution)/shard_map/ppermute | solution.py:425
  6.5 0.8 pad_maximum_fusion.1
  7.3 6.1 %collective-permute-start.1 = (bf16[32,1024]{1,0:T(8,128)(2,1)S(1)}, bf16[32,1024]{1,0:T(8,128)(2,1)S(1)}, u32[]{:S(2)}, u32[]{:S(2)}) collective-permute-start(bf16[32,1024]{1,0:T(8,128)(2,1)S(1)} %pad_maximum_fusion.1), channel_id=1, source_target_pairs={{0,4},{1,5},{2,6},{3,7},{4,0},{5,1},{6,2},{7,3},{8,12},{9,13},{10,... | collective-permute-start | bytes 196616 | tf_op jit(solution)/shard_map/ppermute | solution.py:426
  13.4 2.8 %pack.1 = bf16[8,400,128]{2,1,0:T(8,128)(2,1)} custom-call(s32[1]{0:T(128)} %bitcast.2.place_ref, bf16[3,32,4096]{2,1,0:T(8,128)(2,1)} %f_hbm.1, bf16[1024,128]{1,0:T(8,128)(2,1)} %constant.15.clone.basis_ref), custom_call_target="tpu_custom_call" | custom-call | tf_op jit(solution)/shard_map/pack/pallas_call | solution.py:122
  16.2 0.0 collective-permute-done.1
  16.2 0.0 copy-done.2
  16.2 0.0 copy-start
  16.2 10.7 %all-to-all-start = ((bf16[8,400,128]{2,1,0:T(8,128)(2,1)}), bf16[8,400,128]{2,1,0:T(8,128)(2,1)S(1)}, u32[]{:S(2)}, u32[]{:S(2)}) async-start(bf16[8,400,128]{2,1,0:T(8,128)(2,1)} %pack.1), calls=%async_computation | async-start | bytes 1638400 | tf_op jit(solution)/shard_map/all_to_all | solution.py:428
  27.0 0.0 copy-start.1
  27.0 4.7 %collective-permute-start.2 = (bf16[64,1024]{1,0:T(8,128)(2,1)S(1)}, bf16[64,1024]{1,0:T(8,128)(2,1)S(1)}, u32[]{:S(2)}, u32[]{:S(2)}) collective-permute-start(bf16[64,1024]{1,0:T(8,128)(2,1)S(1)} %pad_maximum_fusion), channel_id=1, source_target_pairs={{0,32},{8,40},{16,48},{24,56},{32,0},{40,8},{48,16},{56,24},{1,33}... | collective-permute-start | bytes 393224 | tf_op jit(solution)/shard_map/ppermute | solution.py:429
  31.7 7.4 %collective-permute-done.2 = bf16[64,1024]{1,0:T(8,128)(2,1)S(1)} collective-permute-done((bf16[64,1024]{1,0:T(8,128)(2,1)S(1)}, bf16[64,1024]{1,0:T(8,128)(2,1)S(1)}, u32[]{:S(2)}, u32[]{:S(2)}) %collective-permute-start.2) | collective-permute-done | bytes 131104 | tf_op jit(solution)/shard_map/ppermute | solution.py:429
  39.2 0.0 copy-done
  39.2 1.0 %edges.1 = (bf16[192,1024]{1,0:T(8,128)(2,1)}, bf16[192,1024]{1,0:T(8,128)(2,1)}, bf16[16,1024]{1,0:T(8,128)(2,1)S(1)}, bf16[16,1024]{1,0:T(8,128)(2,1)S(1)}) custom-call(s32[1]{0:T(128)} %bitcast.3.core_ref, bf16[128,1024]{1,0:T(8,128)(2,1)S(1)} %constant_dynamic-update-slice_fusion.held_ref, bf16[3,32,4096]{2,1,0:T(8,128)(2,1)S(1)} %copy-done), custom_call_target="tpu_custom_call" | custom-call | tf_op jit(solution)/shard_map/edges/pallas_call | solution.py:168
  40.2 2.8 %collective-permute-start.3 = (bf16[192,1024]{1,0:T(8,128)(2,1)}, bf16[192,1024]{1,0:T(8,128)(2,1)S(1)}, u32[]{:S(2)}, u32[]{:S(2)}) collective-permute-start(bf16[192,1024]{1,0:T(8,128)(2,1)} %get-tuple-element.13), channel_id=1, source_target_pairs={{0,56},{8,0},{16,8},{24,16},{32,24},{40,32},{48,40},{56,48},{1,57}... | collective-permute-start | bytes 1179656 | tf_op jit(solution)/shard_map/ppermute | solution.py:431
  42.9 4.3 %collective-permute-start.4 = (bf16[192,1024]{1,0:T(8,128)(2,1)}, bf16[192,1024]{1,0:T(8,128)(2,1)S(1)}, u32[]{:S(2)}, u32[]{:S(2)}) collective-permute-start(bf16[192,1024]{1,0:T(8,128)(2,1)} %get-tuple-element.14), channel_id=1, source_target_pairs={{0,8},{8,16},{16,24},{24,32},{32,40},{40,48},{48,56},{56,0},{1,9},... | collective-permute-start | bytes 1179656 | tf_op jit(solution)/shard_map/ppermute | solution.py:432
  47.2 0.0 copy-done.1
  47.2 0.4 spread.1.mix_ref
  47.6 0.0 all-to-all-done.got_ref
  47.6 2.3 %relax.1 = bf16[8,384,128]{2,1,0:T(8,128)(2,1)} custom-call(s32[1]{0:T(128)} %bitcast.2.place_ref, bf16[8,400,128]{2,1,0:T(8,128)(2,1)S(1)} %all-to-all-done.got_ref, bf16[512,512]{1,0:T(8,128)(2,1)S(1)} %spread.1.mix_ref), custom_call_target="tpu_custom_call" | custom-call | tf_op jit(solution)/shard_map/relax/pallas_call | solution.py:272
  49.9 9.7 %all-to-all-start.1 = ((bf16[8,384,128]{2,1,0:T(8,128)(2,1)}), bf16[8,384,128]{2,1,0:T(8,128)(2,1)S(1)}, u32[]{:S(2)}, u32[]{:S(2)}) async-start(bf16[8,384,128]{2,1,0:T(8,128)(2,1)} %relax.1), calls=%async_computation.1 | async-start | bytes 1572864 | tf_op jit(solution)/shard_map/all_to_all | solution.py:438
  59.7 2.1 %collective-permute-start.5 = (bf16[128,1024]{1,0:T(8,128)(2,1)S(1)}, bf16[128,1024]{1,0:T(8,128)(2,1)S(1)}, u32[]{:S(2)}, u32[]{:S(2)}) collective-permute-start(bf16[128,1024]{1,0:T(8,128)(2,1)S(1)} %constant_dynamic-update-slice_fusion.held_ref), channel_id=1, source_target_pairs={{0,16},{8,56},{16,32},{24,8},{32,48},{40,24},{48,0},{56,40},{1,17}... | collective-permute-start | bytes 786440 | tf_op jit(solution)/shard_map/ppermute | solution.py:433
  61.8 8.2 %collective-permute-done.5.across_ref = bf16[128,1024]{1,0:T(8,128)(2,1)S(1)} collective-permute-done((bf16[128,1024]{1,0:T(8,128)(2,1)S(1)}, bf16[128,1024]{1,0:T(8,128)(2,1)S(1)}, u32[]{:S(2)}, u32[]{:S(2)}) %collective-permute-start.5) | collective-permute-done | bytes 262176 | tf_op jit(solution)/shard_map/ppermute | solution.py:433
  70.0 0.0 collective-permute-done.3.above_ref.above_hbm
  70.0 0.0 collective-permute-done.4.below_ref.below_hbm
  70.0 1.0 %join.1.own_hbm = bf16[528,1024]{1,0:T(8,128)(2,1)} custom-call(bf16[128,1024]{1,0:T(8,128)(2,1)S(1)} %constant_dynamic-update-slice_fusion.held_ref, bf16[192,1024]{1,0:T(8,128)(2,1)S(1)} %collective-permute-done.3.above_ref.above_hbm, bf16[192,1024]{1,0:T(8,128)(2,1)S(1)} %collective-permute-done.4.below_ref.below_hbm, ...), custom_call_target="tpu_custom_call" | custom-call | tf_op jit(solution)/shard_map/join/pallas_call | solution.py:197
  71.1 1.9 %collective-permute-start.6 = (bf16[528,1024]{1,0:T(8,128)(2,1)}, bf16[528,1024]{1,0:T(8,128)(2,1)}, u32[]{:S(2)}, u32[]{:S(2)}) collective-permute-start(bf16[528,1024]{1,0:T(8,128)(2,1)} %join.1.own_hbm), channel_id=1, source_target_pairs={{0,1},{1,0},{2,3},{3,2},{4,5},{5,4},{6,7},{7,6},{8,9},{9,8},{10,11... | collective-permute-start | bytes 3244040 | tf_op jit(solution)/shard_map/ppermute | solution.py:437
  73.0 5.9 %collective-permute-start.7 = (bf16[16,1024]{1,0:T(8,128)(2,1)S(1)}, bf16[16,1024]{1,0:T(8,128)(2,1)S(1)}, u32[]{:S(2)}, u32[]{:S(2)}) collective-permute-start(bf16[16,1024]{1,0:T(8,128)(2,1)S(1)} %get-tuple-element.16), channel_id=1, source_target_pairs={{0,7},{1,2},{2,1},{3,4},{4,3},{5,6},{6,5},{7,0},{8,15},{9,10},{10,... | collective-permute-start | bytes 98312 | tf_op jit(solution)/shard_map/ppermute | solution.py:434
  78.9 0.1 pad_add_fusion.where_ref
  79.0 1.6 %collective-permute-done.7.outer_hbm = bf16[16,1024]{1,0:T(8,128)(2,1)S(1)} collective-permute-done((bf16[16,1024]{1,0:T(8,128)(2,1)S(1)}, bf16[16,1024]{1,0:T(8,128)(2,1)S(1)}, u32[]{:S(2)}, u32[]{:S(2)}) %collective-permute-start.7) | collective-permute-done | bytes 32800 | tf_op jit(solution)/shard_map/ppermute | solution.py:434
  80.6 0.0 collective-permute-done.6.other_hbm
  80.7 0.0 all-to-all-done.1.back_hbm
  80.7 5.2 %advance.1 = bf16[3,32,4096]{2,1,0:T(8,128)(2,1)} custom-call(s32[2]{0:T(128)S(1)} %pad_add_fusion.where_ref, bf16[3,32,4096]{2,1,0:T(8,128)(2,1)S(1)} %copy-done, bf16[8,384,128]{2,1,0:T(8,128)(2,1)S(1)} %all-to-all-done.1.back_hbm, bf16[528,1024]{1,0:T(8,128)(2,1)} %join.1.own_hbm, bf16[528,1024]{1,0:T(8,128)(2,1)} %collective-permute-done.6.other_hbm, ...), custom_call_target="tpu_custom_call" | custom-call | tf_op jit(solution)/shard_map/advance/pallas_call | solution.py:391
  (3 shorter events, 0.0 us)
Async XLA Ops:
  0.0 16.2 %copy-start.2 = (bf16[16,1024]{1,0:T(8,128)(2,1)S(1)}, bf16[16,1024]{1,0:T(8,128)(2,1)}, u32[]{:S(2)}) copy-start(bf16[16,1024]{1,0:T(8,128)(2,1)} %param.5) | copy-start | bytes 98308
  0.0 6.5 %collective-permute-start = (bf16[16,1024]{1,0:T(8,128)(2,1)}, bf16[16,1024]{1,0:T(8,128)(2,1)S(1)}, u32[]{:S(2)}, u32[]{:S(2)}) collective-permute-start(bf16[16,1024]{1,0:T(8,128)(2,1)} %param.5), channel_id=1, source_target_pairs={{0,2},{1,3},{2,0},{3,1},{4,6},{5,7},{6,4},{7,5},{8,10},{9,11},{10,... | collective-permute-start | bytes 98312 | tf_op jit(solution)/shard_map/ppermute | solution.py:425
  7.3 8.9 %collective-permute-start.1 = (bf16[32,1024]{1,0:T(8,128)(2,1)S(1)}, bf16[32,1024]{1,0:T(8,128)(2,1)S(1)}, u32[]{:S(2)}, u32[]{:S(2)}) collective-permute-start(bf16[32,1024]{1,0:T(8,128)(2,1)S(1)} %pad_maximum_fusion.1), channel_id=1, source_target_pairs={{0,4},{1,5},{2,6},{3,7},{4,0},{5,1},{6,2},{7,3},{8,12},{9,13},{10,... | collective-permute-start | bytes 196616 | tf_op jit(solution)/shard_map/ppermute | solution.py:426
  16.2 22.9 %copy-start = (bf16[3,32,4096]{2,1,0:T(8,128)(2,1)S(1)}, bf16[3,32,4096]{2,1,0:T(8,128)(2,1)}, u32[]{:S(2)}) copy-start(bf16[3,32,4096]{2,1,0:T(8,128)(2,1)} %f_hbm.1) | copy-start | bytes 2359300
  16.2 31.4 %all-to-all-start = ((bf16[8,400,128]{2,1,0:T(8,128)(2,1)}), bf16[8,400,128]{2,1,0:T(8,128)(2,1)S(1)}, u32[]{:S(2)}, u32[]{:S(2)}) async-start(bf16[8,400,128]{2,1,0:T(8,128)(2,1)} %pack.1), calls=%async_computation | async-start | bytes 1638400 | tf_op jit(solution)/shard_map/all_to_all | solution.py:428
  27.0 20.2 %copy-start.1 = (bf16[32,32]{1,0:T(8,128)(2,1)S(1)}, bf16[32,32]{1,0:T(8,128)(2,1)}, u32[]{:S(2)}) copy-start(bf16[32,32]{1,0:T(8,128)(2,1)} %depth_ref.1) | copy-start | bytes 6148
  27.0 12.2 %collective-permute-start.2 = (bf16[64,1024]{1,0:T(8,128)(2,1)S(1)}, bf16[64,1024]{1,0:T(8,128)(2,1)S(1)}, u32[]{:S(2)}, u32[]{:S(2)}) collective-permute-start(bf16[64,1024]{1,0:T(8,128)(2,1)S(1)} %pad_maximum_fusion), channel_id=1, source_target_pairs={{0,32},{8,40},{16,48},{24,56},{32,0},{40,8},{48,16},{56,24},{1,33}... | collective-permute-start | bytes 393224 | tf_op jit(solution)/shard_map/ppermute | solution.py:429
  40.2 29.9 %collective-permute-start.3 = (bf16[192,1024]{1,0:T(8,128)(2,1)}, bf16[192,1024]{1,0:T(8,128)(2,1)S(1)}, u32[]{:S(2)}, u32[]{:S(2)}) collective-permute-start(bf16[192,1024]{1,0:T(8,128)(2,1)} %get-tuple-element.13), channel_id=1, source_target_pairs={{0,56},{8,0},{16,8},{24,16},{32,24},{40,32},{48,40},{56,48},{1,57}... | collective-permute-start | bytes 1179656 | tf_op jit(solution)/shard_map/ppermute | solution.py:431
  42.9 27.1 %collective-permute-start.4 = (bf16[192,1024]{1,0:T(8,128)(2,1)}, bf16[192,1024]{1,0:T(8,128)(2,1)S(1)}, u32[]{:S(2)}, u32[]{:S(2)}) collective-permute-start(bf16[192,1024]{1,0:T(8,128)(2,1)} %get-tuple-element.14), channel_id=1, source_target_pairs={{0,8},{8,16},{16,24},{24,32},{32,40},{40,48},{48,56},{56,0},{1,9},... | collective-permute-start | bytes 1179656 | tf_op jit(solution)/shard_map/ppermute | solution.py:432
  49.9 30.7 %all-to-all-start.1 = ((bf16[8,384,128]{2,1,0:T(8,128)(2,1)}), bf16[8,384,128]{2,1,0:T(8,128)(2,1)S(1)}, u32[]{:S(2)}, u32[]{:S(2)}) async-start(bf16[8,384,128]{2,1,0:T(8,128)(2,1)} %relax.1), calls=%async_computation.1 | async-start | bytes 1572864 | tf_op jit(solution)/shard_map/all_to_all | solution.py:438
  59.7 10.4 %collective-permute-start.5 = (bf16[128,1024]{1,0:T(8,128)(2,1)S(1)}, bf16[128,1024]{1,0:T(8,128)(2,1)S(1)}, u32[]{:S(2)}, u32[]{:S(2)}) collective-permute-start(bf16[128,1024]{1,0:T(8,128)(2,1)S(1)} %constant_dynamic-update-slice_fusion.held_ref), channel_id=1, source_target_pairs={{0,16},{8,56},{16,32},{24,8},{32,48},{40,24},{48,0},{56,40},{1,17}... | collective-permute-start | bytes 786440 | tf_op jit(solution)/shard_map/ppermute | solution.py:433
  71.1 9.6 %collective-permute-start.6 = (bf16[528,1024]{1,0:T(8,128)(2,1)}, bf16[528,1024]{1,0:T(8,128)(2,1)}, u32[]{:S(2)}, u32[]{:S(2)}) collective-permute-start(bf16[528,1024]{1,0:T(8,128)(2,1)} %join.1.own_hbm), channel_id=1, source_target_pairs={{0,1},{1,0},{2,3},{3,2},{4,5},{5,4},{6,7},{7,6},{8,9},{9,8},{10,11... | collective-permute-start | bytes 3244040 | tf_op jit(solution)/shard_map/ppermute | solution.py:437
  73.0 7.6 %collective-permute-start.7 = (bf16[16,1024]{1,0:T(8,128)(2,1)S(1)}, bf16[16,1024]{1,0:T(8,128)(2,1)S(1)}, u32[]{:S(2)}, u32[]{:S(2)}) collective-permute-start(bf16[16,1024]{1,0:T(8,128)(2,1)S(1)} %get-tuple-element.16), channel_id=1, source_target_pairs={{0,7},{1,2},{2,1},{3,4},{4,3},{5,6},{6,5},{7,0},{8,15},{9,10},{10,... | collective-permute-start | bytes 98312 | tf_op jit(solution)/shard_map/ppermute | solution.py:434

commit v12 on v11

--- a/solution.py
+++ b/solution.py
@@ -137,7 +137,53 @@
     )(place, f, basis)
 
 
-def edges_kernel(core_ref, held_ref, f_ref, low_ref, high_ref, inner_ref, outer_ref):
+def columns_kernel(core_ref, f_hbm, shard_hbm, pack_ref, inner_ref, first_ref, last_ref, sem):
+    shard = shard_hbm.shape[0]
+    copies = [
+        pltpu.make_async_copy(f_hbm.at[:, pl.ds(0, 8), :], first_ref, sem.at[0]),
+        pltpu.make_async_copy(f_hbm.at[:, pl.ds(COLS - 8, 8), :], last_ref, sem.at[1]),
+        pltpu.make_async_copy(shard_hbm, pack_ref.at[pl.ds(0, shard)], sem.at[2]),
+    ]
+    for copy in copies:
+        copy.start()
+    edge_row = lax.broadcasted_iota(jnp.int32, (16, NXY), 0)
+    first = jnp.zeros((16, NXY), F32)
+    last = jnp.zeros((16, NXY), F32)
+    for copy in copies:
+        copy.wait()
+    for r in range(ROWS):
+        for p in range(PLANES):
+            lanes = slice(p * NXY, (p + 1) * NXY)
+            a = first_ref[r, :, lanes].astype(F32)[0:1, :]
+            b = last_ref[r, :, lanes].astype(F32)[7:8, :]
+            first = jnp.where(edge_row == r * PLANES + p, a, first)
+            last = jnp.where(edge_row == r * PLANES + p, b, last)
+    core = core_ref[0]
+    inner_ref[...] = jnp.where(core == 0, last, first).astype(BF16)
+    pack_ref[shard : shard + 16, :] = jnp.where(core == 0, first, last).astype(BF16)
+
+
+def columns(core, f, shard):
+    f, shard = (pltpu.with_memory_space_constraint(x, pltpu.HBM) for x in (f, shard))
+    return pl.pallas_call(
+        columns_kernel,
+        out_shape=(
+            jax.ShapeDtypeStruct((shard.shape[0] + 16, NXY), BF16),
+            jax.ShapeDtypeStruct((16, NXY), BF16),
+        ),
+        in_specs=[smem(), hbm(), hbm()],
+        out_specs=(vmem(), vmem()),
+        scratch_shapes=[
+            pltpu.VMEM((ROWS, 8, PLANES * NXY), BF16),
+            pltpu.VMEM((ROWS, 8, PLANES * NXY), BF16),
+            pltpu.SemaphoreType.DMA((3,)),
+        ],
+        compiler_params=pltpu.CompilerParams(vmem_limit_bytes=LIMIT),
+        name="columns",
+    )(core, f, shard)
+
+
+def edges_kernel(held_ref, f_ref, low_ref, high_ref):
     half = NXY // 2
     size = held_ref.shape[0]
     low_ref[0:size, :] = held_ref[...]
@@ -147,32 +193,18 @@
         lanes = slice(p % 2 * half, (p % 2 + 1) * half)
         high_ref[rows, lanes] = f_ref[ROWS - 1, :, p * NXY + half : (p + 1) * NXY]
         low_ref[rows, lanes] = f_ref[0, :, p * NXY : p * NXY + half]
-    edge_row = lax.broadcasted_iota(jnp.int32, (16, NXY), 0)
-    first = jnp.zeros((16, NXY), F32)
-    last = jnp.zeros((16, NXY), F32)
-    for r in range(ROWS):
-        for p in range(PLANES):
-            lanes = slice(p * NXY, (p + 1) * NXY)
-            a = f_ref[r, 0:8, lanes].astype(F32)[0:1, :]
-            b = f_ref[r, COLS - 8 : COLS, lanes].astype(F32)[7:8, :]
-            first = jnp.where(edge_row == r * PLANES + p, a, first)
-            last = jnp.where(edge_row == r * PLANES + p, b, last)
-    core = core_ref[0]
-    inner_ref[...] = jnp.where(core == 0, last, first).astype(BF16)
-    outer_ref[...] = jnp.where(core == 0, first, last).astype(BF16)
-
-
-def edges(core, held, f):
+
+
+def edges(held, f):
     row = jax.ShapeDtypeStruct((held.shape[0] + 2 * COLS, NXY), BF16)
-    column = jax.ShapeDtypeStruct((16, NXY), BF16)
     return pl.pallas_call(
         edges_kernel,
-        out_shape=(row, row, column, column),
-        in_specs=[smem(), vmem(), vmem()],
-        out_specs=(vmem(),) * 4,
+        out_shape=(row, row),
+        in_specs=[vmem(), vmem()],
+        out_specs=(vmem(), vmem()),
         compiler_params=pltpu.CompilerParams(vmem_limit_bytes=LIMIT),
         name="edges",
-    )(core, held, f)
+    )(held, f)
 
 
 def join_kernel(held_ref, above_ref, below_ref, across_ref, inner_ref, out_ref, sem):
@@ -314,12 +346,15 @@
     mine, y = where_ref[0], where_ref[1]
     far = jnp.where(y % 2 == 0, y + 6, y + 2)
     for side, ref in ((mine, own_hbm), (jnp.bitwise_xor(mine, 1), other_hbm)):
+        turn = jnp.bitwise_xor(side, 4)
+        step = jnp.where(side % 2 == 1, 1, 7)
+        places = (side, (side + step) % 8, turn, (turn + step) % 8)
         for m, base in enumerate((y, y + 1, y + 7, far)):
             for i in range(2):
                 row = (base + 4 * i) % 8 * 8
                 for j in range(4):
                     block = pl.ds((m * 8 + i * 4 + j) * 16, 16)
-                    place = row + jnp.bitwise_xor(side, 2 * j)
+                    place = row + places[j]
                     second.append(
                         pltpu.make_async_copy(
                             ref.at[block], weights_ref.at[place], sem.at[5 + len(second)]
@@ -422,16 +457,17 @@
     core = jnp.bitwise_and(along, 1).reshape(1)
     where = jnp.stack([along, lax.axis_index("sx").astype(jnp.int32)])
     flip = lambda bit: [(i, i ^ bit) for i in range(8)]
-    held = jnp.concatenate([plane_weights, lax.ppermute(plane_weights, "sy", flip(2))])
+    bundle, inner = columns(core, distribution, plane_weights)
+    outer = lax.ppermute(bundle, "sy", [(i, (i + 1) % 8 if i % 2 else (i - 1) % 8) for i in range(8)])
+    held = jnp.concatenate([plane_weights, outer[: plane_weights.shape[0]]])
     held = jnp.concatenate([held, lax.ppermute(held, "sy", flip(4))])
     send, held = lax.optimization_barrier((pack(place, distribution), held))
     got = lax.all_to_all(send, "vel", 0, 0, tiled=True)
     held = jnp.concatenate([held, lax.ppermute(held, "sx", flip(4))])
-    low, high, inner, outer = edges(core, held, distribution)
+    low, high = edges(held, distribution)
     above = lax.ppermute(low, "sx", ring("sx", -1))
     below = lax.ppermute(high, "sx", ring("sx", 1))
     across = lax.ppermute(held, "sx", [(i, (i + 2) % 8 if i % 2 == 0 else (i - 2) % 8) for i in range(8)])
-    outer = lax.ppermute(outer, "sy", [(i, (i + 1) % 8 if i % 2 else (i - 1) % 8) for i in range(8)])
     send = relax(place, got, spread(depth_weights))
     own = join(held, above, below, across, inner)
     other = lax.ppermute(own, "sy", flip(1))

time: 87.3 us -> 92.4 us (1.058)
  the two profiles are of different devices: /device:TPU:56 before, /device:TPU:64 now
where the time goes in v12:
time: 92.4 us; the launch traced here: 91.7 us
  starting transfers between devices  46.6 us (50%)
  waiting for transfers between devices  30.1 us (33%)
  Pallas kernels  13.9 us (15%)
    all_to_all x1, starting transfers between devices, local(): got = lax.all_to_all(send, 'vel', 0, 0, tiled=True)  10.6 us
    ppermute x1, starting transfers between devices, local(): held = jnp.concatenate([held, lax.ppermute(held, 'sx', flip(4))])  7.73 us
    ppermute x1, waiting for transfers between devices, local(): lax.ppermute(held, 'sx', [(i, (i + 2) % 8 if i % 2 == 0 else (i - 2) % 8)...  7.67 us
    ppermute x1, starting transfers between devices, local(): above = lax.ppermute(low, 'sx', ring('sx', -1))  7.53 us
    all_to_all x1, waiting for transfers between devices, local(): back = lax.all_to_all(send, 'vel', 0, 0, tiled=True)  7.47 us
    ppermute x1, starting transfers between devices, local(): held = jnp.concatenate([held, lax.ppermute(held, 'sy', flip(4))])  6.08 us
    all_to_all x1, starting transfers between devices, local(): back = lax.all_to_all(send, 'vel', 0, 0, tiled=True)  5.45 us
    pallas_call x1, Pallas kernels, advance(): pl.pallas_call(advance_kernel, out_shape=jax.ShapeDtypeStruct(f.shape, BF...  5.29 us
  transfers between devices with their start and end apart: 9, of which 6 were waited for; matrix products, arithmetic and copies ran while one was open for 0% of the time, Pallas kernels for 8%

profile of v12, /device:TPU:64, one launch (start us, length us, event | category | flops | bytes accessed | tf_op | source)
XLA Modules:
  0.0 91.7 jit_solution(9874603705778390385)
XLA Ops:
  0.0 1.1 %columns.1 = (bf16[32,1024]{1,0:T(8,128)(2,1)S(1)}, bf16[16,1024]{1,0:T(8,128)(2,1)S(1)}) custom-call(s32[1]{0:T(128)} %bitcast.3.core_ref, bf16[3,32,4096]{2,1,0:T(8,128)(2,1)} %f_hbm.3, bf16[16,1024]{1,0:T(8,128)(2,1)} %shard_hbm.1), custom_call_target="tpu_custom_call" | custom-call | tf_op jit(solution)/shard_map/columns/pallas_call | solution.py:168
  1.1 0.0 copy-start.2
  1.2 1.9 %collective-permute-start = (bf16[32,1024]{1,0:T(8,128)(2,1)S(1)}, bf16[32,1024]{1,0:T(8,128)(2,1)S(1)}, u32[]{:S(2)}, u32[]{:S(2)}) collective-permute-start(bf16[32,1024]{1,0:T(8,128)(2,1)S(1)} %get-tuple-element.11), channel_id=1, source_target_pairs={{0,7},{1,2},{2,1},{3,4},{4,3},{5,6},{6,5},{7,0},{8,15},{9,10},{10,... | collective-permute-start | bytes 196616 | tf_op jit(solution)/shard_map/ppermute | solution.py:461
  3.1 3.7 %collective-permute-done.outer_hbm = bf16[32,1024]{1,0:T(8,128)(2,1)S(1)} collective-permute-done((bf16[32,1024]{1,0:T(8,128)(2,1)S(1)}, bf16[32,1024]{1,0:T(8,128)(2,1)S(1)}, u32[]{:S(2)}, u32[]{:S(2)}) %collective-permute-start) | collective-permute-done | bytes 65568 | tf_op jit(solution)/shard_map/ppermute | solution.py:461
  6.7 0.8 pad_maximum_fusion.1
  7.5 6.1 %collective-permute-start.1 = (bf16[32,1024]{1,0:T(8,128)(2,1)S(1)}, bf16[32,1024]{1,0:T(8,128)(2,1)S(1)}, u32[]{:S(2)}, u32[]{:S(2)}) collective-permute-start(bf16[32,1024]{1,0:T(8,128)(2,1)S(1)} %pad_maximum_fusion.1), channel_id=1, source_target_pairs={{0,4},{1,5},{2,6},{3,7},{4,0},{5,1},{6,2},{7,3},{8,12},{9,13},{10,... | collective-permute-start | bytes 196616 | tf_op jit(solution)/shard_map/ppermute | solution.py:463
  13.6 2.8 %pack.1 = bf16[8,400,128]{2,1,0:T(8,128)(2,1)} custom-call(s32[1]{0:T(128)} %bitcast.2.place_ref, bf16[3,32,4096]{2,1,0:T(8,128)(2,1)} %f_hbm.3, bf16[1024,128]{1,0:T(8,128)(2,1)} %constant.15.clone.basis_ref), custom_call_target="tpu_custom_call" | custom-call | tf_op jit(solution)/shard_map/pack/pallas_call | solution.py:122
  16.4 0.0 collective-permute-done.1
  16.4 0.0 copy-done.2
  16.5 0.0 copy-start
  16.5 10.6 %all-to-all-start = ((bf16[8,400,128]{2,1,0:T(8,128)(2,1)}), bf16[8,400,128]{2,1,0:T(8,128)(2,1)S(1)}, u32[]{:S(2)}, u32[]{:S(2)}) async-start(bf16[8,400,128]{2,1,0:T(8,128)(2,1)} %pack.1), calls=%async_computation | async-start | bytes 1638400 | tf_op jit(solution)/shard_map/all_to_all | solution.py:465
  27.1 0.0 copy-start.1
  27.1 7.7 %collective-permute-start.2 = (bf16[64,1024]{1,0:T(8,128)(2,1)S(1)}, bf16[64,1024]{1,0:T(8,128)(2,1)S(1)}, u32[]{:S(2)}, u32[]{:S(2)}) collective-permute-start(bf16[64,1024]{1,0:T(8,128)(2,1)S(1)} %pad_maximum_fusion), channel_id=1, source_target_pairs={{0,32},{8,40},{16,48},{24,56},{32,0},{40,8},{48,16},{56,24},{1,33}... | collective-permute-start | bytes 393224 | tf_op jit(solution)/shard_map/ppermute | solution.py:466
  34.9 4.3 %collective-permute-done.2 = bf16[64,1024]{1,0:T(8,128)(2,1)S(1)} collective-permute-done((bf16[64,1024]{1,0:T(8,128)(2,1)S(1)}, bf16[64,1024]{1,0:T(8,128)(2,1)S(1)}, u32[]{:S(2)}, u32[]{:S(2)}) %collective-permute-start.2) | collective-permute-done | bytes 131104 | tf_op jit(solution)/shard_map/ppermute | solution.py:466
  39.3 0.0 copy-done
  39.3 0.9 %edges.1 = (bf16[192,1024]{1,0:T(8,128)(2,1)}, bf16[192,1024]{1,0:T(8,128)(2,1)}) custom-call(bf16[128,1024]{1,0:T(8,128)(2,1)S(1)} %constant_dynamic-update-slice_fusion.held_ref, bf16[3,32,4096]{2,1,0:T(8,128)(2,1)S(1)} %copy-done), custom_call_target="tpu_custom_call" | custom-call | tf_op jit(solution)/shard_map/edges/pallas_call | solution.py:200
  40.2 7.5 %collective-permute-start.3 = (bf16[192,1024]{1,0:T(8,128)(2,1)}, bf16[192,1024]{1,0:T(8,128)(2,1)S(1)}, u32[]{:S(2)}, u32[]{:S(2)}) collective-permute-start(bf16[192,1024]{1,0:T(8,128)(2,1)} %get-tuple-element.14), channel_id=1, source_target_pairs={{0,56},{8,0},{16,8},{24,16},{32,24},{40,32},{48,40},{56,48},{1,57}... | collective-permute-start | bytes 1179656 | tf_op jit(solution)/shard_map/ppermute | solution.py:468
  47.8 1.9 %collective-permute-start.4 = (bf16[192,1024]{1,0:T(8,128)(2,1)}, bf16[192,1024]{1,0:T(8,128)(2,1)S(1)}, u32[]{:S(2)}, u32[]{:S(2)}) collective-permute-start(bf16[192,1024]{1,0:T(8,128)(2,1)} %get-tuple-element.15), channel_id=1, source_target_pairs={{0,8},{8,16},{16,24},{24,32},{32,40},{40,48},{48,56},{56,0},{1,9},... | collective-permute-start | bytes 1179656 | tf_op jit(solution)/shard_map/ppermute | solution.py:469
  49.7 0.0 copy-done.1
  49.7 0.4 spread.1.mix_ref
  50.1 4.0 %all-to-all-done.got_ref = bf16[8,400,128]{2,1,0:T(8,128)(2,1)S(1)} async-done(((bf16[8,400,128]{2,1,0:T(8,128)(2,1)}), bf16[8,400,128]{2,1,0:T(8,128)(2,1)S(1)}, u32[]{:S(2)}, u32[]{:S(2)}) %all-to-all-start) | async-done | bytes 819232 | tf_op jit(solution)/shard_map/all_to_all | solution.py:465
  54.1 2.3 %relax.1 = bf16[8,384,128]{2,1,0:T(8,128)(2,1)} custom-call(s32[1]{0:T(128)} %bitcast.2.place_ref, bf16[8,400,128]{2,1,0:T(8,128)(2,1)S(1)} %all-to-all-done.got_ref, bf16[512,512]{1,0:T(8,128)(2,1)S(1)} %spread.1.mix_ref), custom_call_target="tpu_custom_call" | custom-call | tf_op jit(solution)/shard_map/relax/pallas_call | solution.py:304
  56.4 5.5 %all-to-all-start.1 = ((bf16[8,384,128]{2,1,0:T(8,128)(2,1)}), bf16[8,384,128]{2,1,0:T(8,128)(2,1)S(1)}, u32[]{:S(2)}, u32[]{:S(2)}) async-start(bf16[8,384,128]{2,1,0:T(8,128)(2,1)} %relax.1), calls=%async_computation.1 | async-start | bytes 1572864 | tf_op jit(solution)/shard_map/all_to_all | solution.py:474
  61.8 3.4 %collective-permute-start.5 = (bf16[128,1024]{1,0:T(8,128)(2,1)S(1)}, bf16[128,1024]{1,0:T(8,128)(2,1)S(1)}, u32[]{:S(2)}, u32[]{:S(2)}) collective-permute-start(bf16[128,1024]{1,0:T(8,128)(2,1)S(1)} %constant_dynamic-update-slice_fusion.held_ref), channel_id=1, source_target_pairs={{0,16},{8,56},{16,32},{24,8},{32,48},{40,24},{48,0},{56,40},{1,17}... | collective-permute-start | bytes 786440 | tf_op jit(solution)/shard_map/ppermute | solution.py:470
  65.3 7.7 %collective-permute-done.5.across_ref = bf16[128,1024]{1,0:T(8,128)(2,1)S(1)} collective-permute-done((bf16[128,1024]{1,0:T(8,128)(2,1)S(1)}, bf16[128,1024]{1,0:T(8,128)(2,1)S(1)}, u32[]{:S(2)}, u32[]{:S(2)}) %collective-permute-start.5) | collective-permute-done | bytes 262176 | tf_op jit(solution)/shard_map/ppermute | solution.py:470
  73.0 0.0 collective-permute-done.3.above_ref.above_hbm
  73.0 0.0 collective-permute-done.4.below_ref.below_hbm
  73.0 1.0 %join.1.own_hbm = bf16[528,1024]{1,0:T(8,128)(2,1)} custom-call(bf16[128,1024]{1,0:T(8,128)(2,1)S(1)} %constant_dynamic-update-slice_fusion.held_ref, bf16[192,1024]{1,0:T(8,128)(2,1)S(1)} %collective-permute-done.3.above_ref.above_hbm, bf16[192,1024]{1,0:T(8,128)(2,1)S(1)} %collective-permute-done.4.below_ref.below_hbm, ...), custom_call_target="tpu_custom_call" | custom-call | tf_op jit(solution)/shard_map/join/pallas_call | solution.py:229
  74.0 1.9 %collective-permute-start.6 = (bf16[528,1024]{1,0:T(8,128)(2,1)}, bf16[528,1024]{1,0:T(8,128)(2,1)}, u32[]{:S(2)}, u32[]{:S(2)}) collective-permute-start(bf16[528,1024]{1,0:T(8,128)(2,1)} %join.1.own_hbm), channel_id=1, source_target_pairs={{0,1},{1,0},{2,3},{3,2},{4,5},{5,4},{6,7},{7,6},{8,9},{9,8},{10,11... | collective-permute-start | bytes 3244040 | tf_op jit(solution)/shard_map/ppermute | solution.py:473
  76.0 0.1 pad_add_fusion.where_ref
  76.0 2.9 %collective-permute-done.6.other_hbm = bf16[528,1024]{1,0:T(8,128)(2,1)} collective-permute-done((bf16[528,1024]{1,0:T(8,128)(2,1)}, bf16[528,1024]{1,0:T(8,128)(2,1)}, u32[]{:S(2)}, u32[]{:S(2)}) %collective-permute-start.6) | collective-permute-done | bytes 1081376 | tf_op jit(solution)/shard_map/ppermute | solution.py:473
  79.0 7.5 %all-to-all-done.1.back_hbm = bf16[8,384,128]{2,1,0:T(8,128)(2,1)S(1)} async-done(((bf16[8,384,128]{2,1,0:T(8,128)(2,1)}), bf16[8,384,128]{2,1,0:T(8,128)(2,1)S(1)}, u32[]{:S(2)}, u32[]{:S(2)}) %all-to-all-start.1) | async-done | bytes 786464 | tf_op jit(solution)/shard_map/all_to_all | solution.py:474
  86.4 5.3 %advance.1 = bf16[3,32,4096]{2,1,0:T(8,128)(2,1)} custom-call(s32[2]{0:T(128)S(1)} %pad_add_fusion.where_ref, bf16[3,32,4096]{2,1,0:T(8,128)(2,1)S(1)} %copy-done, bf16[8,384,128]{2,1,0:T(8,128)(2,1)S(1)} %all-to-all-done.1.back_hbm, bf16[528,1024]{1,0:T(8,128)(2,1)} %join.1.own_hbm, bf16[528,1024]{1,0:T(8,128)(2,1)} %collective-permute-done.6.other_hbm, ...), custom_call_target="tpu_custom_call" | custom-call | tf_op jit(solution)/shard_map/advance/pallas_call | solution.py:426
  (4 shorter events, 0.0 us)
Async XLA Ops:
  1.1 15.3 %copy-start.2 = (bf16[16,1024]{1,0:T(8,128)(2,1)S(1)}, bf16[16,1024]{1,0:T(8,128)(2,1)}, u32[]{:S(2)}) copy-start(bf16[16,1024]{1,0:T(8,128)(2,1)} %shard_hbm.1) | copy-start | bytes 98308
  1.2 5.6 %collective-permute-start = (bf16[32,1024]{1,0:T(8,128)(2,1)S(1)}, bf16[32,1024]{1,0:T(8,128)(2,1)S(1)}, u32[]{:S(2)}, u32[]{:S(2)}) collective-permute-start(bf16[32,1024]{1,0:T(8,128)(2,1)S(1)} %get-tuple-element.11), channel_id=1, source_target_pairs={{0,7},{1,2},{2,1},{3,4},{4,3},{5,6},{6,5},{7,0},{8,15},{9,10},{10,... | collective-permute-start | bytes 196616 | tf_op jit(solution)/shard_map/ppermute | solution.py:461
  7.5 8.9 %collective-permute-start.1 = (bf16[32,1024]{1,0:T(8,128)(2,1)S(1)}, bf16[32,1024]{1,0:T(8,128)(2,1)S(1)}, u32[]{:S(2)}, u32[]{:S(2)}) collective-permute-start(bf16[32,1024]{1,0:T(8,128)(2,1)S(1)} %pad_maximum_fusion.1), channel_id=1, source_target_pairs={{0,4},{1,5},{2,6},{3,7},{4,0},{5,1},{6,2},{7,3},{8,12},{9,13},{10,... | collective-permute-start | bytes 196616 | tf_op jit(solution)/shard_map/ppermute | solution.py:463
  16.5 22.8 %copy-start = (bf16[3,32,4096]{2,1,0:T(8,128)(2,1)S(1)}, bf16[3,32,4096]{2,1,0:T(8,128)(2,1)}, u32[]{:S(2)}) copy-start(bf16[3,32,4096]{2,1,0:T(8,128)(2,1)} %f_hbm.3) | copy-start | bytes 2359300
  16.5 37.6 %all-to-all-start = ((bf16[8,400,128]{2,1,0:T(8,128)(2,1)}), bf16[8,400,128]{2,1,0:T(8,128)(2,1)S(1)}, u32[]{:S(2)}, u32[]{:S(2)}) async-start(bf16[8,400,128]{2,1,0:T(8,128)(2,1)} %pack.1), calls=%async_computation | async-start | bytes 1638400 | tf_op jit(solution)/shard_map/all_to_all | solution.py:465
  27.1 22.5 %copy-start.1 = (bf16[32,32]{1,0:T(8,128)(2,1)S(1)}, bf16[32,32]{1,0:T(8,128)(2,1)}, u32[]{:S(2)}) copy-start(bf16[32,32]{1,0:T(8,128)(2,1)} %depth_ref.1) | copy-start | bytes 6148
  27.1 12.1 %collective-permute-start.2 = (bf16[64,1024]{1,0:T(8,128)(2,1)S(1)}, bf16[64,1024]{1,0:T(8,128)(2,1)S(1)}, u32[]{:S(2)}, u32[]{:S(2)}) collective-permute-start(bf16[64,1024]{1,0:T(8,128)(2,1)S(1)} %pad_maximum_fusion), channel_id=1, source_target_pairs={{0,32},{8,40},{16,48},{24,56},{32,0},{40,8},{48,16},{56,24},{1,33}... | collective-permute-start | bytes 393224 | tf_op jit(solution)/shard_map/ppermute | solution.py:466
  40.2 32.8 %collective-permute-start.3 = (bf16[192,1024]{1,0:T(8,128)(2,1)}, bf16[192,1024]{1,0:T(8,128)(2,1)S(1)}, u32[]{:S(2)}, u32[]{:S(2)}) collective-permute-start(bf16[192,1024]{1,0:T(8,128)(2,1)} %get-tuple-element.14), channel_id=1, source_target_pairs={{0,56},{8,0},{16,8},{24,16},{32,24},{40,32},{48,40},{56,48},{1,57}... | collective-permute-start | bytes 1179656 | tf_op jit(solution)/shard_map/ppermute | solution.py:468
  47.8 25.2 %collective-permute-start.4 = (bf16[192,1024]{1,0:T(8,128)(2,1)}, bf16[192,1024]{1,0:T(8,128)(2,1)S(1)}, u32[]{:S(2)}, u32[]{:S(2)}) collective-permute-start(bf16[192,1024]{1,0:T(8,128)(2,1)} %get-tuple-element.15), channel_id=1, source_target_pairs={{0,8},{8,16},{16,24},{24,32},{32,40},{40,48},{48,56},{56,0},{1,9},... | collective-permute-start | bytes 1179656 | tf_op jit(solution)/shard_map/ppermute | solution.py:469
  56.4 30.0 %all-to-all-start.1 = ((bf16[8,384,128]{2,1,0:T(8,128)(2,1)}), bf16[8,384,128]{2,1,0:T(8,128)(2,1)S(1)}, u32[]{:S(2)}, u32[]{:S(2)}) async-start(bf16[8,384,128]{2,1,0:T(8,128)(2,1)} %relax.1), calls=%async_computation.1 | async-start | bytes 1572864 | tf_op jit(solution)/shard_map/all_to_all | solution.py:474
  61.8 11.1 %collective-permute-start.5 = (bf16[128,1024]{1,0:T(8,128)(2,1)S(1)}, bf16[128,1024]{1,0:T(8,128)(2,1)S(1)}, u32[]{:S(2)}, u32[]{:S(2)}) collective-permute-start(bf16[128,1024]{1,0:T(8,128)(2,1)S(1)} %constant_dynamic-update-slice_fusion.held_ref), channel_id=1, source_target_pairs={{0,16},{8,56},{16,32},{24,8},{32,48},{40,24},{48,0},{56,40},{1,17}... | collective-permute-start | bytes 786440 | tf_op jit(solution)/shard_map/ppermute | solution.py:470
  74.0 4.9 %collective-permute-start.6 = (bf16[528,1024]{1,0:T(8,128)(2,1)}, bf16[528,1024]{1,0:T(8,128)(2,1)}, u32[]{:S(2)}, u32[]{:S(2)}) collective-permute-start(bf16[528,1024]{1,0:T(8,128)(2,1)} %join.1.own_hbm), channel_id=1, source_target_pairs={{0,1},{1,0},{2,3},{3,2},{4,5},{5,4},{6,7},{7,6},{8,9},{9,8},{10,11... | collective-permute-start | bytes 3244040 | tf_op jit(solution)/shard_map/ppermute | solution.py:473

commit v13 on v11

--- a/solution.py
+++ b/solution.py
@@ -433,6 +433,7 @@
     across = lax.ppermute(held, "sx", [(i, (i + 2) % 8 if i % 2 == 0 else (i - 2) % 8) for i in range(8)])
     outer = lax.ppermute(outer, "sy", [(i, (i + 1) % 8 if i % 2 else (i - 1) % 8) for i in range(8)])
     send = relax(place, got, spread(depth_weights))
+    send, outer = lax.optimization_barrier((send, outer))
     own = join(held, above, below, across, inner)
     other = lax.ppermute(own, "sy", flip(1))
     back = lax.all_to_all(send, "vel", 0, 0, tiled=True)

time: 87.3 us -> 93.8 us (1.074)
  the two profiles are of different devices: /device:TPU:56 before, /device:TPU:65 now
where the time goes in v13:
time: 93.8 us; the launch traced here: 93.1 us
  starting transfers between devices  54.9 us (59%)
  waiting for transfers between devices  24.4 us (26%)
  Pallas kernels  12.8 us (14%)
    all_to_all x1, starting transfers between devices, local(): got = lax.all_to_all(send, 'vel', 0, 0, tiled=True)  9.91 us
    all_to_all x1, starting transfers between devices, local(): back = lax.all_to_all(send, 'vel', 0, 0, tiled=True)  9.46 us
    ppermute x1, waiting for transfers between devices, local(): lax.ppermute(held, 'sx', [(i, (i + 2) % 8 if i % 2 == 0 else (i - 2) % 8)...  9.28 us
    ppermute x1, starting transfers between devices, local(): held = jnp.concatenate([held, lax.ppermute(held, 'sx', flip(4))])  7.45 us
    all_to_all x1, waiting for transfers between devices, local(): back = lax.all_to_all(send, 'vel', 0, 0, tiled=True)  7.17 us
    ppermute x1, starting transfers between devices, local(): lax.ppermute(outer, 'sy', [(i, (i + 1) % 8 if i % 2 else (i - 1) % 8) for...  6.76 us
    ppermute x1, starting transfers between devices, local(): above = lax.ppermute(low, 'sx', ring('sx', -1))  6.22 us
    ppermute x1, starting transfers between devices, local(): held = jnp.concatenate([held, lax.ppermute(held, 'sy', flip(4))])  5.8 us
  transfers between devices with their start and end apart: 10, of which 5 were waited for; matrix products, arithmetic and copies ran while one was open for 0% of the time, Pallas kernels for 8%

profile of v13, /device:TPU:65, one launch (start us, length us, event | category | flops | bytes accessed | tf_op | source)
XLA Modules:
  0.0 93.1 jit_solution(12451233148444281858)
XLA Ops:
  0.0 0.0 copy-start.2
  0.0 2.0 %collective-permute-start = (bf16[16,1024]{1,0:T(8,128)(2,1)}, bf16[16,1024]{1,0:T(8,128)(2,1)S(1)}, u32[]{:S(2)}, u32[]{:S(2)}) collective-permute-start(bf16[16,1024]{1,0:T(8,128)(2,1)} %param.5), channel_id=1, source_target_pairs={{0,2},{1,3},{2,0},{3,1},{4,6},{5,7},{6,4},{7,5},{8,10},{9,11},{10,... | collective-permute-start | bytes 98312 | tf_op jit(solution)/shard_map/ppermute | solution.py:425
  2.0 2.9 %collective-permute-done = bf16[16,1024]{1,0:T(8,128)(2,1)S(1)} collective-permute-done((bf16[16,1024]{1,0:T(8,128)(2,1)}, bf16[16,1024]{1,0:T(8,128)(2,1)S(1)}, u32[]{:S(2)}, u32[]{:S(2)}) %collective-permute-start) | collective-permute-done | bytes 32800 | tf_op jit(solution)/shard_map/ppermute | solution.py:425
  5.0 0.8 pad_maximum_fusion.1
  5.8 5.8 %collective-permute-start.1 = (bf16[32,1024]{1,0:T(8,128)(2,1)S(1)}, bf16[32,1024]{1,0:T(8,128)(2,1)S(1)}, u32[]{:S(2)}, u32[]{:S(2)}) collective-permute-start(bf16[32,1024]{1,0:T(8,128)(2,1)S(1)} %pad_maximum_fusion.1), channel_id=1, source_target_pairs={{0,4},{1,5},{2,6},{3,7},{4,0},{5,1},{6,2},{7,3},{8,12},{9,13},{10,... | collective-permute-start | bytes 196616 | tf_op jit(solution)/shard_map/ppermute | solution.py:426
  11.6 2.8 %pack.1 = bf16[8,400,128]{2,1,0:T(8,128)(2,1)} custom-call(s32[1]{0:T(128)} %bitcast.2.place_ref, bf16[3,32,4096]{2,1,0:T(8,128)(2,1)} %f_hbm.1, bf16[1024,128]{1,0:T(8,128)(2,1)} %constant.15.clone.basis_ref), custom_call_target="tpu_custom_call" | custom-call | tf_op jit(solution)/shard_map/pack/pallas_call | solution.py:122
  14.4 0.0 collective-permute-done.1
  14.4 0.0 copy-done.2
  14.4 0.0 copy-start
  14.5 9.9 %all-to-all-start = ((bf16[8,400,128]{2,1,0:T(8,128)(2,1)}), bf16[8,400,128]{2,1,0:T(8,128)(2,1)S(1)}, u32[]{:S(2)}, u32[]{:S(2)}) async-start(bf16[8,400,128]{2,1,0:T(8,128)(2,1)} %pack.1), calls=%async_computation | async-start | bytes 1638400 | tf_op jit(solution)/shard_map/all_to_all | solution.py:428
  24.4 0.0 copy-start.1
  24.4 7.5 %collective-permute-start.2 = (bf16[64,1024]{1,0:T(8,128)(2,1)S(1)}, bf16[64,1024]{1,0:T(8,128)(2,1)S(1)}, u32[]{:S(2)}, u32[]{:S(2)}) collective-permute-start(bf16[64,1024]{1,0:T(8,128)(2,1)S(1)} %pad_maximum_fusion), channel_id=1, source_target_pairs={{0,32},{8,40},{16,48},{24,56},{32,0},{40,8},{48,16},{56,24},{1,33}... | collective-permute-start | bytes 393224 | tf_op jit(solution)/shard_map/ppermute | solution.py:429
  31.9 2.4 %collective-permute-done.2 = bf16[64,1024]{1,0:T(8,128)(2,1)S(1)} collective-permute-done((bf16[64,1024]{1,0:T(8,128)(2,1)S(1)}, bf16[64,1024]{1,0:T(8,128)(2,1)S(1)}, u32[]{:S(2)}, u32[]{:S(2)}) %collective-permute-start.2) | collective-permute-done | bytes 131104 | tf_op jit(solution)/shard_map/ppermute | solution.py:429
  34.3 0.0 copy-done
  34.3 1.0 %edges.1 = (bf16[192,1024]{1,0:T(8,128)(2,1)}, bf16[192,1024]{1,0:T(8,128)(2,1)}, bf16[16,1024]{1,0:T(8,128)(2,1)S(1)}, bf16[16,1024]{1,0:T(8,128)(2,1)S(1)}) custom-call(s32[1]{0:T(128)} %bitcast.3.core_ref, bf16[128,1024]{1,0:T(8,128)(2,1)S(1)} %constant_dynamic-update-slice_fusion.held_ref, bf16[3,32,4096]{2,1,0:T(8,128)(2,1)S(1)} %copy-done), custom_call_target="tpu_custom_call" | custom-call | tf_op jit(solution)/shard_map/edges/pallas_call | solution.py:168
  35.3 6.2 %collective-permute-start.4 = (bf16[192,1024]{1,0:T(8,128)(2,1)}, bf16[192,1024]{1,0:T(8,128)(2,1)S(1)}, u32[]{:S(2)}, u32[]{:S(2)}) collective-permute-start(bf16[192,1024]{1,0:T(8,128)(2,1)} %get-tuple-element.17), channel_id=1, source_target_pairs={{0,56},{8,0},{16,8},{24,16},{32,24},{40,32},{48,40},{56,48},{1,57}... | collective-permute-start | bytes 1179656 | tf_op jit(solution)/shard_map/ppermute | solution.py:431
  41.5 1.9 %collective-permute-start.5 = (bf16[192,1024]{1,0:T(8,128)(2,1)}, bf16[192,1024]{1,0:T(8,128)(2,1)S(1)}, u32[]{:S(2)}, u32[]{:S(2)}) collective-permute-start(bf16[192,1024]{1,0:T(8,128)(2,1)} %get-tuple-element.18), channel_id=1, source_target_pairs={{0,8},{8,16},{16,24},{24,32},{32,40},{40,48},{48,56},{56,0},{1,9},... | collective-permute-start | bytes 1179656 | tf_op jit(solution)/shard_map/ppermute | solution.py:432
  43.4 6.8 %collective-permute-start.3 = (bf16[16,1024]{1,0:T(8,128)(2,1)S(1)}, bf16[16,1024]{1,0:T(8,128)(2,1)S(1)}, u32[]{:S(2)}, u32[]{:S(2)}) collective-permute-start(bf16[16,1024]{1,0:T(8,128)(2,1)S(1)} %get-tuple-element.15), channel_id=1, source_target_pairs={{0,7},{1,2},{2,1},{3,4},{4,3},{5,6},{6,5},{7,0},{8,15},{9,10},{10,... | collective-permute-start | bytes 98312 | tf_op jit(solution)/shard_map/ppermute | solution.py:434
  50.2 0.0 copy-done.1
  50.2 0.4 spread.1.mix_ref
  50.6 0.0 all-to-all-done.got_ref
  50.6 2.3 %relax.1 = bf16[8,384,128]{2,1,0:T(8,128)(2,1)} custom-call(s32[1]{0:T(128)} %bitcast.2.place_ref, bf16[8,400,128]{2,1,0:T(8,128)(2,1)S(1)} %all-to-all-done.got_ref, bf16[512,512]{1,0:T(8,128)(2,1)S(1)} %spread.1.mix_ref), custom_call_target="tpu_custom_call" | custom-call | tf_op jit(solution)/shard_map/relax/pallas_call | solution.py:272
  52.9 0.0 collective-permute-done.3.outer_hbm
  52.9 9.5 %all-to-all-start.1 = ((bf16[8,384,128]{2,1,0:T(8,128)(2,1)}), bf16[8,384,128]{2,1,0:T(8,128)(2,1)S(1)}, u32[]{:S(2)}, u32[]{:S(2)}) async-start(bf16[8,384,128]{2,1,0:T(8,128)(2,1)} %relax.1), calls=%async_computation.1 | async-start | bytes 1572864 | tf_op jit(solution)/shard_map/all_to_all | solution.py:439
  62.4 2.8 %collective-permute-start.6 = (bf16[128,1024]{1,0:T(8,128)(2,1)S(1)}, bf16[128,1024]{1,0:T(8,128)(2,1)S(1)}, u32[]{:S(2)}, u32[]{:S(2)}) collective-permute-start(bf16[128,1024]{1,0:T(8,128)(2,1)S(1)} %constant_dynamic-update-slice_fusion.held_ref), channel_id=1, source_target_pairs={{0,16},{8,56},{16,32},{24,8},{32,48},{40,24},{48,0},{56,40},{1,17}... | collective-permute-start | bytes 786440 | tf_op jit(solution)/shard_map/ppermute | solution.py:433
  65.1 9.3 %collective-permute-done.6.across_ref = bf16[128,1024]{1,0:T(8,128)(2,1)S(1)} collective-permute-done((bf16[128,1024]{1,0:T(8,128)(2,1)S(1)}, bf16[128,1024]{1,0:T(8,128)(2,1)S(1)}, u32[]{:S(2)}, u32[]{:S(2)}) %collective-permute-start.6) | collective-permute-done | bytes 262176 | tf_op jit(solution)/shard_map/ppermute | solution.py:433
  74.4 0.0 collective-permute-done.4.above_ref.above_hbm
  74.4 0.0 collective-permute-done.5.below_ref.below_hbm
  74.4 1.0 %join.1.own_hbm = bf16[528,1024]{1,0:T(8,128)(2,1)} custom-call(bf16[128,1024]{1,0:T(8,128)(2,1)S(1)} %constant_dynamic-update-slice_fusion.held_ref, bf16[192,1024]{1,0:T(8,128)(2,1)S(1)} %collective-permute-done.4.above_ref.above_hbm, bf16[192,1024]{1,0:T(8,128)(2,1)S(1)} %collective-permute-done.5.below_ref.below_hbm, ...), custom_call_target="tpu_custom_call" | custom-call | tf_op jit(solution)/shard_map/join/pallas_call | solution.py:197
  75.5 2.6 %collective-permute-start.7 = (bf16[528,1024]{1,0:T(8,128)(2,1)}, bf16[528,1024]{1,0:T(8,128)(2,1)}, u32[]{:S(2)}, u32[]{:S(2)}) collective-permute-start(bf16[528,1024]{1,0:T(8,128)(2,1)} %join.1.own_hbm), channel_id=1, source_target_pairs={{0,1},{1,0},{2,3},{3,2},{4,5},{5,4},{6,7},{7,6},{8,9},{9,8},{10,11... | collective-permute-start | bytes 3244040 | tf_op jit(solution)/shard_map/ppermute | solution.py:438
  78.1 0.1 pad_add_fusion.where_ref
  78.1 2.6 %collective-permute-done.7.other_hbm = bf16[528,1024]{1,0:T(8,128)(2,1)} collective-permute-done((bf16[528,1024]{1,0:T(8,128)(2,1)}, bf16[528,1024]{1,0:T(8,128)(2,1)}, u32[]{:S(2)}, u32[]{:S(2)}) %collective-permute-start.7) | collective-permute-done | bytes 1081376 | tf_op jit(solution)/shard_map/ppermute | solution.py:438
  80.7 7.2 %all-to-all-done.1.back_hbm = bf16[8,384,128]{2,1,0:T(8,128)(2,1)S(1)} async-done(((bf16[8,384,128]{2,1,0:T(8,128)(2,1)}), bf16[8,384,128]{2,1,0:T(8,128)(2,1)S(1)}, u32[]{:S(2)}, u32[]{:S(2)}) %all-to-all-start.1) | async-done | bytes 786464 | tf_op jit(solution)/shard_map/all_to_all | solution.py:439
  87.9 5.2 %advance.1 = bf16[3,32,4096]{2,1,0:T(8,128)(2,1)} custom-call(s32[2]{0:T(128)S(1)} %pad_add_fusion.where_ref, bf16[3,32,4096]{2,1,0:T(8,128)(2,1)S(1)} %copy-done, bf16[8,384,128]{2,1,0:T(8,128)(2,1)S(1)} %all-to-all-done.1.back_hbm, bf16[528,1024]{1,0:T(8,128)(2,1)} %join.1.own_hbm, bf16[528,1024]{1,0:T(8,128)(2,1)} %collective-permute-done.7.other_hbm, ...), custom_call_target="tpu_custom_call" | custom-call | tf_op jit(solution)/shard_map/advance/pallas_call | solution.py:391
  (3 shorter events, 0.0 us)
Async XLA Ops:
  0.0 14.4 %copy-start.2 = (bf16[16,1024]{1,0:T(8,128)(2,1)S(1)}, bf16[16,1024]{1,0:T(8,128)(2,1)}, u32[]{:S(2)}) copy-start(bf16[16,1024]{1,0:T(8,128)(2,1)} %param.5) | copy-start | bytes 98308
  0.0 5.0 %collective-permute-start = (bf16[16,1024]{1,0:T(8,128)(2,1)}, bf16[16,1024]{1,0:T(8,128)(2,1)S(1)}, u32[]{:S(2)}, u32[]{:S(2)}) collective-permute-start(bf16[16,1024]{1,0:T(8,128)(2,1)} %param.5), channel_id=1, source_target_pairs={{0,2},{1,3},{2,0},{3,1},{4,6},{5,7},{6,4},{7,5},{8,10},{9,11},{10,... | collective-permute-start | bytes 98312 | tf_op jit(solution)/shard_map/ppermute | solution.py:425
  5.8 8.7 %collective-permute-start.1 = (bf16[32,1024]{1,0:T(8,128)(2,1)S(1)}, bf16[32,1024]{1,0:T(8,128)(2,1)S(1)}, u32[]{:S(2)}, u32[]{:S(2)}) collective-permute-start(bf16[32,1024]{1,0:T(8,128)(2,1)S(1)} %pad_maximum_fusion.1), channel_id=1, source_target_pairs={{0,4},{1,5},{2,6},{3,7},{4,0},{5,1},{6,2},{7,3},{8,12},{9,13},{10,... | collective-permute-start | bytes 196616 | tf_op jit(solution)/shard_map/ppermute | solution.py:426
  14.4 19.8 %copy-start = (bf16[3,32,4096]{2,1,0:T(8,128)(2,1)S(1)}, bf16[3,32,4096]{2,1,0:T(8,128)(2,1)}, u32[]{:S(2)}) copy-start(bf16[3,32,4096]{2,1,0:T(8,128)(2,1)} %f_hbm.1) | copy-start | bytes 2359300
  14.5 36.2 %all-to-all-start = ((bf16[8,400,128]{2,1,0:T(8,128)(2,1)}), bf16[8,400,128]{2,1,0:T(8,128)(2,1)S(1)}, u32[]{:S(2)}, u32[]{:S(2)}) async-start(bf16[8,400,128]{2,1,0:T(8,128)(2,1)} %pack.1), calls=%async_computation | async-start | bytes 1638400 | tf_op jit(solution)/shard_map/all_to_all | solution.py:428
  24.4 25.8 %copy-start.1 = (bf16[32,32]{1,0:T(8,128)(2,1)S(1)}, bf16[32,32]{1,0:T(8,128)(2,1)}, u32[]{:S(2)}) copy-start(bf16[32,32]{1,0:T(8,128)(2,1)} %depth_ref.1) | copy-start | bytes 6148
  24.4 9.9 %collective-permute-start.2 = (bf16[64,1024]{1,0:T(8,128)(2,1)S(1)}, bf16[64,1024]{1,0:T(8,128)(2,1)S(1)}, u32[]{:S(2)}, u32[]{:S(2)}) collective-permute-start(bf16[64,1024]{1,0:T(8,128)(2,1)S(1)} %pad_maximum_fusion), channel_id=1, source_target_pairs={{0,32},{8,40},{16,48},{24,56},{32,0},{40,8},{48,16},{56,24},{1,33}... | collective-permute-start | bytes 393224 | tf_op jit(solution)/shard_map/ppermute | solution.py:429
  35.3 39.1 %collective-permute-start.4 = (bf16[192,1024]{1,0:T(8,128)(2,1)}, bf16[192,1024]{1,0:T(8,128)(2,1)S(1)}, u32[]{:S(2)}, u32[]{:S(2)}) collective-permute-start(bf16[192,1024]{1,0:T(8,128)(2,1)} %get-tuple-element.17), channel_id=1, source_target_pairs={{0,56},{8,0},{16,8},{24,16},{32,24},{40,32},{48,40},{56,48},{1,57}... | collective-permute-start | bytes 1179656 | tf_op jit(solution)/shard_map/ppermute | solution.py:431
  41.5 32.9 %collective-permute-start.5 = (bf16[192,1024]{1,0:T(8,128)(2,1)}, bf16[192,1024]{1,0:T(8,128)(2,1)S(1)}, u32[]{:S(2)}, u32[]{:S(2)}) collective-permute-start(bf16[192,1024]{1,0:T(8,128)(2,1)} %get-tuple-element.18), channel_id=1, source_target_pairs={{0,8},{8,16},{16,24},{24,32},{32,40},{40,48},{48,56},{56,0},{1,9},... | collective-permute-start | bytes 1179656 | tf_op jit(solution)/shard_map/ppermute | solution.py:432
  43.4 9.5 %collective-permute-start.3 = (bf16[16,1024]{1,0:T(8,128)(2,1)S(1)}, bf16[16,1024]{1,0:T(8,128)(2,1)S(1)}, u32[]{:S(2)}, u32[]{:S(2)}) collective-permute-start(bf16[16,1024]{1,0:T(8,128)(2,1)S(1)} %get-tuple-element.15), channel_id=1, source_target_pairs={{0,7},{1,2},{2,1},{3,4},{4,3},{5,6},{6,5},{7,0},{8,15},{9,10},{10,... | collective-permute-start | bytes 98312 | tf_op jit(solution)/shard_map/ppermute | solution.py:434
  52.9 35.0 %all-to-all-start.1 = ((bf16[8,384,128]{2,1,0:T(8,128)(2,1)}), bf16[8,384,128]{2,1,0:T(8,128)(2,1)S(1)}, u32[]{:S(2)}, u32[]{:S(2)}) async-start(bf16[8,384,128]{2,1,0:T(8,128)(2,1)} %relax.1), calls=%async_computation.1 | async-start | bytes 1572864 | tf_op jit(solution)/shard_map/all_to_all | solution.py:439
  62.4 12.0 %collective-permute-start.6 = (bf16[128,1024]{1,0:T(8,128)(2,1)S(1)}, bf16[128,1024]{1,0:T(8,128)(2,1)S(1)}, u32[]{:S(2)}, u32[]{:S(2)}) collective-permute-start(bf16[128,1024]{1,0:T(8,128)(2,1)S(1)} %constant_dynamic-update-slice_fusion.held_ref), channel_id=1, source_target_pairs={{0,16},{8,56},{16,32},{24,8},{32,48},{40,24},{48,0},{56,40},{1,17}... | collective-permute-start | bytes 786440 | tf_op jit(solution)/shard_map/ppermute | solution.py:433
  75.5 5.2 %collective-permute-start.7 = (bf16[528,1024]{1,0:T(8,128)(2,1)}, bf16[528,1024]{1,0:T(8,128)(2,1)}, u32[]{:S(2)}, u32[]{:S(2)}) collective-permute-start(bf16[528,1024]{1,0:T(8,128)(2,1)} %join.1.own_hbm), channel_id=1, source_target_pairs={{0,1},{1,0},{2,3},{3,2},{4,5},{5,4},{6,7},{7,6},{8,9},{9,8},{10,11... | collective-permute-start | bytes 3244040 | tf_op jit(solution)/shard_map/ppermute | solution.py:438
